TPU v7x, 256 devices: a whole 4x4x8 slice. The times are simulated.
256 devices in a mesh: section: 4 (over x), dp: 64 (over z, y, core).
Axes of the slice: x: 4, y: 4, z: 8, core: 2. Of those that a mesh axis runs over, the one named last changes fastest.
Arguments:
- out_grad: bfloat16 [8192, 5120], P('dp', 'section'), may hold values from -0.26367188 to 0.26367188
- pre_act: bfloat16 [4, 8192, 27648], P('section', 'dp'), may hold values from -6 to 6
- down_a: bfloat16 [4, 27648, 32], P('section'), may hold values from -1 to 1
- down_b: bfloat16 [4, 32, 5120], P('section'), may hold values from -0.078125 to 0.078125
- up_a: bfloat16 [4, 5120, 32], P('section'), may hold values from -1 to 1
- up_b: bfloat16 [4, 27648, 32], P('section'), may hold values from -0.0390625 to 0.0390625
- master: float32 [4, 4, 6912, 32], P('section', None, 'dp'), may hold values from -1 to 1
- moment: float32 [4, 4, 6912, 32], P('section', None, 'dp'), may hold values from -3 to 3
- second: float32 [4, 4, 6912, 32], P('section', None, 'dp'), may hold values from 0.2 to 4
Outputs:
- new_weight: bfloat16 [4, 27648, 32], P('section')
- new_master: float32 [4, 4, 6912, 32], P('section', None, 'dp')
- new_moment: float32 [4, 4, 6912, 32], P('section', None, 'dp')
- new_second: float32 [4, 4, 6912, 32], P('section', None, 'dp')
All inputs are finite; a program needn't handle non-finite values.
Results may differ from a plain program's by a relative error of at most 0.014.
Values may be sent and summed in bfloat16 or wider, within the bound.
No kernel may reach another device: no remote copies, remote signals or barrier semaphores. Data moves between devices by JAX's collectives and lax.ppermute only.
A program may use at most 128 MiB of HBM per device.

v0:
```python
import jax
import jax.numpy as jnp
from jax import lax
from jax.sharding import PartitionSpec as P

BUCKETS = 4
STEP = 20


BETA_ONE = 0.8
BETA_TWO = 0.95
LEARN_RATE = 0.02
DECAY_RATE = 0.1
EPSILON = 1e-08


def shifted(value, axis, steps):
    count = lax.axis_size(axis)
    initial, last = (max(0, -steps), min(count, count - steps))
    return lax.ppermute(value, axis, [(source, source + steps) for source in range(initial, last)])


def slope_of(values):
    sigm = jax.nn.sigmoid(values)
    return sigm * (1.0 + values * (1.0 - sigm))


def adamw(gradient, weights, first, seconds):
    first_new = BETA_ONE * first + (1.0 - BETA_ONE) * gradient
    second_new = BETA_TWO * seconds + (1.0 - BETA_TWO) * gradient * gradient
    first_hat = first_new / (1.0 - BETA_ONE**STEP)
    second_hat = second_new / (1.0 - BETA_TWO**STEP)
    weights_new = weights - LEARN_RATE * (
        first_hat / (jnp.sqrt(second_hat) + EPSILON) + DECAY_RATE * weights
    )
    return (weights_new, first_new, second_new)


def per_device(out_grad, pre_act, down_a, down_b, up_a, up_b, master, moment, second):
    top_grad = lax.all_gather(out_grad, "section", axis=1, tiled=True)
    section_pos = lax.axis_index("section")
    section_count = lax.axis_size("section")
    inputs = pre_act[0].astype(jnp.float32)
    hidden = jax.nn.silu(inputs).astype(jnp.bfloat16)
    slopes = slope_of(inputs)
    factor_a = down_a[0]
    factor_b = down_b[0]
    entry_a = up_a[0]
    entry_b = up_b[0]
    contract_last = (((1,), (1,)), ((), ()))

    def project_low(incoming):
        return lax.dot_general(
            incoming, factor_b, contract_last, preferred_element_type=jnp.float32
        ).astype(jnp.bfloat16)

    current = top_grad
    own_grad = jnp.zeros_like(top_grad)
    for step_index in range(section_count):
        active = section_count - 1 - step_index
        own_grad = jnp.where(section_pos == active, current, own_grad)
        if step_index < section_count - 1:
            low = project_low(current)
            upstream = lax.dot_general(
                low, factor_a, contract_last, preferred_element_type=jnp.float32
            )
            delta = (upstream * slopes).astype(jnp.bfloat16)
            back_low = jnp.dot(delta, entry_b, preferred_element_type=jnp.float32).astype(
                jnp.bfloat16
            )
            carried = lax.dot_general(
                back_low, entry_a, contract_last, preferred_element_type=jnp.float32
            )
            emitted = (current.astype(jnp.float32) + carried).astype(jnp.bfloat16)
            current = shifted(emitted, "section", -1)
    own_low = project_low(own_grad)
    rows_owned = master.shape[2]
    bucket_rows = rows_owned * lax.axis_size("dp")
    contract_first = (((0,), (0,)), ((), ()))
    masters_list = []
    moments_list = []
    seconds_list = []
    pieces = []
    for bucket in range(BUCKETS):
        offset = bucket * bucket_rows

        def bucket_term(start, count, offset=offset):
            columns = lax.dynamic_slice_in_dim(hidden, offset, count, 1)
            return lax.dot_general(
                columns, own_low, contract_first, preferred_element_type=jnp.float32
            )

        shard_grad = lax.psum_scatter(
            bucket_term(jnp.int32(0), rows_owned * lax.axis_size("dp")),
            "dp",
            scatter_dimension=0,
            tiled=True,
        )
        weights_new, first_new, second_new = adamw(
            shard_grad, master[0, bucket], moment[0, bucket], second[0, bucket]
        )
        masters_list.append(weights_new)
        moments_list.append(first_new)
        seconds_list.append(second_new)
        pieces.append(lax.all_gather(weights_new.astype(jnp.bfloat16), "dp", axis=0, tiled=True))
    weights_new = jnp.stack(masters_list)
    first_new = jnp.stack(moments_list)
    second_new = jnp.stack(seconds_list)
    weight_rows = jnp.concatenate(pieces, axis=0)
    return (weight_rows[None], weights_new[None], first_new[None], second_new[None])


def solution(mesh):
    return jax.shard_map(
        per_device,
        mesh=mesh,
        in_specs=(
            P("dp", "section"),
            P("section", "dp", None),
            P("section", None, None),
            P("section", None, None),
            P("section", None, None),
            P("section", None, None),
            P("section", None, "dp", None),
            P("section", None, "dp", None),
            P("section", None, "dp", None),
        ),
        out_specs=(
            P("section", None, None),
            P("section", None, "dp", None),
            P("section", None, "dp", None),
            P("section", None, "dp", None),
        ),
        check_vma=False,
    )
```

profile of v0, /device:TPU:1, one launch (start us, length us, event | category | flops | bytes accessed | tf_op | source)
XLA Modules:
  0.0 589.8 jit_solution(13049837904330362056)
XLA Ops:
  7.2 0.0 copy-start
  7.2 0.0 all-gather.6.cloned.1.call-start
  7.2 0.7 all-gather.6.cloned.1.call-update
  7.9 0.0 all-reduce.7.cloned.1.call-start
  8.0 31.9 %all-gather.6.cloned.1.call-done = bf16[128,5120]{1,0:T(8,128)(2,1)} async-done(((bf16[128,1280]{1,0:T(8,128)(2,1)}), bf16[128,5120]{1,0:T(8,128)(2,1)}) %all-gather.6.cloned.1.call-update) | async-done | bytes 1310736 | tf_op jit(solution)/shard_map/all_gather | solution.py:40
  39.9 1.9 convolution_convert_fusion.2
  41.8 0.0 copy-done
  41.8 0.0 copy-start.2
  41.8 10.0 %fusion.42 = bf16[128,32]{0,1:T(8,128)(2,1)S(1)} fusion(bf16[1,27648,32]{1,2,0:T(8,128)(2,1)S(1)} %copy-done, bf16[128,32]{0,1:T(8,128)(2,1)S(1)} %convolution_convert_fusion.2, bf16[1,27648,32]{1,2,0:T(8,128)(2,1)} %param.11, bf16[1,128,27648]{2,1,0:T(8,128)(2,1)} %param.10), kind=kOutput, calls=%fused_computation.50 | convolution fusion | flops 488378368 | bytes 10633216 | tf_op jit(solution)/shard_map/dot_general | solution.py:68
  51.8 0.1 copy-done.2
  51.9 0.0 copy-start.5
  51.9 1.5 fusion.9
  53.4 1.8 collective-permute-start
  55.2 28.5 %collective-permute-done = bf16[128,5120]{1,0:T(8,128)(2,1)S(1)} collective-permute-done((bf16[128,5120]{1,0:T(8,128)(2,1)S(1)}, bf16[128,5120]{1,0:T(8,128)(2,1)S(1)}, u32[]{:S(2)}, u32[]{:S(2)}) %collective-permute-start) | collective-permute-done | bytes 1310752 | tf_op jit(solution)/shard_map/ppermute | solution.py:20
  83.7 0.0 copy-start.3
  83.7 1.1 copy-done.3
  84.8 0.0 copy-done.5
  84.8 0.5 convolution_convert_fusion.1
  85.3 9.9 %fusion.47 = bf16[128,32]{0,1:T(8,128)(2,1)S(1)} fusion(bf16[1,27648,32]{1,2,0:T(8,128)(2,1)S(1)} %copy-done, bf16[128,32]{0,1:T(8,128)(2,1)S(1)} %convolution_convert_fusion.1, bf16[1,27648,32]{1,2,0:T(8,128)(2,1)} %param.11, bf16[1,128,27648]{2,1,0:T(8,128)(2,1)} %param.10), kind=kOutput, calls=%fused_computation.51 | convolution fusion | flops 488378368 | bytes 10633216 | tf_op jit(solution)/shard_map/dot_general | solution.py:68
  95.2 2.0 add_convert_fusion.1
  97.2 1.5 collective-permute-start.1
  98.7 28.7 %collective-permute-done.1 = bf16[128,5120]{1,0:T(8,128)(2,1)S(1)} collective-permute-done((bf16[128,5120]{1,0:T(8,128)(2,1)S(1)}, bf16[128,5120]{1,0:T(8,128)(2,1)S(1)}, u32[]{:S(2)}, u32[]{:S(2)}) %collective-permute-start.1) | collective-permute-done | bytes 1310752 | tf_op jit(solution)/shard_map/ppermute | solution.py:20
  127.5 0.0 copy-start.4
  127.5 1.1 copy-done.4
  128.6 0.5 convolution_convert_fusion
  129.1 9.9 %fusion.52 = bf16[128,32]{0,1:T(8,128)(2,1)S(1)} fusion(bf16[1,27648,32]{1,2,0:T(8,128)(2,1)S(1)} %copy-done, bf16[128,32]{0,1:T(8,128)(2,1)S(1)} %convolution_convert_fusion, bf16[1,27648,32]{1,2,0:T(8,128)(2,1)} %param.11, bf16[1,128,27648]{2,1,0:T(8,128)(2,1)} %param.10), kind=kOutput, calls=%fused_computation.52 | convolution fusion | flops 488378368 | bytes 10633216 | tf_op jit(solution)/shard_map/dot_general | solution.py:68
  139.0 3.1 add_convert_fusion
  142.1 1.5 collective-permute-start.2
  143.6 9.6 %fusion.6 = bf16[128,27648]{1,0:T(8,128)(2,1)} fusion(bf16[1,128,27648]{2,1,0:T(8,128)(2,1)} %param.10), kind=kLoop, calls=%fused_computation.12 | loop fusion | flops 21233664 | bytes 14155776 | tf_op jit(solution)/shard_map/convert_element_type | solution.py:44
  153.2 0.0 copy-start.1
  153.2 18.8 %collective-permute-done.2 = bf16[128,5120]{1,0:T(8,128)(2,1)} collective-permute-done((bf16[128,5120]{1,0:T(8,128)(2,1)}, bf16[128,5120]{1,0:T(8,128)(2,1)}, u32[]{:S(2)}, u32[]{:S(2)}) %collective-permute-start.2) | collective-permute-done | bytes 1310752 | tf_op jit(solution)/shard_map/ppermute | solution.py:20
  172.0 1.8 fusion.39
  173.8 0.0 copy-done.1
  173.9 1.3 fusion.13
  175.1 1.3 fusion.15
  176.4 1.3 fusion.17
  177.8 0.0 copy-start.9
  177.8 0.0 copy-start.6
  177.8 0.0 copy-start.7
  177.8 1.3 fusion.19
  179.1 0.0 all-reduce.7.cloned.1.call-update
  179.1 0.0 copy-done.9
  179.1 0.6 dynamic-slice
  180.3 194.7 %all-reduce.7.cloned.1.call-done = (f32[6912,32]{0,1:T(8,128)}, f32[6912,32]{0,1:T(8,128)}, f32[6912,32]{0,1:T(8,128)}, f32[6912,32]{0,1:T(8,128)}) async-done(((f32[6912,32]{0,1:T(8,128)}, f32[6912,32]{0,1:T(8,128)}, f32[6912,32]{0,1:T(8,128)}, f32[6912,32]{0,1:T(8,128)}), (f32[6912,32]{0,1:T(8,128)}, f32[6912,32]{0,1:T(8,128)}, f32[6912,32]{0,1:T(8,128)}, ...) | async-done | bytes 3538960
  375.1 0.0 copy-done.6
  375.1 0.0 copy-done.7
  375.1 0.0 copy-done.8
  375.1 0.9 convert_bitcast_fusion.3
  375.9 0.9 convert_bitcast_fusion
  376.9 50.7 %all-gather.1 = bf16[64,108,32]{1,2,0:T(8,128)(2,1)S(1)} all-gather(bf16[1,108,32]{1,2,0:T(8,128)(2,1)S(1)} %get-tuple-element.30), channel_id=1, replica_groups=mesh['section'=4,'dp'=64] {'dp'}, dimensions={0}, use_global_device_ids=true | all-gather | bytes 449280 | tf_op jit(solution)/shard_map/all_gather | solution.py:105
  427.6 0.2 copy.18
  427.8 0.8 reshape.30
  428.6 48.8 %all-gather.2 = bf16[64,108,32]{1,2,0:T(8,128)(2,1)S(1)} all-gather(bf16[1,108,32]{1,2,0:T(8,128)(2,1)S(1)} %get-tuple-element.26), channel_id=1, replica_groups=mesh['section'=4,'dp'=64] {'dp'}, dimensions={0}, use_global_device_ids=true | all-gather | bytes 449280 | tf_op jit(solution)/shard_map/all_gather | solution.py:105
  477.3 0.2 copy.19
  477.5 0.8 reshape.32
  478.3 48.6 %all-gather.3 = bf16[64,108,32]{1,2,0:T(8,128)(2,1)S(1)} all-gather(bf16[1,108,32]{1,2,0:T(8,128)(2,1)S(1)} %get-tuple-element.14), channel_id=1, replica_groups=mesh['section'=4,'dp'=64] {'dp'}, dimensions={0}, use_global_device_ids=true | all-gather | bytes 449280 | tf_op jit(solution)/shard_map/all_gather | solution.py:105
  526.9 0.2 copy.20
  527.1 1.5 reshape.34
  528.7 48.5 %all-gather = bf16[64,108,32]{1,2,0:T(8,128)(2,1)S(1)} all-gather(bf16[1,108,32]{1,2,0:T(8,128)(2,1)S(1)} %get-tuple-element.8), channel_id=1, replica_groups=mesh['section'=4,'dp'=64] {'dp'}, dimensions={0}, use_global_device_ids=true | all-gather | bytes 449280 | tf_op jit(solution)/shard_map/all_gather | solution.py:105
  577.2 0.2 copy.17
  577.4 1.5 reshape.28
  578.9 0.6 maximum_bitcast_fusion.1
  579.5 2.5 maximum_bitcast_fusion
  582.0 0.7 maximum_bitcast_fusion.2
  (1 shorter events, 0.0 us)
Async XLA Ops:
  7.2 34.6 %copy-start = (bf16[1,27648,32]{1,2,0:T(8,128)(2,1)S(1)}, bf16[1,27648,32]{1,2,0:T(8,128)(2,1)}, u32[]{:S(2)}) copy-start(bf16[1,27648,32]{1,2,0:T(8,128)(2,1)} %param.14) | copy-start | bytes 5308420
  7.2 32.7 %all-gather.6.cloned.1.call-start = ((), (), s32[]{:S(2)}) async-start(), calls=%async_computation | async-start | bytes 1638400 | tf_op jit(solution)/shard_map/all_gather | solution.py:40
  7.9 367.1 %all-reduce.7.cloned.1.call-start = ((), (), s32[]{:S(2)}) async-start(), calls=%async_computation.1 | async-start | bytes 7077888
  41.8 10.0 %copy-start.2 = (bf16[128,5120]{1,0:T(8,128)(2,1)S(1)}, bf16[128,5120]{1,0:T(8,128)(2,1)}, u32[]{:S(2)}) copy-start(bf16[128,5120]{1,0:T(8,128)(2,1)} %all-gather.6.cloned.1.call-done) | copy-start | bytes 3932164
  51.9 32.9 %copy-start.5 = (bf16[1,32,5120]{2,1,0:T(8,128)(2,1)S(1)}, bf16[1,32,5120]{2,1,0:T(8,128)(2,1)}, u32[]{:S(2)}) copy-start(bf16[1,32,5120]{2,1,0:T(8,128)(2,1)} %param.12) | copy-start | bytes 983044
  53.4 30.3 %collective-permute-start = (bf16[128,5120]{1,0:T(8,128)(2,1)S(1)}, bf16[128,5120]{1,0:T(8,128)(2,1)S(1)}, u32[]{:S(2)}, u32[]{:S(2)}) collective-permute-start(bf16[128,5120]{1,0:T(8,128)(2,1)S(1)} %fusion.9), channel_id=1, source_target_pairs={{64,0},{128,64},{192,128},{65,1},{129,65},{193,129},{66,2},{130,66... | collective-permute-start | bytes 3932168 | tf_op jit(solution)/shard_map/ppermute | solution.py:20
  83.7 1.1 copy-start.3
  97.2 30.2 %collective-permute-start.1 = (bf16[128,5120]{1,0:T(8,128)(2,1)S(1)}, bf16[128,5120]{1,0:T(8,128)(2,1)S(1)}, u32[]{:S(2)}, u32[]{:S(2)}) collective-permute-start(bf16[128,5120]{1,0:T(8,128)(2,1)S(1)} %add_convert_fusion.1), channel_id=1, source_target_pairs={{64,0},{128,64},{192,128},{65,1},{129,65},{193,129},{66,2},{130,66... | collective-permute-start | bytes 3932168 | tf_op jit(solution)/shard_map/ppermute | solution.py:20
  127.5 1.1 copy-start.4
  142.1 29.9 %collective-permute-start.2 = (bf16[128,5120]{1,0:T(8,128)(2,1)}, bf16[128,5120]{1,0:T(8,128)(2,1)}, u32[]{:S(2)}, u32[]{:S(2)}) collective-permute-start(bf16[128,5120]{1,0:T(8,128)(2,1)} %add_convert_fusion), channel_id=1, source_target_pairs={{64,0},{128,64},{192,128},{65,1},{129,65},{193,129},{66,2},{130,66... | collective-permute-start | bytes 3932168 | tf_op jit(solution)/shard_map/ppermute | solution.py:20
  153.2 20.6 %copy-start.1 = (bf16[128,27648]{1,0:T(8,128)(2,1)S(1)}, bf16[128,27648]{1,0:T(8,128)(2,1)}, u32[]{:S(2)}) copy-start(bf16[128,27648]{1,0:T(8,128)(2,1)} %fusion.6) | copy-start | bytes 21233668
  177.8 1.3 copy-start.9
  177.8 197.3 %copy-start.6 = (f32[1,4,108,32]{2,3,1,0:T(8,128)S(1)}, f32[1,4,108,32]{2,3,1,0:T(8,128)}, u32[]{:S(2)}) copy-start(f32[1,4,108,32]{2,3,1,0:T(8,128)} %param.17) | copy-start | bytes 165892
  177.8 197.3 %copy-start.7 = (f32[1,4,108,32]{2,3,1,0:T(8,128)S(1)}, f32[1,4,108,32]{2,3,1,0:T(8,128)}, u32[]{:S(2)}) copy-start(f32[1,4,108,32]{2,3,1,0:T(8,128)} %param.16) | copy-start | bytes 165892
  177.8 197.3 %copy-start.8 = (f32[1,4,108,32]{2,3,1,0:T(8,128)S(1)}, f32[1,4,108,32]{2,3,1,0:T(8,128)}, u32[]{:S(2)}) copy-start(f32[1,4,108,32]{2,3,1,0:T(8,128)} %param.15) | copy-start | bytes 165892
Sparse Core Ops, SparseCore 0:
  9.8 30.0 all-gather.5
  179.2 195.8 all-reduce.6
where the time goes:
time: 595 us; the launch traced here: 590 us
  waiting for transfers between devices  303 us (51%)
  blocking collectives  197 us (33%)
  matrix products  46.4 us (8%)
  other arithmetic  15.2 us (3%)
  between operations  15.1 us (3%)
  local copies, waits for them, and re-layouts  8.34 us (1%)
    all_gather x4, blocking collectives, per_device(): lax.all_gather(weights_new.astype(jnp.bfloat16), 'dp', axis=0, tiled=True)  197 us
    unnamed x3, waiting for transfers between devices  195 us
    ppermute x3, waiting for transfers between devices, shifted(): lax.ppermute(value, axis, [(source, source + steps) for source in range(i...  76 us
    all_gather x1, waiting for transfers between devices, per_device(): top_grad = lax.all_gather(out_grad, 'section', axis=1, tiled=True)  31.9 us
    dot_general x3, matrix products, per_device(): jnp.dot(delta, entry_b, preferred_element_type=jnp.float32)  29.8 us
  transfers between devices with their start and end apart: 5, of which 5 were waited for; matrix products, arithmetic and copies ran while one was open for 2% of the time, Pallas kernels for 0%

commit v1 on v0

v1 whole, which is shorter than its diff:
```python
import functools

import jax
import jax.numpy as jnp
from jax import lax
from jax.experimental import pallas as pl
from jax.experimental.pallas import tpu as pltpu
from jax.sharding import PartitionSpec as P

BUCKETS = 4
STEP = 20
BETA_ONE = 0.8
BETA_TWO = 0.95
LEARN_RATE = 0.02
DECAY_RATE = 0.1
EPSILON = 1e-08

TOKENS = 128
FF = 27648
RANK = 32
MODEL = 5120
WIDTH = MODEL // 4
BUCKET_ROWS = FF // BUCKETS
OWNED = 108
LANES = 128
ZS, YS = 8, 4
BF16, F32 = jnp.bfloat16, jnp.float32
VMEM = pl.BlockSpec(memory_space=pltpu.VMEM)
CONTRACT_LAST = (((1,), (1,)), ((), ()))


def params(mib=48):
    return pltpu.CompilerParams(vmem_limit_bytes=mib * 1024 * 1024)


def shaped(shape, dtype):
    return jax.ShapeDtypeStruct(shape, dtype)


def z_pos():
    return lax.axis_index("dp") // 8


def y_pos():
    return (lax.axis_index("dp") // 2) % YS


def core_pos():
    return lax.axis_index("dp") % 2


def over_dp(value, dz=0, dy=0, dc=0):
    pairs = []
    for z in range(ZS):
        for y in range(YS):
            for c in range(2):
                target = ((z + dz) % ZS) * 8 + ((y + dy) % YS) * 2 + (c + dc) % 2
                pairs.append((z * 8 + y * 2 + c, target))
    return lax.ppermute(value, "dp", pairs)


def over_section(value, steps):
    return lax.ppermute(value, "section", [(i, (i + steps) % 4) for i in range(4)])


def slice_kernel(db_ref, ua_ref, *outs):
    here = lax.axis_index("section")
    for k, out in enumerate(outs):
        columns = pl.ds(pl.multiple_of(lax.rem(here + k, 4) * WIDTH, LANES), WIDTH)
        out[0:RANK, :] = db_ref[:, columns]
        out[RANK:, :] = ua_ref[:, columns]


def slices(db, ua):
    return pl.pallas_call(
        slice_kernel,
        out_shape=[shaped((2 * RANK, WIDTH), BF16)] * 4,
        in_specs=[VMEM] * 2,
        out_specs=[VMEM] * 4,
        name="slices",
    )(db, ua)


def prep_kernel(pre_ref, hidden_ref, slope_ref):
    v = pre_ref[...].astype(F32)
    s = 0.5 + 0.5 * jnp.tanh(0.5 * v)
    h = v * s
    hidden_ref[...] = h.astype(BF16)
    slope_ref[...] = (s + h * (1.0 - s)).astype(BF16)


def prep(pre):
    block = pl.BlockSpec((TOKENS, 3072), lambda i: (0, i))
    return pl.pallas_call(
        prep_kernel,
        grid=(FF // 3072,),
        out_shape=[shaped((TOKENS, FF), BF16)] * 2,
        in_specs=[block],
        out_specs=[block] * 2,
        compiler_params=params(),
        cost_estimate=pl.CostEstimate(
            flops=10 * TOKENS * FF, bytes_accessed=6 * TOKENS * FF, transcendentals=TOKENS * FF
        ),
        name="prep",
    )(pre)


def share_kernel(g_ref, w0, w1, w2, w3, *outs):
    ws = (w0, w1, w2, w3)
    for k, out in enumerate(outs):
        db = ws[k][0:RANK, :]
        out[:, 0:LANES] = lax.dot_general(
            db, g_ref[...], CONTRACT_LAST, preferred_element_type=F32
        )
        rows = jnp.concatenate([ws[(k - m) % 4][RANK:, :] for m in (1, 2, 3, 0)], axis=0)
        out[:, LANES:] = lax.dot_general(db, rows, CONTRACT_LAST, preferred_element_type=F32)


def shares(g, ws):
    return pl.pallas_call(
        share_kernel,
        out_shape=[shaped((RANK, 2 * LANES), F32)] * 4,
        in_specs=[VMEM] * 5,
        out_specs=[VMEM] * 4,
        compiler_params=params(),
        name="shares",
    )(g, *ws)


def low_of(share_refs, above_ref):
    total = share_refs[0][...] + share_refs[1][...] + share_refs[2][...] + share_refs[3][...]
    low = total[:, 0:LANES]
    if above_ref is not None:
        low = low + jnp.dot(
            total[:, LANES : LANES + 3 * RANK],
            above_ref[...].astype(F32),
            preferred_element_type=F32,
            precision=lax.Precision.HIGHEST,
        )
    return low


RELAY_COLUMNS = 4608


def relay_kernel(first, *refs):
    share_refs, refs = refs[:4], refs[4:]
    above_ref = None
    if not first:
        above_ref, refs = refs[0], refs[1:]
    slope_ref, da_ref, ub_ref, out_ref, low, total = refs
    step = pl.program_id(0)

    @pl.when(step == 0)
    def _():
        low[...] = low_of(share_refs, above_ref).T.astype(BF16)
        total[...] = jnp.zeros_like(total)

    upstream = jnp.dot(low[...], da_ref[...], preferred_element_type=F32)
    delta = (upstream * slope_ref[...].astype(F32)).astype(BF16)
    total[...] += lax.dot_general(
        ub_ref[...], delta, CONTRACT_LAST, preferred_element_type=F32
    )

    @pl.when(step == pl.num_programs(0) - 1)
    def _():
        out_ref[0:RANK, :] = total[...].astype(BF16)
        if first:
            out_ref[RANK:, :] = jnp.zeros((2 * RANK, LANES), BF16)
        else:
            out_ref[RANK:, :] = above_ref[0 : 2 * RANK, :]


def relay(share, above, slope, da, ub):
    whole = pl.BlockSpec((RANK, 2 * LANES), lambda i: (0, 0))
    message = pl.BlockSpec((3 * RANK, LANES), lambda i: (0, 0))
    rank_block = pl.BlockSpec((RANK, RELAY_COLUMNS), lambda i: (0, i))
    first = above is None
    return pl.pallas_call(
        functools.partial(relay_kernel, first),
        grid=(FF // RELAY_COLUMNS,),
        out_shape=shaped((3 * RANK, LANES), BF16),
        in_specs=[whole] * 4
        + ([] if first else [message])
        + [pl.BlockSpec((TOKENS, RELAY_COLUMNS), lambda i: (0, i)), rank_block, rank_block],
        out_specs=message,
        scratch_shapes=[pltpu.VMEM((TOKENS, RANK), BF16), pltpu.VMEM((RANK, TOKENS), F32)],
        compiler_params=params(),
        name="relay_first" if first else "relay",
    )(*share, *([] if first else [above]), slope, da, ub)


def grad_kernel(s0, s1, s2, s3, above_ref, hidden_ref, keep_ref, send_ref, low, grad):
    @pl.when(pl.program_id(0) == 0)
    def _():
        low[...] = low_of((s0, s1, s2, s3), above_ref).astype(BF16)

    grad[...] = jnp.dot(low[...], hidden_ref[...], preferred_element_type=F32)
    core = core_pos()
    lane = lax.broadcasted_iota(jnp.int32, (RANK, LANES), 1)
    for z in range(ZS):
        for y in range(YS):
            pair = []
            for c in range(2):
                start = (z * 8 + y * 2 + c) * OWNED
                base, shift = start // LANES * LANES, start % LANES
                piece = grad[:, base : base + LANES]
                if shift:
                    piece = pltpu.roll(piece, LANES - shift, 1)
                if shift + OWNED > LANES:
                    more = pltpu.roll(
                        grad[:, base + LANES : base + 2 * LANES], LANES - shift, 1
                    )
                    piece = jnp.where(lane < LANES - shift, piece, more)
                pair.append(piece)
            keep_ref[y, z, 0] = jnp.where(core == 0, pair[0], pair[1]).astype(BF16)
            send_ref[y, z, 0] = jnp.where(core == 0, pair[1], pair[0]).astype(BF16)


def grads(share, above, hidden):
    whole = pl.BlockSpec((RANK, 2 * LANES), lambda i: (0, 0))
    half = pl.BlockSpec((YS, ZS, 1, RANK, LANES), lambda i: (0, 0, i, 0, 0))
    return pl.pallas_call(
        grad_kernel,
        grid=(BUCKETS,),
        out_shape=[shaped((YS, ZS, BUCKETS, RANK, LANES), BF16)] * 2,
        in_specs=[whole] * 4
        + [
            pl.BlockSpec((3 * RANK, LANES), lambda i: (0, 0)),
            pl.BlockSpec((TOKENS, BUCKET_ROWS), lambda i: (0, i)),
        ],
        out_specs=[half] * 2,
        scratch_shapes=[
            pltpu.VMEM((RANK, TOKENS), BF16),
            pltpu.VMEM((RANK, BUCKET_ROWS), F32),
        ],
        compiler_params=params(),
        name="grads",
    )(*share, above, hidden)


def core_sum_kernel(keep_ref, got_ref, own_ref, *outs):
    here = y_pos()
    own_ref[...] = keep_ref[here].astype(F32) + got_ref[here].astype(F32)
    for k, out in enumerate(outs):
        there = lax.rem(here + k + 1, YS)
        out[...] = (keep_ref[there].astype(F32) + got_ref[there].astype(F32)).astype(BF16)


def core_sum(keep, got):
    block = (ZS, BUCKETS, RANK, LANES)
    return pl.pallas_call(
        core_sum_kernel,
        out_shape=[shaped(block, F32)] + [shaped(block, BF16)] * 3,
        in_specs=[VMEM] * 2,
        out_specs=[VMEM] * 4,
        compiler_params=params(),
        name="core_sum",
    )(keep, got)


def y_sum_kernel(own_ref, g1, g2, g3, out_own, *outs):
    here = z_pos()

    def total(z):
        return own_ref[z] + g1[z].astype(F32) + g2[z].astype(F32) + g3[z].astype(F32)

    out_own[...] = total(here)
    for k, out in enumerate(outs):
        out[...] = total(lax.rem(here + k + 1, ZS)).astype(BF16)


def y_sum(own, got):
    block = (BUCKETS, RANK, LANES)
    return pl.pallas_call(
        y_sum_kernel,
        out_shape=[shaped(block, F32)] + [shaped(block, BF16)] * 7,
        in_specs=[VMEM] * 4,
        out_specs=[VMEM] * 8,
        compiler_params=params(),
        name="y_sum",
    )(own, *got)


def adamw_kernel(own_ref, g1, g2, g3, g4, g5, g6, g7, master, moment, second, *outs):
    weight_out, master_out, moment_out, second_out = outs
    gradient = own_ref[...]
    for got in (g1, g2, g3, g4, g5, g6, g7):
        gradient = gradient + got[...].astype(F32)
    gradient = gradient[:, :, 0:OWNED]
    weights = master[...]
    first_new = BETA_ONE * moment[...] + (1.0 - BETA_ONE) * gradient
    second_new = BETA_TWO * second[...] + (1.0 - BETA_TWO) * gradient * gradient
    first_hat = first_new / (1.0 - BETA_ONE**STEP)
    second_hat = second_new / (1.0 - BETA_TWO**STEP)
    weights_new = weights - LEARN_RATE * (
        first_hat / (jnp.sqrt(second_hat) + EPSILON) + DECAY_RATE * weights
    )
    weight_out[...] = jnp.zeros_like(weight_out)
    weight_out[:, :, 0:OWNED] = weights_new.astype(BF16)
    master_out[...] = weights_new
    moment_out[...] = first_new
    second_out[...] = second_new


def adamw(own, got, master, moment, second):
    state = shaped((BUCKETS, RANK, OWNED), F32)
    return pl.pallas_call(
        adamw_kernel,
        out_shape=[shaped((BUCKETS, RANK, LANES), BF16)] + [state] * 3,
        in_specs=[VMEM] * 11,
        out_specs=[VMEM] * 4,
        compiler_params=params(),
        name="adamw",
    )(own, *got, master, moment, second)


def assemble_kernel(*refs):
    arrays, (out_ref, blocks, sems) = refs[:8], refs[8:]
    core, y_here, z_here = core_pos(), y_pos(), z_pos()
    copies = []
    for side in range(2):
        for k in range(YS):
            copies.append(
                pltpu.make_async_copy(
                    arrays[side * YS + k],
                    blocks.at[lax.rem(core + side, 2), lax.rem(y_here + YS - k, YS)],
                    sems.at[side * YS + k],
                )
            )
            copies[-1].start()
    for copy in copies:
        copy.wait()
    lane = lax.broadcasted_iota(jnp.int32, (RANK, LANES), 1)
    for tile in range(FF // LANES):
        value = None
        first = tile * LANES // OWNED
        last = (tile * LANES + LANES - 1) // OWNED
        for piece in range(first, last + 1):
            bucket, owner = divmod(piece, 64)
            z, y, c = owner // 8, owner // 2 % YS, owner % 2
            block = blocks[c, y, lax.rem(z_here + ZS - z, ZS), bucket].astype(F32)
            start = piece * OWNED - tile * LANES
            if start % LANES:
                block = pltpu.roll(block, start % LANES, 1)
            value = block if value is None else jnp.where(lane < start, value, block)
        out_ref[:, tile * LANES : (tile + 1) * LANES] = value.astype(BF16)


def assemble(arrays):
    return pl.pallas_call(
        assemble_kernel,
        out_shape=shaped((RANK, FF), BF16),
        in_specs=[pl.BlockSpec(memory_space=pl.ANY)] * 8,
        out_specs=VMEM,
        scratch_shapes=[
            pltpu.VMEM((2, YS, ZS, BUCKETS, RANK, LANES), BF16),
            pltpu.SemaphoreType.DMA((8,)),
        ],
        compiler_params=params(),
        name="assemble",
    )(*arrays)


def per_device(out_grad, pre_act, down_a, down_b, up_a, up_b, master, moment, second):
    da, ub = down_a[0].T, up_b[0].T
    mine = slices(down_b[0], up_a[0].T)
    ws = [mine[0]] + [over_section(mine[k], k) for k in (1, 2, 3)]
    hidden, slope = prep(pre_act[0])
    share = shares(out_grad, ws)
    share = [share[0]] + [over_section(share[k], -k) for k in (1, 2, 3)]
    above = None
    for _ in range(3):
        sent = relay(share, above, slope, da, ub)
        above = lax.ppermute(sent, "section", [(1, 0), (2, 1), (3, 2)])
    keep, send = grads(share, above, hidden)
    own, *sends = core_sum(keep, over_dp(send, dc=1))
    own, *sends = y_sum(own, [over_dp(sends[k - 1], dy=k) for k in (1, 2, 3)])
    got = [over_dp(sends[k - 1], dz=k) for k in range(1, 8)]
    state = [a[0].transpose(0, 2, 1) for a in (master, moment, second)]
    weight, *state = adamw(own, got, *state)
    column = jnp.stack([weight] + [over_dp(weight, dz=k) for k in range(1, 8)])
    plane = [column] + [over_dp(column, dy=k) for k in (1, 2, 3)]
    rows = assemble(plane + [over_dp(a, dc=1) for a in plane])
    return (rows.T[None], *[a.transpose(0, 2, 1)[None] for a in state])


def solution(mesh):
    return jax.shard_map(
        per_device,
        mesh=mesh,
        in_specs=(
            P("dp", "section"),
            P("section", "dp", None),
            P("section", None, None),
            P("section", None, None),
            P("section", None, None),
            P("section", None, None),
            P("section", None, "dp", None),
            P("section", None, "dp", None),
            P("section", None, "dp", None),
        ),
        out_specs=(
            P("section", None, None),
            P("section", None, "dp", None),
            P("section", None, "dp", None),
            P("section", None, "dp", None),
        ),
        check_vma=False,
    )
```

time: 595 us -> 166 us (0.28)
  waiting for transfers between devices: 303 us -> 46.8 us
  blocking collectives: 197 us -> 0 us
  starting transfers between devices: 4.85 us -> 69.8 us
  matrix products: 46.4 us -> 0 us
  Pallas kernels: 0 us -> 45.7 us
  other arithmetic: 15.2 us -> 0 us
  between operations: 15.1 us -> 1.01 us
  local copies, waits for them, and re-layouts: 8.34 us -> 1.99 us
    all_gather x4 -> x0, blocking collectives: 197 us -> none  [per_device(): lax.all_gather(weights_new.astype(jnp.bfloat16), 'dp', axis=0, tiled=True)]
    unnamed x3 -> x0, waiting for transfers between devices: 195 us -> none
    ppermute x3 -> x34, starting transfers between devices: 4.77 us -> 69.8 us  [the longest x25 57.2 us: over_dp(): return lax.ppermute(value, 'dp', pairs)]
    dot_general x14 -> x0, matrix products: 46.4 us -> none  [the longest x3 29.8 us: per_device(): jnp.dot(delta, entry_b, preferred_element_type=jnp.float32)]
    pallas_call x0 -> x11, Pallas kernels: none -> 45.7 us  [the longest x3 22.4 us: relay(): pl.pallas_call(functools.partial(relay_kernel, first), grid=(FF // RELAY_...]
    all_gather x1 -> x0, waiting for transfers between devices: 31.9 us -> none  [per_device(): top_grad = lax.all_gather(out_grad, 'section', axis=1, tiled=True)]
    ppermute x3 -> x34, waiting for transfers between devices: 76 us -> 46.8 us  [the longest x25 30.7 us: over_dp(): return lax.ppermute(value, 'dp', pairs)]
    convert_element_type x1 -> x0, other arithmetic: 9.65 us -> none  [per_device(): hidden = jax.nn.silu(inputs).astype(jnp.bfloat16)]
  transfers between devices with their start and end apart: 5 -> 34, of which waited for: 5 -> 14; matrix products, arithmetic and copies ran while one was open for 2% -> 0% of each run, Pallas kernels for 0% -> 7%
where the time goes in v1:
time: 166 us; the launch traced here: 165 us
  starting transfers between devices  69.8 us (42%)
  waiting for transfers between devices  46.8 us (28%)
  Pallas kernels  45.7 us (28%)
  local copies, waits for them, and re-layouts  1.99 us (1%)
    ppermute x25, starting transfers between devices, over_dp(): return lax.ppermute(value, 'dp', pairs)  57.2 us
    ppermute x25, waiting for transfers between devices, over_dp(): return lax.ppermute(value, 'dp', pairs)  30.7 us
    pallas_call x3, Pallas kernels, relay(): pl.pallas_call(functools.partial(relay_kernel, first), grid=(FF // RELAY_...  22.4 us
    pallas_call x1, Pallas kernels, prep(): pl.pallas_call(prep_kernel, grid=(FF // 3072,), out_shape=[shaped((TOKENS...  11.9 us
    ppermute x3, waiting for transfers between devices, per_device(): above = lax.ppermute(sent, 'section', [(1, 0), (2, 1), (3, 2)])  9.81 us
    ppermute x6, starting transfers between devices, over_section(): lax.ppermute(value, 'section', [(i, (i + steps) % 4) for i in range(4)])  8.59 us
    ppermute x6, waiting for transfers between devices, over_section(): lax.ppermute(value, 'section', [(i, (i + steps) % 4) for i in range(4)])  6.23 us
    pallas_call x1, Pallas kernels, grads(): pl.pallas_call(grad_kernel, grid=(BUCKETS,), out_shape=[shaped((YS, ZS, B...  4.79 us
  transfers between devices with their start and end apart: 34, of which 14 were waited for; matrix products, arithmetic and copies ran while one was open for 0% of the time, Pallas kernels for 7%

profile of v1, /device:TPU:1, one launch (start us, length us, event | category | flops | bytes accessed | tf_op | source)
XLA Modules:
  0.0 165.2 jit_solution(5820029792333745287)
XLA Ops:
  0.7 2.1 %slices.1 = (bf16[64,1280]{1,0:T(8,128)(2,1)}, bf16[64,1280]{1,0:T(8,128)(2,1)}, bf16[64,1280]{1,0:T(8,128)(2,1)}, bf16[64,1280]{1,0:T(8,128)(2,1)}) custom-call(bf16[32,5120]{1,0:T(8,128)(2,1)} %bitcast.59, bf16[32,5120]{1,0:T(8,128)(2,1)} %bitcast.60), custom_call_target="tpu_custom_call" | custom-call | tf_op jit(solution)/shard_map/slices/pallas_call | solution.py:75
  2.7 2.0 %collective-permute-start = (bf16[64,1280]{1,0:T(8,128)(2,1)}, bf16[64,1280]{1,0:T(8,128)(2,1)S(1)}, u32[]{:S(2)}, u32[]{:S(2)}) collective-permute-start(bf16[64,1280]{1,0:T(8,128)(2,1)} %get-tuple-element.33), channel_id=1, source_target_pairs={{0,64},{64,128},{128,192},{192,0},{1,65},{65,129},{129,193},{193,1... | collective-permute-start | bytes 491528 | tf_op jit(solution)/shard_map/ppermute | solution.py:63
  4.8 2.5 %collective-permute-start.1 = (bf16[64,1280]{1,0:T(8,128)(2,1)}, bf16[64,1280]{1,0:T(8,128)(2,1)S(1)}, u32[]{:S(2)}, u32[]{:S(2)}) collective-permute-start(bf16[64,1280]{1,0:T(8,128)(2,1)} %get-tuple-element.34), channel_id=1, source_target_pairs={{0,128},{64,192},{128,0},{192,64},{1,129},{65,193},{129,1},{193,65... | collective-permute-start | bytes 491528 | tf_op jit(solution)/shard_map/ppermute | solution.py:63
  7.2 1.2 collective-permute-start.2
  8.4 0.6 collective-permute-done.w1
  9.0 5.6 %collective-permute-done.1.w2 = bf16[64,1280]{1,0:T(8,128)(2,1)S(1)} collective-permute-done((bf16[64,1280]{1,0:T(8,128)(2,1)}, bf16[64,1280]{1,0:T(8,128)(2,1)S(1)}, u32[]{:S(2)}, u32[]{:S(2)}) %collective-permute-start.1) | collective-permute-done | bytes 163872 | tf_op jit(solution)/shard_map/ppermute | solution.py:63
  14.6 0.0 collective-permute-done.2.w3
  14.6 1.0 copy-done.2
  15.6 0.9 copy-done.3
  16.5 0.9 shares.1
  17.4 1.6 collective-permute-start.3
  19.0 0.7 collective-permute-start.4
  19.8 0.6 collective-permute-start.5
  20.4 11.9 %prep.1 = (bf16[128,27648]{1,0:T(8,128)(2,1)}, bf16[128,27648]{1,0:T(8,128)(2,1)}) custom-call(bf16[128,27648]{1,0:T(8,128)(2,1)} %bitcast.57), custom_call_target="tpu_custom_call" | custom-call | flops 35389440 | bytes 21233664 | tf_op jit(solution)/shard_map/prep/pallas_call | solution.py:94
  32.3 0.0 collective-permute-done.3.refs_1_.s1
  32.3 7.4 %relay_first.1 = bf16[96,128]{1,0:T(8,128)(2,1)S(1)} custom-call(f32[32,256]{1,0:T(8,128)S(1)} %get-tuple-element.36.refs_0_.s0, f32[32,256]{1,0:T(8,128)S(1)} %collective-permute-done.3.refs_1_.s1, f32[32,256]{1,0:T(8,128)S(1)} %collective-permute-done.4.refs_2_.s2, f32[32,256]{1,0:T(8,128)S(1)} %collective-permute-done.5.refs_3_.s3, ...), custom_call_target="tpu_custom_call" | custom-call | tf_op jit(solution)/shard_map/relay_first/pallas_call | solution.py:179
  39.7 1.3 collective-permute-start.6
  41.0 3.3 %collective-permute-done.6.refs_4_ = bf16[96,128]{1,0:T(8,128)(2,1)S(1)} collective-permute-done((bf16[96,128]{1,0:T(8,128)(2,1)S(1)}, bf16[96,128]{1,0:T(8,128)(2,1)S(1)}, u32[]{:S(2)}, u32[]{:S(2)}) %collective-permute-start.6) | collective-permute-done | bytes 24608 | tf_op jit(solution)/shard_map/ppermute | solution.py:375
  44.3 7.5 %relay.2 = bf16[96,128]{1,0:T(8,128)(2,1)S(1)} custom-call(f32[32,256]{1,0:T(8,128)S(1)} %get-tuple-element.36.refs_0_.s0, f32[32,256]{1,0:T(8,128)S(1)} %collective-permute-done.3.refs_1_.s1, f32[32,256]{1,0:T(8,128)S(1)} %collective-permute-done.4.refs_2_.s2, f32[32,256]{1,0:T(8,128)S(1)} %collective-permute-done.5.refs_3_.s3, ...), custom_call_target="tpu_custom_call" | custom-call | tf_op jit(solution)/shard_map/relay/pallas_call | solution.py:179
  51.8 1.3 collective-permute-start.7
  53.1 3.3 %collective-permute-done.7.refs_4_ = bf16[96,128]{1,0:T(8,128)(2,1)S(1)} collective-permute-done((bf16[96,128]{1,0:T(8,128)(2,1)S(1)}, bf16[96,128]{1,0:T(8,128)(2,1)S(1)}, u32[]{:S(2)}, u32[]{:S(2)}) %collective-permute-start.7) | collective-permute-done | bytes 24608 | tf_op jit(solution)/shard_map/ppermute | solution.py:375
  56.4 7.5 %relay.3 = bf16[96,128]{1,0:T(8,128)(2,1)S(1)} custom-call(f32[32,256]{1,0:T(8,128)S(1)} %get-tuple-element.36.refs_0_.s0, f32[32,256]{1,0:T(8,128)S(1)} %collective-permute-done.3.refs_1_.s1, f32[32,256]{1,0:T(8,128)S(1)} %collective-permute-done.4.refs_2_.s2, f32[32,256]{1,0:T(8,128)S(1)} %collective-permute-done.5.refs_3_.s3, ...), custom_call_target="tpu_custom_call" | custom-call | tf_op jit(solution)/shard_map/relay/pallas_call | solution.py:179
  63.9 0.0 copy-start.4
  63.9 0.0 copy-start.5
  63.9 0.0 copy-start.6
  63.9 1.4 collective-permute-start.8
  65.3 3.3 %collective-permute-done.8.above_ref = bf16[96,128]{1,0:T(8,128)(2,1)S(1)} collective-permute-done((bf16[96,128]{1,0:T(8,128)(2,1)S(1)}, bf16[96,128]{1,0:T(8,128)(2,1)S(1)}, u32[]{:S(2)}, u32[]{:S(2)}) %collective-permute-start.8) | collective-permute-done | bytes 24608 | tf_op jit(solution)/shard_map/ppermute | solution.py:375
  68.6 4.8 %grads.1 = (bf16[4,8,4,32,128]{4,3,2,1,0:T(8,128)(2,1)S(1)}, bf16[4,8,4,32,128]{4,3,2,1,0:T(8,128)(2,1)S(1)}) custom-call(f32[32,256]{1,0:T(8,128)S(1)} %get-tuple-element.36.refs_0_.s0, f32[32,256]{1,0:T(8,128)S(1)} %collective-permute-done.3.refs_1_.s1, f32[32,256]{1,0:T(8,128)S(1)} %collective-permute-done.4.refs_2_.s2, ...), custom_call_target="tpu_custom_call" | custom-call | tf_op jit(solution)/shard_map/grads/pallas_call | solution.py:223
  73.4 6.2 %collective-permute-start.9 = (bf16[4,8,4,32,128]{4,3,2,1,0:T(8,128)(2,1)S(1)}, bf16[4,8,4,32,128]{4,3,2,1,0:T(8,128)(2,1)S(1)}, u32[]{:S(2)}, u32[]{:S(2)}) collective-permute-start(bf16[4,8,4,32,128]{4,3,2,1,0:T(8,128)(2,1)S(1)} %get-tuple-element.43), channel_id=1, source_target_pairs={{0,1},{1,0},{2,3},{3,2},{4,5},{5,4},{6,7},{7,6},{8,9},{9,8},{10,11... | collective-permute-start | bytes 3145736 | tf_op jit(solution)/shard_map/ppermute | solution.py:59
  79.6 2.3 %collective-permute-done.9.got_ref = bf16[4,8,4,32,128]{4,3,2,1,0:T(8,128)(2,1)S(1)} collective-permute-done((bf16[4,8,4,32,128]{4,3,2,1,0:T(8,128)(2,1)S(1)}, bf16[4,8,4,32,128]{4,3,2,1,0:T(8,128)(2,1)S(1)}, u32[]{:S(2)}, u32[]{:S(2)}) %collective-permute-start.9) | collective-permute-done | bytes 1048608 | tf_op jit(solution)/shard_map/ppermute | solution.py:59
  81.9 0.2 core_sum.1
  82.2 1.4 collective-permute-start.10
  83.5 2.6 %collective-permute-start.11 = (bf16[8,4,32,128]{3,2,1,0:T(8,128)(2,1)S(1)}, bf16[8,4,32,128]{3,2,1,0:T(8,128)(2,1)S(1)}, u32[]{:S(2)}, u32[]{:S(2)}) collective-permute-start(bf16[8,4,32,128]{3,2,1,0:T(8,128)(2,1)S(1)} %get-tuple-element.46), channel_id=1, source_target_pairs={{0,4},{1,5},{2,6},{3,7},{4,0},{5,1},{6,2},{7,3},{8,12},{9,13},{10,... | collective-permute-start | bytes 786440 | tf_op jit(solution)/shard_map/ppermute | solution.py:59
  86.2 1.1 collective-permute-start.12
  87.2 3.9 %collective-permute-done.10.g1 = bf16[8,4,32,128]{3,2,1,0:T(8,128)(2,1)S(1)} collective-permute-done((bf16[8,4,32,128]{3,2,1,0:T(8,128)(2,1)S(1)}, bf16[8,4,32,128]{3,2,1,0:T(8,128)(2,1)S(1)}, u32[]{:S(2)}, u32[]{:S(2)}) %collective-permute-start.10) | collective-permute-done | bytes 262176 | tf_op jit(solution)/shard_map/ppermute | solution.py:59
  91.1 6.7 %collective-permute-done.11.g2 = bf16[8,4,32,128]{3,2,1,0:T(8,128)(2,1)S(1)} collective-permute-done((bf16[8,4,32,128]{3,2,1,0:T(8,128)(2,1)S(1)}, bf16[8,4,32,128]{3,2,1,0:T(8,128)(2,1)S(1)}, u32[]{:S(2)}, u32[]{:S(2)}) %collective-permute-start.11) | collective-permute-done | bytes 262176 | tf_op jit(solution)/shard_map/ppermute | solution.py:59
  97.8 0.1 y_sum.1
  97.9 1.7 %collective-permute-start.13 = (bf16[4,32,128]{2,1,0:T(8,128)(2,1)S(1)}, bf16[4,32,128]{2,1,0:T(8,128)(2,1)S(1)}, u32[]{:S(2)}, u32[]{:S(2)}) collective-permute-start(bf16[4,32,128]{2,1,0:T(8,128)(2,1)S(1)} %get-tuple-element.49), channel_id=1, source_target_pairs={{0,8},{1,9},{2,10},{3,11},{4,12},{5,13},{6,14},{7,15},{8,16},{9,17... | collective-permute-start | bytes 98312 | tf_op jit(solution)/shard_map/ppermute | solution.py:59
  99.7 3.0 %collective-permute-start.14 = (bf16[4,32,128]{2,1,0:T(8,128)(2,1)S(1)}, bf16[4,32,128]{2,1,0:T(8,128)(2,1)S(1)}, u32[]{:S(2)}, u32[]{:S(2)}) collective-permute-start(bf16[4,32,128]{2,1,0:T(8,128)(2,1)S(1)} %get-tuple-element.50), channel_id=1, source_target_pairs={{0,16},{1,17},{2,18},{3,19},{4,20},{5,21},{6,22},{7,23},{8,24},{9,... | collective-permute-start | bytes 98312 | tf_op jit(solution)/shard_map/ppermute | solution.py:59
  102.7 3.7 %collective-permute-start.15 = (bf16[4,32,128]{2,1,0:T(8,128)(2,1)S(1)}, bf16[4,32,128]{2,1,0:T(8,128)(2,1)S(1)}, u32[]{:S(2)}, u32[]{:S(2)}) collective-permute-start(bf16[4,32,128]{2,1,0:T(8,128)(2,1)S(1)} %get-tuple-element.51), channel_id=1, source_target_pairs={{0,24},{1,25},{2,26},{3,27},{4,28},{5,29},{6,30},{7,31},{8,32},{9,... | collective-permute-start | bytes 98312 | tf_op jit(solution)/shard_map/ppermute | solution.py:59
  106.4 0.5 collective-permute-start.16
  106.9 4.4 %collective-permute-start.17 = (bf16[4,32,128]{2,1,0:T(8,128)(2,1)S(1)}, bf16[4,32,128]{2,1,0:T(8,128)(2,1)S(1)}, u32[]{:S(2)}, u32[]{:S(2)}) collective-permute-start(bf16[4,32,128]{2,1,0:T(8,128)(2,1)S(1)} %get-tuple-element.53), channel_id=1, source_target_pairs={{0,40},{1,41},{2,42},{3,43},{4,44},{5,45},{6,46},{7,47},{8,48},{9,... | collective-permute-start | bytes 98312 | tf_op jit(solution)/shard_map/ppermute | solution.py:59
  111.3 2.4 %collective-permute-start.18 = (bf16[4,32,128]{2,1,0:T(8,128)(2,1)S(1)}, bf16[4,32,128]{2,1,0:T(8,128)(2,1)S(1)}, u32[]{:S(2)}, u32[]{:S(2)}) collective-permute-start(bf16[4,32,128]{2,1,0:T(8,128)(2,1)S(1)} %get-tuple-element.54), channel_id=1, source_target_pairs={{0,48},{1,49},{2,50},{3,51},{4,52},{5,53},{6,54},{7,55},{8,56},{9,... | collective-permute-start | bytes 98312 | tf_op jit(solution)/shard_map/ppermute | solution.py:59
  113.7 0.7 collective-permute-start.19
  114.5 2.3 %collective-permute-done.18.g6 = bf16[4,32,128]{2,1,0:T(8,128)(2,1)S(1)} collective-permute-done((bf16[4,32,128]{2,1,0:T(8,128)(2,1)S(1)}, bf16[4,32,128]{2,1,0:T(8,128)(2,1)S(1)}, u32[]{:S(2)}, u32[]{:S(2)}) %collective-permute-start.18) | collective-permute-done | bytes 32800 | tf_op jit(solution)/shard_map/ppermute | solution.py:59
  116.8 0.2 collective-permute-done.19.g7
  117.0 0.7 adamw.1
  117.8 2.4 %collective-permute-start.26 = (bf16[4,32,128]{2,1,0:T(8,128)(2,1)S(1)}, bf16[4,32,128]{2,1,0:T(8,128)(2,1)S(1)}, u32[]{:S(2)}, u32[]{:S(2)}) collective-permute-start(bf16[4,32,128]{2,1,0:T(8,128)(2,1)S(1)} %get-tuple-element.56), channel_id=1, source_target_pairs={{0,56},{1,57},{2,58},{3,59},{4,60},{5,61},{6,62},{7,63},{8,0},{9,1... | collective-permute-start | bytes 98312 | tf_op jit(solution)/shard_map/ppermute | solution.py:59
  120.1 0.6 collective-permute-start.25
  120.7 1.0 collective-permute-start.24
  121.7 4.6 %collective-permute-start.23 = (bf16[4,32,128]{2,1,0:T(8,128)(2,1)S(1)}, bf16[4,32,128]{2,1,0:T(8,128)(2,1)S(1)}, u32[]{:S(2)}, u32[]{:S(2)}) collective-permute-start(bf16[4,32,128]{2,1,0:T(8,128)(2,1)S(1)} %get-tuple-element.56), channel_id=1, source_target_pairs={{0,32},{1,33},{2,34},{3,35},{4,36},{5,37},{6,38},{7,39},{8,40},{9,... | collective-permute-start | bytes 98312 | tf_op jit(solution)/shard_map/ppermute | solution.py:59
  126.4 0.6 collective-permute-start.20
  127.0 3.4 %collective-permute-done.20 = bf16[4,32,128]{2,1,0:T(8,128)(2,1)S(1)} collective-permute-done((bf16[4,32,128]{2,1,0:T(8,128)(2,1)S(1)}, bf16[4,32,128]{2,1,0:T(8,128)(2,1)S(1)}, u32[]{:S(2)}, u32[]{:S(2)}) %collective-permute-start.20) | collective-permute-done | bytes 32800 | tf_op jit(solution)/shard_map/ppermute | solution.py:59
  130.3 4.9 %collective-permute-done.21 = bf16[4,32,128]{2,1,0:T(8,128)(2,1)S(1)} collective-permute-done((bf16[4,32,128]{2,1,0:T(8,128)(2,1)S(1)}, bf16[4,32,128]{2,1,0:T(8,128)(2,1)S(1)}, u32[]{:S(2)}, u32[]{:S(2)}) %collective-permute-start.21) | collective-permute-done | bytes 32800 | tf_op jit(solution)/shard_map/ppermute | solution.py:59
  135.2 5.9 %collective-permute-done.22 = bf16[4,32,128]{2,1,0:T(8,128)(2,1)S(1)} collective-permute-done((bf16[4,32,128]{2,1,0:T(8,128)(2,1)S(1)}, bf16[4,32,128]{2,1,0:T(8,128)(2,1)S(1)}, u32[]{:S(2)}, u32[]{:S(2)}) %collective-permute-start.22) | collective-permute-done | bytes 32800 | tf_op jit(solution)/shard_map/ppermute | solution.py:59
  141.2 2.1 %collective-permute-start.29 = (bf16[8,4,32,128]{3,2,1,0:T(8,128)(2,1)S(1)}, bf16[8,4,32,128]{3,2,1,0:T(8,128)(2,1)S(1)}, u32[]{:S(2)}, u32[]{:S(2)}) collective-permute-start(bf16[8,4,32,128]{3,2,1,0:T(8,128)(2,1)S(1)} %bitcast_dynamic-update-slice_fusion.refs_0_), channel_id=1, source_target_pairs={{0,6},{1,7},{2,0},{3,1},{4,2},{5,3},{6,4},{7,5},{8,14},{9,15},{10,... | collective-permute-start | bytes 786440 | tf_op jit(solution)/shard_map/ppermute | solution.py:59
  143.4 0.6 collective-permute-start.28
  144.0 0.0 collective-permute-start.27
  144.0 8.5 %collective-permute-start.30 = (bf16[8,4,32,128]{3,2,1,0:T(8,128)(2,1)S(1)}, bf16[8,4,32,128]{3,2,1,0:T(8,128)(2,1)S(1)}, u32[]{:S(2)}, u32[]{:S(2)}) collective-permute-start(bf16[8,4,32,128]{3,2,1,0:T(8,128)(2,1)S(1)} %bitcast_dynamic-update-slice_fusion.refs_0_), channel_id=1, source_target_pairs={{0,1},{1,0},{2,3},{3,2},{4,5},{5,4},{6,7},{7,6},{8,9},{9,8},{10,11... | collective-permute-start | bytes 786440 | tf_op jit(solution)/shard_map/ppermute | solution.py:59
  152.5 5.0 %collective-permute-start.33 = (bf16[8,4,32,128]{3,2,1,0:T(8,128)(2,1)S(1)}, bf16[8,4,32,128]{3,2,1,0:T(8,128)(2,1)S(1)}, u32[]{:S(2)}, u32[]{:S(2)}) collective-permute-start(bf16[8,4,32,128]{3,2,1,0:T(8,128)(2,1)S(1)} %collective-permute-done.29.refs_3_), channel_id=1, source_target_pairs={{0,1},{1,0},{2,3},{3,2},{4,5},{5,4},{6,7},{7,6},{8,9},{9,8},{10,11... | collective-permute-start | bytes 786440 | tf_op jit(solution)/shard_map/ppermute | solution.py:59
  157.5 1.2 collective-permute-start.32
  158.7 2.7 %collective-permute-start.31 = (bf16[8,4,32,128]{3,2,1,0:T(8,128)(2,1)S(1)}, bf16[8,4,32,128]{3,2,1,0:T(8,128)(2,1)S(1)}, u32[]{:S(2)}, u32[]{:S(2)}) collective-permute-start(bf16[8,4,32,128]{3,2,1,0:T(8,128)(2,1)S(1)} %collective-permute-done.27.refs_1_), channel_id=1, source_target_pairs={{0,1},{1,0},{2,3},{3,2},{4,5},{5,4},{6,7},{7,6},{8,9},{9,8},{10,11... | collective-permute-start | bytes 786440 | tf_op jit(solution)/shard_map/ppermute | solution.py:59
  161.4 1.1 collective-permute-done.31.refs_5_
  162.6 2.5 %assemble.1 = bf16[32,27648]{1,0:T(8,128)(2,1)} custom-call(bf16[8,4,32,128]{3,2,1,0:T(8,128)(2,1)S(1)} %bitcast_dynamic-update-slice_fusion.refs_0_, bf16[8,4,32,128]{3,2,1,0:T(8,128)(2,1)S(1)} %collective-permute-done.27.refs_1_, bf16[8,4,32,128]{3,2,1,0:T(8,128)(2,1)S(1)} %collective-permute-done.28.refs_2_, ...), custom_call_target="tpu_custom_call" | custom-call | tf_op jit(solution)/shard_map/assemble/pallas_call | solution.py:351
  (37 shorter events, 0.1 us)
Async XLA Ops:
  0.6 31.7 %copy-start.1 = (bf16[1,27648,32]{1,2,0:T(8,128)(2,1)S(1)}, bf16[1,27648,32]{1,2,0:T(8,128)(2,1)}, u32[]{:S(2)}) copy-start(bf16[1,27648,32]{1,2,0:T(8,128)(2,1)} %param.14) | copy-start | bytes 5308420
  0.6 31.7 %copy-start = (bf16[1,27648,32]{1,2,0:T(8,128)(2,1)S(1)}, bf16[1,27648,32]{1,2,0:T(8,128)(2,1)}, u32[]{:S(2)}) copy-start(bf16[1,27648,32]{1,2,0:T(8,128)(2,1)} %param.11) | copy-start | bytes 5308420
  2.7 6.2 %collective-permute-start = (bf16[64,1280]{1,0:T(8,128)(2,1)}, bf16[64,1280]{1,0:T(8,128)(2,1)S(1)}, u32[]{:S(2)}, u32[]{:S(2)}) collective-permute-start(bf16[64,1280]{1,0:T(8,128)(2,1)} %get-tuple-element.33), channel_id=1, source_target_pairs={{0,64},{64,128},{128,192},{192,0},{1,65},{65,129},{129,193},{193,1... | collective-permute-start | bytes 491528 | tf_op jit(solution)/shard_map/ppermute | solution.py:63
  4.8 9.8 %collective-permute-start.1 = (bf16[64,1280]{1,0:T(8,128)(2,1)}, bf16[64,1280]{1,0:T(8,128)(2,1)S(1)}, u32[]{:S(2)}, u32[]{:S(2)}) collective-permute-start(bf16[64,1280]{1,0:T(8,128)(2,1)} %get-tuple-element.34), channel_id=1, source_target_pairs={{0,128},{64,192},{128,0},{192,64},{1,129},{65,193},{129,1},{193,65... | collective-permute-start | bytes 491528 | tf_op jit(solution)/shard_map/ppermute | solution.py:63
  7.2 7.4 %collective-permute-start.2 = (bf16[64,1280]{1,0:T(8,128)(2,1)}, bf16[64,1280]{1,0:T(8,128)(2,1)S(1)}, u32[]{:S(2)}, u32[]{:S(2)}) collective-permute-start(bf16[64,1280]{1,0:T(8,128)(2,1)} %get-tuple-element.35), channel_id=1, source_target_pairs={{0,192},{64,0},{128,64},{192,128},{1,193},{65,1},{129,65},{193,129... | collective-permute-start | bytes 491528 | tf_op jit(solution)/shard_map/ppermute | solution.py:63
  14.6 1.0 copy-start.2
  15.6 0.9 copy-start.3
  17.4 14.9 %collective-permute-start.3 = (f32[32,256]{1,0:T(8,128)S(1)}, f32[32,256]{1,0:T(8,128)S(1)}, u32[]{:S(2)}, u32[]{:S(2)}) collective-permute-start(f32[32,256]{1,0:T(8,128)S(1)} %get-tuple-element.37), channel_id=1, source_target_pairs={{0,192},{64,0},{128,64},{192,128},{1,193},{65,1},{129,65},{193,129... | collective-permute-start | bytes 98312 | tf_op jit(solution)/shard_map/ppermute | solution.py:63
  19.0 13.3 %collective-permute-start.4 = (f32[32,256]{1,0:T(8,128)S(1)}, f32[32,256]{1,0:T(8,128)S(1)}, u32[]{:S(2)}, u32[]{:S(2)}) collective-permute-start(f32[32,256]{1,0:T(8,128)S(1)} %get-tuple-element.38), channel_id=1, source_target_pairs={{0,128},{64,192},{128,0},{192,64},{1,129},{65,193},{129,1},{193,65... | collective-permute-start | bytes 98312 | tf_op jit(solution)/shard_map/ppermute | solution.py:63
  19.8 12.5 %collective-permute-start.5 = (f32[32,256]{1,0:T(8,128)S(1)}, f32[32,256]{1,0:T(8,128)S(1)}, u32[]{:S(2)}, u32[]{:S(2)}) collective-permute-start(f32[32,256]{1,0:T(8,128)S(1)} %get-tuple-element.39), channel_id=1, source_target_pairs={{0,64},{64,128},{128,192},{192,0},{1,65},{65,129},{129,193},{193,1... | collective-permute-start | bytes 98312 | tf_op jit(solution)/shard_map/ppermute | solution.py:63
  39.7 4.6 %collective-permute-start.6 = (bf16[96,128]{1,0:T(8,128)(2,1)S(1)}, bf16[96,128]{1,0:T(8,128)(2,1)S(1)}, u32[]{:S(2)}, u32[]{:S(2)}) collective-permute-start(bf16[96,128]{1,0:T(8,128)(2,1)S(1)} %relay_first.1), channel_id=1, source_target_pairs={{64,0},{128,64},{192,128},{65,1},{129,65},{193,129},{66,2},{130,66... | collective-permute-start | bytes 73736 | tf_op jit(solution)/shard_map/ppermute | solution.py:375
  51.8 4.6 %collective-permute-start.7 = (bf16[96,128]{1,0:T(8,128)(2,1)S(1)}, bf16[96,128]{1,0:T(8,128)(2,1)S(1)}, u32[]{:S(2)}, u32[]{:S(2)}) collective-permute-start(bf16[96,128]{1,0:T(8,128)(2,1)S(1)} %relay.2), channel_id=1, source_target_pairs={{64,0},{128,64},{192,128},{65,1},{129,65},{193,129},{66,2},{130,66... | collective-permute-start | bytes 73736 | tf_op jit(solution)/shard_map/ppermute | solution.py:375
  63.9 53.1 %copy-start.4 = (f32[1,4,108,32]{2,3,1,0:T(8,128)S(1)}, f32[1,4,108,32]{2,3,1,0:T(8,128)}, u32[]{:S(2)}) copy-start(f32[1,4,108,32]{2,3,1,0:T(8,128)} %param.15) | copy-start | bytes 165892
  63.9 53.1 %copy-start.5 = (f32[1,4,108,32]{2,3,1,0:T(8,128)S(1)}, f32[1,4,108,32]{2,3,1,0:T(8,128)}, u32[]{:S(2)}) copy-start(f32[1,4,108,32]{2,3,1,0:T(8,128)} %param.16) | copy-start | bytes 165892
  63.9 53.1 %copy-start.6 = (f32[1,4,108,32]{2,3,1,0:T(8,128)S(1)}, f32[1,4,108,32]{2,3,1,0:T(8,128)}, u32[]{:S(2)}) copy-start(f32[1,4,108,32]{2,3,1,0:T(8,128)} %param.17) | copy-start | bytes 165892
  63.9 4.7 %collective-permute-start.8 = (bf16[96,128]{1,0:T(8,128)(2,1)S(1)}, bf16[96,128]{1,0:T(8,128)(2,1)S(1)}, u32[]{:S(2)}, u32[]{:S(2)}) collective-permute-start(bf16[96,128]{1,0:T(8,128)(2,1)S(1)} %relay.3), channel_id=1, source_target_pairs={{64,0},{128,64},{192,128},{65,1},{129,65},{193,129},{66,2},{130,66... | collective-permute-start | bytes 73736 | tf_op jit(solution)/shard_map/ppermute | solution.py:375
  73.4 8.5 %collective-permute-start.9 = (bf16[4,8,4,32,128]{4,3,2,1,0:T(8,128)(2,1)S(1)}, bf16[4,8,4,32,128]{4,3,2,1,0:T(8,128)(2,1)S(1)}, u32[]{:S(2)}, u32[]{:S(2)}) collective-permute-start(bf16[4,8,4,32,128]{4,3,2,1,0:T(8,128)(2,1)S(1)} %get-tuple-element.43), channel_id=1, source_target_pairs={{0,1},{1,0},{2,3},{3,2},{4,5},{5,4},{6,7},{7,6},{8,9},{9,8},{10,11... | collective-permute-start | bytes 3145736 | tf_op jit(solution)/shard_map/ppermute | solution.py:59
  82.2 9.0 %collective-permute-start.10 = (bf16[8,4,32,128]{3,2,1,0:T(8,128)(2,1)S(1)}, bf16[8,4,32,128]{3,2,1,0:T(8,128)(2,1)S(1)}, u32[]{:S(2)}, u32[]{:S(2)}) collective-permute-start(bf16[8,4,32,128]{3,2,1,0:T(8,128)(2,1)S(1)} %get-tuple-element.45), channel_id=1, source_target_pairs={{0,2},{1,3},{2,4},{3,5},{4,6},{5,7},{6,0},{7,1},{8,10},{9,11},{10,... | collective-permute-start | bytes 786440 | tf_op jit(solution)/shard_map/ppermute | solution.py:59
  83.5 14.3 %collective-permute-start.11 = (bf16[8,4,32,128]{3,2,1,0:T(8,128)(2,1)S(1)}, bf16[8,4,32,128]{3,2,1,0:T(8,128)(2,1)S(1)}, u32[]{:S(2)}, u32[]{:S(2)}) collective-permute-start(bf16[8,4,32,128]{3,2,1,0:T(8,128)(2,1)S(1)} %get-tuple-element.46), channel_id=1, source_target_pairs={{0,4},{1,5},{2,6},{3,7},{4,0},{5,1},{6,2},{7,3},{8,12},{9,13},{10,... | collective-permute-start | bytes 786440 | tf_op jit(solution)/shard_map/ppermute | solution.py:59
  86.2 11.7 %collective-permute-start.12 = (bf16[8,4,32,128]{3,2,1,0:T(8,128)(2,1)S(1)}, bf16[8,4,32,128]{3,2,1,0:T(8,128)(2,1)S(1)}, u32[]{:S(2)}, u32[]{:S(2)}) collective-permute-start(bf16[8,4,32,128]{3,2,1,0:T(8,128)(2,1)S(1)} %get-tuple-element.47), channel_id=1, source_target_pairs={{0,6},{1,7},{2,0},{3,1},{4,2},{5,3},{6,4},{7,5},{8,14},{9,15},{10,... | collective-permute-start | bytes 786440 | tf_op jit(solution)/shard_map/ppermute | solution.py:59
  97.9 13.4 %collective-permute-start.13 = (bf16[4,32,128]{2,1,0:T(8,128)(2,1)S(1)}, bf16[4,32,128]{2,1,0:T(8,128)(2,1)S(1)}, u32[]{:S(2)}, u32[]{:S(2)}) collective-permute-start(bf16[4,32,128]{2,1,0:T(8,128)(2,1)S(1)} %get-tuple-element.49), channel_id=1, source_target_pairs={{0,8},{1,9},{2,10},{3,11},{4,12},{5,13},{6,14},{7,15},{8,16},{9,17... | collective-permute-start | bytes 98312 | tf_op jit(solution)/shard_map/ppermute | solution.py:59
  99.7 14.1 %collective-permute-start.14 = (bf16[4,32,128]{2,1,0:T(8,128)(2,1)S(1)}, bf16[4,32,128]{2,1,0:T(8,128)(2,1)S(1)}, u32[]{:S(2)}, u32[]{:S(2)}) collective-permute-start(bf16[4,32,128]{2,1,0:T(8,128)(2,1)S(1)} %get-tuple-element.50), channel_id=1, source_target_pairs={{0,16},{1,17},{2,18},{3,19},{4,20},{5,21},{6,22},{7,23},{8,24},{9,... | collective-permute-start | bytes 98312 | tf_op jit(solution)/shard_map/ppermute | solution.py:59
  102.7 11.8 %collective-permute-start.15 = (bf16[4,32,128]{2,1,0:T(8,128)(2,1)S(1)}, bf16[4,32,128]{2,1,0:T(8,128)(2,1)S(1)}, u32[]{:S(2)}, u32[]{:S(2)}) collective-permute-start(bf16[4,32,128]{2,1,0:T(8,128)(2,1)S(1)} %get-tuple-element.51), channel_id=1, source_target_pairs={{0,24},{1,25},{2,26},{3,27},{4,28},{5,29},{6,30},{7,31},{8,32},{9,... | collective-permute-start | bytes 98312 | tf_op jit(solution)/shard_map/ppermute | solution.py:59
  106.4 8.1 %collective-permute-start.16 = (bf16[4,32,128]{2,1,0:T(8,128)(2,1)S(1)}, bf16[4,32,128]{2,1,0:T(8,128)(2,1)S(1)}, u32[]{:S(2)}, u32[]{:S(2)}) collective-permute-start(bf16[4,32,128]{2,1,0:T(8,128)(2,1)S(1)} %get-tuple-element.52), channel_id=1, source_target_pairs={{0,32},{1,33},{2,34},{3,35},{4,36},{5,37},{6,38},{7,39},{8,40},{9,... | collective-permute-start | bytes 98312 | tf_op jit(solution)/shard_map/ppermute | solution.py:59
  106.9 7.5 %collective-permute-start.17 = (bf16[4,32,128]{2,1,0:T(8,128)(2,1)S(1)}, bf16[4,32,128]{2,1,0:T(8,128)(2,1)S(1)}, u32[]{:S(2)}, u32[]{:S(2)}) collective-permute-start(bf16[4,32,128]{2,1,0:T(8,128)(2,1)S(1)} %get-tuple-element.53), channel_id=1, source_target_pairs={{0,40},{1,41},{2,42},{3,43},{4,44},{5,45},{6,46},{7,47},{8,48},{9,... | collective-permute-start | bytes 98312 | tf_op jit(solution)/shard_map/ppermute | solution.py:59
  111.3 5.4 %collective-permute-start.18 = (bf16[4,32,128]{2,1,0:T(8,128)(2,1)S(1)}, bf16[4,32,128]{2,1,0:T(8,128)(2,1)S(1)}, u32[]{:S(2)}, u32[]{:S(2)}) collective-permute-start(bf16[4,32,128]{2,1,0:T(8,128)(2,1)S(1)} %get-tuple-element.54), channel_id=1, source_target_pairs={{0,48},{1,49},{2,50},{3,51},{4,52},{5,53},{6,54},{7,55},{8,56},{9,... | collective-permute-start | bytes 98312 | tf_op jit(solution)/shard_map/ppermute | solution.py:59
  113.7 3.3 %collective-permute-start.19 = (bf16[4,32,128]{2,1,0:T(8,128)(2,1)S(1)}, bf16[4,32,128]{2,1,0:T(8,128)(2,1)S(1)}, u32[]{:S(2)}, u32[]{:S(2)}) collective-permute-start(bf16[4,32,128]{2,1,0:T(8,128)(2,1)S(1)} %get-tuple-element.55), channel_id=1, source_target_pairs={{0,56},{1,57},{2,58},{3,59},{4,60},{5,61},{6,62},{7,63},{8,0},{9,1... | collective-permute-start | bytes 98312 | tf_op jit(solution)/shard_map/ppermute | solution.py:59
  117.8 23.4 %collective-permute-start.26 = (bf16[4,32,128]{2,1,0:T(8,128)(2,1)S(1)}, bf16[4,32,128]{2,1,0:T(8,128)(2,1)S(1)}, u32[]{:S(2)}, u32[]{:S(2)}) collective-permute-start(bf16[4,32,128]{2,1,0:T(8,128)(2,1)S(1)} %get-tuple-element.56), channel_id=1, source_target_pairs={{0,56},{1,57},{2,58},{3,59},{4,60},{5,61},{6,62},{7,63},{8,0},{9,1... | collective-permute-start | bytes 98312 | tf_op jit(solution)/shard_map/ppermute | solution.py:59
  120.1 21.0 %collective-permute-start.25 = (bf16[4,32,128]{2,1,0:T(8,128)(2,1)S(1)}, bf16[4,32,128]{2,1,0:T(8,128)(2,1)S(1)}, u32[]{:S(2)}, u32[]{:S(2)}) collective-permute-start(bf16[4,32,128]{2,1,0:T(8,128)(2,1)S(1)} %get-tuple-element.56), channel_id=1, source_target_pairs={{0,48},{1,49},{2,50},{3,51},{4,52},{5,53},{6,54},{7,55},{8,56},{9,... | collective-permute-start | bytes 98312 | tf_op jit(solution)/shard_map/ppermute | solution.py:59
  120.7 20.5 %collective-permute-start.24 = (bf16[4,32,128]{2,1,0:T(8,128)(2,1)S(1)}, bf16[4,32,128]{2,1,0:T(8,128)(2,1)S(1)}, u32[]{:S(2)}, u32[]{:S(2)}) collective-permute-start(bf16[4,32,128]{2,1,0:T(8,128)(2,1)S(1)} %get-tuple-element.56), channel_id=1, source_target_pairs={{0,40},{1,41},{2,42},{3,43},{4,44},{5,45},{6,46},{7,47},{8,48},{9,... | collective-permute-start | bytes 98312 | tf_op jit(solution)/shard_map/ppermute | solution.py:59
  121.7 19.4 %collective-permute-start.23 = (bf16[4,32,128]{2,1,0:T(8,128)(2,1)S(1)}, bf16[4,32,128]{2,1,0:T(8,128)(2,1)S(1)}, u32[]{:S(2)}, u32[]{:S(2)}) collective-permute-start(bf16[4,32,128]{2,1,0:T(8,128)(2,1)S(1)} %get-tuple-element.56), channel_id=1, source_target_pairs={{0,32},{1,33},{2,34},{3,35},{4,36},{5,37},{6,38},{7,39},{8,40},{9,... | collective-permute-start | bytes 98312 | tf_op jit(solution)/shard_map/ppermute | solution.py:59
  126.4 4.0 %collective-permute-start.20 = (bf16[4,32,128]{2,1,0:T(8,128)(2,1)S(1)}, bf16[4,32,128]{2,1,0:T(8,128)(2,1)S(1)}, u32[]{:S(2)}, u32[]{:S(2)}) collective-permute-start(bf16[4,32,128]{2,1,0:T(8,128)(2,1)S(1)} %get-tuple-element.56), channel_id=1, source_target_pairs={{0,8},{1,9},{2,10},{3,11},{4,12},{5,13},{6,14},{7,15},{8,16},{9,17... | collective-permute-start | bytes 98312 | tf_op jit(solution)/shard_map/ppermute | solution.py:59
  130.3 4.9 %collective-permute-start.21 = (bf16[4,32,128]{2,1,0:T(8,128)(2,1)S(1)}, bf16[4,32,128]{2,1,0:T(8,128)(2,1)S(1)}, u32[]{:S(2)}, u32[]{:S(2)}) collective-permute-start(bf16[4,32,128]{2,1,0:T(8,128)(2,1)S(1)} %get-tuple-element.56), channel_id=1, source_target_pairs={{0,16},{1,17},{2,18},{3,19},{4,20},{5,21},{6,22},{7,23},{8,24},{9,... | collective-permute-start | bytes 98312 | tf_op jit(solution)/shard_map/ppermute | solution.py:59
  135.2 5.9 %collective-permute-start.22 = (bf16[4,32,128]{2,1,0:T(8,128)(2,1)S(1)}, bf16[4,32,128]{2,1,0:T(8,128)(2,1)S(1)}, u32[]{:S(2)}, u32[]{:S(2)}) collective-permute-start(bf16[4,32,128]{2,1,0:T(8,128)(2,1)S(1)} %get-tuple-element.56), channel_id=1, source_target_pairs={{0,24},{1,25},{2,26},{3,27},{4,28},{5,29},{6,30},{7,31},{8,32},{9,... | collective-permute-start | bytes 98312 | tf_op jit(solution)/shard_map/ppermute | solution.py:59
  141.2 11.3 %collective-permute-start.29 = (bf16[8,4,32,128]{3,2,1,0:T(8,128)(2,1)S(1)}, bf16[8,4,32,128]{3,2,1,0:T(8,128)(2,1)S(1)}, u32[]{:S(2)}, u32[]{:S(2)}) collective-permute-start(bf16[8,4,32,128]{3,2,1,0:T(8,128)(2,1)S(1)} %bitcast_dynamic-update-slice_fusion.refs_0_), channel_id=1, source_target_pairs={{0,6},{1,7},{2,0},{3,1},{4,2},{5,3},{6,4},{7,5},{8,14},{9,15},{10,... | collective-permute-start | bytes 786440 | tf_op jit(solution)/shard_map/ppermute | solution.py:59
  143.4 14.1 %collective-permute-start.28 = (bf16[8,4,32,128]{3,2,1,0:T(8,128)(2,1)S(1)}, bf16[8,4,32,128]{3,2,1,0:T(8,128)(2,1)S(1)}, u32[]{:S(2)}, u32[]{:S(2)}) collective-permute-start(bf16[8,4,32,128]{3,2,1,0:T(8,128)(2,1)S(1)} %bitcast_dynamic-update-slice_fusion.refs_0_), channel_id=1, source_target_pairs={{0,4},{1,5},{2,6},{3,7},{4,0},{5,1},{6,2},{7,3},{8,12},{9,13},{10,... | collective-permute-start | bytes 786440 | tf_op jit(solution)/shard_map/ppermute | solution.py:59
  144.0 14.7 %collective-permute-start.27 = (bf16[8,4,32,128]{3,2,1,0:T(8,128)(2,1)S(1)}, bf16[8,4,32,128]{3,2,1,0:T(8,128)(2,1)S(1)}, u32[]{:S(2)}, u32[]{:S(2)}) collective-permute-start(bf16[8,4,32,128]{3,2,1,0:T(8,128)(2,1)S(1)} %bitcast_dynamic-update-slice_fusion.refs_0_), channel_id=1, source_target_pairs={{0,2},{1,3},{2,4},{3,5},{4,6},{5,7},{6,0},{7,1},{8,10},{9,11},{10,... | collective-permute-start | bytes 786440 | tf_op jit(solution)/shard_map/ppermute | solution.py:59
  144.0 17.4 %collective-permute-start.30 = (bf16[8,4,32,128]{3,2,1,0:T(8,128)(2,1)S(1)}, bf16[8,4,32,128]{3,2,1,0:T(8,128)(2,1)S(1)}, u32[]{:S(2)}, u32[]{:S(2)}) collective-permute-start(bf16[8,4,32,128]{3,2,1,0:T(8,128)(2,1)S(1)} %bitcast_dynamic-update-slice_fusion.refs_0_), channel_id=1, source_target_pairs={{0,1},{1,0},{2,3},{3,2},{4,5},{5,4},{6,7},{7,6},{8,9},{9,8},{10,11... | collective-permute-start | bytes 786440 | tf_op jit(solution)/shard_map/ppermute | solution.py:59
  152.5 8.9 %collective-permute-start.33 = (bf16[8,4,32,128]{3,2,1,0:T(8,128)(2,1)S(1)}, bf16[8,4,32,128]{3,2,1,0:T(8,128)(2,1)S(1)}, u32[]{:S(2)}, u32[]{:S(2)}) collective-permute-start(bf16[8,4,32,128]{3,2,1,0:T(8,128)(2,1)S(1)} %collective-permute-done.29.refs_3_), channel_id=1, source_target_pairs={{0,1},{1,0},{2,3},{3,2},{4,5},{5,4},{6,7},{7,6},{8,9},{9,8},{10,11... | collective-permute-start | bytes 786440 | tf_op jit(solution)/shard_map/ppermute | solution.py:59
  157.5 4.0 %collective-permute-start.32 = (bf16[8,4,32,128]{3,2,1,0:T(8,128)(2,1)S(1)}, bf16[8,4,32,128]{3,2,1,0:T(8,128)(2,1)S(1)}, u32[]{:S(2)}, u32[]{:S(2)}) collective-permute-start(bf16[8,4,32,128]{3,2,1,0:T(8,128)(2,1)S(1)} %collective-permute-done.28.refs_2_), channel_id=1, source_target_pairs={{0,1},{1,0},{2,3},{3,2},{4,5},{5,4},{6,7},{7,6},{8,9},{9,8},{10,11... | collective-permute-start | bytes 786440 | tf_op jit(solution)/shard_map/ppermute | solution.py:59
  158.7 3.9 %collective-permute-start.31 = (bf16[8,4,32,128]{3,2,1,0:T(8,128)(2,1)S(1)}, bf16[8,4,32,128]{3,2,1,0:T(8,128)(2,1)S(1)}, u32[]{:S(2)}, u32[]{:S(2)}) collective-permute-start(bf16[8,4,32,128]{3,2,1,0:T(8,128)(2,1)S(1)} %collective-permute-done.27.refs_1_), channel_id=1, source_target_pairs={{0,1},{1,0},{2,3},{3,2},{4,5},{5,4},{6,7},{7,6},{8,9},{9,8},{10,11... | collective-permute-start | bytes 786440 | tf_op jit(solution)/shard_map/ppermute | solution.py:59

commit v2 on v1

v2 whole, which is shorter than its diff:
```python
import functools

import jax
import jax.numpy as jnp
from jax import lax
from jax.experimental import pallas as pl
from jax.experimental.pallas import tpu as pltpu
from jax.sharding import PartitionSpec as P

BUCKETS = 4
STEP = 20
BETA_ONE = 0.8
BETA_TWO = 0.95
LEARN_RATE = 0.02
DECAY_RATE = 0.1
EPSILON = 1e-08

TOKENS = 128
FF = 27648
RANK = 32
MODEL = 5120
WIDTH = MODEL // 4
BUCKET_ROWS = FF // BUCKETS
OWNED = 108
LANES = 128
ZS, YS = 8, 4
BF16, F32 = jnp.bfloat16, jnp.float32
VMEM = pl.BlockSpec(memory_space=pltpu.VMEM)
ANY = pl.BlockSpec(memory_space=pl.ANY)
HBM = pl.BlockSpec(memory_space=pltpu.HBM)
CONTRACT_LAST = (((1,), (1,)), ((), ()))


def params(mib=16):
    return pltpu.CompilerParams(vmem_limit_bytes=mib * 1024 * 1024)


def shaped(shape, dtype):
    return jax.ShapeDtypeStruct(shape, dtype)


def z_pos():
    return lax.axis_index("dp") // 8


def y_pos():
    return (lax.axis_index("dp") // 2) % YS


def core_pos():
    return lax.axis_index("dp") % 2


def over_dp(value, zx=0, dy=0, dc=0):
    pairs = []
    for z in range(ZS):
        for y in range(YS):
            for c in range(2):
                target = (z ^ zx) * 8 + ((y + dy) % YS) * 2 + (c + dc) % 2
                pairs.append((z * 8 + y * 2 + c, target))
    return lax.ppermute(value, "dp", pairs)


def over_section(value, steps):
    return lax.ppermute(value, "section", [(i, (i + steps) % 4) for i in range(4)])


def slice_kernel(db_ref, ua_ref, *refs):
    outs, sems = refs[:4], refs[4]
    here = lax.axis_index("section")
    copies = []
    for k, out in enumerate(outs):
        columns = pl.ds(pl.multiple_of(lax.rem(here + k, 4) * WIDTH, LANES), WIDTH)
        for i, ref in enumerate((db_ref, ua_ref)):
            copies.append(
                pltpu.make_async_copy(
                    ref.at[:, columns], out.at[pl.ds(i * RANK, RANK), :], sems.at[2 * k + i]
                )
            )
            copies[-1].start()
    for copy in copies:
        copy.wait()


def slices(db, ua):
    return pl.pallas_call(
        slice_kernel,
        out_shape=[shaped((2 * RANK, WIDTH), BF16)] * 4,
        in_specs=[ANY] * 2,
        out_specs=[ANY] * 4,
        scratch_shapes=[pltpu.SemaphoreType.DMA((8,))],
        name="slices",
    )(db, ua)


def activation_kernel(slope, first, size, pre_ref, out_ref, held, sems):
    parts = held.shape[1] // size
    copies = []
    for i in range(parts):
        copies.append(
            pltpu.make_async_copy(
                pre_ref.at[:, pl.ds(first + i * size, size)],
                held.at[:, pl.ds(i * size, size)],
                sems.at[i],
            )
        )
        copies[-1].start()

    def chunk(i, _):
        columns = pl.ds(pl.multiple_of(i * 256, 256), 256)
        for row in range(0, TOKENS, 32):
            rows = slice(row, row + 32)
            half = 0.5 * held[rows, columns].astype(F32)
            t = jnp.tanh(half)
            h = half + half * t
            if slope:
                h = 0.5 * ((1.0 + t) + h * (1.0 - t))
            out_ref[rows, columns] = h.astype(BF16)
        return 0

    for i, copy in enumerate(copies):
        copy.wait()
        lax.fori_loop(i * size // 256, (i + 1) * size // 256, chunk, 0)


def activation(pre, bucket=None):
    slope = bucket is None
    width, first, size = (FF, 0, 6912) if slope else (BUCKET_ROWS, bucket * BUCKET_ROWS, 2304)
    parts = width // size
    return pl.pallas_call(
        functools.partial(activation_kernel, slope, first, size),
        out_shape=shaped((TOKENS, width), BF16),
        in_specs=[HBM],
        out_specs=VMEM,
        scratch_shapes=[
            pltpu.VMEM((TOKENS, width), BF16),
            pltpu.SemaphoreType.DMA((parts,)),
        ],
        compiler_params=params(18 if slope else 6),
        cost_estimate=pl.CostEstimate(
            flops=10 * TOKENS * width,
            bytes_accessed=4 * TOKENS * width,
            transcendentals=TOKENS * width,
        ),
        name="slope" if slope else "hidden",
    )(pre)


def share_kernel(g_ref, w0, w1, w2, w3, *outs):
    ws = (w0, w1, w2, w3)
    for k, out in enumerate(outs):
        db = ws[k][0:RANK, :]
        out[:, 0:LANES] = lax.dot_general(
            db, g_ref[...], CONTRACT_LAST, preferred_element_type=F32
        )
        rows = jnp.concatenate([ws[(k - m) % 4][RANK:, :] for m in (1, 2, 3, 0)], axis=0)
        out[:, LANES:] = lax.dot_general(db, rows, CONTRACT_LAST, preferred_element_type=F32)


def shares(g, ws):
    return pl.pallas_call(
        share_kernel,
        out_shape=[shaped((RANK, 2 * LANES), F32)] * 4,
        in_specs=[VMEM] * 5,
        out_specs=[VMEM] * 4,
        compiler_params=params(),
        name="shares",
    )(g, *ws)


def low_of(share_refs, above_ref):
    total = share_refs[0][...] + share_refs[1][...] + share_refs[2][...] + share_refs[3][...]
    low = total[:, 0:LANES]
    if above_ref is not None:
        low = low + jnp.dot(
            total[:, LANES : LANES + 3 * RANK],
            above_ref[...].astype(F32),
            preferred_element_type=F32,
            precision=lax.Precision.HIGHEST,
        )
    return low


def relay_kernel(first, *refs):
    share_refs, refs = refs[:4], refs[4:]
    above_ref = None
    if not first:
        above_ref, refs = refs[0], refs[1:]
    slope_ref, da_ref, ub_ref, out_ref = refs
    low = low_of(share_refs, above_ref).T.astype(BF16)

    def chunk(i, total):
        columns = pl.ds(pl.multiple_of(i * 512, 512), 512)
        upstream = jnp.dot(low, da_ref[:, columns], preferred_element_type=F32)
        delta = (upstream * slope_ref[:, columns].astype(F32)).astype(BF16)
        return total + lax.dot_general(
            ub_ref[:, columns], delta, CONTRACT_LAST, preferred_element_type=F32
        )

    total = lax.fori_loop(
        0, FF // 512, chunk, jnp.zeros((RANK, TOKENS), F32), unroll=18
    )
    out_ref[0:RANK, :] = total.astype(BF16)
    if first:
        out_ref[RANK:, :] = jnp.zeros((2 * RANK, LANES), BF16)
    else:
        out_ref[RANK:, :] = above_ref[0 : 2 * RANK, :]


def relay(share, above, slope, da, ub):
    first = above is None
    return pl.pallas_call(
        functools.partial(relay_kernel, first),
        out_shape=shaped((3 * RANK, LANES), BF16),
        in_specs=[VMEM] * (7 if first else 8),
        out_specs=VMEM,
        compiler_params=params(14),
        name="relay_first" if first else "relay",
    )(*share, *([] if first else [above]), slope, da, ub)


def grad_kernel(s0, s1, s2, s3, above_ref, h0, h1, h2, h3, keep_ref, send_ref, grad):
    low = low_of((s0, s1, s2, s3), above_ref).astype(BF16)
    core = core_pos()
    lane = lax.broadcasted_iota(jnp.int32, (RANK, LANES), 1)
    for bucket, hidden_ref in enumerate((h0, h1, h2, h3)):
        grad[...] = jnp.dot(low, hidden_ref[...], preferred_element_type=F32)
        for z in range(ZS):
            for y in range(YS):
                pair = []
                for c in range(2):
                    start = (z * 8 + y * 2 + c) * OWNED
                    base, shift = start // LANES * LANES, start % LANES
                    piece = grad[:, base : base + LANES]
                    if shift:
                        piece = pltpu.roll(piece, LANES - shift, 1)
                    if shift + OWNED > LANES:
                        more = pltpu.roll(
                            grad[:, base + LANES : base + 2 * LANES], LANES - shift, 1
                        )
                        piece = jnp.where(lane < LANES - shift, piece, more)
                    pair.append(piece)
                keep_ref[y, z, bucket] = jnp.where(core == 0, pair[0], pair[1]).astype(BF16)
                send_ref[y, z, bucket] = jnp.where(core == 0, pair[1], pair[0]).astype(BF16)


def grads(share, above, hidden):
    return pl.pallas_call(
        grad_kernel,
        out_shape=[shaped((YS, ZS, BUCKETS, RANK, LANES), BF16)] * 2,
        in_specs=[VMEM] * 9,
        out_specs=[VMEM] * 2,
        scratch_shapes=[pltpu.VMEM((RANK, BUCKET_ROWS), F32)],
        compiler_params=params(14),
        name="grads",
    )(*share, above, *hidden)


def core_sum_kernel(keep_ref, got_ref, own_ref, *outs):
    here = y_pos()
    own_ref[...] = keep_ref[here].astype(F32) + got_ref[here].astype(F32)
    for k, out in enumerate(outs):
        there = lax.rem(here + k + 1, YS)
        out[...] = (keep_ref[there].astype(F32) + got_ref[there].astype(F32)).astype(BF16)


def core_sum(keep, got):
    block = (ZS, BUCKETS, RANK, LANES)
    return pl.pallas_call(
        core_sum_kernel,
        out_shape=[shaped(block, F32)] + [shaped(block, BF16)] * 3,
        in_specs=[VMEM] * 2,
        out_specs=[VMEM] * 4,
        compiler_params=params(),
        name="core_sum",
    )(keep, got)


def y_sum_kernel(own_ref, g1, g2, g3, out_own, *outs):
    here = z_pos()
    for k, out in enumerate((out_own, *outs)):
        for far in range(2):
            z = here ^ (k + 4 * far)
            total = own_ref[z] + g1[z].astype(F32) + g2[z].astype(F32) + g3[z].astype(F32)
            out[far] = total.astype(out.dtype)


def y_sum(own, got):
    block = (2, BUCKETS, RANK, LANES)
    return pl.pallas_call(
        y_sum_kernel,
        out_shape=[shaped(block, F32)] + [shaped(block, BF16)] * 3,
        in_specs=[VMEM] * 4,
        out_specs=[VMEM] * 4,
        compiler_params=params(8),
        name="y_sum",
    )(own, *got)


def z_sum_kernel(own_ref, g1, g2, g3, out_own, out_far):
    total = [
        own_ref[far] + g1[far].astype(F32) + g2[far].astype(F32) + g3[far].astype(F32)
        for far in range(2)
    ]
    out_own[...] = total[0]
    out_far[...] = total[1].astype(BF16)


def z_sum(own, got):
    block = (BUCKETS, RANK, LANES)
    return pl.pallas_call(
        z_sum_kernel,
        out_shape=[shaped(block, F32), shaped(block, BF16)],
        in_specs=[VMEM] * 4,
        out_specs=[VMEM] * 2,
        compiler_params=params(4),
        name="z_sum",
    )(own, *got)


def adamw_kernel(own_ref, got_ref, master, moment, second, *outs):
    weight_out, master_out, moment_out, second_out = outs
    gradient = (own_ref[...] + got_ref[...].astype(F32))[:, :, 0:OWNED]
    weights = master[...]
    first_new = BETA_ONE * moment[...] + (1.0 - BETA_ONE) * gradient
    second_new = BETA_TWO * second[...] + (1.0 - BETA_TWO) * gradient * gradient
    first_hat = first_new / (1.0 - BETA_ONE**STEP)
    second_hat = second_new / (1.0 - BETA_TWO**STEP)
    weights_new = weights - LEARN_RATE * (
        first_hat / (jnp.sqrt(second_hat) + EPSILON) + DECAY_RATE * weights
    )
    weight_out[...] = jnp.zeros_like(weight_out)
    weight_out[:, :, 0:OWNED] = weights_new.astype(BF16)
    master_out[...] = weights_new
    moment_out[...] = first_new
    second_out[...] = second_new


def adamw(own, got, master, moment, second):
    state = shaped((BUCKETS, RANK, OWNED), F32)
    return pl.pallas_call(
        adamw_kernel,
        out_shape=[shaped((BUCKETS, RANK, LANES), BF16)] + [state] * 3,
        in_specs=[VMEM] * 5,
        out_specs=[VMEM] * 4,
        compiler_params=params(4),
        name="adamw",
    )(own, got, master, moment, second)


def assemble_kernel(*refs):
    arrays, (out_ref, blocks, sems) = refs[:8], refs[8:]
    core, y_here, z_here = core_pos(), y_pos(), z_pos()
    copies = []
    for side in range(2):
        for k in range(YS):
            copies.append(
                pltpu.make_async_copy(
                    arrays[side * YS + k],
                    blocks.at[lax.rem(core + side, 2), lax.rem(y_here + YS - k, YS)],
                    sems.at[side * YS + k],
                )
            )
            copies[-1].start()
    for copy in copies:
        copy.wait()
    lane = lax.broadcasted_iota(jnp.int32, (RANK, LANES), 1)
    places = [2 * ((z_here ^ z) & 3) + ((z_here ^ z) >> 2) for z in range(ZS)]
    for tile in range(FF // LANES):
        value = None
        first = tile * LANES // OWNED
        last = (tile * LANES + LANES - 1) // OWNED
        for piece in range(first, last + 1):
            bucket, owner = divmod(piece, 64)
            z, y, c = owner // 8, owner // 2 % YS, owner % 2
            block = blocks[c, y, places[z], bucket].astype(F32)
            start = piece * OWNED - tile * LANES
            if start % LANES:
                block = pltpu.roll(block, start % LANES, 1)
            value = block if value is None else jnp.where(lane < start, value, block)
        out_ref[:, tile * LANES : (tile + 1) * LANES] = value.astype(BF16)


def assemble(arrays):
    return pl.pallas_call(
        assemble_kernel,
        out_shape=shaped((RANK, FF), BF16),
        in_specs=[ANY] * 8,
        out_specs=VMEM,
        scratch_shapes=[
            pltpu.VMEM((2, YS, ZS, BUCKETS, RANK, LANES), BF16),
            pltpu.SemaphoreType.DMA((8,)),
        ],
        compiler_params=params(),
        name="assemble",
    )(*arrays)


def per_device(out_grad, pre_act, down_a, down_b, up_a, up_b, master, moment, second):
    da, ub = down_a[0].T, up_b[0].T
    mine = slices(down_b[0], up_a[0].T)
    ws = [mine[0]] + [over_section(mine[k], k) for k in (1, 2, 3)]
    slope = activation(pre_act[0])
    ws, slope = lax.optimization_barrier((ws, slope))
    share = shares(out_grad, ws)
    share = [share[0]] + [over_section(share[k], -k) for k in (1, 2, 3)]
    above, hidden, pre = None, [], pre_act[0]
    for i in range(3):
        sent = relay(share, above, slope, da, ub)
        above = lax.ppermute(sent, "section", [(1, 0), (2, 1), (3, 2)])
        if i < 2:
            pre, _ = lax.optimization_barrier((pre, sent))
            hidden += [activation(pre, 2 * i + b) for b in range(2)]
            above, *hidden = lax.optimization_barrier((above, *hidden))
    keep, send = grads(share, above, hidden)
    own, *sends = core_sum(keep, over_dp(send, dc=1))
    own, *sends = y_sum(own, [over_dp(sends[k - 1], dy=k) for k in (1, 2, 3)])
    own, send = z_sum(own, [over_dp(sends[k - 1], zx=k) for k in (1, 2, 3)])
    state = [a[0].transpose(0, 2, 1) for a in (master, moment, second)]
    weight, *state = adamw(own, over_dp(send, zx=4), *state)
    pair = jnp.stack([weight, over_dp(weight, zx=4)])
    column = jnp.concatenate([pair] + [over_dp(pair, zx=k) for k in (1, 2, 3)])
    plane = [column] + [over_dp(column, dy=k) for k in (1, 2, 3)]
    rows = assemble(plane + [over_dp(a, dc=1) for a in plane])
    return (rows.T[None], *[a.transpose(0, 2, 1)[None] for a in state])


def solution(mesh):
    return jax.shard_map(
        per_device,
        mesh=mesh,
        in_specs=(
            P("dp", "section"),
            P("section", "dp", None),
            P("section", None, None),
            P("section", None, None),
            P("section", None, None),
            P("section", None, None),
            P("section", None, "dp", None),
            P("section", None, "dp", None),
            P("section", None, "dp", None),
        ),
        out_specs=(
            P("section", None, None),
            P("section", None, "dp", None),
            P("section", None, "dp", None),
            P("section", None, "dp", None),
        ),
        check_vma=False,
    )
```

time: 166 us -> 153 us (0.922)
  waiting for transfers between devices: 46.8 us -> 36 us
  starting transfers between devices: 69.8 us -> 60.5 us
  Pallas kernels: 45.7 us -> 52.3 us
    pallas_call x1, Pallas kernels: 2.09 us -> 21 us  [slices(): pl.pallas_call(slice_kernel, out_shape=[shaped((2 * RANK, WIDTH), BF16)]...]
    pallas_call x5 -> x10, Pallas kernels: 39.1 us -> 26.8 us  [the longest x3 14.8 us: relay(): pl.pallas_call(functools.partial(relay_kernel, first), out_shape=shaped((...]
    ppermute x25 -> x19, starting transfers between devices: 57.2 us -> 48.7 us  [over_dp(): return lax.ppermute(value, 'dp', pairs)]
    ppermute x25 -> x19, waiting for transfers between devices: 30.7 us -> 26.3 us  [over_dp(): return lax.ppermute(value, 'dp', pairs)]
    ppermute x3, waiting for transfers between devices: 9.81 us -> 5.74 us  [per_device(): above = lax.ppermute(sent, 'section', [(1, 0), (2, 1), (3, 2)])]
    ppermute x6, waiting for transfers between devices: 6.23 us -> 3.98 us  [over_section(): lax.ppermute(value, 'section', [(i, (i + steps) % 4) for i in range(4)])]
  transfers between devices with their start and end apart: 34 -> 28, of which waited for: 14 -> 16; matrix products, arithmetic and copies ran while one was open for 0% -> 0% of each run, Pallas kernels for 7% -> 7%
where the time goes in v2:
time: 153 us
  starting transfers between devices  60.5 us (40%)
  Pallas kernels  52.3 us (34%)
  waiting for transfers between devices  36 us (24%)
  local copies, waits for them, and re-layouts  3.09 us (2%)
    ppermute x19, starting transfers between devices, over_dp(): return lax.ppermute(value, 'dp', pairs)  48.7 us
    ppermute x19, waiting for transfers between devices, over_dp(): return lax.ppermute(value, 'dp', pairs)  26.3 us
    pallas_call x1, Pallas kernels, slices(): pl.pallas_call(slice_kernel, out_shape=[shaped((2 * RANK, WIDTH), BF16)]...  21 us
    pallas_call x3, Pallas kernels, relay(): pl.pallas_call(functools.partial(relay_kernel, first), out_shape=shaped((...  14.8 us
    pallas_call x5, Pallas kernels, activation(): pl.pallas_call(functools.partial(activation_kernel, slope, first, size),...  10.6 us
    ppermute x6, starting transfers between devices, over_section(): lax.ppermute(value, 'section', [(i, (i + steps) % 4) for i in range(4)])  7.85 us
    ppermute x3, waiting for transfers between devices, per_device(): above = lax.ppermute(sent, 'section', [(1, 0), (2, 1), (3, 2)])  5.74 us
    ppermute x6, waiting for transfers between devices, over_section(): lax.ppermute(value, 'section', [(i, (i + steps) % 4) for i in range(4)])  3.98 us
  transfers between devices with their start and end apart: 28, of which 16 were waited for; matrix products, arithmetic and copies ran while one was open for 0% of the time, Pallas kernels for 7%

profile of v2, /device:TPU:1, one launch (start us, length us, event | category | flops | bytes accessed | tf_op | source)
XLA Modules:
  0.0 152.9 jit_solution(4555419177804151386)
XLA Ops:
  0.6 21.0 %slices.1 = (bf16[64,1280]{1,0:T(8,128)(2,1)}, bf16[64,1280]{1,0:T(8,128)(2,1)}, bf16[64,1280]{1,0:T(8,128)(2,1)}, bf16[64,1280]{1,0:T(8,128)(2,1)}) custom-call(bf16[32,5120]{1,0:T(8,128)(2,1)} %bitcast.52, bf16[32,5120]{1,0:T(8,128)(2,1)} %bitcast.53), custom_call_target="tpu_custom_call" | custom-call | tf_op jit(solution)/shard_map/slices/pallas_call | solution.py:86
  21.7 2.1 %collective-permute-start = (bf16[64,1280]{1,0:T(8,128)(2,1)}, bf16[64,1280]{1,0:T(8,128)(2,1)S(1)}, u32[]{:S(2)}, u32[]{:S(2)}) collective-permute-start(bf16[64,1280]{1,0:T(8,128)(2,1)} %get-tuple-element.44), channel_id=1, source_target_pairs={{0,64},{64,128},{128,192},{192,0},{1,65},{65,129},{129,193},{193,1... | collective-permute-start | bytes 491528 | tf_op jit(solution)/shard_map/ppermute | solution.py:65
  23.8 2.5 %collective-permute-start.1 = (bf16[64,1280]{1,0:T(8,128)(2,1)}, bf16[64,1280]{1,0:T(8,128)(2,1)S(1)}, u32[]{:S(2)}, u32[]{:S(2)}) collective-permute-start(bf16[64,1280]{1,0:T(8,128)(2,1)} %get-tuple-element.45), channel_id=1, source_target_pairs={{0,128},{64,192},{128,0},{192,64},{1,129},{65,193},{129,1},{193,65... | collective-permute-start | bytes 491528 | tf_op jit(solution)/shard_map/ppermute | solution.py:65
  26.2 1.2 collective-permute-start.2
  27.4 3.0 %copy-done = bf16[1,128,27648]{2,1,0:T(8,128)(2,1)S(1)} copy-done((bf16[1,128,27648]{2,1,0:T(8,128)(2,1)S(1)}, bf16[1,128,27648]{2,1,0:T(8,128)(2,1)}, u32[]{:S(2)}) %copy-start) | copy-done | bytes 7077912
  30.4 6.6 %slope.1.refs_4_.refs_5_ = bf16[128,27648]{1,0:T(8,128)(2,1)S(1)} custom-call(bf16[128,27648]{1,0:T(8,128)(2,1)S(1)} %bitcast.36), custom_call_target="tpu_custom_call" | custom-call | flops 35389440 | bytes 14155776 | tf_op jit(solution)/shard_map/slope/pallas_call | solution.py:130
  37.0 0.0 collective-permute-done.w1
  37.1 0.0 collective-permute-done.2.w3
  37.1 0.9 shares.1
  38.0 0.0 collective-permute-start.3
  38.1 2.1 %collective-permute-start.4 = (f32[32,256]{1,0:T(8,128)S(1)}, f32[32,256]{1,0:T(8,128)S(1)}, u32[]{:S(2)}, u32[]{:S(2)}) collective-permute-start(f32[32,256]{1,0:T(8,128)S(1)} %get-tuple-element.53), channel_id=1, source_target_pairs={{0,128},{64,192},{128,0},{192,64},{1,129},{65,193},{129,1},{193,65... | collective-permute-start | bytes 98312 | tf_op jit(solution)/shard_map/ppermute | solution.py:65
  40.2 0.0 collective-permute-start.5
  40.2 0.7 collective-permute-done.3.refs_1_.s1
  40.8 1.6 %collective-permute-done.4.refs_2_.s2 = f32[32,256]{1,0:T(8,128)S(1)} collective-permute-done((f32[32,256]{1,0:T(8,128)S(1)}, f32[32,256]{1,0:T(8,128)S(1)}, u32[]{:S(2)}, u32[]{:S(2)}) %collective-permute-start.4) | collective-permute-done | bytes 32800 | tf_op jit(solution)/shard_map/ppermute | solution.py:65
  42.4 1.7 %collective-permute-done.5.refs_3_.s3 = f32[32,256]{1,0:T(8,128)S(1)} collective-permute-done((f32[32,256]{1,0:T(8,128)S(1)}, f32[32,256]{1,0:T(8,128)S(1)}, u32[]{:S(2)}, u32[]{:S(2)}) %collective-permute-start.5) | collective-permute-done | bytes 32800 | tf_op jit(solution)/shard_map/ppermute | solution.py:65
  44.1 4.8 %relay_first.1 = bf16[96,128]{1,0:T(8,128)(2,1)S(1)} custom-call(f32[32,256]{1,0:T(8,128)S(1)} %get-tuple-element.51.refs_0_.s0, f32[32,256]{1,0:T(8,128)S(1)} %collective-permute-done.3.refs_1_.s1, f32[32,256]{1,0:T(8,128)S(1)} %collective-permute-done.4.refs_2_.s2, f32[32,256]{1,0:T(8,128)S(1)} %collective-permute-done.5.refs_3_.s3, ...), custom_call_target="tpu_custom_call" | custom-call | tf_op jit(solution)/shard_map/relay_first/pallas_call | solution.py:212
  49.0 1.3 collective-permute-start.6
  50.3 1.0 hidden.5.h1
  51.3 1.0 hidden.4.h0
  52.3 1.2 collective-permute-done.6.refs_4_
  53.5 5.0 %relay.2 = bf16[96,128]{1,0:T(8,128)(2,1)S(1)} custom-call(f32[32,256]{1,0:T(8,128)S(1)} %get-tuple-element.51.refs_0_.s0, f32[32,256]{1,0:T(8,128)S(1)} %collective-permute-done.3.refs_1_.s1, f32[32,256]{1,0:T(8,128)S(1)} %collective-permute-done.4.refs_2_.s2, f32[32,256]{1,0:T(8,128)S(1)} %collective-permute-done.5.refs_3_.s3, ...), custom_call_target="tpu_custom_call" | custom-call | tf_op jit(solution)/shard_map/relay/pallas_call | solution.py:212
  58.5 1.3 collective-permute-start.7
  59.8 1.0 hidden.7.h3
  60.8 1.0 hidden.6.h2
  61.8 1.2 collective-permute-done.7.refs_4_
  63.1 5.0 %relay.3 = bf16[96,128]{1,0:T(8,128)(2,1)S(1)} custom-call(f32[32,256]{1,0:T(8,128)S(1)} %get-tuple-element.51.refs_0_.s0, f32[32,256]{1,0:T(8,128)S(1)} %collective-permute-done.3.refs_1_.s1, f32[32,256]{1,0:T(8,128)S(1)} %collective-permute-done.4.refs_2_.s2, f32[32,256]{1,0:T(8,128)S(1)} %collective-permute-done.5.refs_3_.s3, ...), custom_call_target="tpu_custom_call" | custom-call | tf_op jit(solution)/shard_map/relay/pallas_call | solution.py:212
  68.0 1.3 collective-permute-start.8
  69.3 3.3 %collective-permute-done.8.above_ref = bf16[96,128]{1,0:T(8,128)(2,1)S(1)} collective-permute-done((bf16[96,128]{1,0:T(8,128)(2,1)S(1)}, bf16[96,128]{1,0:T(8,128)(2,1)S(1)}, u32[]{:S(2)}, u32[]{:S(2)}) %collective-permute-start.8) | collective-permute-done | bytes 24608 | tf_op jit(solution)/shard_map/ppermute | solution.py:410
  72.6 1.4 grads.1
  74.0 7.0 %collective-permute-start.9 = (bf16[4,8,4,32,128]{4,3,2,1,0:T(8,128)(2,1)S(1)}, bf16[4,8,4,32,128]{4,3,2,1,0:T(8,128)(2,1)S(1)}, u32[]{:S(2)}, u32[]{:S(2)}) collective-permute-start(bf16[4,8,4,32,128]{4,3,2,1,0:T(8,128)(2,1)S(1)} %get-tuple-element.67), channel_id=1, source_target_pairs={{0,1},{1,0},{2,3},{3,2},{4,5},{5,4},{6,7},{7,6},{8,9},{9,8},{10,11... | collective-permute-start | bytes 3145736 | tf_op jit(solution)/shard_map/ppermute | solution.py:61
  81.0 2.3 %collective-permute-done.9.got_ref = bf16[4,8,4,32,128]{4,3,2,1,0:T(8,128)(2,1)S(1)} collective-permute-done((bf16[4,8,4,32,128]{4,3,2,1,0:T(8,128)(2,1)S(1)}, bf16[4,8,4,32,128]{4,3,2,1,0:T(8,128)(2,1)S(1)}, u32[]{:S(2)}, u32[]{:S(2)}) %collective-permute-start.9) | collective-permute-done | bytes 1048608 | tf_op jit(solution)/shard_map/ppermute | solution.py:61
  83.3 0.2 core_sum.1
  83.5 1.4 collective-permute-start.10
  84.9 2.6 %collective-permute-start.11 = (bf16[8,4,32,128]{3,2,1,0:T(8,128)(2,1)S(1)}, bf16[8,4,32,128]{3,2,1,0:T(8,128)(2,1)S(1)}, u32[]{:S(2)}, u32[]{:S(2)}) collective-permute-start(bf16[8,4,32,128]{3,2,1,0:T(8,128)(2,1)S(1)} %get-tuple-element.70), channel_id=1, source_target_pairs={{0,4},{1,5},{2,6},{3,7},{4,0},{5,1},{6,2},{7,3},{8,12},{9,13},{10,... | collective-permute-start | bytes 786440 | tf_op jit(solution)/shard_map/ppermute | solution.py:61
  87.5 1.1 collective-permute-start.12
  88.6 3.9 %collective-permute-done.10.g1 = bf16[8,4,32,128]{3,2,1,0:T(8,128)(2,1)S(1)} collective-permute-done((bf16[8,4,32,128]{3,2,1,0:T(8,128)(2,1)S(1)}, bf16[8,4,32,128]{3,2,1,0:T(8,128)(2,1)S(1)}, u32[]{:S(2)}, u32[]{:S(2)}) %collective-permute-start.10) | collective-permute-done | bytes 262176 | tf_op jit(solution)/shard_map/ppermute | solution.py:61
  92.4 6.7 %collective-permute-done.11.g2 = bf16[8,4,32,128]{3,2,1,0:T(8,128)(2,1)S(1)} collective-permute-done((bf16[8,4,32,128]{3,2,1,0:T(8,128)(2,1)S(1)}, bf16[8,4,32,128]{3,2,1,0:T(8,128)(2,1)S(1)}, u32[]{:S(2)}, u32[]{:S(2)}) %collective-permute-start.11) | collective-permute-done | bytes 262176 | tf_op jit(solution)/shard_map/ppermute | solution.py:61
  99.2 0.1 y_sum.1
  99.3 1.7 %collective-permute-start.13 = (bf16[2,4,32,128]{3,2,1,0:T(8,128)(2,1)S(1)}, bf16[2,4,32,128]{3,2,1,0:T(8,128)(2,1)S(1)}, u32[]{:S(2)}, u32[]{:S(2)}) collective-permute-start(bf16[2,4,32,128]{3,2,1,0:T(8,128)(2,1)S(1)} %get-tuple-element.73), channel_id=1, source_target_pairs={{0,8},{1,9},{2,10},{3,11},{4,12},{5,13},{6,14},{7,15},{8,0},{9,1},... | collective-permute-start | bytes 196616 | tf_op jit(solution)/shard_map/ppermute | solution.py:61
  101.0 3.0 %collective-permute-start.14 = (bf16[2,4,32,128]{3,2,1,0:T(8,128)(2,1)S(1)}, bf16[2,4,32,128]{3,2,1,0:T(8,128)(2,1)S(1)}, u32[]{:S(2)}, u32[]{:S(2)}) collective-permute-start(bf16[2,4,32,128]{3,2,1,0:T(8,128)(2,1)S(1)} %get-tuple-element.74), channel_id=1, source_target_pairs={{0,16},{1,17},{2,18},{3,19},{4,20},{5,21},{6,22},{7,23},{8,24},{9,... | collective-permute-start | bytes 196616 | tf_op jit(solution)/shard_map/ppermute | solution.py:61
  104.0 0.0 collective-permute-start.15
  104.0 0.0 collective-permute-done.13.g1
  104.0 2.3 %collective-permute-done.14.g2 = bf16[2,4,32,128]{3,2,1,0:T(8,128)(2,1)S(1)} collective-permute-done((bf16[2,4,32,128]{3,2,1,0:T(8,128)(2,1)S(1)}, bf16[2,4,32,128]{3,2,1,0:T(8,128)(2,1)S(1)}, u32[]{:S(2)}, u32[]{:S(2)}) %collective-permute-start.14) | collective-permute-done | bytes 65568 | tf_op jit(solution)/shard_map/ppermute | solution.py:61
  106.3 2.7 %collective-permute-done.15.g3 = bf16[2,4,32,128]{3,2,1,0:T(8,128)(2,1)S(1)} collective-permute-done((bf16[2,4,32,128]{3,2,1,0:T(8,128)(2,1)S(1)}, bf16[2,4,32,128]{3,2,1,0:T(8,128)(2,1)S(1)}, u32[]{:S(2)}, u32[]{:S(2)}) %collective-permute-start.15) | collective-permute-done | bytes 65568 | tf_op jit(solution)/shard_map/ppermute | solution.py:61
  109.0 4.7 %collective-permute-start.16 = (bf16[4,32,128]{2,1,0:T(8,128)(2,1)S(1)}, bf16[4,32,128]{2,1,0:T(8,128)(2,1)S(1)}, u32[]{:S(2)}, u32[]{:S(2)}) collective-permute-start(bf16[4,32,128]{2,1,0:T(8,128)(2,1)S(1)} %get-tuple-element.77), channel_id=1, source_target_pairs={{0,32},{1,33},{2,34},{3,35},{4,36},{5,37},{6,38},{7,39},{8,40},{9,... | collective-permute-start | bytes 98312 | tf_op jit(solution)/shard_map/ppermute | solution.py:61
  113.7 2.1 %collective-permute-done.16.got_ref = bf16[4,32,128]{2,1,0:T(8,128)(2,1)S(1)} collective-permute-done((bf16[4,32,128]{2,1,0:T(8,128)(2,1)S(1)}, bf16[4,32,128]{2,1,0:T(8,128)(2,1)S(1)}, u32[]{:S(2)}, u32[]{:S(2)}) %collective-permute-start.16) | collective-permute-done | bytes 32800 | tf_op jit(solution)/shard_map/ppermute | solution.py:61
  115.8 0.7 adamw.1
  116.5 4.6 %collective-permute-start.17 = (bf16[4,32,128]{2,1,0:T(8,128)(2,1)S(1)}, bf16[4,32,128]{2,1,0:T(8,128)(2,1)S(1)}, u32[]{:S(2)}, u32[]{:S(2)}) collective-permute-start(bf16[4,32,128]{2,1,0:T(8,128)(2,1)S(1)} %get-tuple-element.78), channel_id=1, source_target_pairs={{0,32},{1,33},{2,34},{3,35},{4,36},{5,37},{6,38},{7,39},{8,40},{9,... | collective-permute-start | bytes 98312 | tf_op jit(solution)/shard_map/ppermute | solution.py:61
  121.2 2.1 %collective-permute-done.17 = bf16[4,32,128]{2,1,0:T(8,128)(2,1)S(1)} collective-permute-done((bf16[4,32,128]{2,1,0:T(8,128)(2,1)S(1)}, bf16[4,32,128]{2,1,0:T(8,128)(2,1)S(1)}, u32[]{:S(2)}, u32[]{:S(2)}) %collective-permute-start.17) | collective-permute-done | bytes 32800 | tf_op jit(solution)/shard_map/ppermute | solution.py:61
  123.2 1.1 collective-permute-start.20
  124.3 0.2 collective-permute-start.19
  124.6 2.3 %collective-permute-start.18 = (bf16[2,4,32,128]{3,2,1,0:T(8,128)(2,1)S(1)}, bf16[2,4,32,128]{3,2,1,0:T(8,128)(2,1)S(1)}, u32[]{:S(2)}, u32[]{:S(2)}) collective-permute-start(bf16[2,4,32,128]{3,2,1,0:T(8,128)(2,1)S(1)} %pad_maximum_fusion), channel_id=1, source_target_pairs={{0,8},{1,9},{2,10},{3,11},{4,12},{5,13},{6,14},{7,15},{8,0},{9,1},... | collective-permute-start | bytes 196616 | tf_op jit(solution)/shard_map/ppermute | solution.py:61
  126.9 2.5 %collective-permute-done.18 = bf16[2,4,32,128]{3,2,1,0:T(8,128)(2,1)S(1)} collective-permute-done((bf16[2,4,32,128]{3,2,1,0:T(8,128)(2,1)S(1)}, bf16[2,4,32,128]{3,2,1,0:T(8,128)(2,1)S(1)}, u32[]{:S(2)}, u32[]{:S(2)}) %collective-permute-start.18) | collective-permute-done | bytes 65568 | tf_op jit(solution)/shard_map/ppermute | solution.py:61
  129.4 0.6 collective-permute-done.19
  130.0 2.9 %collective-permute-start.23 = (bf16[8,4,32,128]{3,2,1,0:T(8,128)(2,1)S(1)}, bf16[8,4,32,128]{3,2,1,0:T(8,128)(2,1)S(1)}, u32[]{:S(2)}, u32[]{:S(2)}) collective-permute-start(bf16[8,4,32,128]{3,2,1,0:T(8,128)(2,1)S(1)} %constant_dynamic-update-slice_fusion.refs_0_), channel_id=1, source_target_pairs={{0,6},{1,7},{2,0},{3,1},{4,2},{5,3},{6,4},{7,5},{8,14},{9,15},{10,... | collective-permute-start | bytes 786440 | tf_op jit(solution)/shard_map/ppermute | solution.py:61
  132.9 0.7 collective-permute-start.21
  133.6 6.4 %collective-permute-start.24 = (bf16[8,4,32,128]{3,2,1,0:T(8,128)(2,1)S(1)}, bf16[8,4,32,128]{3,2,1,0:T(8,128)(2,1)S(1)}, u32[]{:S(2)}, u32[]{:S(2)}) collective-permute-start(bf16[8,4,32,128]{3,2,1,0:T(8,128)(2,1)S(1)} %constant_dynamic-update-slice_fusion.refs_0_), channel_id=1, source_target_pairs={{0,1},{1,0},{2,3},{3,2},{4,5},{5,4},{6,7},{7,6},{8,9},{9,8},{10,11... | collective-permute-start | bytes 786440 | tf_op jit(solution)/shard_map/ppermute | solution.py:61
  140.0 5.1 %collective-permute-start.27 = (bf16[8,4,32,128]{3,2,1,0:T(8,128)(2,1)S(1)}, bf16[8,4,32,128]{3,2,1,0:T(8,128)(2,1)S(1)}, u32[]{:S(2)}, u32[]{:S(2)}) collective-permute-start(bf16[8,4,32,128]{3,2,1,0:T(8,128)(2,1)S(1)} %collective-permute-done.23.refs_3_), channel_id=1, source_target_pairs={{0,1},{1,0},{2,3},{3,2},{4,5},{5,4},{6,7},{7,6},{8,9},{9,8},{10,11... | collective-permute-start | bytes 786440 | tf_op jit(solution)/shard_map/ppermute | solution.py:61
  145.1 0.0 collective-permute-done.22.refs_2_
  145.1 1.2 collective-permute-start.26
  146.4 0.0 collective-permute-done.21.refs_1_
  146.4 2.7 %collective-permute-start.25 = (bf16[8,4,32,128]{3,2,1,0:T(8,128)(2,1)S(1)}, bf16[8,4,32,128]{3,2,1,0:T(8,128)(2,1)S(1)}, u32[]{:S(2)}, u32[]{:S(2)}) collective-permute-start(bf16[8,4,32,128]{3,2,1,0:T(8,128)(2,1)S(1)} %collective-permute-done.21.refs_1_), channel_id=1, source_target_pairs={{0,1},{1,0},{2,3},{3,2},{4,5},{5,4},{6,7},{7,6},{8,9},{9,8},{10,11... | collective-permute-start | bytes 786440 | tf_op jit(solution)/shard_map/ppermute | solution.py:61
  149.1 1.1 collective-permute-done.25.refs_5_
  150.2 2.5 %assemble.1 = bf16[32,27648]{1,0:T(8,128)(2,1)} custom-call(bf16[8,4,32,128]{3,2,1,0:T(8,128)(2,1)S(1)} %constant_dynamic-update-slice_fusion.refs_0_, bf16[8,4,32,128]{3,2,1,0:T(8,128)(2,1)S(1)} %collective-permute-done.21.refs_1_, bf16[8,4,32,128]{3,2,1,0:T(8,128)(2,1)S(1)} %collective-permute-done.22.refs_2_, ...), custom_call_target="tpu_custom_call" | custom-call | tf_op jit(solution)/shard_map/assemble/pallas_call | solution.py:385
  (32 shorter events, 0.1 us)
Async XLA Ops:
  21.7 15.4 %collective-permute-start = (bf16[64,1280]{1,0:T(8,128)(2,1)}, bf16[64,1280]{1,0:T(8,128)(2,1)S(1)}, u32[]{:S(2)}, u32[]{:S(2)}) collective-permute-start(bf16[64,1280]{1,0:T(8,128)(2,1)} %get-tuple-element.44), channel_id=1, source_target_pairs={{0,64},{64,128},{128,192},{192,0},{1,65},{65,129},{129,193},{193,1... | collective-permute-start | bytes 491528 | tf_op jit(solution)/shard_map/ppermute | solution.py:65
  23.8 13.3 %collective-permute-start.1 = (bf16[64,1280]{1,0:T(8,128)(2,1)}, bf16[64,1280]{1,0:T(8,128)(2,1)S(1)}, u32[]{:S(2)}, u32[]{:S(2)}) collective-permute-start(bf16[64,1280]{1,0:T(8,128)(2,1)} %get-tuple-element.45), channel_id=1, source_target_pairs={{0,128},{64,192},{128,0},{192,64},{1,129},{65,193},{129,1},{193,65... | collective-permute-start | bytes 491528 | tf_op jit(solution)/shard_map/ppermute | solution.py:65
  26.2 10.8 %collective-permute-start.2 = (bf16[64,1280]{1,0:T(8,128)(2,1)}, bf16[64,1280]{1,0:T(8,128)(2,1)S(1)}, u32[]{:S(2)}, u32[]{:S(2)}) collective-permute-start(bf16[64,1280]{1,0:T(8,128)(2,1)} %get-tuple-element.46), channel_id=1, source_target_pairs={{0,192},{64,0},{128,64},{192,128},{1,193},{65,1},{129,65},{193,129... | collective-permute-start | bytes 491528 | tf_op jit(solution)/shard_map/ppermute | solution.py:65
  27.4 3.0 %copy-start = (bf16[1,128,27648]{2,1,0:T(8,128)(2,1)S(1)}, bf16[1,128,27648]{2,1,0:T(8,128)(2,1)}, u32[]{:S(2)}) copy-start(bf16[1,128,27648]{2,1,0:T(8,128)(2,1)} %param.10) | copy-start | bytes 21233668
  30.4 6.7 %copy-start.4 = (bf16[128,1280]{1,0:T(8,128)(2,1)S(1)}, bf16[128,1280]{1,0:T(8,128)(2,1)}, u32[]{:S(2)}) copy-start(bf16[128,1280]{1,0:T(8,128)(2,1)} %g_ref.1) | copy-start | bytes 983044
  30.4 6.7 %copy-start.5 = (bf16[64,1280]{1,0:T(8,128)(2,1)S(1)}, bf16[64,1280]{1,0:T(8,128)(2,1)}, u32[]{:S(2)}) copy-start(bf16[64,1280]{1,0:T(8,128)(2,1)} %get-tuple-element.47.w0) | copy-start | bytes 491524
  30.4 13.7 %copy-start.2 = (bf16[1,27648,32]{1,2,0:T(8,128)(2,1)S(1)}, bf16[1,27648,32]{1,2,0:T(8,128)(2,1)}, u32[]{:S(2)}) copy-start(bf16[1,27648,32]{1,2,0:T(8,128)(2,1)} %param.11) | copy-start | bytes 5308420
  30.4 13.7 %copy-start.3 = (bf16[1,27648,32]{1,2,0:T(8,128)(2,1)S(1)}, bf16[1,27648,32]{1,2,0:T(8,128)(2,1)}, u32[]{:S(2)}) copy-start(bf16[1,27648,32]{1,2,0:T(8,128)(2,1)} %param.14) | copy-start | bytes 5308420
  38.0 2.8 %collective-permute-start.3 = (f32[32,256]{1,0:T(8,128)S(1)}, f32[32,256]{1,0:T(8,128)S(1)}, u32[]{:S(2)}, u32[]{:S(2)}) collective-permute-start(f32[32,256]{1,0:T(8,128)S(1)} %get-tuple-element.52), channel_id=1, source_target_pairs={{0,192},{64,0},{128,64},{192,128},{1,193},{65,1},{129,65},{193,129... | collective-permute-start | bytes 98312 | tf_op jit(solution)/shard_map/ppermute | solution.py:65
  38.1 4.3 %collective-permute-start.4 = (f32[32,256]{1,0:T(8,128)S(1)}, f32[32,256]{1,0:T(8,128)S(1)}, u32[]{:S(2)}, u32[]{:S(2)}) collective-permute-start(f32[32,256]{1,0:T(8,128)S(1)} %get-tuple-element.53), channel_id=1, source_target_pairs={{0,128},{64,192},{128,0},{192,64},{1,129},{65,193},{129,1},{193,65... | collective-permute-start | bytes 98312 | tf_op jit(solution)/shard_map/ppermute | solution.py:65
  40.2 4.0 %collective-permute-start.5 = (f32[32,256]{1,0:T(8,128)S(1)}, f32[32,256]{1,0:T(8,128)S(1)}, u32[]{:S(2)}, u32[]{:S(2)}) collective-permute-start(f32[32,256]{1,0:T(8,128)S(1)} %get-tuple-element.54), channel_id=1, source_target_pairs={{0,64},{64,128},{128,192},{192,0},{1,65},{65,129},{129,193},{193,1... | collective-permute-start | bytes 98312 | tf_op jit(solution)/shard_map/ppermute | solution.py:65
  44.1 6.1 %copy-start.1 = (bf16[1,128,27648]{2,1,0:T(8,128)(2,1)S(1)}, bf16[1,128,27648]{2,1,0:T(8,128)(2,1)}, u32[]{:S(2)}) copy-start(bf16[1,128,27648]{2,1,0:T(8,128)(2,1)} %param.10) | copy-start | bytes 21233668
  49.0 4.6 %collective-permute-start.6 = (bf16[96,128]{1,0:T(8,128)(2,1)S(1)}, bf16[96,128]{1,0:T(8,128)(2,1)S(1)}, u32[]{:S(2)}, u32[]{:S(2)}) collective-permute-start(bf16[96,128]{1,0:T(8,128)(2,1)S(1)} %relay_first.1), channel_id=1, source_target_pairs={{64,0},{128,64},{192,128},{65,1},{129,65},{193,129},{66,2},{130,66... | collective-permute-start | bytes 73736 | tf_op jit(solution)/shard_map/ppermute | solution.py:410
  58.5 4.6 %collective-permute-start.7 = (bf16[96,128]{1,0:T(8,128)(2,1)S(1)}, bf16[96,128]{1,0:T(8,128)(2,1)S(1)}, u32[]{:S(2)}, u32[]{:S(2)}) collective-permute-start(bf16[96,128]{1,0:T(8,128)(2,1)S(1)} %relay.2), channel_id=1, source_target_pairs={{64,0},{128,64},{192,128},{65,1},{129,65},{193,129},{66,2},{130,66... | collective-permute-start | bytes 73736 | tf_op jit(solution)/shard_map/ppermute | solution.py:410
  68.0 4.6 %collective-permute-start.8 = (bf16[96,128]{1,0:T(8,128)(2,1)S(1)}, bf16[96,128]{1,0:T(8,128)(2,1)S(1)}, u32[]{:S(2)}, u32[]{:S(2)}) collective-permute-start(bf16[96,128]{1,0:T(8,128)(2,1)S(1)} %relay.3), channel_id=1, source_target_pairs={{64,0},{128,64},{192,128},{65,1},{129,65},{193,129},{66,2},{130,66... | collective-permute-start | bytes 73736 | tf_op jit(solution)/shard_map/ppermute | solution.py:410
  74.0 9.2 %collective-permute-start.9 = (bf16[4,8,4,32,128]{4,3,2,1,0:T(8,128)(2,1)S(1)}, bf16[4,8,4,32,128]{4,3,2,1,0:T(8,128)(2,1)S(1)}, u32[]{:S(2)}, u32[]{:S(2)}) collective-permute-start(bf16[4,8,4,32,128]{4,3,2,1,0:T(8,128)(2,1)S(1)} %get-tuple-element.67), channel_id=1, source_target_pairs={{0,1},{1,0},{2,3},{3,2},{4,5},{5,4},{6,7},{7,6},{8,9},{9,8},{10,11... | collective-permute-start | bytes 3145736 | tf_op jit(solution)/shard_map/ppermute | solution.py:61
  83.3 32.6 %copy-start.6 = (f32[1,4,108,32]{2,3,1,0:T(8,128)S(1)}, f32[1,4,108,32]{2,3,1,0:T(8,128)}, u32[]{:S(2)}) copy-start(f32[1,4,108,32]{2,3,1,0:T(8,128)} %param.15) | copy-start | bytes 165892
  83.3 32.6 %copy-start.7 = (f32[1,4,108,32]{2,3,1,0:T(8,128)S(1)}, f32[1,4,108,32]{2,3,1,0:T(8,128)}, u32[]{:S(2)}) copy-start(f32[1,4,108,32]{2,3,1,0:T(8,128)} %param.16) | copy-start | bytes 165892
  83.3 32.6 %copy-start.8 = (f32[1,4,108,32]{2,3,1,0:T(8,128)S(1)}, f32[1,4,108,32]{2,3,1,0:T(8,128)}, u32[]{:S(2)}) copy-start(f32[1,4,108,32]{2,3,1,0:T(8,128)} %param.17) | copy-start | bytes 165892
  83.5 8.9 %collective-permute-start.10 = (bf16[8,4,32,128]{3,2,1,0:T(8,128)(2,1)S(1)}, bf16[8,4,32,128]{3,2,1,0:T(8,128)(2,1)S(1)}, u32[]{:S(2)}, u32[]{:S(2)}) collective-permute-start(bf16[8,4,32,128]{3,2,1,0:T(8,128)(2,1)S(1)} %get-tuple-element.69), channel_id=1, source_target_pairs={{0,2},{1,3},{2,4},{3,5},{4,6},{5,7},{6,0},{7,1},{8,10},{9,11},{10,... | collective-permute-start | bytes 786440 | tf_op jit(solution)/shard_map/ppermute | solution.py:61
  84.9 14.3 %collective-permute-start.11 = (bf16[8,4,32,128]{3,2,1,0:T(8,128)(2,1)S(1)}, bf16[8,4,32,128]{3,2,1,0:T(8,128)(2,1)S(1)}, u32[]{:S(2)}, u32[]{:S(2)}) collective-permute-start(bf16[8,4,32,128]{3,2,1,0:T(8,128)(2,1)S(1)} %get-tuple-element.70), channel_id=1, source_target_pairs={{0,4},{1,5},{2,6},{3,7},{4,0},{5,1},{6,2},{7,3},{8,12},{9,13},{10,... | collective-permute-start | bytes 786440 | tf_op jit(solution)/shard_map/ppermute | solution.py:61
  87.5 11.7 %collective-permute-start.12 = (bf16[8,4,32,128]{3,2,1,0:T(8,128)(2,1)S(1)}, bf16[8,4,32,128]{3,2,1,0:T(8,128)(2,1)S(1)}, u32[]{:S(2)}, u32[]{:S(2)}) collective-permute-start(bf16[8,4,32,128]{3,2,1,0:T(8,128)(2,1)S(1)} %get-tuple-element.71), channel_id=1, source_target_pairs={{0,6},{1,7},{2,0},{3,1},{4,2},{5,3},{6,4},{7,5},{8,14},{9,15},{10,... | collective-permute-start | bytes 786440 | tf_op jit(solution)/shard_map/ppermute | solution.py:61
  99.3 4.7 %collective-permute-start.13 = (bf16[2,4,32,128]{3,2,1,0:T(8,128)(2,1)S(1)}, bf16[2,4,32,128]{3,2,1,0:T(8,128)(2,1)S(1)}, u32[]{:S(2)}, u32[]{:S(2)}) collective-permute-start(bf16[2,4,32,128]{3,2,1,0:T(8,128)(2,1)S(1)} %get-tuple-element.73), channel_id=1, source_target_pairs={{0,8},{1,9},{2,10},{3,11},{4,12},{5,13},{6,14},{7,15},{8,0},{9,1},... | collective-permute-start | bytes 196616 | tf_op jit(solution)/shard_map/ppermute | solution.py:61
  101.0 5.3 %collective-permute-start.14 = (bf16[2,4,32,128]{3,2,1,0:T(8,128)(2,1)S(1)}, bf16[2,4,32,128]{3,2,1,0:T(8,128)(2,1)S(1)}, u32[]{:S(2)}, u32[]{:S(2)}) collective-permute-start(bf16[2,4,32,128]{3,2,1,0:T(8,128)(2,1)S(1)} %get-tuple-element.74), channel_id=1, source_target_pairs={{0,16},{1,17},{2,18},{3,19},{4,20},{5,21},{6,22},{7,23},{8,24},{9,... | collective-permute-start | bytes 196616 | tf_op jit(solution)/shard_map/ppermute | solution.py:61
  104.0 5.0 %collective-permute-start.15 = (bf16[2,4,32,128]{3,2,1,0:T(8,128)(2,1)S(1)}, bf16[2,4,32,128]{3,2,1,0:T(8,128)(2,1)S(1)}, u32[]{:S(2)}, u32[]{:S(2)}) collective-permute-start(bf16[2,4,32,128]{3,2,1,0:T(8,128)(2,1)S(1)} %get-tuple-element.75), channel_id=1, source_target_pairs={{0,24},{1,25},{2,26},{3,27},{4,28},{5,29},{6,30},{7,31},{8,16},{9,... | collective-permute-start | bytes 196616 | tf_op jit(solution)/shard_map/ppermute | solution.py:61
  109.0 6.8 %collective-permute-start.16 = (bf16[4,32,128]{2,1,0:T(8,128)(2,1)S(1)}, bf16[4,32,128]{2,1,0:T(8,128)(2,1)S(1)}, u32[]{:S(2)}, u32[]{:S(2)}) collective-permute-start(bf16[4,32,128]{2,1,0:T(8,128)(2,1)S(1)} %get-tuple-element.77), channel_id=1, source_target_pairs={{0,32},{1,33},{2,34},{3,35},{4,36},{5,37},{6,38},{7,39},{8,40},{9,... | collective-permute-start | bytes 98312 | tf_op jit(solution)/shard_map/ppermute | solution.py:61
  116.5 6.7 %collective-permute-start.17 = (bf16[4,32,128]{2,1,0:T(8,128)(2,1)S(1)}, bf16[4,32,128]{2,1,0:T(8,128)(2,1)S(1)}, u32[]{:S(2)}, u32[]{:S(2)}) collective-permute-start(bf16[4,32,128]{2,1,0:T(8,128)(2,1)S(1)} %get-tuple-element.78), channel_id=1, source_target_pairs={{0,32},{1,33},{2,34},{3,35},{4,36},{5,37},{6,38},{7,39},{8,40},{9,... | collective-permute-start | bytes 98312 | tf_op jit(solution)/shard_map/ppermute | solution.py:61
  123.2 6.8 %collective-permute-start.20 = (bf16[2,4,32,128]{3,2,1,0:T(8,128)(2,1)S(1)}, bf16[2,4,32,128]{3,2,1,0:T(8,128)(2,1)S(1)}, u32[]{:S(2)}, u32[]{:S(2)}) collective-permute-start(bf16[2,4,32,128]{3,2,1,0:T(8,128)(2,1)S(1)} %pad_maximum_fusion), channel_id=1, source_target_pairs={{0,24},{1,25},{2,26},{3,27},{4,28},{5,29},{6,30},{7,31},{8,16},{9,... | collective-permute-start | bytes 196616 | tf_op jit(solution)/shard_map/ppermute | solution.py:61
  124.3 5.6 %collective-permute-start.19 = (bf16[2,4,32,128]{3,2,1,0:T(8,128)(2,1)S(1)}, bf16[2,4,32,128]{3,2,1,0:T(8,128)(2,1)S(1)}, u32[]{:S(2)}, u32[]{:S(2)}) collective-permute-start(bf16[2,4,32,128]{3,2,1,0:T(8,128)(2,1)S(1)} %pad_maximum_fusion), channel_id=1, source_target_pairs={{0,16},{1,17},{2,18},{3,19},{4,20},{5,21},{6,22},{7,23},{8,24},{9,... | collective-permute-start | bytes 196616 | tf_op jit(solution)/shard_map/ppermute | solution.py:61
  124.6 4.8 %collective-permute-start.18 = (bf16[2,4,32,128]{3,2,1,0:T(8,128)(2,1)S(1)}, bf16[2,4,32,128]{3,2,1,0:T(8,128)(2,1)S(1)}, u32[]{:S(2)}, u32[]{:S(2)}) collective-permute-start(bf16[2,4,32,128]{3,2,1,0:T(8,128)(2,1)S(1)} %pad_maximum_fusion), channel_id=1, source_target_pairs={{0,8},{1,9},{2,10},{3,11},{4,12},{5,13},{6,14},{7,15},{8,0},{9,1},... | collective-permute-start | bytes 196616 | tf_op jit(solution)/shard_map/ppermute | solution.py:61
  130.0 10.0 %collective-permute-start.23 = (bf16[8,4,32,128]{3,2,1,0:T(8,128)(2,1)S(1)}, bf16[8,4,32,128]{3,2,1,0:T(8,128)(2,1)S(1)}, u32[]{:S(2)}, u32[]{:S(2)}) collective-permute-start(bf16[8,4,32,128]{3,2,1,0:T(8,128)(2,1)S(1)} %constant_dynamic-update-slice_fusion.refs_0_), channel_id=1, source_target_pairs={{0,6},{1,7},{2,0},{3,1},{4,2},{5,3},{6,4},{7,5},{8,14},{9,15},{10,... | collective-permute-start | bytes 786440 | tf_op jit(solution)/shard_map/ppermute | solution.py:61
  132.9 12.2 %collective-permute-start.22 = (bf16[8,4,32,128]{3,2,1,0:T(8,128)(2,1)S(1)}, bf16[8,4,32,128]{3,2,1,0:T(8,128)(2,1)S(1)}, u32[]{:S(2)}, u32[]{:S(2)}) collective-permute-start(bf16[8,4,32,128]{3,2,1,0:T(8,128)(2,1)S(1)} %constant_dynamic-update-slice_fusion.refs_0_), channel_id=1, source_target_pairs={{0,4},{1,5},{2,6},{3,7},{4,0},{5,1},{6,2},{7,3},{8,12},{9,13},{10,... | collective-permute-start | bytes 786440 | tf_op jit(solution)/shard_map/ppermute | solution.py:61
  132.9 13.4 %collective-permute-start.21 = (bf16[8,4,32,128]{3,2,1,0:T(8,128)(2,1)S(1)}, bf16[8,4,32,128]{3,2,1,0:T(8,128)(2,1)S(1)}, u32[]{:S(2)}, u32[]{:S(2)}) collective-permute-start(bf16[8,4,32,128]{3,2,1,0:T(8,128)(2,1)S(1)} %constant_dynamic-update-slice_fusion.refs_0_), channel_id=1, source_target_pairs={{0,2},{1,3},{2,4},{3,5},{4,6},{5,7},{6,0},{7,1},{8,10},{9,11},{10,... | collective-permute-start | bytes 786440 | tf_op jit(solution)/shard_map/ppermute | solution.py:61
  133.6 15.5 %collective-permute-start.24 = (bf16[8,4,32,128]{3,2,1,0:T(8,128)(2,1)S(1)}, bf16[8,4,32,128]{3,2,1,0:T(8,128)(2,1)S(1)}, u32[]{:S(2)}, u32[]{:S(2)}) collective-permute-start(bf16[8,4,32,128]{3,2,1,0:T(8,128)(2,1)S(1)} %constant_dynamic-update-slice_fusion.refs_0_), channel_id=1, source_target_pairs={{0,1},{1,0},{2,3},{3,2},{4,5},{5,4},{6,7},{7,6},{8,9},{9,8},{10,11... | collective-permute-start | bytes 786440 | tf_op jit(solution)/shard_map/ppermute | solution.py:61
  140.0 9.1 %collective-permute-start.27 = (bf16[8,4,32,128]{3,2,1,0:T(8,128)(2,1)S(1)}, bf16[8,4,32,128]{3,2,1,0:T(8,128)(2,1)S(1)}, u32[]{:S(2)}, u32[]{:S(2)}) collective-permute-start(bf16[8,4,32,128]{3,2,1,0:T(8,128)(2,1)S(1)} %collective-permute-done.23.refs_3_), channel_id=1, source_target_pairs={{0,1},{1,0},{2,3},{3,2},{4,5},{5,4},{6,7},{7,6},{8,9},{9,8},{10,11... | collective-permute-start | bytes 786440 | tf_op jit(solution)/shard_map/ppermute | solution.py:61
  145.1 4.0 %collective-permute-start.26 = (bf16[8,4,32,128]{3,2,1,0:T(8,128)(2,1)S(1)}, bf16[8,4,32,128]{3,2,1,0:T(8,128)(2,1)S(1)}, u32[]{:S(2)}, u32[]{:S(2)}) collective-permute-start(bf16[8,4,32,128]{3,2,1,0:T(8,128)(2,1)S(1)} %collective-permute-done.22.refs_2_), channel_id=1, source_target_pairs={{0,1},{1,0},{2,3},{3,2},{4,5},{5,4},{6,7},{7,6},{8,9},{9,8},{10,11... | collective-permute-start | bytes 786440 | tf_op jit(solution)/shard_map/ppermute | solution.py:61
  146.4 3.9 %collective-permute-start.25 = (bf16[8,4,32,128]{3,2,1,0:T(8,128)(2,1)S(1)}, bf16[8,4,32,128]{3,2,1,0:T(8,128)(2,1)S(1)}, u32[]{:S(2)}, u32[]{:S(2)}) collective-permute-start(bf16[8,4,32,128]{3,2,1,0:T(8,128)(2,1)S(1)} %collective-permute-done.21.refs_1_), channel_id=1, source_target_pairs={{0,1},{1,0},{2,3},{3,2},{4,5},{5,4},{6,7},{7,6},{8,9},{9,8},{10,11... | collective-permute-start | bytes 786440 | tf_op jit(solution)/shard_map/ppermute | solution.py:61

commit v3 on v2

--- a/solution.py
+++ b/solution.py
@@ -24,6 +24,7 @@
 OWNED = 108
 LANES = 128
 ZS, YS = 8, 4
+Y_ORDER = (0, 2, 3, 1)
 BF16, F32 = jnp.bfloat16, jnp.float32
 VMEM = pl.BlockSpec(memory_space=pltpu.VMEM)
 ANY = pl.BlockSpec(memory_space=pl.ANY)
@@ -33,6 +34,10 @@
 
 def params(mib=16):
     return pltpu.CompilerParams(vmem_limit_bytes=mib * 1024 * 1024)
+
+
+def in_hbm(array):
+    return pltpu.with_memory_space_constraint(array, pltpu.HBM)
 
 
 def shaped(shape, dtype):
@@ -86,15 +91,16 @@
     return pl.pallas_call(
         slice_kernel,
         out_shape=[shaped((2 * RANK, WIDTH), BF16)] * 4,
-        in_specs=[ANY] * 2,
-        out_specs=[ANY] * 4,
+        in_specs=[HBM] * 2,
+        out_specs=[VMEM] * 4,
         scratch_shapes=[pltpu.SemaphoreType.DMA((8,))],
+        compiler_params=params(4),
         name="slices",
-    )(db, ua)
-
-
-def activation_kernel(slope, first, size, pre_ref, out_ref, held, sems):
-    parts = held.shape[1] // size
+    )(in_hbm(db), in_hbm(ua))
+
+
+def activation_kernel(slope, first, parts, pre_ref, out_ref, held, sems):
+    size = held.shape[1] // parts
     copies = []
     for i in range(parts):
         copies.append(
@@ -123,12 +129,10 @@
         lax.fori_loop(i * size // 256, (i + 1) * size // 256, chunk, 0)
 
 
-def activation(pre, bucket=None):
-    slope = bucket is None
-    width, first, size = (FF, 0, 6912) if slope else (BUCKET_ROWS, bucket * BUCKET_ROWS, 2304)
-    parts = width // size
-    return pl.pallas_call(
-        functools.partial(activation_kernel, slope, first, size),
+def activation(pre, slope, bucket, count=1):
+    width, parts = BUCKET_ROWS * count, 3 * count
+    return pl.pallas_call(
+        functools.partial(activation_kernel, slope, bucket * BUCKET_ROWS, parts),
         out_shape=shaped((TOKENS, width), BF16),
         in_specs=[HBM],
         out_specs=VMEM,
@@ -136,14 +140,14 @@
             pltpu.VMEM((TOKENS, width), BF16),
             pltpu.SemaphoreType.DMA((parts,)),
         ],
-        compiler_params=params(18 if slope else 6),
+        compiler_params=params(4 * count + 2),
         cost_estimate=pl.CostEstimate(
             flops=10 * TOKENS * width,
             bytes_accessed=4 * TOKENS * width,
             transcendentals=TOKENS * width,
         ),
         name="slope" if slope else "hidden",
-    )(pre)
+    )(in_hbm(pre))
 
 
 def share_kernel(g_ref, w0, w1, w2, w3, *outs):
@@ -181,27 +185,28 @@
     return low
 
 
-def relay_kernel(first, *refs):
+def relay_kernel(top, *refs):
     share_refs, refs = refs[:4], refs[4:]
     above_ref = None
-    if not first:
+    if not top:
         above_ref, refs = refs[0], refs[1:]
-    slope_ref, da_ref, ub_ref, out_ref = refs
+    slope_refs, (da_ref, ub_ref, out_ref) = refs[:2], refs[2:]
     low = low_of(share_refs, above_ref).T.astype(BF16)
-
-    def chunk(i, total):
-        columns = pl.ds(pl.multiple_of(i * 512, 512), 512)
-        upstream = jnp.dot(low, da_ref[:, columns], preferred_element_type=F32)
-        delta = (upstream * slope_ref[:, columns].astype(F32)).astype(BF16)
-        return total + lax.dot_general(
-            ub_ref[:, columns], delta, CONTRACT_LAST, preferred_element_type=F32
-        )
-
-    total = lax.fori_loop(
-        0, FF // 512, chunk, jnp.zeros((RANK, TOKENS), F32), unroll=18
-    )
+    total = jnp.zeros((RANK, TOKENS), F32)
+
+    start = 0
+    for slope_ref in slope_refs:
+        for first in range(0, slope_ref.shape[1], 768):
+            columns = slice(start, start + 768)
+            upstream = jnp.dot(low, da_ref[:, columns], preferred_element_type=F32)
+            slope = slope_ref[:, first : first + 768].astype(F32)
+            delta = (upstream * slope).astype(BF16)
+            total = total + lax.dot_general(
+                ub_ref[:, columns], delta, CONTRACT_LAST, preferred_element_type=F32
+            )
+            start += 768
     out_ref[0:RANK, :] = total.astype(BF16)
-    if first:
+    if top:
         out_ref[RANK:, :] = jnp.zeros((2 * RANK, LANES), BF16)
     else:
         out_ref[RANK:, :] = above_ref[0 : 2 * RANK, :]
@@ -212,11 +217,11 @@
     return pl.pallas_call(
         functools.partial(relay_kernel, first),
         out_shape=shaped((3 * RANK, LANES), BF16),
-        in_specs=[VMEM] * (7 if first else 8),
+        in_specs=[VMEM] * (8 if first else 9),
         out_specs=VMEM,
         compiler_params=params(14),
         name="relay_first" if first else "relay",
-    )(*share, *([] if first else [above]), slope, da, ub)
+    )(*share, *([] if first else [above]), *slope, da, ub)
 
 
 def grad_kernel(s0, s1, s2, s3, above_ref, h0, h1, h2, h3, keep_ref, send_ref, grad):
@@ -353,12 +358,12 @@
     core, y_here, z_here = core_pos(), y_pos(), z_pos()
     copies = []
     for side in range(2):
-        for k in range(YS):
+        for i, k in enumerate(Y_ORDER):
             copies.append(
                 pltpu.make_async_copy(
-                    arrays[side * YS + k],
+                    arrays[side * YS + i],
                     blocks.at[lax.rem(core + side, 2), lax.rem(y_here + YS - k, YS)],
-                    sems.at[side * YS + k],
+                    sems.at[side * YS + i],
                 )
             )
             copies[-1].start()
@@ -399,28 +404,31 @@
 def per_device(out_grad, pre_act, down_a, down_b, up_a, up_b, master, moment, second):
     da, ub = down_a[0].T, up_b[0].T
     mine = slices(down_b[0], up_a[0].T)
-    ws = [mine[0]] + [over_section(mine[k], k) for k in (1, 2, 3)]
-    slope = activation(pre_act[0])
+    ws = [mine[0]] + [over_section(mine[k], k) for k in (1, 3, 2)]
+    pre = pre_act[0]
+    slope = activation(pre, True, 0, 3)
     ws, slope = lax.optimization_barrier((ws, slope))
-    share = shares(out_grad, ws)
-    share = [share[0]] + [over_section(share[k], -k) for k in (1, 2, 3)]
-    above, hidden, pre = None, [], pre_act[0]
+    share = shares(out_grad, [ws[0], ws[1], ws[3], ws[2]])
+    pre, _ = lax.optimization_barrier((pre, share[0]))
+    slope = [slope, activation(pre, True, 3)]
+    share = [share[0]] + [over_section(share[k], -k) for k in (1, 3, 2)]
+    above, hidden = None, []
     for i in range(3):
         sent = relay(share, above, slope, da, ub)
         above = lax.ppermute(sent, "section", [(1, 0), (2, 1), (3, 2)])
         if i < 2:
             pre, _ = lax.optimization_barrier((pre, sent))
-            hidden += [activation(pre, 2 * i + b) for b in range(2)]
+            hidden += [activation(pre, False, 2 * i + b) for b in range(2)]
             above, *hidden = lax.optimization_barrier((above, *hidden))
     keep, send = grads(share, above, hidden)
     own, *sends = core_sum(keep, over_dp(send, dc=1))
-    own, *sends = y_sum(own, [over_dp(sends[k - 1], dy=k) for k in (1, 2, 3)])
-    own, send = z_sum(own, [over_dp(sends[k - 1], zx=k) for k in (1, 2, 3)])
+    own, *sends = y_sum(own, [over_dp(sends[k - 1], dy=k) for k in (1, 3, 2)])
+    own, send = z_sum(own, [over_dp(sends[k - 1], zx=k) for k in (3, 2, 1)])
     state = [a[0].transpose(0, 2, 1) for a in (master, moment, second)]
     weight, *state = adamw(own, over_dp(send, zx=4), *state)
     pair = jnp.stack([weight, over_dp(weight, zx=4)])
     column = jnp.concatenate([pair] + [over_dp(pair, zx=k) for k in (1, 2, 3)])
-    plane = [column] + [over_dp(column, dy=k) for k in (1, 2, 3)]
+    plane = [column] + [over_dp(column, dy=k) for k in Y_ORDER[1:]]
     rows = assemble(plane + [over_dp(a, dc=1) for a in plane])
     return (rows.T[None], *[a.transpose(0, 2, 1)[None] for a in state])
 

time: 153 us -> 125 us (0.82)
  Pallas kernels: 52.3 us -> 35.9 us
  waiting for transfers between devices: 36 us -> 30.1 us
  starting transfers between devices: 60.5 us -> 57.1 us
  local copies, waits for them, and re-layouts: 3.09 us -> 0.08 us
    pallas_call x1, Pallas kernels: 21 us -> 1.26 us  [slices(): pl.pallas_call(slice_kernel, out_shape=[shaped((2 * RANK, WIDTH), BF16)]...]
    pallas_call x5 -> x6, Pallas kernels: 10.6 us -> 16.2 us  [activation(): pl.pallas_call(functools.partial(activation_kernel, slope, bucket * BUCKE...]
    ppermute x19, starting transfers between devices: 48.7 us -> 44.9 us  [over_dp(): return lax.ppermute(value, 'dp', pairs)]
    ppermute x6, waiting for transfers between devices: 3.98 us -> 0.35 us  [over_section(): lax.ppermute(value, 'section', [(i, (i + steps) % 4) for i in range(4)])]
    unnamed x22 -> x16, local copies, waits for them, and re-layouts: 3.08 us -> 0.06 us
    pallas_call x3, Pallas kernels: 14.8 us -> 12.5 us  [relay(): pl.pallas_call(functools.partial(relay_kernel, first), out_shape=shaped((...]
  transfers between devices with their start and end apart: 28 -> 28, of which waited for: 16 -> 14; matrix products, arithmetic and copies ran while one was open for 0% -> 0% of each run, Pallas kernels for 7% -> 13%
where the time goes in v3:
time: 125 us; the launch traced here: 124 us
  starting transfers between devices  57.1 us (46%)
  Pallas kernels  35.9 us (29%)
  waiting for transfers between devices  30.1 us (24%)
    ppermute x19, starting transfers between devices, over_dp(): return lax.ppermute(value, 'dp', pairs)  44.9 us
    ppermute x19, waiting for transfers between devices, over_dp(): return lax.ppermute(value, 'dp', pairs)  24.9 us
    pallas_call x6, Pallas kernels, activation(): pl.pallas_call(functools.partial(activation_kernel, slope, bucket * BUCKE...  16.2 us
    pallas_call x3, Pallas kernels, relay(): pl.pallas_call(functools.partial(relay_kernel, first), out_shape=shaped((...  12.5 us
    ppermute x6, starting transfers between devices, over_section(): lax.ppermute(value, 'section', [(i, (i + steps) % 4) for i in range(4)])  8.07 us
    ppermute x3, waiting for transfers between devices, per_device(): above = lax.ppermute(sent, 'section', [(1, 0), (2, 1), (3, 2)])  4.82 us
    ppermute x3, starting transfers between devices, per_device(): above = lax.ppermute(sent, 'section', [(1, 0), (2, 1), (3, 2)])  4.09 us
  transfers between devices with their start and end apart: 28, of which 14 were waited for; matrix products, arithmetic and copies ran while one was open for 0% of the time, Pallas kernels for 13%

profile of v3, /device:TPU:1, one launch (start us, length us, event | category | flops | bytes accessed | tf_op | source)
XLA Modules:
  0.0 124.1 jit_solution(191980389760510823)
XLA Ops:
  0.6 1.3 %slices.1 = (bf16[64,1280]{1,0:T(8,128)(2,1)S(1)}, bf16[64,1280]{1,0:T(8,128)(2,1)S(1)}, bf16[64,1280]{1,0:T(8,128)(2,1)S(1)}, bf16[64,1280]{1,0:T(8,128)(2,1)S(1)}) custom-call(bf16[32,5120]{1,0:T(8,128)(2,1)} %bitcast.53, bf16[32,5120]{1,0:T(8,128)(2,1)} %bitcast.54), custom_call_target="tpu_custom_call" | custom-call | tf_op jit(solution)/shard_map/slices/pallas_call | solution.py:91
  1.9 2.1 %collective-permute-start = (bf16[64,1280]{1,0:T(8,128)(2,1)S(1)}, bf16[64,1280]{1,0:T(8,128)(2,1)S(1)}, u32[]{:S(2)}, u32[]{:S(2)}) collective-permute-start(bf16[64,1280]{1,0:T(8,128)(2,1)S(1)} %get-tuple-element.45), channel_id=1, source_target_pairs={{0,64},{64,128},{128,192},{192,0},{1,65},{65,129},{129,193},{193,1... | collective-permute-start | bytes 491528 | tf_op jit(solution)/shard_map/ppermute | solution.py:70
  4.0 1.4 %collective-permute-start.1 = (bf16[64,1280]{1,0:T(8,128)(2,1)S(1)}, bf16[64,1280]{1,0:T(8,128)(2,1)S(1)}, u32[]{:S(2)}, u32[]{:S(2)}) collective-permute-start(bf16[64,1280]{1,0:T(8,128)(2,1)S(1)} %get-tuple-element.46), channel_id=1, source_target_pairs={{0,192},{64,0},{128,64},{192,128},{1,193},{65,1},{129,65},{193,129... | collective-permute-start | bytes 491528 | tf_op jit(solution)/shard_map/ppermute | solution.py:70
  5.4 1.6 %collective-permute-start.2 = (bf16[64,1280]{1,0:T(8,128)(2,1)S(1)}, bf16[64,1280]{1,0:T(8,128)(2,1)S(1)}, u32[]{:S(2)}, u32[]{:S(2)}) collective-permute-start(bf16[64,1280]{1,0:T(8,128)(2,1)S(1)} %get-tuple-element.47), channel_id=1, source_target_pairs={{0,128},{64,192},{128,0},{192,64},{1,129},{65,193},{129,1},{193,65... | collective-permute-start | bytes 491528 | tf_op jit(solution)/shard_map/ppermute | solution.py:70
  7.0 5.7 %slope.2.refs_4_.refs_5_ = bf16[128,20736]{1,0:T(8,128)(2,1)S(1)} custom-call(bf16[128,27648]{1,0:T(8,128)(2,1)} %bitcast.46), custom_call_target="tpu_custom_call" | custom-call | flops 26542080 | bytes 10616832 | tf_op jit(solution)/shard_map/slope/pallas_call | solution.py:134
  12.7 0.0 collective-permute-done.w1
  12.7 0.0 collective-permute-done.1.w3
  12.8 0.0 collective-permute-done.2.w2
  12.8 0.9 shares.1
  13.7 1.7 %collective-permute-start.3 = (f32[32,256]{1,0:T(8,128)S(1)}, f32[32,256]{1,0:T(8,128)S(1)}, u32[]{:S(2)}, u32[]{:S(2)}) collective-permute-start(f32[32,256]{1,0:T(8,128)S(1)} %get-tuple-element.53), channel_id=1, source_target_pairs={{0,192},{64,0},{128,64},{192,128},{1,193},{65,1},{129,65},{193,129... | collective-permute-start | bytes 98312 | tf_op jit(solution)/shard_map/ppermute | solution.py:70
  15.4 0.0 collective-permute-start.4
  15.4 1.2 %collective-permute-start.5 = (f32[32,256]{1,0:T(8,128)S(1)}, f32[32,256]{1,0:T(8,128)S(1)}, u32[]{:S(2)}, u32[]{:S(2)}) collective-permute-start(f32[32,256]{1,0:T(8,128)S(1)} %get-tuple-element.55), channel_id=1, source_target_pairs={{0,128},{64,192},{128,0},{192,64},{1,129},{65,193},{129,1},{193,65... | collective-permute-start | bytes 98312 | tf_op jit(solution)/shard_map/ppermute | solution.py:70
  16.7 2.7 %slope.3.refs_5_.refs_6_ = bf16[128,6912]{1,0:T(8,128)(2,1)S(1)} custom-call(bf16[128,27648]{1,0:T(8,128)(2,1)} %bitcast.47), custom_call_target="tpu_custom_call" | custom-call | flops 8847360 | bytes 3538944 | tf_op jit(solution)/shard_map/slope/pallas_call | solution.py:134
  19.4 0.0 collective-permute-done.4.refs_2_.s2
  19.5 0.3 collective-permute-done.5.refs_3_.s3
  19.8 4.1 %relay_first.1 = bf16[96,128]{1,0:T(8,128)(2,1)S(1)} custom-call(f32[32,256]{1,0:T(8,128)S(1)} %get-tuple-element.52.refs_0_.s0, f32[32,256]{1,0:T(8,128)S(1)} %collective-permute-done.3.refs_1_.s1, f32[32,256]{1,0:T(8,128)S(1)} %collective-permute-done.4.refs_2_.s2, f32[32,256]{1,0:T(8,128)S(1)} %collective-permute-done.5.refs_3_.s3, ...), custom_call_target="tpu_custom_call" | custom-call | tf_op jit(solution)/shard_map/relay_first/pallas_call | solution.py:217
  23.8 1.5 %collective-permute-start.6 = (bf16[96,128]{1,0:T(8,128)(2,1)S(1)}, bf16[96,128]{1,0:T(8,128)(2,1)S(1)}, u32[]{:S(2)}, u32[]{:S(2)}) collective-permute-start(bf16[96,128]{1,0:T(8,128)(2,1)S(1)} %relay_first.1), channel_id=1, source_target_pairs={{64,0},{128,64},{192,128},{65,1},{129,65},{193,129},{66,2},{130,66... | collective-permute-start | bytes 73736 | tf_op jit(solution)/shard_map/ppermute | solution.py:418
  25.3 1.9 %hidden.5.h1 = bf16[128,6912]{1,0:T(8,128)(2,1)S(1)} custom-call(bf16[128,27648]{1,0:T(8,128)(2,1)} %bitcast.48), custom_call_target="tpu_custom_call" | custom-call | flops 8847360 | bytes 3538944 | tf_op jit(solution)/shard_map/hidden/pallas_call | solution.py:134
  27.3 1.9 %hidden.4.h0 = bf16[128,6912]{1,0:T(8,128)(2,1)S(1)} custom-call(bf16[128,27648]{1,0:T(8,128)(2,1)} %bitcast.49), custom_call_target="tpu_custom_call" | custom-call | flops 8847360 | bytes 3538944 | tf_op jit(solution)/shard_map/hidden/pallas_call | solution.py:134
  29.2 4.2 %relay.2 = bf16[96,128]{1,0:T(8,128)(2,1)S(1)} custom-call(f32[32,256]{1,0:T(8,128)S(1)} %get-tuple-element.52.refs_0_.s0, f32[32,256]{1,0:T(8,128)S(1)} %collective-permute-done.3.refs_1_.s1, f32[32,256]{1,0:T(8,128)S(1)} %collective-permute-done.4.refs_2_.s2, f32[32,256]{1,0:T(8,128)S(1)} %collective-permute-done.5.refs_3_.s3, ...), custom_call_target="tpu_custom_call" | custom-call | tf_op jit(solution)/shard_map/relay/pallas_call | solution.py:217
  33.4 1.3 %collective-permute-start.7 = (bf16[96,128]{1,0:T(8,128)(2,1)S(1)}, bf16[96,128]{1,0:T(8,128)(2,1)S(1)}, u32[]{:S(2)}, u32[]{:S(2)}) collective-permute-start(bf16[96,128]{1,0:T(8,128)(2,1)S(1)} %relay.2), channel_id=1, source_target_pairs={{64,0},{128,64},{192,128},{65,1},{129,65},{193,129},{66,2},{130,66... | collective-permute-start | bytes 73736 | tf_op jit(solution)/shard_map/ppermute | solution.py:418
  34.7 1.9 %hidden.7.h3 = bf16[128,6912]{1,0:T(8,128)(2,1)S(1)} custom-call(bf16[128,27648]{1,0:T(8,128)(2,1)} %bitcast.50), custom_call_target="tpu_custom_call" | custom-call | flops 8847360 | bytes 3538944 | tf_op jit(solution)/shard_map/hidden/pallas_call | solution.py:134
  36.7 1.9 %hidden.6.h2 = bf16[128,6912]{1,0:T(8,128)(2,1)S(1)} custom-call(bf16[128,27648]{1,0:T(8,128)(2,1)} %bitcast.51), custom_call_target="tpu_custom_call" | custom-call | flops 8847360 | bytes 3538944 | tf_op jit(solution)/shard_map/hidden/pallas_call | solution.py:134
  38.6 0.3 collective-permute-done.7.refs_4_
  38.9 4.2 %relay.3 = bf16[96,128]{1,0:T(8,128)(2,1)S(1)} custom-call(f32[32,256]{1,0:T(8,128)S(1)} %get-tuple-element.52.refs_0_.s0, f32[32,256]{1,0:T(8,128)S(1)} %collective-permute-done.3.refs_1_.s1, f32[32,256]{1,0:T(8,128)S(1)} %collective-permute-done.4.refs_2_.s2, f32[32,256]{1,0:T(8,128)S(1)} %collective-permute-done.5.refs_3_.s3, ...), custom_call_target="tpu_custom_call" | custom-call | tf_op jit(solution)/shard_map/relay/pallas_call | solution.py:217
  43.1 1.3 %collective-permute-start.8 = (bf16[96,128]{1,0:T(8,128)(2,1)S(1)}, bf16[96,128]{1,0:T(8,128)(2,1)S(1)}, u32[]{:S(2)}, u32[]{:S(2)}) collective-permute-start(bf16[96,128]{1,0:T(8,128)(2,1)S(1)} %relay.3), channel_id=1, source_target_pairs={{64,0},{128,64},{192,128},{65,1},{129,65},{193,129},{66,2},{130,66... | collective-permute-start | bytes 73736 | tf_op jit(solution)/shard_map/ppermute | solution.py:418
  44.5 4.5 %collective-permute-done.8.above_ref = bf16[96,128]{1,0:T(8,128)(2,1)S(1)} collective-permute-done((bf16[96,128]{1,0:T(8,128)(2,1)S(1)}, bf16[96,128]{1,0:T(8,128)(2,1)S(1)}, u32[]{:S(2)}, u32[]{:S(2)}) %collective-permute-start.8) | collective-permute-done | bytes 24608 | tf_op jit(solution)/shard_map/ppermute | solution.py:418
  49.0 1.4 %grads.1 = (bf16[4,8,4,32,128]{4,3,2,1,0:T(8,128)(2,1)S(1)}, bf16[4,8,4,32,128]{4,3,2,1,0:T(8,128)(2,1)S(1)}) custom-call(f32[32,256]{1,0:T(8,128)S(1)} %get-tuple-element.52.refs_0_.s0, f32[32,256]{1,0:T(8,128)S(1)} %collective-permute-done.3.refs_1_.s1, f32[32,256]{1,0:T(8,128)S(1)} %collective-permute-done.4.refs_2_.s2, ...), custom_call_target="tpu_custom_call" | custom-call | tf_op jit(solution)/shard_map/grads/pallas_call | solution.py:253
  50.4 5.3 %collective-permute-start.9 = (bf16[4,8,4,32,128]{4,3,2,1,0:T(8,128)(2,1)S(1)}, bf16[4,8,4,32,128]{4,3,2,1,0:T(8,128)(2,1)S(1)}, u32[]{:S(2)}, u32[]{:S(2)}) collective-permute-start(bf16[4,8,4,32,128]{4,3,2,1,0:T(8,128)(2,1)S(1)} %get-tuple-element.69), channel_id=1, source_target_pairs={{0,1},{1,0},{2,3},{3,2},{4,5},{5,4},{6,7},{7,6},{8,9},{9,8},{10,11... | collective-permute-start | bytes 3145736 | tf_op jit(solution)/shard_map/ppermute | solution.py:66
  55.7 2.3 %collective-permute-done.9.got_ref = bf16[4,8,4,32,128]{4,3,2,1,0:T(8,128)(2,1)S(1)} collective-permute-done((bf16[4,8,4,32,128]{4,3,2,1,0:T(8,128)(2,1)S(1)}, bf16[4,8,4,32,128]{4,3,2,1,0:T(8,128)(2,1)S(1)}, u32[]{:S(2)}, u32[]{:S(2)}) %collective-permute-start.9) | collective-permute-done | bytes 1048608 | tf_op jit(solution)/shard_map/ppermute | solution.py:66
  58.0 0.2 core_sum.1
  58.2 0.8 collective-permute-start.10
  59.0 2.0 %collective-permute-start.11 = (bf16[8,4,32,128]{3,2,1,0:T(8,128)(2,1)S(1)}, bf16[8,4,32,128]{3,2,1,0:T(8,128)(2,1)S(1)}, u32[]{:S(2)}, u32[]{:S(2)}) collective-permute-start(bf16[8,4,32,128]{3,2,1,0:T(8,128)(2,1)S(1)} %get-tuple-element.72), channel_id=1, source_target_pairs={{0,6},{1,7},{2,0},{3,1},{4,2},{5,3},{6,4},{7,5},{8,14},{9,15},{10,... | collective-permute-start | bytes 786440 | tf_op jit(solution)/shard_map/ppermute | solution.py:66
  61.0 1.1 collective-permute-start.12
  62.1 4.9 %collective-permute-done.10.g1 = bf16[8,4,32,128]{3,2,1,0:T(8,128)(2,1)S(1)} collective-permute-done((bf16[8,4,32,128]{3,2,1,0:T(8,128)(2,1)S(1)}, bf16[8,4,32,128]{3,2,1,0:T(8,128)(2,1)S(1)}, u32[]{:S(2)}, u32[]{:S(2)}) %collective-permute-start.10) | collective-permute-done | bytes 262176 | tf_op jit(solution)/shard_map/ppermute | solution.py:66
  67.1 0.0 collective-permute-done.11.g2
  67.1 6.3 %collective-permute-done.12.g3 = bf16[8,4,32,128]{3,2,1,0:T(8,128)(2,1)S(1)} collective-permute-done((bf16[8,4,32,128]{3,2,1,0:T(8,128)(2,1)S(1)}, bf16[8,4,32,128]{3,2,1,0:T(8,128)(2,1)S(1)}, u32[]{:S(2)}, u32[]{:S(2)}) %collective-permute-start.12) | collective-permute-done | bytes 262176 | tf_op jit(solution)/shard_map/ppermute | solution.py:66
  73.3 0.1 y_sum.1
  73.4 4.4 %collective-permute-start.13 = (bf16[2,4,32,128]{3,2,1,0:T(8,128)(2,1)S(1)}, bf16[2,4,32,128]{3,2,1,0:T(8,128)(2,1)S(1)}, u32[]{:S(2)}, u32[]{:S(2)}) collective-permute-start(bf16[2,4,32,128]{3,2,1,0:T(8,128)(2,1)S(1)} %get-tuple-element.75), channel_id=1, source_target_pairs={{0,24},{1,25},{2,26},{3,27},{4,28},{5,29},{6,30},{7,31},{8,16},{9,... | collective-permute-start | bytes 196616 | tf_op jit(solution)/shard_map/ppermute | solution.py:66
  77.9 0.0 collective-permute-start.14
  77.9 0.4 collective-permute-start.15
  78.2 1.3 %collective-permute-done.13.g1 = bf16[2,4,32,128]{3,2,1,0:T(8,128)(2,1)S(1)} collective-permute-done((bf16[2,4,32,128]{3,2,1,0:T(8,128)(2,1)S(1)}, bf16[2,4,32,128]{3,2,1,0:T(8,128)(2,1)S(1)}, u32[]{:S(2)}, u32[]{:S(2)}) %collective-permute-start.13) | collective-permute-done | bytes 65568 | tf_op jit(solution)/shard_map/ppermute | solution.py:66
  79.6 3.6 %collective-permute-done.14.g2 = bf16[2,4,32,128]{3,2,1,0:T(8,128)(2,1)S(1)} collective-permute-done((bf16[2,4,32,128]{3,2,1,0:T(8,128)(2,1)S(1)}, bf16[2,4,32,128]{3,2,1,0:T(8,128)(2,1)S(1)}, u32[]{:S(2)}, u32[]{:S(2)}) %collective-permute-start.14) | collective-permute-done | bytes 65568 | tf_op jit(solution)/shard_map/ppermute | solution.py:66
  83.1 0.0 collective-permute-done.15.g3
  83.2 6.1 %collective-permute-start.16 = (bf16[4,32,128]{2,1,0:T(8,128)(2,1)S(1)}, bf16[4,32,128]{2,1,0:T(8,128)(2,1)S(1)}, u32[]{:S(2)}, u32[]{:S(2)}) collective-permute-start(bf16[4,32,128]{2,1,0:T(8,128)(2,1)S(1)} %get-tuple-element.79), channel_id=1, source_target_pairs={{0,32},{1,33},{2,34},{3,35},{4,36},{5,37},{6,38},{7,39},{8,40},{9,... | collective-permute-start | bytes 98312 | tf_op jit(solution)/shard_map/ppermute | solution.py:66
  89.3 1.3 %collective-permute-done.16.got_ref = bf16[4,32,128]{2,1,0:T(8,128)(2,1)S(1)} collective-permute-done((bf16[4,32,128]{2,1,0:T(8,128)(2,1)S(1)}, bf16[4,32,128]{2,1,0:T(8,128)(2,1)S(1)}, u32[]{:S(2)}, u32[]{:S(2)}) %collective-permute-start.16) | collective-permute-done | bytes 32800 | tf_op jit(solution)/shard_map/ppermute | solution.py:66
  90.6 0.7 adamw.1
  91.3 5.4 %collective-permute-start.17 = (bf16[4,32,128]{2,1,0:T(8,128)(2,1)S(1)}, bf16[4,32,128]{2,1,0:T(8,128)(2,1)S(1)}, u32[]{:S(2)}, u32[]{:S(2)}) collective-permute-start(bf16[4,32,128]{2,1,0:T(8,128)(2,1)S(1)} %get-tuple-element.80), channel_id=1, source_target_pairs={{0,32},{1,33},{2,34},{3,35},{4,36},{5,37},{6,38},{7,39},{8,40},{9,... | collective-permute-start | bytes 98312 | tf_op jit(solution)/shard_map/ppermute | solution.py:66
  96.7 1.3 %collective-permute-done.17 = bf16[4,32,128]{2,1,0:T(8,128)(2,1)S(1)} collective-permute-done((bf16[4,32,128]{2,1,0:T(8,128)(2,1)S(1)}, bf16[4,32,128]{2,1,0:T(8,128)(2,1)S(1)}, u32[]{:S(2)}, u32[]{:S(2)}) %collective-permute-start.17) | collective-permute-done | bytes 32800 | tf_op jit(solution)/shard_map/ppermute | solution.py:66
  98.0 2.1 %collective-permute-start.20 = (bf16[2,4,32,128]{3,2,1,0:T(8,128)(2,1)S(1)}, bf16[2,4,32,128]{3,2,1,0:T(8,128)(2,1)S(1)}, u32[]{:S(2)}, u32[]{:S(2)}) collective-permute-start(bf16[2,4,32,128]{3,2,1,0:T(8,128)(2,1)S(1)} %pad_maximum_fusion), channel_id=1, source_target_pairs={{0,24},{1,25},{2,26},{3,27},{4,28},{5,29},{6,30},{7,31},{8,16},{9,... | collective-permute-start | bytes 196616 | tf_op jit(solution)/shard_map/ppermute | solution.py:66
  100.1 1.6 %collective-permute-start.18 = (bf16[2,4,32,128]{3,2,1,0:T(8,128)(2,1)S(1)}, bf16[2,4,32,128]{3,2,1,0:T(8,128)(2,1)S(1)}, u32[]{:S(2)}, u32[]{:S(2)}) collective-permute-start(bf16[2,4,32,128]{3,2,1,0:T(8,128)(2,1)S(1)} %pad_maximum_fusion), channel_id=1, source_target_pairs={{0,8},{1,9},{2,10},{3,11},{4,12},{5,13},{6,14},{7,15},{8,0},{9,1},... | collective-permute-start | bytes 196616 | tf_op jit(solution)/shard_map/ppermute | solution.py:66
  101.7 2.1 %collective-permute-done.18 = bf16[2,4,32,128]{3,2,1,0:T(8,128)(2,1)S(1)} collective-permute-done((bf16[2,4,32,128]{3,2,1,0:T(8,128)(2,1)S(1)}, bf16[2,4,32,128]{3,2,1,0:T(8,128)(2,1)S(1)}, u32[]{:S(2)}, u32[]{:S(2)}) %collective-permute-start.18) | collective-permute-done | bytes 65568 | tf_op jit(solution)/shard_map/ppermute | solution.py:66
  103.8 0.7 collective-permute-done.19
  104.5 0.6 collective-permute-start.23
  105.1 2.1 %collective-permute-start.22 = (bf16[8,4,32,128]{3,2,1,0:T(8,128)(2,1)S(1)}, bf16[8,4,32,128]{3,2,1,0:T(8,128)(2,1)S(1)}, u32[]{:S(2)}, u32[]{:S(2)}) collective-permute-start(bf16[8,4,32,128]{3,2,1,0:T(8,128)(2,1)S(1)} %constant_dynamic-update-slice_fusion.refs_0_), channel_id=1, source_target_pairs={{0,6},{1,7},{2,0},{3,1},{4,2},{5,3},{6,4},{7,5},{8,14},{9,15},{10,... | collective-permute-start | bytes 786440 | tf_op jit(solution)/shard_map/ppermute | solution.py:66
  107.2 5.5 %collective-permute-start.24 = (bf16[8,4,32,128]{3,2,1,0:T(8,128)(2,1)S(1)}, bf16[8,4,32,128]{3,2,1,0:T(8,128)(2,1)S(1)}, u32[]{:S(2)}, u32[]{:S(2)}) collective-permute-start(bf16[8,4,32,128]{3,2,1,0:T(8,128)(2,1)S(1)} %constant_dynamic-update-slice_fusion.refs_0_), channel_id=1, source_target_pairs={{0,1},{1,0},{2,3},{3,2},{4,5},{5,4},{6,7},{7,6},{8,9},{9,8},{10,11... | collective-permute-start | bytes 786440 | tf_op jit(solution)/shard_map/ppermute | solution.py:66
  112.7 0.0 collective-permute-done.23.refs_3_
  112.7 4.8 %collective-permute-start.27 = (bf16[8,4,32,128]{3,2,1,0:T(8,128)(2,1)S(1)}, bf16[8,4,32,128]{3,2,1,0:T(8,128)(2,1)S(1)}, u32[]{:S(2)}, u32[]{:S(2)}) collective-permute-start(bf16[8,4,32,128]{3,2,1,0:T(8,128)(2,1)S(1)} %collective-permute-done.23.refs_3_), channel_id=1, source_target_pairs={{0,1},{1,0},{2,3},{3,2},{4,5},{5,4},{6,7},{7,6},{8,9},{9,8},{10,11... | collective-permute-start | bytes 786440 | tf_op jit(solution)/shard_map/ppermute | solution.py:66
  117.5 1.9 %collective-permute-start.26 = (bf16[8,4,32,128]{3,2,1,0:T(8,128)(2,1)S(1)}, bf16[8,4,32,128]{3,2,1,0:T(8,128)(2,1)S(1)}, u32[]{:S(2)}, u32[]{:S(2)}) collective-permute-start(bf16[8,4,32,128]{3,2,1,0:T(8,128)(2,1)S(1)} %collective-permute-done.22.refs_2_), channel_id=1, source_target_pairs={{0,1},{1,0},{2,3},{3,2},{4,5},{5,4},{6,7},{7,6},{8,9},{9,8},{10,11... | collective-permute-start | bytes 786440 | tf_op jit(solution)/shard_map/ppermute | solution.py:66
  119.4 0.0 collective-permute-done.21.refs_1_
  119.4 0.9 collective-permute-start.25
  120.3 0.3 collective-permute-done.26.refs_6_
  120.6 0.9 collective-permute-done.25.refs_5_
  121.4 2.5 %assemble.1 = bf16[32,27648]{1,0:T(8,128)(2,1)} custom-call(bf16[8,4,32,128]{3,2,1,0:T(8,128)(2,1)S(1)} %constant_dynamic-update-slice_fusion.refs_0_, bf16[8,4,32,128]{3,2,1,0:T(8,128)(2,1)S(1)} %collective-permute-done.21.refs_1_, bf16[8,4,32,128]{3,2,1,0:T(8,128)(2,1)S(1)} %collective-permute-done.22.refs_2_, ...), custom_call_target="tpu_custom_call" | custom-call | tf_op jit(solution)/shard_map/assemble/pallas_call | solution.py:390
  (27 shorter events, 0.1 us)
Async XLA Ops:
  1.9 10.8 %collective-permute-start = (bf16[64,1280]{1,0:T(8,128)(2,1)S(1)}, bf16[64,1280]{1,0:T(8,128)(2,1)S(1)}, u32[]{:S(2)}, u32[]{:S(2)}) collective-permute-start(bf16[64,1280]{1,0:T(8,128)(2,1)S(1)} %get-tuple-element.45), channel_id=1, source_target_pairs={{0,64},{64,128},{128,192},{192,0},{1,65},{65,129},{129,193},{193,1... | collective-permute-start | bytes 491528 | tf_op jit(solution)/shard_map/ppermute | solution.py:70
  4.0 8.7 %collective-permute-start.1 = (bf16[64,1280]{1,0:T(8,128)(2,1)S(1)}, bf16[64,1280]{1,0:T(8,128)(2,1)S(1)}, u32[]{:S(2)}, u32[]{:S(2)}) collective-permute-start(bf16[64,1280]{1,0:T(8,128)(2,1)S(1)} %get-tuple-element.46), channel_id=1, source_target_pairs={{0,192},{64,0},{128,64},{192,128},{1,193},{65,1},{129,65},{193,129... | collective-permute-start | bytes 491528 | tf_op jit(solution)/shard_map/ppermute | solution.py:70
  5.4 7.4 %collective-permute-start.2 = (bf16[64,1280]{1,0:T(8,128)(2,1)S(1)}, bf16[64,1280]{1,0:T(8,128)(2,1)S(1)}, u32[]{:S(2)}, u32[]{:S(2)}) collective-permute-start(bf16[64,1280]{1,0:T(8,128)(2,1)S(1)} %get-tuple-element.47), channel_id=1, source_target_pairs={{0,128},{64,192},{128,0},{192,64},{1,129},{65,193},{129,1},{193,65... | collective-permute-start | bytes 491528 | tf_op jit(solution)/shard_map/ppermute | solution.py:70
  7.0 5.8 %copy-start.2 = (bf16[128,1280]{1,0:T(8,128)(2,1)S(1)}, bf16[128,1280]{1,0:T(8,128)(2,1)}, u32[]{:S(2)}) copy-start(bf16[128,1280]{1,0:T(8,128)(2,1)} %g_ref.1) | copy-start | bytes 983044
  13.7 5.7 %collective-permute-start.3 = (f32[32,256]{1,0:T(8,128)S(1)}, f32[32,256]{1,0:T(8,128)S(1)}, u32[]{:S(2)}, u32[]{:S(2)}) collective-permute-start(f32[32,256]{1,0:T(8,128)S(1)} %get-tuple-element.53), channel_id=1, source_target_pairs={{0,192},{64,0},{128,64},{192,128},{1,193},{65,1},{129,65},{193,129... | collective-permute-start | bytes 98312 | tf_op jit(solution)/shard_map/ppermute | solution.py:70
  15.4 4.0 %collective-permute-start.4 = (f32[32,256]{1,0:T(8,128)S(1)}, f32[32,256]{1,0:T(8,128)S(1)}, u32[]{:S(2)}, u32[]{:S(2)}) collective-permute-start(f32[32,256]{1,0:T(8,128)S(1)} %get-tuple-element.54), channel_id=1, source_target_pairs={{0,64},{64,128},{128,192},{192,0},{1,65},{65,129},{129,193},{193,1... | collective-permute-start | bytes 98312 | tf_op jit(solution)/shard_map/ppermute | solution.py:70
  15.4 4.3 %collective-permute-start.5 = (f32[32,256]{1,0:T(8,128)S(1)}, f32[32,256]{1,0:T(8,128)S(1)}, u32[]{:S(2)}, u32[]{:S(2)}) collective-permute-start(f32[32,256]{1,0:T(8,128)S(1)} %get-tuple-element.55), channel_id=1, source_target_pairs={{0,128},{64,192},{128,0},{192,64},{1,129},{65,193},{129,1},{193,65... | collective-permute-start | bytes 98312 | tf_op jit(solution)/shard_map/ppermute | solution.py:70
  16.7 3.1 %copy-start = (bf16[1,27648,32]{1,2,0:T(8,128)(2,1)S(1)}, bf16[1,27648,32]{1,2,0:T(8,128)(2,1)}, u32[]{:S(2)}) copy-start(bf16[1,27648,32]{1,2,0:T(8,128)(2,1)} %param.11) | copy-start | bytes 5308420
  16.7 3.1 %copy-start.1 = (bf16[1,27648,32]{1,2,0:T(8,128)(2,1)S(1)}, bf16[1,27648,32]{1,2,0:T(8,128)(2,1)}, u32[]{:S(2)}) copy-start(bf16[1,27648,32]{1,2,0:T(8,128)(2,1)} %param.14) | copy-start | bytes 5308420
  23.8 5.4 %collective-permute-start.6 = (bf16[96,128]{1,0:T(8,128)(2,1)S(1)}, bf16[96,128]{1,0:T(8,128)(2,1)S(1)}, u32[]{:S(2)}, u32[]{:S(2)}) collective-permute-start(bf16[96,128]{1,0:T(8,128)(2,1)S(1)} %relay_first.1), channel_id=1, source_target_pairs={{64,0},{128,64},{192,128},{65,1},{129,65},{193,129},{66,2},{130,66... | collective-permute-start | bytes 73736 | tf_op jit(solution)/shard_map/ppermute | solution.py:418
  33.4 5.5 %collective-permute-start.7 = (bf16[96,128]{1,0:T(8,128)(2,1)S(1)}, bf16[96,128]{1,0:T(8,128)(2,1)S(1)}, u32[]{:S(2)}, u32[]{:S(2)}) collective-permute-start(bf16[96,128]{1,0:T(8,128)(2,1)S(1)} %relay.2), channel_id=1, source_target_pairs={{64,0},{128,64},{192,128},{65,1},{129,65},{193,129},{66,2},{130,66... | collective-permute-start | bytes 73736 | tf_op jit(solution)/shard_map/ppermute | solution.py:418
  43.1 5.8 %collective-permute-start.8 = (bf16[96,128]{1,0:T(8,128)(2,1)S(1)}, bf16[96,128]{1,0:T(8,128)(2,1)S(1)}, u32[]{:S(2)}, u32[]{:S(2)}) collective-permute-start(bf16[96,128]{1,0:T(8,128)(2,1)S(1)} %relay.3), channel_id=1, source_target_pairs={{64,0},{128,64},{192,128},{65,1},{129,65},{193,129},{66,2},{130,66... | collective-permute-start | bytes 73736 | tf_op jit(solution)/shard_map/ppermute | solution.py:418
  50.4 7.6 %collective-permute-start.9 = (bf16[4,8,4,32,128]{4,3,2,1,0:T(8,128)(2,1)S(1)}, bf16[4,8,4,32,128]{4,3,2,1,0:T(8,128)(2,1)S(1)}, u32[]{:S(2)}, u32[]{:S(2)}) collective-permute-start(bf16[4,8,4,32,128]{4,3,2,1,0:T(8,128)(2,1)S(1)} %get-tuple-element.69), channel_id=1, source_target_pairs={{0,1},{1,0},{2,3},{3,2},{4,5},{5,4},{6,7},{7,6},{8,9},{9,8},{10,11... | collective-permute-start | bytes 3145736 | tf_op jit(solution)/shard_map/ppermute | solution.py:66
  58.0 32.6 %copy-start.3 = (f32[1,4,108,32]{2,3,1,0:T(8,128)S(1)}, f32[1,4,108,32]{2,3,1,0:T(8,128)}, u32[]{:S(2)}) copy-start(f32[1,4,108,32]{2,3,1,0:T(8,128)} %param.15) | copy-start | bytes 165892
  58.0 32.6 %copy-start.4 = (f32[1,4,108,32]{2,3,1,0:T(8,128)S(1)}, f32[1,4,108,32]{2,3,1,0:T(8,128)}, u32[]{:S(2)}) copy-start(f32[1,4,108,32]{2,3,1,0:T(8,128)} %param.16) | copy-start | bytes 165892
  58.0 32.6 %copy-start.5 = (f32[1,4,108,32]{2,3,1,0:T(8,128)S(1)}, f32[1,4,108,32]{2,3,1,0:T(8,128)}, u32[]{:S(2)}) copy-start(f32[1,4,108,32]{2,3,1,0:T(8,128)} %param.17) | copy-start | bytes 165892
  58.2 8.8 %collective-permute-start.10 = (bf16[8,4,32,128]{3,2,1,0:T(8,128)(2,1)S(1)}, bf16[8,4,32,128]{3,2,1,0:T(8,128)(2,1)S(1)}, u32[]{:S(2)}, u32[]{:S(2)}) collective-permute-start(bf16[8,4,32,128]{3,2,1,0:T(8,128)(2,1)S(1)} %get-tuple-element.71), channel_id=1, source_target_pairs={{0,2},{1,3},{2,4},{3,5},{4,6},{5,7},{6,0},{7,1},{8,10},{9,11},{10,... | collective-permute-start | bytes 786440 | tf_op jit(solution)/shard_map/ppermute | solution.py:66
  59.0 8.0 %collective-permute-start.11 = (bf16[8,4,32,128]{3,2,1,0:T(8,128)(2,1)S(1)}, bf16[8,4,32,128]{3,2,1,0:T(8,128)(2,1)S(1)}, u32[]{:S(2)}, u32[]{:S(2)}) collective-permute-start(bf16[8,4,32,128]{3,2,1,0:T(8,128)(2,1)S(1)} %get-tuple-element.72), channel_id=1, source_target_pairs={{0,6},{1,7},{2,0},{3,1},{4,2},{5,3},{6,4},{7,5},{8,14},{9,15},{10,... | collective-permute-start | bytes 786440 | tf_op jit(solution)/shard_map/ppermute | solution.py:66
  61.0 12.3 %collective-permute-start.12 = (bf16[8,4,32,128]{3,2,1,0:T(8,128)(2,1)S(1)}, bf16[8,4,32,128]{3,2,1,0:T(8,128)(2,1)S(1)}, u32[]{:S(2)}, u32[]{:S(2)}) collective-permute-start(bf16[8,4,32,128]{3,2,1,0:T(8,128)(2,1)S(1)} %get-tuple-element.73), channel_id=1, source_target_pairs={{0,4},{1,5},{2,6},{3,7},{4,0},{5,1},{6,2},{7,3},{8,12},{9,13},{10,... | collective-permute-start | bytes 786440 | tf_op jit(solution)/shard_map/ppermute | solution.py:66
  73.4 6.1 %collective-permute-start.13 = (bf16[2,4,32,128]{3,2,1,0:T(8,128)(2,1)S(1)}, bf16[2,4,32,128]{3,2,1,0:T(8,128)(2,1)S(1)}, u32[]{:S(2)}, u32[]{:S(2)}) collective-permute-start(bf16[2,4,32,128]{3,2,1,0:T(8,128)(2,1)S(1)} %get-tuple-element.75), channel_id=1, source_target_pairs={{0,24},{1,25},{2,26},{3,27},{4,28},{5,29},{6,30},{7,31},{8,16},{9,... | collective-permute-start | bytes 196616 | tf_op jit(solution)/shard_map/ppermute | solution.py:66
  77.9 5.3 %collective-permute-start.14 = (bf16[2,4,32,128]{3,2,1,0:T(8,128)(2,1)S(1)}, bf16[2,4,32,128]{3,2,1,0:T(8,128)(2,1)S(1)}, u32[]{:S(2)}, u32[]{:S(2)}) collective-permute-start(bf16[2,4,32,128]{3,2,1,0:T(8,128)(2,1)S(1)} %get-tuple-element.76), channel_id=1, source_target_pairs={{0,16},{1,17},{2,18},{3,19},{4,20},{5,21},{6,22},{7,23},{8,24},{9,... | collective-permute-start | bytes 196616 | tf_op jit(solution)/shard_map/ppermute | solution.py:66
  77.9 5.3 %collective-permute-start.15 = (bf16[2,4,32,128]{3,2,1,0:T(8,128)(2,1)S(1)}, bf16[2,4,32,128]{3,2,1,0:T(8,128)(2,1)S(1)}, u32[]{:S(2)}, u32[]{:S(2)}) collective-permute-start(bf16[2,4,32,128]{3,2,1,0:T(8,128)(2,1)S(1)} %get-tuple-element.77), channel_id=1, source_target_pairs={{0,8},{1,9},{2,10},{3,11},{4,12},{5,13},{6,14},{7,15},{8,0},{9,1},... | collective-permute-start | bytes 196616 | tf_op jit(solution)/shard_map/ppermute | solution.py:66
  83.2 7.4 %collective-permute-start.16 = (bf16[4,32,128]{2,1,0:T(8,128)(2,1)S(1)}, bf16[4,32,128]{2,1,0:T(8,128)(2,1)S(1)}, u32[]{:S(2)}, u32[]{:S(2)}) collective-permute-start(bf16[4,32,128]{2,1,0:T(8,128)(2,1)S(1)} %get-tuple-element.79), channel_id=1, source_target_pairs={{0,32},{1,33},{2,34},{3,35},{4,36},{5,37},{6,38},{7,39},{8,40},{9,... | collective-permute-start | bytes 98312 | tf_op jit(solution)/shard_map/ppermute | solution.py:66
  91.3 6.7 %collective-permute-start.17 = (bf16[4,32,128]{2,1,0:T(8,128)(2,1)S(1)}, bf16[4,32,128]{2,1,0:T(8,128)(2,1)S(1)}, u32[]{:S(2)}, u32[]{:S(2)}) collective-permute-start(bf16[4,32,128]{2,1,0:T(8,128)(2,1)S(1)} %get-tuple-element.80), channel_id=1, source_target_pairs={{0,32},{1,33},{2,34},{3,35},{4,36},{5,37},{6,38},{7,39},{8,40},{9,... | collective-permute-start | bytes 98312 | tf_op jit(solution)/shard_map/ppermute | solution.py:66
  98.0 6.4 %collective-permute-start.20 = (bf16[2,4,32,128]{3,2,1,0:T(8,128)(2,1)S(1)}, bf16[2,4,32,128]{3,2,1,0:T(8,128)(2,1)S(1)}, u32[]{:S(2)}, u32[]{:S(2)}) collective-permute-start(bf16[2,4,32,128]{3,2,1,0:T(8,128)(2,1)S(1)} %pad_maximum_fusion), channel_id=1, source_target_pairs={{0,24},{1,25},{2,26},{3,27},{4,28},{5,29},{6,30},{7,31},{8,16},{9,... | collective-permute-start | bytes 196616 | tf_op jit(solution)/shard_map/ppermute | solution.py:66
  100.1 4.3 %collective-permute-start.19 = (bf16[2,4,32,128]{3,2,1,0:T(8,128)(2,1)S(1)}, bf16[2,4,32,128]{3,2,1,0:T(8,128)(2,1)S(1)}, u32[]{:S(2)}, u32[]{:S(2)}) collective-permute-start(bf16[2,4,32,128]{3,2,1,0:T(8,128)(2,1)S(1)} %pad_maximum_fusion), channel_id=1, source_target_pairs={{0,16},{1,17},{2,18},{3,19},{4,20},{5,21},{6,22},{7,23},{8,24},{9,... | collective-permute-start | bytes 196616 | tf_op jit(solution)/shard_map/ppermute | solution.py:66
  100.1 3.7 %collective-permute-start.18 = (bf16[2,4,32,128]{3,2,1,0:T(8,128)(2,1)S(1)}, bf16[2,4,32,128]{3,2,1,0:T(8,128)(2,1)S(1)}, u32[]{:S(2)}, u32[]{:S(2)}) collective-permute-start(bf16[2,4,32,128]{3,2,1,0:T(8,128)(2,1)S(1)} %pad_maximum_fusion), channel_id=1, source_target_pairs={{0,8},{1,9},{2,10},{3,11},{4,12},{5,13},{6,14},{7,15},{8,0},{9,1},... | collective-permute-start | bytes 196616 | tf_op jit(solution)/shard_map/ppermute | solution.py:66
  104.5 8.2 %collective-permute-start.23 = (bf16[8,4,32,128]{3,2,1,0:T(8,128)(2,1)S(1)}, bf16[8,4,32,128]{3,2,1,0:T(8,128)(2,1)S(1)}, u32[]{:S(2)}, u32[]{:S(2)}) collective-permute-start(bf16[8,4,32,128]{3,2,1,0:T(8,128)(2,1)S(1)} %constant_dynamic-update-slice_fusion.refs_0_), channel_id=1, source_target_pairs={{0,2},{1,3},{2,4},{3,5},{4,6},{5,7},{6,0},{7,1},{8,10},{9,11},{10,... | collective-permute-start | bytes 786440 | tf_op jit(solution)/shard_map/ppermute | solution.py:66
  105.1 12.4 %collective-permute-start.22 = (bf16[8,4,32,128]{3,2,1,0:T(8,128)(2,1)S(1)}, bf16[8,4,32,128]{3,2,1,0:T(8,128)(2,1)S(1)}, u32[]{:S(2)}, u32[]{:S(2)}) collective-permute-start(bf16[8,4,32,128]{3,2,1,0:T(8,128)(2,1)S(1)} %constant_dynamic-update-slice_fusion.refs_0_), channel_id=1, source_target_pairs={{0,6},{1,7},{2,0},{3,1},{4,2},{5,3},{6,4},{7,5},{8,14},{9,15},{10,... | collective-permute-start | bytes 786440 | tf_op jit(solution)/shard_map/ppermute | solution.py:66
  107.2 12.2 %collective-permute-start.21 = (bf16[8,4,32,128]{3,2,1,0:T(8,128)(2,1)S(1)}, bf16[8,4,32,128]{3,2,1,0:T(8,128)(2,1)S(1)}, u32[]{:S(2)}, u32[]{:S(2)}) collective-permute-start(bf16[8,4,32,128]{3,2,1,0:T(8,128)(2,1)S(1)} %constant_dynamic-update-slice_fusion.refs_0_), channel_id=1, source_target_pairs={{0,4},{1,5},{2,6},{3,7},{4,0},{5,1},{6,2},{7,3},{8,12},{9,13},{10,... | collective-permute-start | bytes 786440 | tf_op jit(solution)/shard_map/ppermute | solution.py:66
  107.2 13.0 %collective-permute-start.24 = (bf16[8,4,32,128]{3,2,1,0:T(8,128)(2,1)S(1)}, bf16[8,4,32,128]{3,2,1,0:T(8,128)(2,1)S(1)}, u32[]{:S(2)}, u32[]{:S(2)}) collective-permute-start(bf16[8,4,32,128]{3,2,1,0:T(8,128)(2,1)S(1)} %constant_dynamic-update-slice_fusion.refs_0_), channel_id=1, source_target_pairs={{0,1},{1,0},{2,3},{3,2},{4,5},{5,4},{6,7},{7,6},{8,9},{9,8},{10,11... | collective-permute-start | bytes 786440 | tf_op jit(solution)/shard_map/ppermute | solution.py:66
  112.7 7.6 %collective-permute-start.27 = (bf16[8,4,32,128]{3,2,1,0:T(8,128)(2,1)S(1)}, bf16[8,4,32,128]{3,2,1,0:T(8,128)(2,1)S(1)}, u32[]{:S(2)}, u32[]{:S(2)}) collective-permute-start(bf16[8,4,32,128]{3,2,1,0:T(8,128)(2,1)S(1)} %collective-permute-done.23.refs_3_), channel_id=1, source_target_pairs={{0,1},{1,0},{2,3},{3,2},{4,5},{5,4},{6,7},{7,6},{8,9},{9,8},{10,11... | collective-permute-start | bytes 786440 | tf_op jit(solution)/shard_map/ppermute | solution.py:66
  117.5 3.1 %collective-permute-start.26 = (bf16[8,4,32,128]{3,2,1,0:T(8,128)(2,1)S(1)}, bf16[8,4,32,128]{3,2,1,0:T(8,128)(2,1)S(1)}, u32[]{:S(2)}, u32[]{:S(2)}) collective-permute-start(bf16[8,4,32,128]{3,2,1,0:T(8,128)(2,1)S(1)} %collective-permute-done.22.refs_2_), channel_id=1, source_target_pairs={{0,1},{1,0},{2,3},{3,2},{4,5},{5,4},{6,7},{7,6},{8,9},{9,8},{10,11... | collective-permute-start | bytes 786440 | tf_op jit(solution)/shard_map/ppermute | solution.py:66
  119.4 2.0 %collective-permute-start.25 = (bf16[8,4,32,128]{3,2,1,0:T(8,128)(2,1)S(1)}, bf16[8,4,32,128]{3,2,1,0:T(8,128)(2,1)S(1)}, u32[]{:S(2)}, u32[]{:S(2)}) collective-permute-start(bf16[8,4,32,128]{3,2,1,0:T(8,128)(2,1)S(1)} %collective-permute-done.21.refs_1_), channel_id=1, source_target_pairs={{0,1},{1,0},{2,3},{3,2},{4,5},{5,4},{6,7},{7,6},{8,9},{9,8},{10,11... | collective-permute-start | bytes 786440 | tf_op jit(solution)/shard_map/ppermute | solution.py:66

commit v4 on v3

--- a/solution.py
+++ b/solution.py
@@ -24,6 +24,7 @@
 OWNED = 108
 LANES = 128
 ZS, YS = 8, 4
+Z_STEPS = (5, 6, 2)
 Y_ORDER = (0, 2, 3, 1)
 BF16, F32 = jnp.bfloat16, jnp.float32
 VMEM = pl.BlockSpec(memory_space=pltpu.VMEM)
@@ -120,7 +121,7 @@
             t = jnp.tanh(half)
             h = half + half * t
             if slope:
-                h = 0.5 * ((1.0 + t) + h * (1.0 - t))
+                h = (1.0 + t) + h * (1.0 - t)
             out_ref[rows, columns] = h.astype(BF16)
         return 0
 
@@ -205,7 +206,7 @@
                 ub_ref[:, columns], delta, CONTRACT_LAST, preferred_element_type=F32
             )
             start += 768
-    out_ref[0:RANK, :] = total.astype(BF16)
+    out_ref[0:RANK, :] = (0.5 * total).astype(BF16)
     if top:
         out_ref[RANK:, :] = jnp.zeros((2 * RANK, LANES), BF16)
     else:
@@ -283,9 +284,9 @@
 
 def y_sum_kernel(own_ref, g1, g2, g3, out_own, *outs):
     here = z_pos()
-    for k, out in enumerate((out_own, *outs)):
+    for step, out in zip((0, *Z_STEPS), (out_own, *outs)):
         for far in range(2):
-            z = here ^ (k + 4 * far)
+            z = here ^ (step ^ far)
             total = own_ref[z] + g1[z].astype(F32) + g2[z].astype(F32) + g3[z].astype(F32)
             out[far] = total.astype(out.dtype)
 
@@ -370,7 +371,10 @@
     for copy in copies:
         copy.wait()
     lane = lax.broadcasted_iota(jnp.int32, (RANK, LANES), 1)
-    places = [2 * ((z_here ^ z) & 3) + ((z_here ^ z) >> 2) for z in range(ZS)]
+    apart = [z_here ^ z for z in range(ZS)]
+    places = [
+        jnp.where(a < 4, a, jnp.where(a < 6, 11 - a, a - 2)) for a in apart
+    ]
     for tile in range(FF // LANES):
         value = None
         first = tile * LANES // OWNED
@@ -423,11 +427,11 @@
     keep, send = grads(share, above, hidden)
     own, *sends = core_sum(keep, over_dp(send, dc=1))
     own, *sends = y_sum(own, [over_dp(sends[k - 1], dy=k) for k in (1, 3, 2)])
-    own, send = z_sum(own, [over_dp(sends[k - 1], zx=k) for k in (3, 2, 1)])
+    own, send = z_sum(own, [over_dp(a, zx=k) for a, k in zip(sends, Z_STEPS)])
     state = [a[0].transpose(0, 2, 1) for a in (master, moment, second)]
-    weight, *state = adamw(own, over_dp(send, zx=4), *state)
-    pair = jnp.stack([weight, over_dp(weight, zx=4)])
-    column = jnp.concatenate([pair] + [over_dp(pair, zx=k) for k in (1, 2, 3)])
+    weight, *state = adamw(own, over_dp(send, zx=1), *state)
+    pair = jnp.stack([weight, over_dp(weight, zx=1)])
+    column = jnp.concatenate([pair] + [over_dp(pair, zx=k) for k in Z_STEPS[::-1]])
     plane = [column] + [over_dp(column, dy=k) for k in Y_ORDER[1:]]
     rows = assemble(plane + [over_dp(a, dc=1) for a in plane])
     return (rows.T[None], *[a.transpose(0, 2, 1)[None] for a in state])

time: 125 us -> 123 us (0.984)
  starting transfers between devices: 57.1 us -> 53 us
  waiting for transfers between devices: 30.1 us -> 33.3 us
    ppermute x19, starting transfers between devices: 44.9 us -> 40.8 us  [over_dp(): return lax.ppermute(value, 'dp', pairs)]
    ppermute x19, waiting for transfers between devices: 24.9 us -> 27.6 us  [over_dp(): return lax.ppermute(value, 'dp', pairs)]
  transfers between devices with their start and end apart: 28 -> 28, of which waited for: 14 -> 16; matrix products, arithmetic and copies ran while one was open for 0% -> 0% of each run, Pallas kernels for 13% -> 13%
where the time goes in v4:
time: 123 us
  starting transfers between devices  53 us (43%)
  Pallas kernels  35.2 us (29%)
  waiting for transfers between devices  33.3 us (27%)
    ppermute x19, starting transfers between devices, over_dp(): return lax.ppermute(value, 'dp', pairs)  40.8 us
    ppermute x19, waiting for transfers between devices, over_dp(): return lax.ppermute(value, 'dp', pairs)  27.6 us
    pallas_call x6, Pallas kernels, activation(): pl.pallas_call(functools.partial(activation_kernel, slope, bucket * BUCKE...  15.5 us
    pallas_call x3, Pallas kernels, relay(): pl.pallas_call(functools.partial(relay_kernel, first), out_shape=shaped((...  12.5 us
    ppermute x6, starting transfers between devices, over_section(): lax.ppermute(value, 'section', [(i, (i + steps) % 4) for i in range(4)])  8.07 us
    ppermute x3, waiting for transfers between devices, per_device(): above = lax.ppermute(sent, 'section', [(1, 0), (2, 1), (3, 2)])  4.66 us
    ppermute x3, starting transfers between devices, per_device(): above = lax.ppermute(sent, 'section', [(1, 0), (2, 1), (3, 2)])  4.09 us
    pallas_call x1, Pallas kernels, assemble(): pl.pallas_call(assemble_kernel, out_shape=shaped((RANK, FF), BF16), in_sp...  2.48 us
  transfers between devices with their start and end apart: 28, of which 16 were waited for; matrix products, arithmetic and copies ran while one was open for 0% of the time, Pallas kernels for 13%

profile of v4, /device:TPU:1, one launch (start us, length us, event | category | flops | bytes accessed | tf_op | source)
XLA Modules:
  0.0 122.6 jit_solution(6372012461693010302)
XLA Ops:
  0.6 1.3 %slices.1 = (bf16[64,1280]{1,0:T(8,128)(2,1)S(1)}, bf16[64,1280]{1,0:T(8,128)(2,1)S(1)}, bf16[64,1280]{1,0:T(8,128)(2,1)S(1)}, bf16[64,1280]{1,0:T(8,128)(2,1)S(1)}) custom-call(bf16[32,5120]{1,0:T(8,128)(2,1)} %bitcast.53, bf16[32,5120]{1,0:T(8,128)(2,1)} %bitcast.54), custom_call_target="tpu_custom_call" | custom-call | tf_op jit(solution)/shard_map/slices/pallas_call | solution.py:92
  1.9 2.1 %collective-permute-start = (bf16[64,1280]{1,0:T(8,128)(2,1)S(1)}, bf16[64,1280]{1,0:T(8,128)(2,1)S(1)}, u32[]{:S(2)}, u32[]{:S(2)}) collective-permute-start(bf16[64,1280]{1,0:T(8,128)(2,1)S(1)} %get-tuple-element.45), channel_id=1, source_target_pairs={{0,64},{64,128},{128,192},{192,0},{1,65},{65,129},{129,193},{193,1... | collective-permute-start | bytes 491528 | tf_op jit(solution)/shard_map/ppermute | solution.py:71
  4.0 1.4 %collective-permute-start.1 = (bf16[64,1280]{1,0:T(8,128)(2,1)S(1)}, bf16[64,1280]{1,0:T(8,128)(2,1)S(1)}, u32[]{:S(2)}, u32[]{:S(2)}) collective-permute-start(bf16[64,1280]{1,0:T(8,128)(2,1)S(1)} %get-tuple-element.46), channel_id=1, source_target_pairs={{0,192},{64,0},{128,64},{192,128},{1,193},{65,1},{129,65},{193,129... | collective-permute-start | bytes 491528 | tf_op jit(solution)/shard_map/ppermute | solution.py:71
  5.4 1.6 %collective-permute-start.2 = (bf16[64,1280]{1,0:T(8,128)(2,1)S(1)}, bf16[64,1280]{1,0:T(8,128)(2,1)S(1)}, u32[]{:S(2)}, u32[]{:S(2)}) collective-permute-start(bf16[64,1280]{1,0:T(8,128)(2,1)S(1)} %get-tuple-element.47), channel_id=1, source_target_pairs={{0,128},{64,192},{128,0},{192,64},{1,129},{65,193},{129,1},{193,65... | collective-permute-start | bytes 491528 | tf_op jit(solution)/shard_map/ppermute | solution.py:71
  7.0 5.2 %slope.2.refs_4_.refs_5_ = bf16[128,20736]{1,0:T(8,128)(2,1)S(1)} custom-call(bf16[128,27648]{1,0:T(8,128)(2,1)} %bitcast.46), custom_call_target="tpu_custom_call" | custom-call | flops 26542080 | bytes 10616832 | tf_op jit(solution)/shard_map/slope/pallas_call | solution.py:135
  12.3 0.0 collective-permute-done.1.w3
  12.3 0.5 collective-permute-done.2.w2
  12.8 0.9 shares.1
  13.7 1.7 %collective-permute-start.3 = (f32[32,256]{1,0:T(8,128)S(1)}, f32[32,256]{1,0:T(8,128)S(1)}, u32[]{:S(2)}, u32[]{:S(2)}) collective-permute-start(f32[32,256]{1,0:T(8,128)S(1)} %get-tuple-element.53), channel_id=1, source_target_pairs={{0,192},{64,0},{128,64},{192,128},{1,193},{65,1},{129,65},{193,129... | collective-permute-start | bytes 98312 | tf_op jit(solution)/shard_map/ppermute | solution.py:71
  15.4 0.0 collective-permute-start.4
  15.4 1.2 %collective-permute-start.5 = (f32[32,256]{1,0:T(8,128)S(1)}, f32[32,256]{1,0:T(8,128)S(1)}, u32[]{:S(2)}, u32[]{:S(2)}) collective-permute-start(f32[32,256]{1,0:T(8,128)S(1)} %get-tuple-element.55), channel_id=1, source_target_pairs={{0,128},{64,192},{128,0},{192,64},{1,129},{65,193},{129,1},{193,65... | collective-permute-start | bytes 98312 | tf_op jit(solution)/shard_map/ppermute | solution.py:71
  16.7 2.6 %slope.3.refs_5_.refs_6_ = bf16[128,6912]{1,0:T(8,128)(2,1)S(1)} custom-call(bf16[128,27648]{1,0:T(8,128)(2,1)} %bitcast.47), custom_call_target="tpu_custom_call" | custom-call | flops 8847360 | bytes 3538944 | tf_op jit(solution)/shard_map/slope/pallas_call | solution.py:135
  19.3 0.0 collective-permute-done.3.refs_1_.s1
  19.3 0.1 collective-permute-done.4.refs_2_.s2
  19.4 0.3 collective-permute-done.5.refs_3_.s3
  19.8 4.1 %relay_first.1 = bf16[96,128]{1,0:T(8,128)(2,1)S(1)} custom-call(f32[32,256]{1,0:T(8,128)S(1)} %get-tuple-element.52.refs_0_.s0, f32[32,256]{1,0:T(8,128)S(1)} %collective-permute-done.3.refs_1_.s1, f32[32,256]{1,0:T(8,128)S(1)} %collective-permute-done.4.refs_2_.s2, f32[32,256]{1,0:T(8,128)S(1)} %collective-permute-done.5.refs_3_.s3, ...), custom_call_target="tpu_custom_call" | custom-call | tf_op jit(solution)/shard_map/relay_first/pallas_call | solution.py:218
  23.8 1.5 %collective-permute-start.6 = (bf16[96,128]{1,0:T(8,128)(2,1)S(1)}, bf16[96,128]{1,0:T(8,128)(2,1)S(1)}, u32[]{:S(2)}, u32[]{:S(2)}) collective-permute-start(bf16[96,128]{1,0:T(8,128)(2,1)S(1)} %relay_first.1), channel_id=1, source_target_pairs={{64,0},{128,64},{192,128},{65,1},{129,65},{193,129},{66,2},{130,66... | collective-permute-start | bytes 73736 | tf_op jit(solution)/shard_map/ppermute | solution.py:422
  25.3 1.9 %hidden.5.h1 = bf16[128,6912]{1,0:T(8,128)(2,1)S(1)} custom-call(bf16[128,27648]{1,0:T(8,128)(2,1)} %bitcast.48), custom_call_target="tpu_custom_call" | custom-call | flops 8847360 | bytes 3538944 | tf_op jit(solution)/shard_map/hidden/pallas_call | solution.py:135
  27.3 1.9 %hidden.4.h0 = bf16[128,6912]{1,0:T(8,128)(2,1)S(1)} custom-call(bf16[128,27648]{1,0:T(8,128)(2,1)} %bitcast.49), custom_call_target="tpu_custom_call" | custom-call | flops 8847360 | bytes 3538944 | tf_op jit(solution)/shard_map/hidden/pallas_call | solution.py:135
  29.2 0.0 collective-permute-done.6.refs_4_
  29.2 4.2 %relay.2 = bf16[96,128]{1,0:T(8,128)(2,1)S(1)} custom-call(f32[32,256]{1,0:T(8,128)S(1)} %get-tuple-element.52.refs_0_.s0, f32[32,256]{1,0:T(8,128)S(1)} %collective-permute-done.3.refs_1_.s1, f32[32,256]{1,0:T(8,128)S(1)} %collective-permute-done.4.refs_2_.s2, f32[32,256]{1,0:T(8,128)S(1)} %collective-permute-done.5.refs_3_.s3, ...), custom_call_target="tpu_custom_call" | custom-call | tf_op jit(solution)/shard_map/relay/pallas_call | solution.py:218
  33.4 1.3 %collective-permute-start.7 = (bf16[96,128]{1,0:T(8,128)(2,1)S(1)}, bf16[96,128]{1,0:T(8,128)(2,1)S(1)}, u32[]{:S(2)}, u32[]{:S(2)}) collective-permute-start(bf16[96,128]{1,0:T(8,128)(2,1)S(1)} %relay.2), channel_id=1, source_target_pairs={{64,0},{128,64},{192,128},{65,1},{129,65},{193,129},{66,2},{130,66... | collective-permute-start | bytes 73736 | tf_op jit(solution)/shard_map/ppermute | solution.py:422
  34.7 1.9 %hidden.7.h3 = bf16[128,6912]{1,0:T(8,128)(2,1)S(1)} custom-call(bf16[128,27648]{1,0:T(8,128)(2,1)} %bitcast.50), custom_call_target="tpu_custom_call" | custom-call | flops 8847360 | bytes 3538944 | tf_op jit(solution)/shard_map/hidden/pallas_call | solution.py:135
  36.7 1.9 %hidden.6.h2 = bf16[128,6912]{1,0:T(8,128)(2,1)S(1)} custom-call(bf16[128,27648]{1,0:T(8,128)(2,1)} %bitcast.51), custom_call_target="tpu_custom_call" | custom-call | flops 8847360 | bytes 3538944 | tf_op jit(solution)/shard_map/hidden/pallas_call | solution.py:135
  38.6 0.2 collective-permute-done.7.refs_4_
  38.8 4.2 %relay.3 = bf16[96,128]{1,0:T(8,128)(2,1)S(1)} custom-call(f32[32,256]{1,0:T(8,128)S(1)} %get-tuple-element.52.refs_0_.s0, f32[32,256]{1,0:T(8,128)S(1)} %collective-permute-done.3.refs_1_.s1, f32[32,256]{1,0:T(8,128)S(1)} %collective-permute-done.4.refs_2_.s2, f32[32,256]{1,0:T(8,128)S(1)} %collective-permute-done.5.refs_3_.s3, ...), custom_call_target="tpu_custom_call" | custom-call | tf_op jit(solution)/shard_map/relay/pallas_call | solution.py:218
  43.0 1.3 %collective-permute-start.8 = (bf16[96,128]{1,0:T(8,128)(2,1)S(1)}, bf16[96,128]{1,0:T(8,128)(2,1)S(1)}, u32[]{:S(2)}, u32[]{:S(2)}) collective-permute-start(bf16[96,128]{1,0:T(8,128)(2,1)S(1)} %relay.3), channel_id=1, source_target_pairs={{64,0},{128,64},{192,128},{65,1},{129,65},{193,129},{66,2},{130,66... | collective-permute-start | bytes 73736 | tf_op jit(solution)/shard_map/ppermute | solution.py:422
  44.3 4.5 %collective-permute-done.8.above_ref = bf16[96,128]{1,0:T(8,128)(2,1)S(1)} collective-permute-done((bf16[96,128]{1,0:T(8,128)(2,1)S(1)}, bf16[96,128]{1,0:T(8,128)(2,1)S(1)}, u32[]{:S(2)}, u32[]{:S(2)}) %collective-permute-start.8) | collective-permute-done | bytes 24608 | tf_op jit(solution)/shard_map/ppermute | solution.py:422
  48.8 1.4 %grads.1 = (bf16[4,8,4,32,128]{4,3,2,1,0:T(8,128)(2,1)S(1)}, bf16[4,8,4,32,128]{4,3,2,1,0:T(8,128)(2,1)S(1)}) custom-call(f32[32,256]{1,0:T(8,128)S(1)} %get-tuple-element.52.refs_0_.s0, f32[32,256]{1,0:T(8,128)S(1)} %collective-permute-done.3.refs_1_.s1, f32[32,256]{1,0:T(8,128)S(1)} %collective-permute-done.4.refs_2_.s2, ...), custom_call_target="tpu_custom_call" | custom-call | tf_op jit(solution)/shard_map/grads/pallas_call | solution.py:254
  50.2 5.5 %collective-permute-start.9 = (bf16[4,8,4,32,128]{4,3,2,1,0:T(8,128)(2,1)S(1)}, bf16[4,8,4,32,128]{4,3,2,1,0:T(8,128)(2,1)S(1)}, u32[]{:S(2)}, u32[]{:S(2)}) collective-permute-start(bf16[4,8,4,32,128]{4,3,2,1,0:T(8,128)(2,1)S(1)} %get-tuple-element.69), channel_id=1, source_target_pairs={{0,1},{1,0},{2,3},{3,2},{4,5},{5,4},{6,7},{7,6},{8,9},{9,8},{10,11... | collective-permute-start | bytes 3145736 | tf_op jit(solution)/shard_map/ppermute | solution.py:67
  55.7 2.3 %collective-permute-done.9.got_ref = bf16[4,8,4,32,128]{4,3,2,1,0:T(8,128)(2,1)S(1)} collective-permute-done((bf16[4,8,4,32,128]{4,3,2,1,0:T(8,128)(2,1)S(1)}, bf16[4,8,4,32,128]{4,3,2,1,0:T(8,128)(2,1)S(1)}, u32[]{:S(2)}, u32[]{:S(2)}) %collective-permute-start.9) | collective-permute-done | bytes 1048608 | tf_op jit(solution)/shard_map/ppermute | solution.py:67
  58.0 0.2 core_sum.1
  58.2 0.8 collective-permute-start.10
  59.0 2.0 %collective-permute-start.11 = (bf16[8,4,32,128]{3,2,1,0:T(8,128)(2,1)S(1)}, bf16[8,4,32,128]{3,2,1,0:T(8,128)(2,1)S(1)}, u32[]{:S(2)}, u32[]{:S(2)}) collective-permute-start(bf16[8,4,32,128]{3,2,1,0:T(8,128)(2,1)S(1)} %get-tuple-element.72), channel_id=1, source_target_pairs={{0,6},{1,7},{2,0},{3,1},{4,2},{5,3},{6,4},{7,5},{8,14},{9,15},{10,... | collective-permute-start | bytes 786440 | tf_op jit(solution)/shard_map/ppermute | solution.py:67
  61.0 1.1 collective-permute-start.12
  62.1 4.9 %collective-permute-done.10.g1 = bf16[8,4,32,128]{3,2,1,0:T(8,128)(2,1)S(1)} collective-permute-done((bf16[8,4,32,128]{3,2,1,0:T(8,128)(2,1)S(1)}, bf16[8,4,32,128]{3,2,1,0:T(8,128)(2,1)S(1)}, u32[]{:S(2)}, u32[]{:S(2)}) %collective-permute-start.10) | collective-permute-done | bytes 262176 | tf_op jit(solution)/shard_map/ppermute | solution.py:67
  67.1 0.0 collective-permute-done.11.g2
  67.1 6.3 %collective-permute-done.12.g3 = bf16[8,4,32,128]{3,2,1,0:T(8,128)(2,1)S(1)} collective-permute-done((bf16[8,4,32,128]{3,2,1,0:T(8,128)(2,1)S(1)}, bf16[8,4,32,128]{3,2,1,0:T(8,128)(2,1)S(1)}, u32[]{:S(2)}, u32[]{:S(2)}) %collective-permute-start.12) | collective-permute-done | bytes 262176 | tf_op jit(solution)/shard_map/ppermute | solution.py:67
  73.3 0.1 y_sum.1
  73.4 6.6 %collective-permute-start.13 = (bf16[2,4,32,128]{3,2,1,0:T(8,128)(2,1)S(1)}, bf16[2,4,32,128]{3,2,1,0:T(8,128)(2,1)S(1)}, u32[]{:S(2)}, u32[]{:S(2)}) collective-permute-start(bf16[2,4,32,128]{3,2,1,0:T(8,128)(2,1)S(1)} %get-tuple-element.75), channel_id=1, source_target_pairs={{0,40},{1,41},{2,42},{3,43},{4,44},{5,45},{6,46},{7,47},{8,32},{9,... | collective-permute-start | bytes 196616 | tf_op jit(solution)/shard_map/ppermute | solution.py:67
  80.0 0.3 collective-permute-start.14
  80.3 0.9 collective-permute-start.15
  81.2 0.5 collective-permute-done.13.g1
  81.6 3.7 %collective-permute-done.14.g2 = bf16[2,4,32,128]{3,2,1,0:T(8,128)(2,1)S(1)} collective-permute-done((bf16[2,4,32,128]{3,2,1,0:T(8,128)(2,1)S(1)}, bf16[2,4,32,128]{3,2,1,0:T(8,128)(2,1)S(1)}, u32[]{:S(2)}, u32[]{:S(2)}) %collective-permute-start.14) | collective-permute-done | bytes 65568 | tf_op jit(solution)/shard_map/ppermute | solution.py:67
  85.3 0.5 collective-permute-done.15.g3
  85.9 0.9 collective-permute-start.16
  86.8 2.0 %collective-permute-done.16.got_ref = bf16[4,32,128]{2,1,0:T(8,128)(2,1)S(1)} collective-permute-done((bf16[4,32,128]{2,1,0:T(8,128)(2,1)S(1)}, bf16[4,32,128]{2,1,0:T(8,128)(2,1)S(1)}, u32[]{:S(2)}, u32[]{:S(2)}) %collective-permute-start.16) | collective-permute-done | bytes 32800 | tf_op jit(solution)/shard_map/ppermute | solution.py:67
  88.7 0.7 adamw.1
  89.5 0.8 collective-permute-start.17
  90.3 2.0 %collective-permute-done.17 = bf16[4,32,128]{2,1,0:T(8,128)(2,1)S(1)} collective-permute-done((bf16[4,32,128]{2,1,0:T(8,128)(2,1)S(1)}, bf16[4,32,128]{2,1,0:T(8,128)(2,1)S(1)}, u32[]{:S(2)}, u32[]{:S(2)}) %collective-permute-start.17) | collective-permute-done | bytes 32800 | tf_op jit(solution)/shard_map/ppermute | solution.py:67
  92.2 4.5 %collective-permute-start.20 = (bf16[2,4,32,128]{3,2,1,0:T(8,128)(2,1)S(1)}, bf16[2,4,32,128]{3,2,1,0:T(8,128)(2,1)S(1)}, u32[]{:S(2)}, u32[]{:S(2)}) collective-permute-start(bf16[2,4,32,128]{3,2,1,0:T(8,128)(2,1)S(1)} %pad_maximum_fusion), channel_id=1, source_target_pairs={{0,40},{1,41},{2,42},{3,43},{4,44},{5,45},{6,46},{7,47},{8,32},{9,... | collective-permute-start | bytes 196616 | tf_op jit(solution)/shard_map/ppermute | solution.py:67
  96.7 0.9 collective-permute-start.18
  97.6 3.9 %collective-permute-done.18 = bf16[2,4,32,128]{3,2,1,0:T(8,128)(2,1)S(1)} collective-permute-done((bf16[2,4,32,128]{3,2,1,0:T(8,128)(2,1)S(1)}, bf16[2,4,32,128]{3,2,1,0:T(8,128)(2,1)S(1)}, u32[]{:S(2)}, u32[]{:S(2)}) %collective-permute-start.18) | collective-permute-done | bytes 65568 | tf_op jit(solution)/shard_map/ppermute | solution.py:67
  101.5 0.5 collective-permute-done.19
  102.0 0.0 collective-permute-done.20
  102.0 0.6 collective-permute-start.23
  102.6 2.2 %collective-permute-start.22 = (bf16[8,4,32,128]{3,2,1,0:T(8,128)(2,1)S(1)}, bf16[8,4,32,128]{3,2,1,0:T(8,128)(2,1)S(1)}, u32[]{:S(2)}, u32[]{:S(2)}) collective-permute-start(bf16[8,4,32,128]{3,2,1,0:T(8,128)(2,1)S(1)} %constant_dynamic-update-slice_fusion.refs_0_), channel_id=1, source_target_pairs={{0,6},{1,7},{2,0},{3,1},{4,2},{5,3},{6,4},{7,5},{8,14},{9,15},{10,... | collective-permute-start | bytes 786440 | tf_op jit(solution)/shard_map/ppermute | solution.py:67
  104.8 6.1 %collective-permute-start.24 = (bf16[8,4,32,128]{3,2,1,0:T(8,128)(2,1)S(1)}, bf16[8,4,32,128]{3,2,1,0:T(8,128)(2,1)S(1)}, u32[]{:S(2)}, u32[]{:S(2)}) collective-permute-start(bf16[8,4,32,128]{3,2,1,0:T(8,128)(2,1)S(1)} %constant_dynamic-update-slice_fusion.refs_0_), channel_id=1, source_target_pairs={{0,1},{1,0},{2,3},{3,2},{4,5},{5,4},{6,7},{7,6},{8,9},{9,8},{10,11... | collective-permute-start | bytes 786440 | tf_op jit(solution)/shard_map/ppermute | solution.py:67
  110.9 4.3 %collective-permute-start.27 = (bf16[8,4,32,128]{3,2,1,0:T(8,128)(2,1)S(1)}, bf16[8,4,32,128]{3,2,1,0:T(8,128)(2,1)S(1)}, u32[]{:S(2)}, u32[]{:S(2)}) collective-permute-start(bf16[8,4,32,128]{3,2,1,0:T(8,128)(2,1)S(1)} %collective-permute-done.23.refs_3_), channel_id=1, source_target_pairs={{0,1},{1,0},{2,3},{3,2},{4,5},{5,4},{6,7},{7,6},{8,9},{9,8},{10,11... | collective-permute-start | bytes 786440 | tf_op jit(solution)/shard_map/ppermute | solution.py:67
  115.2 2.4 %collective-permute-start.26 = (bf16[8,4,32,128]{3,2,1,0:T(8,128)(2,1)S(1)}, bf16[8,4,32,128]{3,2,1,0:T(8,128)(2,1)S(1)}, u32[]{:S(2)}, u32[]{:S(2)}) collective-permute-start(bf16[8,4,32,128]{3,2,1,0:T(8,128)(2,1)S(1)} %collective-permute-done.22.refs_2_), channel_id=1, source_target_pairs={{0,1},{1,0},{2,3},{3,2},{4,5},{5,4},{6,7},{7,6},{8,9},{9,8},{10,11... | collective-permute-start | bytes 786440 | tf_op jit(solution)/shard_map/ppermute | solution.py:67
  117.6 1.1 collective-permute-start.25
  118.7 0.0 collective-permute-done.26.refs_6_
  118.8 1.1 collective-permute-done.25.refs_5_
  119.9 2.5 %assemble.1 = bf16[32,27648]{1,0:T(8,128)(2,1)} custom-call(bf16[8,4,32,128]{3,2,1,0:T(8,128)(2,1)S(1)} %constant_dynamic-update-slice_fusion.refs_0_, bf16[8,4,32,128]{3,2,1,0:T(8,128)(2,1)S(1)} %collective-permute-done.21.refs_1_, bf16[8,4,32,128]{3,2,1,0:T(8,128)(2,1)S(1)} %collective-permute-done.22.refs_2_, ...), custom_call_target="tpu_custom_call" | custom-call | tf_op jit(solution)/shard_map/assemble/pallas_call | solution.py:394
  (27 shorter events, 0.1 us)
Async XLA Ops:
  1.9 10.4 %collective-permute-start = (bf16[64,1280]{1,0:T(8,128)(2,1)S(1)}, bf16[64,1280]{1,0:T(8,128)(2,1)S(1)}, u32[]{:S(2)}, u32[]{:S(2)}) collective-permute-start(bf16[64,1280]{1,0:T(8,128)(2,1)S(1)} %get-tuple-element.45), channel_id=1, source_target_pairs={{0,64},{64,128},{128,192},{192,0},{1,65},{65,129},{129,193},{193,1... | collective-permute-start | bytes 491528 | tf_op jit(solution)/shard_map/ppermute | solution.py:71
  4.0 8.3 %collective-permute-start.1 = (bf16[64,1280]{1,0:T(8,128)(2,1)S(1)}, bf16[64,1280]{1,0:T(8,128)(2,1)S(1)}, u32[]{:S(2)}, u32[]{:S(2)}) collective-permute-start(bf16[64,1280]{1,0:T(8,128)(2,1)S(1)} %get-tuple-element.46), channel_id=1, source_target_pairs={{0,192},{64,0},{128,64},{192,128},{1,193},{65,1},{129,65},{193,129... | collective-permute-start | bytes 491528 | tf_op jit(solution)/shard_map/ppermute | solution.py:71
  5.4 7.4 %collective-permute-start.2 = (bf16[64,1280]{1,0:T(8,128)(2,1)S(1)}, bf16[64,1280]{1,0:T(8,128)(2,1)S(1)}, u32[]{:S(2)}, u32[]{:S(2)}) collective-permute-start(bf16[64,1280]{1,0:T(8,128)(2,1)S(1)} %get-tuple-element.47), channel_id=1, source_target_pairs={{0,128},{64,192},{128,0},{192,64},{1,129},{65,193},{129,1},{193,65... | collective-permute-start | bytes 491528 | tf_op jit(solution)/shard_map/ppermute | solution.py:71
  7.0 5.8 %copy-start.2 = (bf16[128,1280]{1,0:T(8,128)(2,1)S(1)}, bf16[128,1280]{1,0:T(8,128)(2,1)}, u32[]{:S(2)}) copy-start(bf16[128,1280]{1,0:T(8,128)(2,1)} %g_ref.1) | copy-start | bytes 983044
  13.7 5.6 %collective-permute-start.3 = (f32[32,256]{1,0:T(8,128)S(1)}, f32[32,256]{1,0:T(8,128)S(1)}, u32[]{:S(2)}, u32[]{:S(2)}) collective-permute-start(f32[32,256]{1,0:T(8,128)S(1)} %get-tuple-element.53), channel_id=1, source_target_pairs={{0,192},{64,0},{128,64},{192,128},{1,193},{65,1},{129,65},{193,129... | collective-permute-start | bytes 98312 | tf_op jit(solution)/shard_map/ppermute | solution.py:71
  15.4 4.0 %collective-permute-start.4 = (f32[32,256]{1,0:T(8,128)S(1)}, f32[32,256]{1,0:T(8,128)S(1)}, u32[]{:S(2)}, u32[]{:S(2)}) collective-permute-start(f32[32,256]{1,0:T(8,128)S(1)} %get-tuple-element.54), channel_id=1, source_target_pairs={{0,64},{64,128},{128,192},{192,0},{1,65},{65,129},{129,193},{193,1... | collective-permute-start | bytes 98312 | tf_op jit(solution)/shard_map/ppermute | solution.py:71
  15.4 4.3 %collective-permute-start.5 = (f32[32,256]{1,0:T(8,128)S(1)}, f32[32,256]{1,0:T(8,128)S(1)}, u32[]{:S(2)}, u32[]{:S(2)}) collective-permute-start(f32[32,256]{1,0:T(8,128)S(1)} %get-tuple-element.55), channel_id=1, source_target_pairs={{0,128},{64,192},{128,0},{192,64},{1,129},{65,193},{129,1},{193,65... | collective-permute-start | bytes 98312 | tf_op jit(solution)/shard_map/ppermute | solution.py:71
  16.7 3.1 %copy-start = (bf16[1,27648,32]{1,2,0:T(8,128)(2,1)S(1)}, bf16[1,27648,32]{1,2,0:T(8,128)(2,1)}, u32[]{:S(2)}) copy-start(bf16[1,27648,32]{1,2,0:T(8,128)(2,1)} %param.11) | copy-start | bytes 5308420
  16.7 3.1 %copy-start.1 = (bf16[1,27648,32]{1,2,0:T(8,128)(2,1)S(1)}, bf16[1,27648,32]{1,2,0:T(8,128)(2,1)}, u32[]{:S(2)}) copy-start(bf16[1,27648,32]{1,2,0:T(8,128)(2,1)} %param.14) | copy-start | bytes 5308420
  23.8 5.4 %collective-permute-start.6 = (bf16[96,128]{1,0:T(8,128)(2,1)S(1)}, bf16[96,128]{1,0:T(8,128)(2,1)S(1)}, u32[]{:S(2)}, u32[]{:S(2)}) collective-permute-start(bf16[96,128]{1,0:T(8,128)(2,1)S(1)} %relay_first.1), channel_id=1, source_target_pairs={{64,0},{128,64},{192,128},{65,1},{129,65},{193,129},{66,2},{130,66... | collective-permute-start | bytes 73736 | tf_op jit(solution)/shard_map/ppermute | solution.py:422
  33.4 5.3 %collective-permute-start.7 = (bf16[96,128]{1,0:T(8,128)(2,1)S(1)}, bf16[96,128]{1,0:T(8,128)(2,1)S(1)}, u32[]{:S(2)}, u32[]{:S(2)}) collective-permute-start(bf16[96,128]{1,0:T(8,128)(2,1)S(1)} %relay.2), channel_id=1, source_target_pairs={{64,0},{128,64},{192,128},{65,1},{129,65},{193,129},{66,2},{130,66... | collective-permute-start | bytes 73736 | tf_op jit(solution)/shard_map/ppermute | solution.py:422
  43.0 5.8 %collective-permute-start.8 = (bf16[96,128]{1,0:T(8,128)(2,1)S(1)}, bf16[96,128]{1,0:T(8,128)(2,1)S(1)}, u32[]{:S(2)}, u32[]{:S(2)}) collective-permute-start(bf16[96,128]{1,0:T(8,128)(2,1)S(1)} %relay.3), channel_id=1, source_target_pairs={{64,0},{128,64},{192,128},{65,1},{129,65},{193,129},{66,2},{130,66... | collective-permute-start | bytes 73736 | tf_op jit(solution)/shard_map/ppermute | solution.py:422
  50.2 7.8 %collective-permute-start.9 = (bf16[4,8,4,32,128]{4,3,2,1,0:T(8,128)(2,1)S(1)}, bf16[4,8,4,32,128]{4,3,2,1,0:T(8,128)(2,1)S(1)}, u32[]{:S(2)}, u32[]{:S(2)}) collective-permute-start(bf16[4,8,4,32,128]{4,3,2,1,0:T(8,128)(2,1)S(1)} %get-tuple-element.69), channel_id=1, source_target_pairs={{0,1},{1,0},{2,3},{3,2},{4,5},{5,4},{6,7},{7,6},{8,9},{9,8},{10,11... | collective-permute-start | bytes 3145736 | tf_op jit(solution)/shard_map/ppermute | solution.py:67
  58.0 30.7 %copy-start.3 = (f32[1,4,108,32]{2,3,1,0:T(8,128)S(1)}, f32[1,4,108,32]{2,3,1,0:T(8,128)}, u32[]{:S(2)}) copy-start(f32[1,4,108,32]{2,3,1,0:T(8,128)} %param.15) | copy-start | bytes 165892
  58.0 30.7 %copy-start.4 = (f32[1,4,108,32]{2,3,1,0:T(8,128)S(1)}, f32[1,4,108,32]{2,3,1,0:T(8,128)}, u32[]{:S(2)}) copy-start(f32[1,4,108,32]{2,3,1,0:T(8,128)} %param.16) | copy-start | bytes 165892
  58.0 30.7 %copy-start.5 = (f32[1,4,108,32]{2,3,1,0:T(8,128)S(1)}, f32[1,4,108,32]{2,3,1,0:T(8,128)}, u32[]{:S(2)}) copy-start(f32[1,4,108,32]{2,3,1,0:T(8,128)} %param.17) | copy-start | bytes 165892
  58.2 8.8 %collective-permute-start.10 = (bf16[8,4,32,128]{3,2,1,0:T(8,128)(2,1)S(1)}, bf16[8,4,32,128]{3,2,1,0:T(8,128)(2,1)S(1)}, u32[]{:S(2)}, u32[]{:S(2)}) collective-permute-start(bf16[8,4,32,128]{3,2,1,0:T(8,128)(2,1)S(1)} %get-tuple-element.71), channel_id=1, source_target_pairs={{0,2},{1,3},{2,4},{3,5},{4,6},{5,7},{6,0},{7,1},{8,10},{9,11},{10,... | collective-permute-start | bytes 786440 | tf_op jit(solution)/shard_map/ppermute | solution.py:67
  59.0 8.0 %collective-permute-start.11 = (bf16[8,4,32,128]{3,2,1,0:T(8,128)(2,1)S(1)}, bf16[8,4,32,128]{3,2,1,0:T(8,128)(2,1)S(1)}, u32[]{:S(2)}, u32[]{:S(2)}) collective-permute-start(bf16[8,4,32,128]{3,2,1,0:T(8,128)(2,1)S(1)} %get-tuple-element.72), channel_id=1, source_target_pairs={{0,6},{1,7},{2,0},{3,1},{4,2},{5,3},{6,4},{7,5},{8,14},{9,15},{10,... | collective-permute-start | bytes 786440 | tf_op jit(solution)/shard_map/ppermute | solution.py:67
  61.0 12.3 %collective-permute-start.12 = (bf16[8,4,32,128]{3,2,1,0:T(8,128)(2,1)S(1)}, bf16[8,4,32,128]{3,2,1,0:T(8,128)(2,1)S(1)}, u32[]{:S(2)}, u32[]{:S(2)}) collective-permute-start(bf16[8,4,32,128]{3,2,1,0:T(8,128)(2,1)S(1)} %get-tuple-element.73), channel_id=1, source_target_pairs={{0,4},{1,5},{2,6},{3,7},{4,0},{5,1},{6,2},{7,3},{8,12},{9,13},{10,... | collective-permute-start | bytes 786440 | tf_op jit(solution)/shard_map/ppermute | solution.py:67
  73.4 8.2 %collective-permute-start.13 = (bf16[2,4,32,128]{3,2,1,0:T(8,128)(2,1)S(1)}, bf16[2,4,32,128]{3,2,1,0:T(8,128)(2,1)S(1)}, u32[]{:S(2)}, u32[]{:S(2)}) collective-permute-start(bf16[2,4,32,128]{3,2,1,0:T(8,128)(2,1)S(1)} %get-tuple-element.75), channel_id=1, source_target_pairs={{0,40},{1,41},{2,42},{3,43},{4,44},{5,45},{6,46},{7,47},{8,32},{9,... | collective-permute-start | bytes 196616 | tf_op jit(solution)/shard_map/ppermute | solution.py:67
  80.0 5.3 %collective-permute-start.14 = (bf16[2,4,32,128]{3,2,1,0:T(8,128)(2,1)S(1)}, bf16[2,4,32,128]{3,2,1,0:T(8,128)(2,1)S(1)}, u32[]{:S(2)}, u32[]{:S(2)}) collective-permute-start(bf16[2,4,32,128]{3,2,1,0:T(8,128)(2,1)S(1)} %get-tuple-element.76), channel_id=1, source_target_pairs={{0,48},{1,49},{2,50},{3,51},{4,52},{5,53},{6,54},{7,55},{8,56},{9,... | collective-permute-start | bytes 196616 | tf_op jit(solution)/shard_map/ppermute | solution.py:67
  80.3 5.6 %collective-permute-start.15 = (bf16[2,4,32,128]{3,2,1,0:T(8,128)(2,1)S(1)}, bf16[2,4,32,128]{3,2,1,0:T(8,128)(2,1)S(1)}, u32[]{:S(2)}, u32[]{:S(2)}) collective-permute-start(bf16[2,4,32,128]{3,2,1,0:T(8,128)(2,1)S(1)} %get-tuple-element.77), channel_id=1, source_target_pairs={{0,16},{1,17},{2,18},{3,19},{4,20},{5,21},{6,22},{7,23},{8,24},{9,... | collective-permute-start | bytes 196616 | tf_op jit(solution)/shard_map/ppermute | solution.py:67
  85.9 2.9 %collective-permute-start.16 = (bf16[4,32,128]{2,1,0:T(8,128)(2,1)S(1)}, bf16[4,32,128]{2,1,0:T(8,128)(2,1)S(1)}, u32[]{:S(2)}, u32[]{:S(2)}) collective-permute-start(bf16[4,32,128]{2,1,0:T(8,128)(2,1)S(1)} %get-tuple-element.79), channel_id=1, source_target_pairs={{0,8},{1,9},{2,10},{3,11},{4,12},{5,13},{6,14},{7,15},{8,0},{9,1},... | collective-permute-start | bytes 98312 | tf_op jit(solution)/shard_map/ppermute | solution.py:67
  89.5 2.8 %collective-permute-start.17 = (bf16[4,32,128]{2,1,0:T(8,128)(2,1)S(1)}, bf16[4,32,128]{2,1,0:T(8,128)(2,1)S(1)}, u32[]{:S(2)}, u32[]{:S(2)}) collective-permute-start(bf16[4,32,128]{2,1,0:T(8,128)(2,1)S(1)} %get-tuple-element.80), channel_id=1, source_target_pairs={{0,8},{1,9},{2,10},{3,11},{4,12},{5,13},{6,14},{7,15},{8,0},{9,1},... | collective-permute-start | bytes 98312 | tf_op jit(solution)/shard_map/ppermute | solution.py:67
  92.2 9.8 %collective-permute-start.20 = (bf16[2,4,32,128]{3,2,1,0:T(8,128)(2,1)S(1)}, bf16[2,4,32,128]{3,2,1,0:T(8,128)(2,1)S(1)}, u32[]{:S(2)}, u32[]{:S(2)}) collective-permute-start(bf16[2,4,32,128]{3,2,1,0:T(8,128)(2,1)S(1)} %pad_maximum_fusion), channel_id=1, source_target_pairs={{0,40},{1,41},{2,42},{3,43},{4,44},{5,45},{6,46},{7,47},{8,32},{9,... | collective-permute-start | bytes 196616 | tf_op jit(solution)/shard_map/ppermute | solution.py:67
  96.7 5.3 %collective-permute-start.19 = (bf16[2,4,32,128]{3,2,1,0:T(8,128)(2,1)S(1)}, bf16[2,4,32,128]{3,2,1,0:T(8,128)(2,1)S(1)}, u32[]{:S(2)}, u32[]{:S(2)}) collective-permute-start(bf16[2,4,32,128]{3,2,1,0:T(8,128)(2,1)S(1)} %pad_maximum_fusion), channel_id=1, source_target_pairs={{0,48},{1,49},{2,50},{3,51},{4,52},{5,53},{6,54},{7,55},{8,56},{9,... | collective-permute-start | bytes 196616 | tf_op jit(solution)/shard_map/ppermute | solution.py:67
  96.7 4.7 %collective-permute-start.18 = (bf16[2,4,32,128]{3,2,1,0:T(8,128)(2,1)S(1)}, bf16[2,4,32,128]{3,2,1,0:T(8,128)(2,1)S(1)}, u32[]{:S(2)}, u32[]{:S(2)}) collective-permute-start(bf16[2,4,32,128]{3,2,1,0:T(8,128)(2,1)S(1)} %pad_maximum_fusion), channel_id=1, source_target_pairs={{0,16},{1,17},{2,18},{3,19},{4,20},{5,21},{6,22},{7,23},{8,24},{9,... | collective-permute-start | bytes 196616 | tf_op jit(solution)/shard_map/ppermute | solution.py:67
  102.0 8.8 %collective-permute-start.23 = (bf16[8,4,32,128]{3,2,1,0:T(8,128)(2,1)S(1)}, bf16[8,4,32,128]{3,2,1,0:T(8,128)(2,1)S(1)}, u32[]{:S(2)}, u32[]{:S(2)}) collective-permute-start(bf16[8,4,32,128]{3,2,1,0:T(8,128)(2,1)S(1)} %constant_dynamic-update-slice_fusion.refs_0_), channel_id=1, source_target_pairs={{0,2},{1,3},{2,4},{3,5},{4,6},{5,7},{6,0},{7,1},{8,10},{9,11},{10,... | collective-permute-start | bytes 786440 | tf_op jit(solution)/shard_map/ppermute | solution.py:67
  102.6 12.6 %collective-permute-start.22 = (bf16[8,4,32,128]{3,2,1,0:T(8,128)(2,1)S(1)}, bf16[8,4,32,128]{3,2,1,0:T(8,128)(2,1)S(1)}, u32[]{:S(2)}, u32[]{:S(2)}) collective-permute-start(bf16[8,4,32,128]{3,2,1,0:T(8,128)(2,1)S(1)} %constant_dynamic-update-slice_fusion.refs_0_), channel_id=1, source_target_pairs={{0,6},{1,7},{2,0},{3,1},{4,2},{5,3},{6,4},{7,5},{8,14},{9,15},{10,... | collective-permute-start | bytes 786440 | tf_op jit(solution)/shard_map/ppermute | solution.py:67
  104.8 12.8 %collective-permute-start.21 = (bf16[8,4,32,128]{3,2,1,0:T(8,128)(2,1)S(1)}, bf16[8,4,32,128]{3,2,1,0:T(8,128)(2,1)S(1)}, u32[]{:S(2)}, u32[]{:S(2)}) collective-permute-start(bf16[8,4,32,128]{3,2,1,0:T(8,128)(2,1)S(1)} %constant_dynamic-update-slice_fusion.refs_0_), channel_id=1, source_target_pairs={{0,4},{1,5},{2,6},{3,7},{4,0},{5,1},{6,2},{7,3},{8,12},{9,13},{10,... | collective-permute-start | bytes 786440 | tf_op jit(solution)/shard_map/ppermute | solution.py:67
  104.8 13.9 %collective-permute-start.24 = (bf16[8,4,32,128]{3,2,1,0:T(8,128)(2,1)S(1)}, bf16[8,4,32,128]{3,2,1,0:T(8,128)(2,1)S(1)}, u32[]{:S(2)}, u32[]{:S(2)}) collective-permute-start(bf16[8,4,32,128]{3,2,1,0:T(8,128)(2,1)S(1)} %constant_dynamic-update-slice_fusion.refs_0_), channel_id=1, source_target_pairs={{0,1},{1,0},{2,3},{3,2},{4,5},{5,4},{6,7},{7,6},{8,9},{9,8},{10,11... | collective-permute-start | bytes 786440 | tf_op jit(solution)/shard_map/ppermute | solution.py:67
  110.9 7.9 %collective-permute-start.27 = (bf16[8,4,32,128]{3,2,1,0:T(8,128)(2,1)S(1)}, bf16[8,4,32,128]{3,2,1,0:T(8,128)(2,1)S(1)}, u32[]{:S(2)}, u32[]{:S(2)}) collective-permute-start(bf16[8,4,32,128]{3,2,1,0:T(8,128)(2,1)S(1)} %collective-permute-done.23.refs_3_), channel_id=1, source_target_pairs={{0,1},{1,0},{2,3},{3,2},{4,5},{5,4},{6,7},{7,6},{8,9},{9,8},{10,11... | collective-permute-start | bytes 786440 | tf_op jit(solution)/shard_map/ppermute | solution.py:67
  115.2 3.5 %collective-permute-start.26 = (bf16[8,4,32,128]{3,2,1,0:T(8,128)(2,1)S(1)}, bf16[8,4,32,128]{3,2,1,0:T(8,128)(2,1)S(1)}, u32[]{:S(2)}, u32[]{:S(2)}) collective-permute-start(bf16[8,4,32,128]{3,2,1,0:T(8,128)(2,1)S(1)} %collective-permute-done.22.refs_2_), channel_id=1, source_target_pairs={{0,1},{1,0},{2,3},{3,2},{4,5},{5,4},{6,7},{7,6},{8,9},{9,8},{10,11... | collective-permute-start | bytes 786440 | tf_op jit(solution)/shard_map/ppermute | solution.py:67
  117.6 2.3 %collective-permute-start.25 = (bf16[8,4,32,128]{3,2,1,0:T(8,128)(2,1)S(1)}, bf16[8,4,32,128]{3,2,1,0:T(8,128)(2,1)S(1)}, u32[]{:S(2)}, u32[]{:S(2)}) collective-permute-start(bf16[8,4,32,128]{3,2,1,0:T(8,128)(2,1)S(1)} %collective-permute-done.21.refs_1_), channel_id=1, source_target_pairs={{0,1},{1,0},{2,3},{3,2},{4,5},{5,4},{6,7},{7,6},{8,9},{9,8},{10,11... | collective-permute-start | bytes 786440 | tf_op jit(solution)/shard_map/ppermute | solution.py:67

commit v5 on v4

--- a/solution.py
+++ b/solution.py
@@ -24,7 +24,8 @@
 OWNED = 108
 LANES = 128
 ZS, YS = 8, 4
-Z_STEPS = (5, 6, 2)
+Z_STEPS = (3, 2, 1)
+Z_PARTNER = 7
 Y_ORDER = (0, 2, 3, 1)
 BF16, F32 = jnp.bfloat16, jnp.float32
 VMEM = pl.BlockSpec(memory_space=pltpu.VMEM)
@@ -286,7 +287,7 @@
     here = z_pos()
     for step, out in zip((0, *Z_STEPS), (out_own, *outs)):
         for far in range(2):
-            z = here ^ (step ^ far)
+            z = here ^ (step ^ (far * Z_PARTNER))
             total = own_ref[z] + g1[z].astype(F32) + g2[z].astype(F32) + g3[z].astype(F32)
             out[far] = total.astype(out.dtype)
 
@@ -303,55 +304,56 @@
     )(own, *got)
 
 
-def z_sum_kernel(own_ref, g1, g2, g3, out_own, out_far):
-    total = [
-        own_ref[far] + g1[far].astype(F32) + g2[far].astype(F32) + g3[far].astype(F32)
-        for far in range(2)
-    ]
-    out_own[...] = total[0]
-    out_far[...] = total[1].astype(BF16)
+def z_sum_kernel(own_ref, g1, g2, g3, out_ref):
+    total = own_ref[...] + g1[...].astype(F32) + g2[...].astype(F32) + g3[...].astype(F32)
+    out_ref[...] = total.astype(BF16)
 
 
 def z_sum(own, got):
-    block = (BUCKETS, RANK, LANES)
     return pl.pallas_call(
         z_sum_kernel,
-        out_shape=[shaped(block, F32), shaped(block, BF16)],
+        out_shape=shaped((2, BUCKETS, RANK, LANES), BF16),
         in_specs=[VMEM] * 4,
-        out_specs=[VMEM] * 2,
+        out_specs=VMEM,
         compiler_params=params(4),
         name="z_sum",
     )(own, *got)
 
 
-def adamw_kernel(own_ref, got_ref, master, moment, second, *outs):
-    weight_out, master_out, moment_out, second_out = outs
-    gradient = (own_ref[...] + got_ref[...].astype(F32))[:, :, 0:OWNED]
-    weights = master[...]
-    first_new = BETA_ONE * moment[...] + (1.0 - BETA_ONE) * gradient
-    second_new = BETA_TWO * second[...] + (1.0 - BETA_TWO) * gradient * gradient
-    first_hat = first_new / (1.0 - BETA_ONE**STEP)
-    second_hat = second_new / (1.0 - BETA_TWO**STEP)
-    weights_new = weights - LEARN_RATE * (
-        first_hat / (jnp.sqrt(second_hat) + EPSILON) + DECAY_RATE * weights
-    )
+def adamw_kernel(mine_ref, got_ref, own_state, partner_state, weight_out, state_out):
     weight_out[...] = jnp.zeros_like(weight_out)
-    weight_out[:, :, 0:OWNED] = weights_new.astype(BF16)
-    master_out[...] = weights_new
-    moment_out[...] = first_new
-    second_out[...] = second_new
-
-
-def adamw(own, got, master, moment, second):
-    state = shaped((BUCKETS, RANK, OWNED), F32)
-    return pl.pallas_call(
-        adamw_kernel,
-        out_shape=[shaped((BUCKETS, RANK, LANES), BF16)] + [state] * 3,
-        in_specs=[VMEM] * 5,
+    for side, state in enumerate((own_state, partner_state)):
+        gradient = mine_ref[side].astype(F32) + got_ref[1 - side].astype(F32)
+        gradient = gradient[:, :, 0:OWNED]
+        weights = state[0]
+        first_new = BETA_ONE * state[1] + (1.0 - BETA_ONE) * gradient
+        second_new = BETA_TWO * state[2] + (1.0 - BETA_TWO) * gradient * gradient
+        first_hat = first_new / (1.0 - BETA_ONE**STEP)
+        second_hat = second_new / (1.0 - BETA_TWO**STEP)
+        weights_new = weights - LEARN_RATE * (
+            first_hat / (jnp.sqrt(second_hat) + EPSILON) + DECAY_RATE * weights
+        )
+        weight_out[side, :, :, 0:OWNED] = weights_new.astype(BF16)
+        if side == 0:
+            state_out[0][...] = weights_new
+            state_out[1][...] = first_new
+            state_out[2][...] = second_new
+
+
+def adamw(mine, got, state, partner_state):
+    block = shaped((BUCKETS, RANK, OWNED), F32)
+
+    def kernel(mine_ref, got_ref, state_ref, partner_ref, weight_out, *state_out):
+        adamw_kernel(mine_ref, got_ref, state_ref, partner_ref, weight_out, state_out)
+
+    return pl.pallas_call(
+        kernel,
+        out_shape=[shaped((2, BUCKETS, RANK, LANES), BF16)] + [block] * 3,
+        in_specs=[VMEM] * 4,
         out_specs=[VMEM] * 4,
         compiler_params=params(4),
         name="adamw",
-    )(own, got, master, moment, second)
+    )(mine, got, state, partner_state)
 
 
 def assemble_kernel(*refs):
@@ -371,10 +373,10 @@
     for copy in copies:
         copy.wait()
     lane = lax.broadcasted_iota(jnp.int32, (RANK, LANES), 1)
-    apart = [z_here ^ z for z in range(ZS)]
-    places = [
-        jnp.where(a < 4, a, jnp.where(a < 6, 11 - a, a - 2)) for a in apart
-    ]
+    places = []
+    for z in range(ZS):
+        apart = z_here ^ z
+        places.append(jnp.where(apart < 4, 2 * apart, 2 * (apart ^ Z_PARTNER) + 1))
     for tile in range(FF // LANES):
         value = None
         first = tile * LANES // OWNED
@@ -416,21 +418,21 @@
     pre, _ = lax.optimization_barrier((pre, share[0]))
     slope = [slope, activation(pre, True, 3)]
     share = [share[0]] + [over_section(share[k], -k) for k in (1, 3, 2)]
+    state = jnp.stack([a[0].transpose(0, 2, 1) for a in (master, moment, second)])
     above, hidden = None, []
     for i in range(3):
         sent = relay(share, above, slope, da, ub)
         above = lax.ppermute(sent, "section", [(1, 0), (2, 1), (3, 2)])
+        pre, state, _ = lax.optimization_barrier((pre, state, sent))
         if i < 2:
-            pre, _ = lax.optimization_barrier((pre, sent))
             hidden += [activation(pre, False, 2 * i + b) for b in range(2)]
             above, *hidden = lax.optimization_barrier((above, *hidden))
+    partner_state = over_dp(state, zx=Z_PARTNER)
     keep, send = grads(share, above, hidden)
     own, *sends = core_sum(keep, over_dp(send, dc=1))
     own, *sends = y_sum(own, [over_dp(sends[k - 1], dy=k) for k in (1, 3, 2)])
-    own, send = z_sum(own, [over_dp(a, zx=k) for a, k in zip(sends, Z_STEPS)])
-    state = [a[0].transpose(0, 2, 1) for a in (master, moment, second)]
-    weight, *state = adamw(own, over_dp(send, zx=1), *state)
-    pair = jnp.stack([weight, over_dp(weight, zx=1)])
+    mine = z_sum(own, [over_dp(a, zx=k) for a, k in zip(sends, Z_STEPS)])
+    pair, *state = adamw(mine, over_dp(mine, zx=Z_PARTNER), state, partner_state)
     column = jnp.concatenate([pair] + [over_dp(pair, zx=k) for k in Z_STEPS[::-1]])
     plane = [column] + [over_dp(column, dy=k) for k in Y_ORDER[1:]]
     rows = assemble(plane + [over_dp(a, dc=1) for a in plane])

time: 123 us -> 119 us (0.967)
  waiting for transfers between devices: 33.3 us -> 24.9 us
  starting transfers between devices: 53 us -> 56.8 us
    ppermute x19, waiting for transfers between devices: 27.6 us -> 19.3 us  [over_dp(): return lax.ppermute(value, 'dp', pairs)]
    ppermute x19, starting transfers between devices: 40.8 us -> 44.6 us  [over_dp(): return lax.ppermute(value, 'dp', pairs)]
  transfers between devices with their start and end apart: 28 -> 28, of which waited for: 16 -> 15; matrix products, arithmetic and copies ran while one was open for 0% -> 0% of each run, Pallas kernels for 13% -> 13%
where the time goes in v5:
time: 119 us; the launch traced here: 118 us
  starting transfers between devices  56.8 us (48%)
  Pallas kernels  35.2 us (30%)
  waiting for transfers between devices  24.9 us (21%)
    ppermute x19, starting transfers between devices, over_dp(): return lax.ppermute(value, 'dp', pairs)  44.6 us
    ppermute x19, waiting for transfers between devices, over_dp(): return lax.ppermute(value, 'dp', pairs)  19.3 us
    pallas_call x6, Pallas kernels, activation(): pl.pallas_call(functools.partial(activation_kernel, slope, bucket * BUCKE...  15.5 us
    pallas_call x3, Pallas kernels, relay(): pl.pallas_call(functools.partial(relay_kernel, first), out_shape=shaped((...  12.5 us
    ppermute x6, starting transfers between devices, over_section(): lax.ppermute(value, 'section', [(i, (i + steps) % 4) for i in range(4)])  8.07 us
    ppermute x3, waiting for transfers between devices, per_device(): above = lax.ppermute(sent, 'section', [(1, 0), (2, 1), (3, 2)])  4.68 us
    ppermute x3, starting transfers between devices, per_device(): above = lax.ppermute(sent, 'section', [(1, 0), (2, 1), (3, 2)])  4.09 us
    pallas_call x1, Pallas kernels, assemble(): pl.pallas_call(assemble_kernel, out_shape=shaped((RANK, FF), BF16), in_sp...  2.48 us
  transfers between devices with their start and end apart: 28, of which 15 were waited for; matrix products, arithmetic and copies ran while one was open for 0% of the time, Pallas kernels for 13%

profile of v5, /device:TPU:1, one launch (start us, length us, event | category | flops | bytes accessed | tf_op | source)
XLA Modules:
  0.0 118.1 jit_solution(15138728725934344182)
XLA Ops:
  0.6 1.3 %slices.1 = (bf16[64,1280]{1,0:T(8,128)(2,1)S(1)}, bf16[64,1280]{1,0:T(8,128)(2,1)S(1)}, bf16[64,1280]{1,0:T(8,128)(2,1)S(1)}, bf16[64,1280]{1,0:T(8,128)(2,1)S(1)}) custom-call(bf16[32,5120]{1,0:T(8,128)(2,1)} %bitcast.51, bf16[32,5120]{1,0:T(8,128)(2,1)} %bitcast.52), custom_call_target="tpu_custom_call" | custom-call | tf_op jit(solution)/shard_map/slices/pallas_call | solution.py:93
  1.9 2.1 %collective-permute-start = (bf16[64,1280]{1,0:T(8,128)(2,1)S(1)}, bf16[64,1280]{1,0:T(8,128)(2,1)S(1)}, u32[]{:S(2)}, u32[]{:S(2)}) collective-permute-start(bf16[64,1280]{1,0:T(8,128)(2,1)S(1)} %get-tuple-element.46), channel_id=1, source_target_pairs={{0,64},{64,128},{128,192},{192,0},{1,65},{65,129},{129,193},{193,1... | collective-permute-start | bytes 491528 | tf_op jit(solution)/shard_map/ppermute | solution.py:72
  4.0 1.4 %collective-permute-start.1 = (bf16[64,1280]{1,0:T(8,128)(2,1)S(1)}, bf16[64,1280]{1,0:T(8,128)(2,1)S(1)}, u32[]{:S(2)}, u32[]{:S(2)}) collective-permute-start(bf16[64,1280]{1,0:T(8,128)(2,1)S(1)} %get-tuple-element.47), channel_id=1, source_target_pairs={{0,192},{64,0},{128,64},{192,128},{1,193},{65,1},{129,65},{193,129... | collective-permute-start | bytes 491528 | tf_op jit(solution)/shard_map/ppermute | solution.py:72
  5.4 1.6 %collective-permute-start.2 = (bf16[64,1280]{1,0:T(8,128)(2,1)S(1)}, bf16[64,1280]{1,0:T(8,128)(2,1)S(1)}, u32[]{:S(2)}, u32[]{:S(2)}) collective-permute-start(bf16[64,1280]{1,0:T(8,128)(2,1)S(1)} %get-tuple-element.48), channel_id=1, source_target_pairs={{0,128},{64,192},{128,0},{192,64},{1,129},{65,193},{129,1},{193,65... | collective-permute-start | bytes 491528 | tf_op jit(solution)/shard_map/ppermute | solution.py:72
  7.0 5.2 %slope.2.refs_4_.refs_5_ = bf16[128,20736]{1,0:T(8,128)(2,1)S(1)} custom-call(bf16[128,27648]{1,0:T(8,128)(2,1)} %bitcast.44), custom_call_target="tpu_custom_call" | custom-call | flops 26542080 | bytes 10616832 | tf_op jit(solution)/shard_map/slope/pallas_call | solution.py:136
  12.3 0.0 collective-permute-done.w1
  12.3 0.5 collective-permute-done.2.w2
  12.8 0.9 shares.1
  13.7 1.7 %collective-permute-start.3 = (f32[32,256]{1,0:T(8,128)S(1)}, f32[32,256]{1,0:T(8,128)S(1)}, u32[]{:S(2)}, u32[]{:S(2)}) collective-permute-start(f32[32,256]{1,0:T(8,128)S(1)} %get-tuple-element.54), channel_id=1, source_target_pairs={{0,192},{64,0},{128,64},{192,128},{1,193},{65,1},{129,65},{193,129... | collective-permute-start | bytes 98312 | tf_op jit(solution)/shard_map/ppermute | solution.py:72
  15.4 1.2 %collective-permute-start.5 = (f32[32,256]{1,0:T(8,128)S(1)}, f32[32,256]{1,0:T(8,128)S(1)}, u32[]{:S(2)}, u32[]{:S(2)}) collective-permute-start(f32[32,256]{1,0:T(8,128)S(1)} %get-tuple-element.56), channel_id=1, source_target_pairs={{0,128},{64,192},{128,0},{192,64},{1,129},{65,193},{129,1},{193,65... | collective-permute-start | bytes 98312 | tf_op jit(solution)/shard_map/ppermute | solution.py:72
  16.7 2.6 %slope.3.refs_5_.refs_6_ = bf16[128,6912]{1,0:T(8,128)(2,1)S(1)} custom-call(bf16[128,27648]{1,0:T(8,128)(2,1)} %bitcast.45), custom_call_target="tpu_custom_call" | custom-call | flops 8847360 | bytes 3538944 | tf_op jit(solution)/shard_map/slope/pallas_call | solution.py:136
  19.3 0.1 collective-permute-done.4.refs_2_.s2
  19.4 0.3 collective-permute-done.5.refs_3_.s3
  19.8 0.0 copy-start.5
  19.8 4.1 %relay_first.1 = bf16[96,128]{1,0:T(8,128)(2,1)S(1)} custom-call(f32[32,256]{1,0:T(8,128)S(1)} %get-tuple-element.53.refs_0_.s0, f32[32,256]{1,0:T(8,128)S(1)} %collective-permute-done.3.refs_1_.s1, f32[32,256]{1,0:T(8,128)S(1)} %collective-permute-done.4.refs_2_.s2, f32[32,256]{1,0:T(8,128)S(1)} %collective-permute-done.5.refs_3_.s3, ...), custom_call_target="tpu_custom_call" | custom-call | tf_op jit(solution)/shard_map/relay_first/pallas_call | solution.py:219
  23.9 1.5 %collective-permute-start.6 = (bf16[96,128]{1,0:T(8,128)(2,1)S(1)}, bf16[96,128]{1,0:T(8,128)(2,1)S(1)}, u32[]{:S(2)}, u32[]{:S(2)}) collective-permute-start(bf16[96,128]{1,0:T(8,128)(2,1)S(1)} %relay_first.1), channel_id=1, source_target_pairs={{64,0},{128,64},{192,128},{65,1},{129,65},{193,129},{66,2},{130,66... | collective-permute-start | bytes 73736 | tf_op jit(solution)/shard_map/ppermute | solution.py:425
  25.4 1.9 %hidden.5.h1 = bf16[128,6912]{1,0:T(8,128)(2,1)S(1)} custom-call(bf16[128,27648]{1,0:T(8,128)(2,1)} %bitcast.46), custom_call_target="tpu_custom_call" | custom-call | flops 8847360 | bytes 3538944 | tf_op jit(solution)/shard_map/hidden/pallas_call | solution.py:136
  27.3 1.9 %hidden.4.h0 = bf16[128,6912]{1,0:T(8,128)(2,1)S(1)} custom-call(bf16[128,27648]{1,0:T(8,128)(2,1)} %bitcast.47), custom_call_target="tpu_custom_call" | custom-call | flops 8847360 | bytes 3538944 | tf_op jit(solution)/shard_map/hidden/pallas_call | solution.py:136
  29.3 4.2 %relay.2 = bf16[96,128]{1,0:T(8,128)(2,1)S(1)} custom-call(f32[32,256]{1,0:T(8,128)S(1)} %get-tuple-element.53.refs_0_.s0, f32[32,256]{1,0:T(8,128)S(1)} %collective-permute-done.3.refs_1_.s1, f32[32,256]{1,0:T(8,128)S(1)} %collective-permute-done.4.refs_2_.s2, f32[32,256]{1,0:T(8,128)S(1)} %collective-permute-done.5.refs_3_.s3, ...), custom_call_target="tpu_custom_call" | custom-call | tf_op jit(solution)/shard_map/relay/pallas_call | solution.py:219
  33.5 1.3 %collective-permute-start.7 = (bf16[96,128]{1,0:T(8,128)(2,1)S(1)}, bf16[96,128]{1,0:T(8,128)(2,1)S(1)}, u32[]{:S(2)}, u32[]{:S(2)}) collective-permute-start(bf16[96,128]{1,0:T(8,128)(2,1)S(1)} %relay.2), channel_id=1, source_target_pairs={{64,0},{128,64},{192,128},{65,1},{129,65},{193,129},{66,2},{130,66... | collective-permute-start | bytes 73736 | tf_op jit(solution)/shard_map/ppermute | solution.py:425
  34.8 1.9 %hidden.7.h3 = bf16[128,6912]{1,0:T(8,128)(2,1)S(1)} custom-call(bf16[128,27648]{1,0:T(8,128)(2,1)} %bitcast.48), custom_call_target="tpu_custom_call" | custom-call | flops 8847360 | bytes 3538944 | tf_op jit(solution)/shard_map/hidden/pallas_call | solution.py:136
  36.8 1.9 %hidden.6.h2 = bf16[128,6912]{1,0:T(8,128)(2,1)S(1)} custom-call(bf16[128,27648]{1,0:T(8,128)(2,1)} %bitcast.49), custom_call_target="tpu_custom_call" | custom-call | flops 8847360 | bytes 3538944 | tf_op jit(solution)/shard_map/hidden/pallas_call | solution.py:136
  38.7 0.2 collective-permute-done.7.refs_4_
  38.9 4.2 %relay.3 = bf16[96,128]{1,0:T(8,128)(2,1)S(1)} custom-call(f32[32,256]{1,0:T(8,128)S(1)} %get-tuple-element.53.refs_0_.s0, f32[32,256]{1,0:T(8,128)S(1)} %collective-permute-done.3.refs_1_.s1, f32[32,256]{1,0:T(8,128)S(1)} %collective-permute-done.4.refs_2_.s2, f32[32,256]{1,0:T(8,128)S(1)} %collective-permute-done.5.refs_3_.s3, ...), custom_call_target="tpu_custom_call" | custom-call | tf_op jit(solution)/shard_map/relay/pallas_call | solution.py:219
  43.1 1.3 %collective-permute-start.8 = (bf16[96,128]{1,0:T(8,128)(2,1)S(1)}, bf16[96,128]{1,0:T(8,128)(2,1)S(1)}, u32[]{:S(2)}, u32[]{:S(2)}) collective-permute-start(bf16[96,128]{1,0:T(8,128)(2,1)S(1)} %relay.3), channel_id=1, source_target_pairs={{64,0},{128,64},{192,128},{65,1},{129,65},{193,129},{66,2},{130,66... | collective-permute-start | bytes 73736 | tf_op jit(solution)/shard_map/ppermute | solution.py:425
  44.4 4.5 %collective-permute-done.8.above_ref = bf16[96,128]{1,0:T(8,128)(2,1)S(1)} collective-permute-done((bf16[96,128]{1,0:T(8,128)(2,1)S(1)}, bf16[96,128]{1,0:T(8,128)(2,1)S(1)}, u32[]{:S(2)}, u32[]{:S(2)}) %collective-permute-start.8) | collective-permute-done | bytes 24608 | tf_op jit(solution)/shard_map/ppermute | solution.py:425
  48.9 1.4 %grads.1 = (bf16[4,8,4,32,128]{4,3,2,1,0:T(8,128)(2,1)S(1)}, bf16[4,8,4,32,128]{4,3,2,1,0:T(8,128)(2,1)S(1)}) custom-call(f32[32,256]{1,0:T(8,128)S(1)} %get-tuple-element.53.refs_0_.s0, f32[32,256]{1,0:T(8,128)S(1)} %collective-permute-done.3.refs_1_.s1, f32[32,256]{1,0:T(8,128)S(1)} %collective-permute-done.4.refs_2_.s2, ...), custom_call_target="tpu_custom_call" | custom-call | tf_op jit(solution)/shard_map/grads/pallas_call | solution.py:255
  50.3 5.5 %collective-permute-start.9 = (bf16[4,8,4,32,128]{4,3,2,1,0:T(8,128)(2,1)S(1)}, bf16[4,8,4,32,128]{4,3,2,1,0:T(8,128)(2,1)S(1)}, u32[]{:S(2)}, u32[]{:S(2)}) collective-permute-start(bf16[4,8,4,32,128]{4,3,2,1,0:T(8,128)(2,1)S(1)} %get-tuple-element.71), channel_id=1, source_target_pairs={{0,1},{1,0},{2,3},{3,2},{4,5},{5,4},{6,7},{7,6},{8,9},{9,8},{10,11... | collective-permute-start | bytes 3145736 | tf_op jit(solution)/shard_map/ppermute | solution.py:68
  55.8 2.3 %collective-permute-done.9.got_ref = bf16[4,8,4,32,128]{4,3,2,1,0:T(8,128)(2,1)S(1)} collective-permute-done((bf16[4,8,4,32,128]{4,3,2,1,0:T(8,128)(2,1)S(1)}, bf16[4,8,4,32,128]{4,3,2,1,0:T(8,128)(2,1)S(1)}, u32[]{:S(2)}, u32[]{:S(2)}) %collective-permute-start.9) | collective-permute-done | bytes 1048608 | tf_op jit(solution)/shard_map/ppermute | solution.py:68
  58.1 0.2 core_sum.1
  58.3 0.8 collective-permute-start.10
  59.1 2.0 %collective-permute-start.11 = (bf16[8,4,32,128]{3,2,1,0:T(8,128)(2,1)S(1)}, bf16[8,4,32,128]{3,2,1,0:T(8,128)(2,1)S(1)}, u32[]{:S(2)}, u32[]{:S(2)}) collective-permute-start(bf16[8,4,32,128]{3,2,1,0:T(8,128)(2,1)S(1)} %get-tuple-element.74), channel_id=1, source_target_pairs={{0,6},{1,7},{2,0},{3,1},{4,2},{5,3},{6,4},{7,5},{8,14},{9,15},{10,... | collective-permute-start | bytes 786440 | tf_op jit(solution)/shard_map/ppermute | solution.py:68
  61.1 1.1 collective-permute-start.12
  62.2 5.6 %collective-permute-start.17 = (f32[3,4,32,108]{3,2,1,0:T(8,128)S(1)}, f32[3,4,32,108]{3,2,1,0:T(8,128)S(1)}, u32[]{:S(2)}, u32[]{:S(2)}) collective-permute-start(f32[3,4,32,108]{3,2,1,0:T(8,128)S(1)} %pad_maximum_fusion.state_ref), channel_id=1, source_target_pairs={{0,56},{1,57},{2,58},{3,59},{4,60},{5,61},{6,62},{7,63},{8,48},{9,... | collective-permute-start | bytes 497672 | tf_op jit(solution)/shard_map/ppermute | solution.py:68
  67.7 0.0 collective-permute-done.11.g2
  67.7 5.6 %collective-permute-done.12.g3 = bf16[8,4,32,128]{3,2,1,0:T(8,128)(2,1)S(1)} collective-permute-done((bf16[8,4,32,128]{3,2,1,0:T(8,128)(2,1)S(1)}, bf16[8,4,32,128]{3,2,1,0:T(8,128)(2,1)S(1)}, u32[]{:S(2)}, u32[]{:S(2)}) %collective-permute-start.12) | collective-permute-done | bytes 262176 | tf_op jit(solution)/shard_map/ppermute | solution.py:68
  73.4 0.1 y_sum.1
  73.5 4.4 %collective-permute-start.13 = (bf16[2,4,32,128]{3,2,1,0:T(8,128)(2,1)S(1)}, bf16[2,4,32,128]{3,2,1,0:T(8,128)(2,1)S(1)}, u32[]{:S(2)}, u32[]{:S(2)}) collective-permute-start(bf16[2,4,32,128]{3,2,1,0:T(8,128)(2,1)S(1)} %get-tuple-element.77), channel_id=1, source_target_pairs={{0,24},{1,25},{2,26},{3,27},{4,28},{5,29},{6,30},{7,31},{8,16},{9,... | collective-permute-start | bytes 196616 | tf_op jit(solution)/shard_map/ppermute | solution.py:68
  77.9 0.0 collective-permute-start.14
  77.9 0.4 collective-permute-start.15
  78.3 1.3 %collective-permute-done.13.g1 = bf16[2,4,32,128]{3,2,1,0:T(8,128)(2,1)S(1)} collective-permute-done((bf16[2,4,32,128]{3,2,1,0:T(8,128)(2,1)S(1)}, bf16[2,4,32,128]{3,2,1,0:T(8,128)(2,1)S(1)}, u32[]{:S(2)}, u32[]{:S(2)}) %collective-permute-start.13) | collective-permute-done | bytes 65568 | tf_op jit(solution)/shard_map/ppermute | solution.py:68
  79.6 3.6 %collective-permute-done.14.g2 = bf16[2,4,32,128]{3,2,1,0:T(8,128)(2,1)S(1)} collective-permute-done((bf16[2,4,32,128]{3,2,1,0:T(8,128)(2,1)S(1)}, bf16[2,4,32,128]{3,2,1,0:T(8,128)(2,1)S(1)}, u32[]{:S(2)}, u32[]{:S(2)}) %collective-permute-start.14) | collective-permute-done | bytes 65568 | tf_op jit(solution)/shard_map/ppermute | solution.py:68
  83.2 0.0 collective-permute-done.15.g3
  83.2 4.8 %collective-permute-start.16 = (bf16[2,4,32,128]{3,2,1,0:T(8,128)(2,1)S(1)}, bf16[2,4,32,128]{3,2,1,0:T(8,128)(2,1)S(1)}, u32[]{:S(2)}, u32[]{:S(2)}) collective-permute-start(bf16[2,4,32,128]{3,2,1,0:T(8,128)(2,1)S(1)} %z_sum.1.mine_ref), channel_id=1, source_target_pairs={{0,56},{1,57},{2,58},{3,59},{4,60},{5,61},{6,62},{7,63},{8,48},{9,... | collective-permute-start | bytes 196616 | tf_op jit(solution)/shard_map/ppermute | solution.py:68
  88.0 0.0 collective-permute-done.17.partner_ref
  88.0 1.7 %collective-permute-done.16.got_ref = bf16[2,4,32,128]{3,2,1,0:T(8,128)(2,1)S(1)} collective-permute-done((bf16[2,4,32,128]{3,2,1,0:T(8,128)(2,1)S(1)}, bf16[2,4,32,128]{3,2,1,0:T(8,128)(2,1)S(1)}, u32[]{:S(2)}, u32[]{:S(2)}) %collective-permute-start.16) | collective-permute-done | bytes 65568 | tf_op jit(solution)/shard_map/ppermute | solution.py:68
  89.7 0.7 adamw.1
  90.4 1.6 %collective-permute-start.20 = (bf16[2,4,32,128]{3,2,1,0:T(8,128)(2,1)S(1)}, bf16[2,4,32,128]{3,2,1,0:T(8,128)(2,1)S(1)}, u32[]{:S(2)}, u32[]{:S(2)}) collective-permute-start(bf16[2,4,32,128]{3,2,1,0:T(8,128)(2,1)S(1)} %get-tuple-element.82), channel_id=1, source_target_pairs={{0,24},{1,25},{2,26},{3,27},{4,28},{5,29},{6,30},{7,31},{8,16},{9,... | collective-permute-start | bytes 196616 | tf_op jit(solution)/shard_map/ppermute | solution.py:68
  92.0 0.0 collective-permute-start.19
  92.0 1.9 %collective-permute-start.18 = (bf16[2,4,32,128]{3,2,1,0:T(8,128)(2,1)S(1)}, bf16[2,4,32,128]{3,2,1,0:T(8,128)(2,1)S(1)}, u32[]{:S(2)}, u32[]{:S(2)}) collective-permute-start(bf16[2,4,32,128]{3,2,1,0:T(8,128)(2,1)S(1)} %get-tuple-element.82), channel_id=1, source_target_pairs={{0,8},{1,9},{2,10},{3,11},{4,12},{5,13},{6,14},{7,15},{8,0},{9,1},... | collective-permute-start | bytes 196616 | tf_op jit(solution)/shard_map/ppermute | solution.py:68
  94.0 2.1 %collective-permute-done.18 = bf16[2,4,32,128]{3,2,1,0:T(8,128)(2,1)S(1)} collective-permute-done((bf16[2,4,32,128]{3,2,1,0:T(8,128)(2,1)S(1)}, bf16[2,4,32,128]{3,2,1,0:T(8,128)(2,1)S(1)}, u32[]{:S(2)}, u32[]{:S(2)}) %collective-permute-start.18) | collective-permute-done | bytes 65568 | tf_op jit(solution)/shard_map/ppermute | solution.py:68
  96.1 1.3 %collective-permute-done.19 = bf16[2,4,32,128]{3,2,1,0:T(8,128)(2,1)S(1)} collective-permute-done((bf16[2,4,32,128]{3,2,1,0:T(8,128)(2,1)S(1)}, bf16[2,4,32,128]{3,2,1,0:T(8,128)(2,1)S(1)}, u32[]{:S(2)}, u32[]{:S(2)}) %collective-permute-start.19) | collective-permute-done | bytes 65568 | tf_op jit(solution)/shard_map/ppermute | solution.py:68
  97.4 0.0 collective-permute-done.20
  97.4 0.1 collective-permute-start.23
  97.5 2.7 %collective-permute-start.22 = (bf16[8,4,32,128]{3,2,1,0:T(8,128)(2,1)S(1)}, bf16[8,4,32,128]{3,2,1,0:T(8,128)(2,1)S(1)}, u32[]{:S(2)}, u32[]{:S(2)}) collective-permute-start(bf16[8,4,32,128]{3,2,1,0:T(8,128)(2,1)S(1)} %constant_dynamic-update-slice_fusion.refs_0_), channel_id=1, source_target_pairs={{0,6},{1,7},{2,0},{3,1},{4,2},{5,3},{6,4},{7,5},{8,14},{9,15},{10,... | collective-permute-start | bytes 786440 | tf_op jit(solution)/shard_map/ppermute | solution.py:68
  100.2 0.0 collective-permute-start.21
  100.2 3.9 %collective-permute-start.24 = (bf16[8,4,32,128]{3,2,1,0:T(8,128)(2,1)S(1)}, bf16[8,4,32,128]{3,2,1,0:T(8,128)(2,1)S(1)}, u32[]{:S(2)}, u32[]{:S(2)}) collective-permute-start(bf16[8,4,32,128]{3,2,1,0:T(8,128)(2,1)S(1)} %constant_dynamic-update-slice_fusion.refs_0_), channel_id=1, source_target_pairs={{0,1},{1,0},{2,3},{3,2},{4,5},{5,4},{6,7},{7,6},{8,9},{9,8},{10,11... | collective-permute-start | bytes 786440 | tf_op jit(solution)/shard_map/ppermute | solution.py:68
  104.0 9.4 %collective-permute-start.27 = (bf16[8,4,32,128]{3,2,1,0:T(8,128)(2,1)S(1)}, bf16[8,4,32,128]{3,2,1,0:T(8,128)(2,1)S(1)}, u32[]{:S(2)}, u32[]{:S(2)}) collective-permute-start(bf16[8,4,32,128]{3,2,1,0:T(8,128)(2,1)S(1)} %collective-permute-done.23.refs_3_), channel_id=1, source_target_pairs={{0,1},{1,0},{2,3},{3,2},{4,5},{5,4},{6,7},{7,6},{8,9},{9,8},{10,11... | collective-permute-start | bytes 786440 | tf_op jit(solution)/shard_map/ppermute | solution.py:68
  113.5 0.0 collective-permute-start.26
  113.5 0.5 collective-permute-start.25
  114.0 0.6 collective-permute-done.27.refs_7_
  114.6 0.4 collective-permute-done.26.refs_6_
  115.0 0.4 collective-permute-done.25.refs_5_
  115.4 2.5 %assemble.1 = bf16[32,27648]{1,0:T(8,128)(2,1)} custom-call(bf16[8,4,32,128]{3,2,1,0:T(8,128)(2,1)S(1)} %constant_dynamic-update-slice_fusion.refs_0_, bf16[8,4,32,128]{3,2,1,0:T(8,128)(2,1)S(1)} %collective-permute-done.21.refs_1_, bf16[8,4,32,128]{3,2,1,0:T(8,128)(2,1)S(1)} %collective-permute-done.22.refs_2_, ...), custom_call_target="tpu_custom_call" | custom-call | tf_op jit(solution)/shard_map/assemble/pallas_call | solution.py:396
  (26 shorter events, 0.1 us)
Async XLA Ops:
  1.9 10.4 %collective-permute-start = (bf16[64,1280]{1,0:T(8,128)(2,1)S(1)}, bf16[64,1280]{1,0:T(8,128)(2,1)S(1)}, u32[]{:S(2)}, u32[]{:S(2)}) collective-permute-start(bf16[64,1280]{1,0:T(8,128)(2,1)S(1)} %get-tuple-element.46), channel_id=1, source_target_pairs={{0,64},{64,128},{128,192},{192,0},{1,65},{65,129},{129,193},{193,1... | collective-permute-start | bytes 491528 | tf_op jit(solution)/shard_map/ppermute | solution.py:72
  4.0 8.3 %collective-permute-start.1 = (bf16[64,1280]{1,0:T(8,128)(2,1)S(1)}, bf16[64,1280]{1,0:T(8,128)(2,1)S(1)}, u32[]{:S(2)}, u32[]{:S(2)}) collective-permute-start(bf16[64,1280]{1,0:T(8,128)(2,1)S(1)} %get-tuple-element.47), channel_id=1, source_target_pairs={{0,192},{64,0},{128,64},{192,128},{1,193},{65,1},{129,65},{193,129... | collective-permute-start | bytes 491528 | tf_op jit(solution)/shard_map/ppermute | solution.py:72
  5.4 7.4 %collective-permute-start.2 = (bf16[64,1280]{1,0:T(8,128)(2,1)S(1)}, bf16[64,1280]{1,0:T(8,128)(2,1)S(1)}, u32[]{:S(2)}, u32[]{:S(2)}) collective-permute-start(bf16[64,1280]{1,0:T(8,128)(2,1)S(1)} %get-tuple-element.48), channel_id=1, source_target_pairs={{0,128},{64,192},{128,0},{192,64},{1,129},{65,193},{129,1},{193,65... | collective-permute-start | bytes 491528 | tf_op jit(solution)/shard_map/ppermute | solution.py:72
  7.0 5.8 %copy-start.2 = (bf16[128,1280]{1,0:T(8,128)(2,1)S(1)}, bf16[128,1280]{1,0:T(8,128)(2,1)}, u32[]{:S(2)}) copy-start(bf16[128,1280]{1,0:T(8,128)(2,1)} %g_ref.1) | copy-start | bytes 983044
  13.7 5.6 %collective-permute-start.3 = (f32[32,256]{1,0:T(8,128)S(1)}, f32[32,256]{1,0:T(8,128)S(1)}, u32[]{:S(2)}, u32[]{:S(2)}) collective-permute-start(f32[32,256]{1,0:T(8,128)S(1)} %get-tuple-element.54), channel_id=1, source_target_pairs={{0,192},{64,0},{128,64},{192,128},{1,193},{65,1},{129,65},{193,129... | collective-permute-start | bytes 98312 | tf_op jit(solution)/shard_map/ppermute | solution.py:72
  15.4 4.0 %collective-permute-start.4 = (f32[32,256]{1,0:T(8,128)S(1)}, f32[32,256]{1,0:T(8,128)S(1)}, u32[]{:S(2)}, u32[]{:S(2)}) collective-permute-start(f32[32,256]{1,0:T(8,128)S(1)} %get-tuple-element.55), channel_id=1, source_target_pairs={{0,64},{64,128},{128,192},{192,0},{1,65},{65,129},{129,193},{193,1... | collective-permute-start | bytes 98312 | tf_op jit(solution)/shard_map/ppermute | solution.py:72
  15.4 4.3 %collective-permute-start.5 = (f32[32,256]{1,0:T(8,128)S(1)}, f32[32,256]{1,0:T(8,128)S(1)}, u32[]{:S(2)}, u32[]{:S(2)}) collective-permute-start(f32[32,256]{1,0:T(8,128)S(1)} %get-tuple-element.56), channel_id=1, source_target_pairs={{0,128},{64,192},{128,0},{192,64},{1,129},{65,193},{129,1},{193,65... | collective-permute-start | bytes 98312 | tf_op jit(solution)/shard_map/ppermute | solution.py:72
  16.7 3.1 %copy-start = (bf16[1,27648,32]{1,2,0:T(8,128)(2,1)S(1)}, bf16[1,27648,32]{1,2,0:T(8,128)(2,1)}, u32[]{:S(2)}) copy-start(bf16[1,27648,32]{1,2,0:T(8,128)(2,1)} %param.11) | copy-start | bytes 5308420
  16.7 3.1 %copy-start.1 = (bf16[1,27648,32]{1,2,0:T(8,128)(2,1)S(1)}, bf16[1,27648,32]{1,2,0:T(8,128)(2,1)}, u32[]{:S(2)}) copy-start(bf16[1,27648,32]{1,2,0:T(8,128)(2,1)} %param.14) | copy-start | bytes 5308420
  19.8 5.6 %copy-start.3 = (f32[1,4,108,32]{2,3,1,0:T(8,128)S(1)}, f32[1,4,108,32]{2,3,1,0:T(8,128)}, u32[]{:S(2)}) copy-start(f32[1,4,108,32]{2,3,1,0:T(8,128)} %param.17) | copy-start | bytes 165892
  19.8 5.6 %copy-start.4 = (f32[1,4,108,32]{2,3,1,0:T(8,128)S(1)}, f32[1,4,108,32]{2,3,1,0:T(8,128)}, u32[]{:S(2)}) copy-start(f32[1,4,108,32]{2,3,1,0:T(8,128)} %param.16) | copy-start | bytes 165892
  19.8 5.6 %copy-start.5 = (f32[1,4,108,32]{2,3,1,0:T(8,128)S(1)}, f32[1,4,108,32]{2,3,1,0:T(8,128)}, u32[]{:S(2)}) copy-start(f32[1,4,108,32]{2,3,1,0:T(8,128)} %param.15) | copy-start | bytes 165892
  23.9 5.4 %collective-permute-start.6 = (bf16[96,128]{1,0:T(8,128)(2,1)S(1)}, bf16[96,128]{1,0:T(8,128)(2,1)S(1)}, u32[]{:S(2)}, u32[]{:S(2)}) collective-permute-start(bf16[96,128]{1,0:T(8,128)(2,1)S(1)} %relay_first.1), channel_id=1, source_target_pairs={{64,0},{128,64},{192,128},{65,1},{129,65},{193,129},{66,2},{130,66... | collective-permute-start | bytes 73736 | tf_op jit(solution)/shard_map/ppermute | solution.py:425
  33.5 5.3 %collective-permute-start.7 = (bf16[96,128]{1,0:T(8,128)(2,1)S(1)}, bf16[96,128]{1,0:T(8,128)(2,1)S(1)}, u32[]{:S(2)}, u32[]{:S(2)}) collective-permute-start(bf16[96,128]{1,0:T(8,128)(2,1)S(1)} %relay.2), channel_id=1, source_target_pairs={{64,0},{128,64},{192,128},{65,1},{129,65},{193,129},{66,2},{130,66... | collective-permute-start | bytes 73736 | tf_op jit(solution)/shard_map/ppermute | solution.py:425
  43.1 5.8 %collective-permute-start.8 = (bf16[96,128]{1,0:T(8,128)(2,1)S(1)}, bf16[96,128]{1,0:T(8,128)(2,1)S(1)}, u32[]{:S(2)}, u32[]{:S(2)}) collective-permute-start(bf16[96,128]{1,0:T(8,128)(2,1)S(1)} %relay.3), channel_id=1, source_target_pairs={{64,0},{128,64},{192,128},{65,1},{129,65},{193,129},{66,2},{130,66... | collective-permute-start | bytes 73736 | tf_op jit(solution)/shard_map/ppermute | solution.py:425
  50.3 7.8 %collective-permute-start.9 = (bf16[4,8,4,32,128]{4,3,2,1,0:T(8,128)(2,1)S(1)}, bf16[4,8,4,32,128]{4,3,2,1,0:T(8,128)(2,1)S(1)}, u32[]{:S(2)}, u32[]{:S(2)}) collective-permute-start(bf16[4,8,4,32,128]{4,3,2,1,0:T(8,128)(2,1)S(1)} %get-tuple-element.71), channel_id=1, source_target_pairs={{0,1},{1,0},{2,3},{3,2},{4,5},{5,4},{6,7},{7,6},{8,9},{9,8},{10,11... | collective-permute-start | bytes 3145736 | tf_op jit(solution)/shard_map/ppermute | solution.py:68
  58.3 9.4 %collective-permute-start.10 = (bf16[8,4,32,128]{3,2,1,0:T(8,128)(2,1)S(1)}, bf16[8,4,32,128]{3,2,1,0:T(8,128)(2,1)S(1)}, u32[]{:S(2)}, u32[]{:S(2)}) collective-permute-start(bf16[8,4,32,128]{3,2,1,0:T(8,128)(2,1)S(1)} %get-tuple-element.73), channel_id=1, source_target_pairs={{0,2},{1,3},{2,4},{3,5},{4,6},{5,7},{6,0},{7,1},{8,10},{9,11},{10,... | collective-permute-start | bytes 786440 | tf_op jit(solution)/shard_map/ppermute | solution.py:68
  59.1 8.7 %collective-permute-start.11 = (bf16[8,4,32,128]{3,2,1,0:T(8,128)(2,1)S(1)}, bf16[8,4,32,128]{3,2,1,0:T(8,128)(2,1)S(1)}, u32[]{:S(2)}, u32[]{:S(2)}) collective-permute-start(bf16[8,4,32,128]{3,2,1,0:T(8,128)(2,1)S(1)} %get-tuple-element.74), channel_id=1, source_target_pairs={{0,6},{1,7},{2,0},{3,1},{4,2},{5,3},{6,4},{7,5},{8,14},{9,15},{10,... | collective-permute-start | bytes 786440 | tf_op jit(solution)/shard_map/ppermute | solution.py:68
  61.1 12.3 %collective-permute-start.12 = (bf16[8,4,32,128]{3,2,1,0:T(8,128)(2,1)S(1)}, bf16[8,4,32,128]{3,2,1,0:T(8,128)(2,1)S(1)}, u32[]{:S(2)}, u32[]{:S(2)}) collective-permute-start(bf16[8,4,32,128]{3,2,1,0:T(8,128)(2,1)S(1)} %get-tuple-element.75), channel_id=1, source_target_pairs={{0,4},{1,5},{2,6},{3,7},{4,0},{5,1},{6,2},{7,3},{8,12},{9,13},{10,... | collective-permute-start | bytes 786440 | tf_op jit(solution)/shard_map/ppermute | solution.py:68
  62.2 25.9 %collective-permute-start.17 = (f32[3,4,32,108]{3,2,1,0:T(8,128)S(1)}, f32[3,4,32,108]{3,2,1,0:T(8,128)S(1)}, u32[]{:S(2)}, u32[]{:S(2)}) collective-permute-start(f32[3,4,32,108]{3,2,1,0:T(8,128)S(1)} %pad_maximum_fusion.state_ref), channel_id=1, source_target_pairs={{0,56},{1,57},{2,58},{3,59},{4,60},{5,61},{6,62},{7,63},{8,48},{9,... | collective-permute-start | bytes 497672 | tf_op jit(solution)/shard_map/ppermute | solution.py:68
  73.5 6.1 %collective-permute-start.13 = (bf16[2,4,32,128]{3,2,1,0:T(8,128)(2,1)S(1)}, bf16[2,4,32,128]{3,2,1,0:T(8,128)(2,1)S(1)}, u32[]{:S(2)}, u32[]{:S(2)}) collective-permute-start(bf16[2,4,32,128]{3,2,1,0:T(8,128)(2,1)S(1)} %get-tuple-element.77), channel_id=1, source_target_pairs={{0,24},{1,25},{2,26},{3,27},{4,28},{5,29},{6,30},{7,31},{8,16},{9,... | collective-permute-start | bytes 196616 | tf_op jit(solution)/shard_map/ppermute | solution.py:68
  77.9 5.3 %collective-permute-start.14 = (bf16[2,4,32,128]{3,2,1,0:T(8,128)(2,1)S(1)}, bf16[2,4,32,128]{3,2,1,0:T(8,128)(2,1)S(1)}, u32[]{:S(2)}, u32[]{:S(2)}) collective-permute-start(bf16[2,4,32,128]{3,2,1,0:T(8,128)(2,1)S(1)} %get-tuple-element.78), channel_id=1, source_target_pairs={{0,16},{1,17},{2,18},{3,19},{4,20},{5,21},{6,22},{7,23},{8,24},{9,... | collective-permute-start | bytes 196616 | tf_op jit(solution)/shard_map/ppermute | solution.py:68
  77.9 5.3 %collective-permute-start.15 = (bf16[2,4,32,128]{3,2,1,0:T(8,128)(2,1)S(1)}, bf16[2,4,32,128]{3,2,1,0:T(8,128)(2,1)S(1)}, u32[]{:S(2)}, u32[]{:S(2)}) collective-permute-start(bf16[2,4,32,128]{3,2,1,0:T(8,128)(2,1)S(1)} %get-tuple-element.79), channel_id=1, source_target_pairs={{0,8},{1,9},{2,10},{3,11},{4,12},{5,13},{6,14},{7,15},{8,0},{9,1},... | collective-permute-start | bytes 196616 | tf_op jit(solution)/shard_map/ppermute | solution.py:68
  83.2 6.5 %collective-permute-start.16 = (bf16[2,4,32,128]{3,2,1,0:T(8,128)(2,1)S(1)}, bf16[2,4,32,128]{3,2,1,0:T(8,128)(2,1)S(1)}, u32[]{:S(2)}, u32[]{:S(2)}) collective-permute-start(bf16[2,4,32,128]{3,2,1,0:T(8,128)(2,1)S(1)} %z_sum.1.mine_ref), channel_id=1, source_target_pairs={{0,56},{1,57},{2,58},{3,59},{4,60},{5,61},{6,62},{7,63},{8,48},{9,... | collective-permute-start | bytes 196616 | tf_op jit(solution)/shard_map/ppermute | solution.py:68
  90.4 7.0 %collective-permute-start.20 = (bf16[2,4,32,128]{3,2,1,0:T(8,128)(2,1)S(1)}, bf16[2,4,32,128]{3,2,1,0:T(8,128)(2,1)S(1)}, u32[]{:S(2)}, u32[]{:S(2)}) collective-permute-start(bf16[2,4,32,128]{3,2,1,0:T(8,128)(2,1)S(1)} %get-tuple-element.82), channel_id=1, source_target_pairs={{0,24},{1,25},{2,26},{3,27},{4,28},{5,29},{6,30},{7,31},{8,16},{9,... | collective-permute-start | bytes 196616 | tf_op jit(solution)/shard_map/ppermute | solution.py:68
  92.0 5.3 %collective-permute-start.19 = (bf16[2,4,32,128]{3,2,1,0:T(8,128)(2,1)S(1)}, bf16[2,4,32,128]{3,2,1,0:T(8,128)(2,1)S(1)}, u32[]{:S(2)}, u32[]{:S(2)}) collective-permute-start(bf16[2,4,32,128]{3,2,1,0:T(8,128)(2,1)S(1)} %get-tuple-element.82), channel_id=1, source_target_pairs={{0,16},{1,17},{2,18},{3,19},{4,20},{5,21},{6,22},{7,23},{8,24},{9,... | collective-permute-start | bytes 196616 | tf_op jit(solution)/shard_map/ppermute | solution.py:68
  92.0 4.1 %collective-permute-start.18 = (bf16[2,4,32,128]{3,2,1,0:T(8,128)(2,1)S(1)}, bf16[2,4,32,128]{3,2,1,0:T(8,128)(2,1)S(1)}, u32[]{:S(2)}, u32[]{:S(2)}) collective-permute-start(bf16[2,4,32,128]{3,2,1,0:T(8,128)(2,1)S(1)} %get-tuple-element.82), channel_id=1, source_target_pairs={{0,8},{1,9},{2,10},{3,11},{4,12},{5,13},{6,14},{7,15},{8,0},{9,1},... | collective-permute-start | bytes 196616 | tf_op jit(solution)/shard_map/ppermute | solution.py:68
  97.4 6.6 %collective-permute-start.23 = (bf16[8,4,32,128]{3,2,1,0:T(8,128)(2,1)S(1)}, bf16[8,4,32,128]{3,2,1,0:T(8,128)(2,1)S(1)}, u32[]{:S(2)}, u32[]{:S(2)}) collective-permute-start(bf16[8,4,32,128]{3,2,1,0:T(8,128)(2,1)S(1)} %constant_dynamic-update-slice_fusion.refs_0_), channel_id=1, source_target_pairs={{0,2},{1,3},{2,4},{3,5},{4,6},{5,7},{6,0},{7,1},{8,10},{9,11},{10,... | collective-permute-start | bytes 786440 | tf_op jit(solution)/shard_map/ppermute | solution.py:68
  97.5 16.0 %collective-permute-start.22 = (bf16[8,4,32,128]{3,2,1,0:T(8,128)(2,1)S(1)}, bf16[8,4,32,128]{3,2,1,0:T(8,128)(2,1)S(1)}, u32[]{:S(2)}, u32[]{:S(2)}) collective-permute-start(bf16[8,4,32,128]{3,2,1,0:T(8,128)(2,1)S(1)} %constant_dynamic-update-slice_fusion.refs_0_), channel_id=1, source_target_pairs={{0,6},{1,7},{2,0},{3,1},{4,2},{5,3},{6,4},{7,5},{8,14},{9,15},{10,... | collective-permute-start | bytes 786440 | tf_op jit(solution)/shard_map/ppermute | solution.py:68
  100.2 13.3 %collective-permute-start.21 = (bf16[8,4,32,128]{3,2,1,0:T(8,128)(2,1)S(1)}, bf16[8,4,32,128]{3,2,1,0:T(8,128)(2,1)S(1)}, u32[]{:S(2)}, u32[]{:S(2)}) collective-permute-start(bf16[8,4,32,128]{3,2,1,0:T(8,128)(2,1)S(1)} %constant_dynamic-update-slice_fusion.refs_0_), channel_id=1, source_target_pairs={{0,4},{1,5},{2,6},{3,7},{4,0},{5,1},{6,2},{7,3},{8,12},{9,13},{10,... | collective-permute-start | bytes 786440 | tf_op jit(solution)/shard_map/ppermute | solution.py:68
  100.2 13.8 %collective-permute-start.24 = (bf16[8,4,32,128]{3,2,1,0:T(8,128)(2,1)S(1)}, bf16[8,4,32,128]{3,2,1,0:T(8,128)(2,1)S(1)}, u32[]{:S(2)}, u32[]{:S(2)}) collective-permute-start(bf16[8,4,32,128]{3,2,1,0:T(8,128)(2,1)S(1)} %constant_dynamic-update-slice_fusion.refs_0_), channel_id=1, source_target_pairs={{0,1},{1,0},{2,3},{3,2},{4,5},{5,4},{6,7},{7,6},{8,9},{9,8},{10,11... | collective-permute-start | bytes 786440 | tf_op jit(solution)/shard_map/ppermute | solution.py:68
  104.0 10.6 %collective-permute-start.27 = (bf16[8,4,32,128]{3,2,1,0:T(8,128)(2,1)S(1)}, bf16[8,4,32,128]{3,2,1,0:T(8,128)(2,1)S(1)}, u32[]{:S(2)}, u32[]{:S(2)}) collective-permute-start(bf16[8,4,32,128]{3,2,1,0:T(8,128)(2,1)S(1)} %collective-permute-done.23.refs_3_), channel_id=1, source_target_pairs={{0,1},{1,0},{2,3},{3,2},{4,5},{5,4},{6,7},{7,6},{8,9},{9,8},{10,11... | collective-permute-start | bytes 786440 | tf_op jit(solution)/shard_map/ppermute | solution.py:68
  113.5 1.5 %collective-permute-start.26 = (bf16[8,4,32,128]{3,2,1,0:T(8,128)(2,1)S(1)}, bf16[8,4,32,128]{3,2,1,0:T(8,128)(2,1)S(1)}, u32[]{:S(2)}, u32[]{:S(2)}) collective-permute-start(bf16[8,4,32,128]{3,2,1,0:T(8,128)(2,1)S(1)} %collective-permute-done.22.refs_2_), channel_id=1, source_target_pairs={{0,1},{1,0},{2,3},{3,2},{4,5},{5,4},{6,7},{7,6},{8,9},{9,8},{10,11... | collective-permute-start | bytes 786440 | tf_op jit(solution)/shard_map/ppermute | solution.py:68
  113.5 1.9 %collective-permute-start.25 = (bf16[8,4,32,128]{3,2,1,0:T(8,128)(2,1)S(1)}, bf16[8,4,32,128]{3,2,1,0:T(8,128)(2,1)S(1)}, u32[]{:S(2)}, u32[]{:S(2)}) collective-permute-start(bf16[8,4,32,128]{3,2,1,0:T(8,128)(2,1)S(1)} %collective-permute-done.21.refs_1_), channel_id=1, source_target_pairs={{0,1},{1,0},{2,3},{3,2},{4,5},{5,4},{6,7},{7,6},{8,9},{9,8},{10,11... | collective-permute-start | bytes 786440 | tf_op jit(solution)/shard_map/ppermute | solution.py:68

commit v6 on v5

--- a/solution.py
+++ b/solution.py
@@ -24,6 +24,7 @@
 OWNED = 108
 LANES = 128
 ZS, YS = 8, 4
+HALF = ZS // 2
 Z_STEPS = (3, 2, 1)
 Z_PARTNER = 7
 Y_ORDER = (0, 2, 3, 1)
@@ -120,10 +121,8 @@
             rows = slice(row, row + 32)
             half = 0.5 * held[rows, columns].astype(F32)
             t = jnp.tanh(half)
-            h = half + half * t
-            if slope:
-                h = (1.0 + t) + h * (1.0 - t)
-            out_ref[rows, columns] = h.astype(BF16)
+            value = (1.0 + t) * (1.0 + half * (1.0 - t)) if slope else half + half * t
+            out_ref[rows, columns] = value.astype(BF16)
         return 0
 
     for i, copy in enumerate(copies):
@@ -192,21 +191,17 @@
     above_ref = None
     if not top:
         above_ref, refs = refs[0], refs[1:]
-    slope_refs, (da_ref, ub_ref, out_ref) = refs[:2], refs[2:]
+    slope_ref, da_ref, ub_ref, out_ref = refs
     low = low_of(share_refs, above_ref).T.astype(BF16)
     total = jnp.zeros((RANK, TOKENS), F32)
 
-    start = 0
-    for slope_ref in slope_refs:
-        for first in range(0, slope_ref.shape[1], 768):
-            columns = slice(start, start + 768)
-            upstream = jnp.dot(low, da_ref[:, columns], preferred_element_type=F32)
-            slope = slope_ref[:, first : first + 768].astype(F32)
-            delta = (upstream * slope).astype(BF16)
-            total = total + lax.dot_general(
-                ub_ref[:, columns], delta, CONTRACT_LAST, preferred_element_type=F32
-            )
-            start += 768
+    for start in range(0, FF, 768):
+        columns = slice(start, start + 768)
+        upstream = jnp.dot(low, da_ref[:, columns], preferred_element_type=F32)
+        delta = (upstream * slope_ref[:, columns].astype(F32)).astype(BF16)
+        total = total + lax.dot_general(
+            ub_ref[:, columns], delta, CONTRACT_LAST, preferred_element_type=F32
+        )
     out_ref[0:RANK, :] = (0.5 * total).astype(BF16)
     if top:
         out_ref[RANK:, :] = jnp.zeros((2 * RANK, LANES), BF16)
@@ -219,11 +214,11 @@
     return pl.pallas_call(
         functools.partial(relay_kernel, first),
         out_shape=shaped((3 * RANK, LANES), BF16),
-        in_specs=[VMEM] * (8 if first else 9),
+        in_specs=[VMEM] * (7 if first else 8),
         out_specs=VMEM,
         compiler_params=params(14),
         name="relay_first" if first else "relay",
-    )(*share, *([] if first else [above]), *slope, da, ub)
+    )(*share, *([] if first else [above]), slope, da, ub)
 
 
 def grad_kernel(s0, s1, s2, s3, above_ref, h0, h1, h2, h3, keep_ref, send_ref, grad):
@@ -263,45 +258,76 @@
     )(*share, above, *hidden)
 
 
-def core_sum_kernel(keep_ref, got_ref, own_ref, *outs):
+def core_sum_kernel(keep_ref, got_ref, own_ref, up_ref, down_ref, up_held, down_held):
     here = y_pos()
-    own_ref[...] = keep_ref[here].astype(F32) + got_ref[here].astype(F32)
-    for k, out in enumerate(outs):
-        there = lax.rem(here + k + 1, YS)
-        out[...] = (keep_ref[there].astype(F32) + got_ref[there].astype(F32)).astype(BF16)
+    first, second = slice(0, HALF), slice(HALF, ZS)
+
+    def block(ahead, half):
+        y = lax.rem(here + ahead, YS)
+        return keep_ref[y, half].astype(F32) + got_ref[y, half].astype(F32)
+
+    own_ref[first] = block(0, first)
+    own_ref[second] = block(0, second)
+    up_ref[0] = block(2, first).astype(BF16)
+    up_ref[1] = block(1, second).astype(BF16)
+    down_ref[0] = block(2, second).astype(BF16)
+    down_ref[1] = block(3, first).astype(BF16)
+    up_held[...] = block(1, first)
+    down_held[...] = block(3, second)
 
 
 def core_sum(keep, got):
-    block = (ZS, BUCKETS, RANK, LANES)
+    half = (HALF, BUCKETS, RANK, LANES)
     return pl.pallas_call(
         core_sum_kernel,
-        out_shape=[shaped(block, F32)] + [shaped(block, BF16)] * 3,
+        out_shape=[shaped((ZS, BUCKETS, RANK, LANES), F32)]
+        + [shaped((2, *half), BF16)] * 2
+        + [shaped(half, F32)] * 2,
         in_specs=[VMEM] * 2,
-        out_specs=[VMEM] * 4,
-        compiler_params=params(),
+        out_specs=[VMEM] * 5,
+        compiler_params=params(8),
         name="core_sum",
     )(keep, got)
 
 
-def y_sum_kernel(own_ref, g1, g2, g3, out_own, *outs):
+def y_pass_kernel(up_held, from_below, down_held, from_above, up_ref, down_ref):
+    up_ref[...] = (up_held[...] + from_below[0].astype(F32)).astype(BF16)
+    down_ref[...] = (down_held[...] + from_above[0].astype(F32)).astype(BF16)
+
+
+def y_pass(up_held, from_below, down_held, from_above):
+    return pl.pallas_call(
+        y_pass_kernel,
+        out_shape=[shaped((HALF, BUCKETS, RANK, LANES), BF16)] * 2,
+        in_specs=[VMEM] * 4,
+        out_specs=[VMEM] * 2,
+        compiler_params=params(4),
+        name="y_pass",
+    )(up_held, from_below, down_held, from_above)
+
+
+def y_sum_kernel(own_ref, from_below, from_above, last_below, last_above, out_own, *outs):
     here = z_pos()
     for step, out in zip((0, *Z_STEPS), (out_own, *outs)):
         for far in range(2):
             z = here ^ (step ^ (far * Z_PARTNER))
-            total = own_ref[z] + g1[z].astype(F32) + g2[z].astype(F32) + g3[z].astype(F32)
+            place = z & (HALF - 1)
+            first = from_above[1, place].astype(F32) + last_below[place].astype(F32)
+            second = from_below[1, place].astype(F32) + last_above[place].astype(F32)
+            total = own_ref[z] + jnp.where(z < HALF, first, second)
             out[far] = total.astype(out.dtype)
 
 
-def y_sum(own, got):
+def y_sum(*terms):
     block = (2, BUCKETS, RANK, LANES)
     return pl.pallas_call(
         y_sum_kernel,
         out_shape=[shaped(block, F32)] + [shaped(block, BF16)] * 3,
-        in_specs=[VMEM] * 4,
+        in_specs=[VMEM] * 5,
         out_specs=[VMEM] * 4,
         compiler_params=params(8),
         name="y_sum",
-    )(own, *got)
+    )(*terms)
 
 
 def z_sum_kernel(own_ref, g1, g2, g3, out_ref):
@@ -412,25 +438,31 @@
     mine = slices(down_b[0], up_a[0].T)
     ws = [mine[0]] + [over_section(mine[k], k) for k in (1, 3, 2)]
     pre = pre_act[0]
-    slope = activation(pre, True, 0, 3)
+    slope = activation(pre, True, 0, BUCKETS)
     ws, slope = lax.optimization_barrier((ws, slope))
     share = shares(out_grad, [ws[0], ws[1], ws[3], ws[2]])
     pre, _ = lax.optimization_barrier((pre, share[0]))
-    slope = [slope, activation(pre, True, 3)]
+    hidden = [activation(pre, False, 0)]
     share = [share[0]] + [over_section(share[k], -k) for k in (1, 3, 2)]
     state = jnp.stack([a[0].transpose(0, 2, 1) for a in (master, moment, second)])
-    above, hidden = None, []
-    for i in range(3):
+    *share, first_hidden = lax.optimization_barrier((*share, hidden[0]))
+    above, hidden = None, [first_hidden]
+    for buckets in ((1, 2), (3,), ()):
         sent = relay(share, above, slope, da, ub)
         above = lax.ppermute(sent, "section", [(1, 0), (2, 1), (3, 2)])
-        pre, state, _ = lax.optimization_barrier((pre, state, sent))
-        if i < 2:
-            hidden += [activation(pre, False, 2 * i + b) for b in range(2)]
-            above, *hidden = lax.optimization_barrier((above, *hidden))
+        if buckets:
+            pre, _ = lax.optimization_barrier((pre, sent))
+            hidden += [activation(pre, False, b) for b in buckets]
+            above, state, *hidden = lax.optimization_barrier((above, state, *hidden))
+    keep, send = grads(share, above, hidden)
+    own, up, down, up_held, down_held = core_sum(keep, over_dp(send, dc=1))
+    state, own = lax.optimization_barrier((state, own))
     partner_state = over_dp(state, zx=Z_PARTNER)
-    keep, send = grads(share, above, hidden)
-    own, *sends = core_sum(keep, over_dp(send, dc=1))
-    own, *sends = y_sum(own, [over_dp(sends[k - 1], dy=k) for k in (1, 3, 2)])
+    from_below, from_above = over_dp(up, dy=1), over_dp(down, dy=-1)
+    up, down = y_pass(up_held, from_below, down_held, from_above)
+    last_below, last_above = over_dp(up, dy=1), over_dp(down, dy=-1)
+    last_below, partner_state = lax.optimization_barrier((last_below, partner_state))
+    own, *sends = y_sum(own, from_below, from_above, last_below, last_above)
     mine = z_sum(own, [over_dp(a, zx=k) for a, k in zip(sends, Z_STEPS)])
     pair, *state = adamw(mine, over_dp(mine, zx=Z_PARTNER), state, partner_state)
     column = jnp.concatenate([pair] + [over_dp(pair, zx=k) for k in Z_STEPS[::-1]])

time: 119 us -> 115 us (0.966)
  starting transfers between devices: 56.8 us -> 54.2 us
  Pallas kernels: 35.2 us -> 33.9 us
    ppermute x19 -> x20, starting transfers between devices: 44.6 us -> 42.2 us  [over_dp(): return lax.ppermute(value, 'dp', pairs)]
    pallas_call x6 -> x5, Pallas kernels: 15.5 us -> 14.1 us  [activation(): pl.pallas_call(functools.partial(activation_kernel, slope, bucket * BUCKE...]
    ppermute x19 -> x20, waiting for transfers between devices: 19.3 us -> 19.6 us  [over_dp(): return lax.ppermute(value, 'dp', pairs)]
  transfers between devices with their start and end apart: 28 -> 29, of which waited for: 15 -> 14; matrix products, arithmetic and copies ran while one was open for 0% -> 0% of each run, Pallas kernels for 13% -> 12%
where the time goes in v6:
time: 115 us
  starting transfers between devices  54.2 us (47%)
  Pallas kernels  33.9 us (29%)
  waiting for transfers between devices  25.7 us (22%)
    ppermute x20, starting transfers between devices, over_dp(): return lax.ppermute(value, 'dp', pairs)  42.2 us
    ppermute x20, waiting for transfers between devices, over_dp(): return lax.ppermute(value, 'dp', pairs)  19.6 us
    pallas_call x5, Pallas kernels, activation(): pl.pallas_call(functools.partial(activation_kernel, slope, bucket * BUCKE...  14.1 us
    pallas_call x3, Pallas kernels, relay(): pl.pallas_call(functools.partial(relay_kernel, first), out_shape=shaped((...  12.5 us
    ppermute x6, starting transfers between devices, over_section(): lax.ppermute(value, 'section', [(i, (i + steps) % 4) for i in range(4)])  7.94 us
    ppermute x3, waiting for transfers between devices, per_device(): above = lax.ppermute(sent, 'section', [(1, 0), (2, 1), (3, 2)])  5.23 us
    ppermute x3, starting transfers between devices, per_device(): above = lax.ppermute(sent, 'section', [(1, 0), (2, 1), (3, 2)])  4.09 us
    pallas_call x1, Pallas kernels, assemble(): pl.pallas_call(assemble_kernel, out_shape=shaped((RANK, FF), BF16), in_sp...  2.48 us
  transfers between devices with their start and end apart: 29, of which 14 were waited for; matrix products, arithmetic and copies ran while one was open for 0% of the time, Pallas kernels for 12%

profile of v6, /device:TPU:1, one launch (start us, length us, event | category | flops | bytes accessed | tf_op | source)
XLA Modules:
  0.0 115.0 jit_solution(7633344939770724614)
XLA Ops:
  0.6 1.3 %slices.1 = (bf16[64,1280]{1,0:T(8,128)(2,1)S(1)}, bf16[64,1280]{1,0:T(8,128)(2,1)S(1)}, bf16[64,1280]{1,0:T(8,128)(2,1)S(1)}, bf16[64,1280]{1,0:T(8,128)(2,1)S(1)}) custom-call(bf16[32,5120]{1,0:T(8,128)(2,1)} %bitcast.50, bf16[32,5120]{1,0:T(8,128)(2,1)} %bitcast.51), custom_call_target="tpu_custom_call" | custom-call | tf_op jit(solution)/shard_map/slices/pallas_call | solution.py:94
  1.9 2.1 %collective-permute-start = (bf16[64,1280]{1,0:T(8,128)(2,1)S(1)}, bf16[64,1280]{1,0:T(8,128)(2,1)S(1)}, u32[]{:S(2)}, u32[]{:S(2)}) collective-permute-start(bf16[64,1280]{1,0:T(8,128)(2,1)S(1)} %get-tuple-element.58), channel_id=1, source_target_pairs={{0,64},{64,128},{128,192},{192,0},{1,65},{65,129},{129,193},{193,1... | collective-permute-start | bytes 491528 | tf_op jit(solution)/shard_map/ppermute | solution.py:73
  4.0 1.4 %collective-permute-start.1 = (bf16[64,1280]{1,0:T(8,128)(2,1)S(1)}, bf16[64,1280]{1,0:T(8,128)(2,1)S(1)}, u32[]{:S(2)}, u32[]{:S(2)}) collective-permute-start(bf16[64,1280]{1,0:T(8,128)(2,1)S(1)} %get-tuple-element.59), channel_id=1, source_target_pairs={{0,192},{64,0},{128,64},{192,128},{1,193},{65,1},{129,65},{193,129... | collective-permute-start | bytes 491528 | tf_op jit(solution)/shard_map/ppermute | solution.py:73
  5.4 1.6 %collective-permute-start.2 = (bf16[64,1280]{1,0:T(8,128)(2,1)S(1)}, bf16[64,1280]{1,0:T(8,128)(2,1)S(1)}, u32[]{:S(2)}, u32[]{:S(2)}) collective-permute-start(bf16[64,1280]{1,0:T(8,128)(2,1)S(1)} %get-tuple-element.60), channel_id=1, source_target_pairs={{0,128},{64,192},{128,0},{192,64},{1,129},{65,193},{129,1},{193,65... | collective-permute-start | bytes 491528 | tf_op jit(solution)/shard_map/ppermute | solution.py:73
  7.0 6.3 %slope.1.refs_4_.refs_5_ = bf16[128,27648]{1,0:T(8,128)(2,1)S(1)} custom-call(bf16[128,27648]{1,0:T(8,128)(2,1)} %bitcast.44), custom_call_target="tpu_custom_call" | custom-call | flops 35389440 | bytes 14155776 | tf_op jit(solution)/shard_map/slope/pallas_call | solution.py:135
  13.3 0.0 collective-permute-done.w1
  13.3 0.0 collective-permute-done.1.w3
  13.3 0.0 collective-permute-done.2.w2
  13.3 0.9 shares.1
  14.3 1.2 %collective-permute-start.3 = (f32[32,256]{1,0:T(8,128)S(1)}, f32[32,256]{1,0:T(8,128)S(1)}, u32[]{:S(2)}, u32[]{:S(2)}) collective-permute-start(f32[32,256]{1,0:T(8,128)S(1)} %get-tuple-element.66), channel_id=1, source_target_pairs={{0,192},{64,0},{128,64},{192,128},{1,193},{65,1},{129,65},{193,129... | collective-permute-start | bytes 98312 | tf_op jit(solution)/shard_map/ppermute | solution.py:73
  15.4 0.3 collective-permute-start.4
  15.8 1.3 %collective-permute-start.5 = (f32[32,256]{1,0:T(8,128)S(1)}, f32[32,256]{1,0:T(8,128)S(1)}, u32[]{:S(2)}, u32[]{:S(2)}) collective-permute-start(f32[32,256]{1,0:T(8,128)S(1)} %get-tuple-element.68), channel_id=1, source_target_pairs={{0,128},{64,192},{128,0},{192,64},{1,129},{65,193},{129,1},{193,65... | collective-permute-start | bytes 98312 | tf_op jit(solution)/shard_map/ppermute | solution.py:73
  17.1 2.1 %hidden.4.h0 = bf16[128,6912]{1,0:T(8,128)(2,1)S(1)} custom-call(bf16[128,27648]{1,0:T(8,128)(2,1)} %bitcast.45), custom_call_target="tpu_custom_call" | custom-call | flops 8847360 | bytes 3538944 | tf_op jit(solution)/shard_map/hidden/pallas_call | solution.py:135
  19.2 0.2 collective-permute-done.4.refs_2_.s2
  19.4 0.6 collective-permute-done.5.refs_3_.s3
  20.1 0.0 copy-start.5
  20.1 4.1 %relay_first.1 = bf16[96,128]{1,0:T(8,128)(2,1)S(1)} custom-call(f32[32,256]{1,0:T(8,128)S(1)} %get-tuple-element.70.refs_0_.s0, f32[32,256]{1,0:T(8,128)S(1)} %collective-permute-done.3.refs_1_.s1, f32[32,256]{1,0:T(8,128)S(1)} %collective-permute-done.4.refs_2_.s2, f32[32,256]{1,0:T(8,128)S(1)} %collective-permute-done.5.refs_3_.s3, ...), custom_call_target="tpu_custom_call" | custom-call | tf_op jit(solution)/shard_map/relay_first/pallas_call | solution.py:214
  24.1 1.5 %collective-permute-start.6 = (bf16[96,128]{1,0:T(8,128)(2,1)S(1)}, bf16[96,128]{1,0:T(8,128)(2,1)S(1)}, u32[]{:S(2)}, u32[]{:S(2)}) collective-permute-start(bf16[96,128]{1,0:T(8,128)(2,1)S(1)} %relay_first.1), channel_id=1, source_target_pairs={{64,0},{128,64},{192,128},{65,1},{129,65},{193,129},{66,2},{130,66... | collective-permute-start | bytes 73736 | tf_op jit(solution)/shard_map/ppermute | solution.py:452
  25.7 1.9 %hidden.6.h2 = bf16[128,6912]{1,0:T(8,128)(2,1)S(1)} custom-call(bf16[128,27648]{1,0:T(8,128)(2,1)} %bitcast.46), custom_call_target="tpu_custom_call" | custom-call | flops 8847360 | bytes 3538944 | tf_op jit(solution)/shard_map/hidden/pallas_call | solution.py:135
  27.6 1.9 %hidden.5.h1 = bf16[128,6912]{1,0:T(8,128)(2,1)S(1)} custom-call(bf16[128,27648]{1,0:T(8,128)(2,1)} %bitcast.47), custom_call_target="tpu_custom_call" | custom-call | flops 8847360 | bytes 3538944 | tf_op jit(solution)/shard_map/hidden/pallas_call | solution.py:135
  29.6 4.2 %relay.2 = bf16[96,128]{1,0:T(8,128)(2,1)S(1)} custom-call(f32[32,256]{1,0:T(8,128)S(1)} %get-tuple-element.70.refs_0_.s0, f32[32,256]{1,0:T(8,128)S(1)} %collective-permute-done.3.refs_1_.s1, f32[32,256]{1,0:T(8,128)S(1)} %collective-permute-done.4.refs_2_.s2, f32[32,256]{1,0:T(8,128)S(1)} %collective-permute-done.5.refs_3_.s3, ...), custom_call_target="tpu_custom_call" | custom-call | tf_op jit(solution)/shard_map/relay/pallas_call | solution.py:214
  33.8 1.3 %collective-permute-start.7 = (bf16[96,128]{1,0:T(8,128)(2,1)S(1)}, bf16[96,128]{1,0:T(8,128)(2,1)S(1)}, u32[]{:S(2)}, u32[]{:S(2)}) collective-permute-start(bf16[96,128]{1,0:T(8,128)(2,1)S(1)} %relay.2), channel_id=1, source_target_pairs={{64,0},{128,64},{192,128},{65,1},{129,65},{193,129},{66,2},{130,66... | collective-permute-start | bytes 73736 | tf_op jit(solution)/shard_map/ppermute | solution.py:452
  35.1 1.9 %hidden.7.h3 = bf16[128,6912]{1,0:T(8,128)(2,1)S(1)} custom-call(bf16[128,27648]{1,0:T(8,128)(2,1)} %bitcast.48), custom_call_target="tpu_custom_call" | custom-call | flops 8847360 | bytes 3538944 | tf_op jit(solution)/shard_map/hidden/pallas_call | solution.py:135
  37.1 2.0 %collective-permute-done.7.refs_4_ = bf16[96,128]{1,0:T(8,128)(2,1)S(1)} collective-permute-done((bf16[96,128]{1,0:T(8,128)(2,1)S(1)}, bf16[96,128]{1,0:T(8,128)(2,1)S(1)}, u32[]{:S(2)}, u32[]{:S(2)}) %collective-permute-start.7) | collective-permute-done | bytes 24608 | tf_op jit(solution)/shard_map/ppermute | solution.py:452
  39.0 4.2 %relay.3 = bf16[96,128]{1,0:T(8,128)(2,1)S(1)} custom-call(f32[32,256]{1,0:T(8,128)S(1)} %get-tuple-element.70.refs_0_.s0, f32[32,256]{1,0:T(8,128)S(1)} %collective-permute-done.3.refs_1_.s1, f32[32,256]{1,0:T(8,128)S(1)} %collective-permute-done.4.refs_2_.s2, f32[32,256]{1,0:T(8,128)S(1)} %collective-permute-done.5.refs_3_.s3, ...), custom_call_target="tpu_custom_call" | custom-call | tf_op jit(solution)/shard_map/relay/pallas_call | solution.py:214
  43.2 1.3 %collective-permute-start.8 = (bf16[96,128]{1,0:T(8,128)(2,1)S(1)}, bf16[96,128]{1,0:T(8,128)(2,1)S(1)}, u32[]{:S(2)}, u32[]{:S(2)}) collective-permute-start(bf16[96,128]{1,0:T(8,128)(2,1)S(1)} %relay.3), channel_id=1, source_target_pairs={{64,0},{128,64},{192,128},{65,1},{129,65},{193,129},{66,2},{130,66... | collective-permute-start | bytes 73736 | tf_op jit(solution)/shard_map/ppermute | solution.py:452
  44.5 3.3 %collective-permute-done.8.above_ref = bf16[96,128]{1,0:T(8,128)(2,1)S(1)} collective-permute-done((bf16[96,128]{1,0:T(8,128)(2,1)S(1)}, bf16[96,128]{1,0:T(8,128)(2,1)S(1)}, u32[]{:S(2)}, u32[]{:S(2)}) %collective-permute-start.8) | collective-permute-done | bytes 24608 | tf_op jit(solution)/shard_map/ppermute | solution.py:452
  47.8 1.4 %grads.1 = (bf16[4,8,4,32,128]{4,3,2,1,0:T(8,128)(2,1)S(1)}, bf16[4,8,4,32,128]{4,3,2,1,0:T(8,128)(2,1)S(1)}) custom-call(f32[32,256]{1,0:T(8,128)S(1)} %get-tuple-element.70.refs_0_.s0, f32[32,256]{1,0:T(8,128)S(1)} %collective-permute-done.3.refs_1_.s1, f32[32,256]{1,0:T(8,128)S(1)} %collective-permute-done.4.refs_2_.s2, ...), custom_call_target="tpu_custom_call" | custom-call | tf_op jit(solution)/shard_map/grads/pallas_call | solution.py:250
  49.2 6.5 %collective-permute-start.9 = (bf16[4,8,4,32,128]{4,3,2,1,0:T(8,128)(2,1)S(1)}, bf16[4,8,4,32,128]{4,3,2,1,0:T(8,128)(2,1)S(1)}, u32[]{:S(2)}, u32[]{:S(2)}) collective-permute-start(bf16[4,8,4,32,128]{4,3,2,1,0:T(8,128)(2,1)S(1)} %get-tuple-element.90), channel_id=1, source_target_pairs={{0,1},{1,0},{2,3},{3,2},{4,5},{5,4},{6,7},{7,6},{8,9},{9,8},{10,11... | collective-permute-start | bytes 3145736 | tf_op jit(solution)/shard_map/ppermute | solution.py:69
  55.7 2.3 %collective-permute-done.9.got_ref = bf16[4,8,4,32,128]{4,3,2,1,0:T(8,128)(2,1)S(1)} collective-permute-done((bf16[4,8,4,32,128]{4,3,2,1,0:T(8,128)(2,1)S(1)}, bf16[4,8,4,32,128]{4,3,2,1,0:T(8,128)(2,1)S(1)}, u32[]{:S(2)}, u32[]{:S(2)}) %collective-permute-start.9) | collective-permute-done | bytes 1048608 | tf_op jit(solution)/shard_map/ppermute | solution.py:69
  58.0 0.2 core_sum.1
  58.2 0.8 collective-permute-start.10
  59.0 2.0 %collective-permute-start.11 = (bf16[2,4,4,32,128]{4,3,2,1,0:T(8,128)(2,1)S(1)}, bf16[2,4,4,32,128]{4,3,2,1,0:T(8,128)(2,1)S(1)}, u32[]{:S(2)}, u32[]{:S(2)}) collective-permute-start(bf16[2,4,4,32,128]{4,3,2,1,0:T(8,128)(2,1)S(1)} %get-tuple-element.94), channel_id=1, source_target_pairs={{0,6},{1,7},{2,0},{3,1},{4,2},{5,3},{6,4},{7,5},{8,14},{9,15},{10,... | collective-permute-start | bytes 786440 | tf_op jit(solution)/shard_map/ppermute | solution.py:69
  61.0 5.1 %collective-permute-start.13 = (f32[3,4,32,108]{3,2,1,0:T(8,128)S(1)}, f32[3,4,32,108]{3,2,1,0:T(8,128)S(1)}, u32[]{:S(2)}, u32[]{:S(2)}) collective-permute-start(f32[3,4,32,108]{3,2,1,0:T(8,128)S(1)} %pad_maximum_fusion.state_ref), channel_id=1, source_target_pairs={{0,56},{1,57},{2,58},{3,59},{4,60},{5,61},{6,62},{7,63},{8,48},{9,... | collective-permute-start | bytes 497672 | tf_op jit(solution)/shard_map/ppermute | solution.py:69
  66.1 0.9 collective-permute-done.10.from_below
  67.1 0.5 collective-permute-start.12
  67.6 2.2 %collective-permute-start.14 = (bf16[4,4,32,128]{3,2,1,0:T(8,128)(2,1)S(1)}, bf16[4,4,32,128]{3,2,1,0:T(8,128)(2,1)S(1)}, u32[]{:S(2)}, u32[]{:S(2)}) collective-permute-start(bf16[4,4,32,128]{3,2,1,0:T(8,128)(2,1)S(1)} %get-tuple-element.100), channel_id=1, source_target_pairs={{0,6},{1,7},{2,0},{3,1},{4,2},{5,3},{6,4},{7,5},{8,14},{9,15},{10,... | collective-permute-start | bytes 393224 | tf_op jit(solution)/shard_map/ppermute | solution.py:69
  69.8 5.4 %collective-permute-done.13.partner_ref = f32[3,4,32,108]{3,2,1,0:T(8,128)S(1)} collective-permute-done((f32[3,4,32,108]{3,2,1,0:T(8,128)S(1)}, f32[3,4,32,108]{3,2,1,0:T(8,128)S(1)}, u32[]{:S(2)}, u32[]{:S(2)}) %collective-permute-start.13) | collective-permute-done | bytes 165920 | tf_op jit(solution)/shard_map/ppermute | solution.py:69
  75.2 0.1 y_sum.1
  75.4 1.7 %collective-permute-start.15 = (bf16[2,4,32,128]{3,2,1,0:T(8,128)(2,1)S(1)}, bf16[2,4,32,128]{3,2,1,0:T(8,128)(2,1)S(1)}, u32[]{:S(2)}, u32[]{:S(2)}) collective-permute-start(bf16[2,4,32,128]{3,2,1,0:T(8,128)(2,1)S(1)} %get-tuple-element.102), channel_id=1, source_target_pairs={{0,24},{1,25},{2,26},{3,27},{4,28},{5,29},{6,30},{7,31},{8,16},{9,... | collective-permute-start | bytes 196616 | tf_op jit(solution)/shard_map/ppermute | solution.py:69
  77.1 0.0 collective-permute-start.16
  77.1 2.0 %collective-permute-start.17 = (bf16[2,4,32,128]{3,2,1,0:T(8,128)(2,1)S(1)}, bf16[2,4,32,128]{3,2,1,0:T(8,128)(2,1)S(1)}, u32[]{:S(2)}, u32[]{:S(2)}) collective-permute-start(bf16[2,4,32,128]{3,2,1,0:T(8,128)(2,1)S(1)} %get-tuple-element.104), channel_id=1, source_target_pairs={{0,8},{1,9},{2,10},{3,11},{4,12},{5,13},{6,14},{7,15},{8,0},{9,1},... | collective-permute-start | bytes 196616 | tf_op jit(solution)/shard_map/ppermute | solution.py:69
  79.0 1.4 %collective-permute-done.15.g1 = bf16[2,4,32,128]{3,2,1,0:T(8,128)(2,1)S(1)} collective-permute-done((bf16[2,4,32,128]{3,2,1,0:T(8,128)(2,1)S(1)}, bf16[2,4,32,128]{3,2,1,0:T(8,128)(2,1)S(1)}, u32[]{:S(2)}, u32[]{:S(2)}) %collective-permute-start.15) | collective-permute-done | bytes 65568 | tf_op jit(solution)/shard_map/ppermute | solution.py:69
  80.4 2.5 %collective-permute-done.16.g2 = bf16[2,4,32,128]{3,2,1,0:T(8,128)(2,1)S(1)} collective-permute-done((bf16[2,4,32,128]{3,2,1,0:T(8,128)(2,1)S(1)}, bf16[2,4,32,128]{3,2,1,0:T(8,128)(2,1)S(1)}, u32[]{:S(2)}, u32[]{:S(2)}) %collective-permute-start.16) | collective-permute-done | bytes 65568 | tf_op jit(solution)/shard_map/ppermute | solution.py:69
  82.9 2.0 %collective-permute-start.18 = (bf16[2,4,32,128]{3,2,1,0:T(8,128)(2,1)S(1)}, bf16[2,4,32,128]{3,2,1,0:T(8,128)(2,1)S(1)}, u32[]{:S(2)}, u32[]{:S(2)}) collective-permute-start(bf16[2,4,32,128]{3,2,1,0:T(8,128)(2,1)S(1)} %z_sum.1.mine_ref), channel_id=1, source_target_pairs={{0,56},{1,57},{2,58},{3,59},{4,60},{5,61},{6,62},{7,63},{8,48},{9,... | collective-permute-start | bytes 196616 | tf_op jit(solution)/shard_map/ppermute | solution.py:69
  84.9 3.1 %collective-permute-done.18.got_ref = bf16[2,4,32,128]{3,2,1,0:T(8,128)(2,1)S(1)} collective-permute-done((bf16[2,4,32,128]{3,2,1,0:T(8,128)(2,1)S(1)}, bf16[2,4,32,128]{3,2,1,0:T(8,128)(2,1)S(1)}, u32[]{:S(2)}, u32[]{:S(2)}) %collective-permute-start.18) | collective-permute-done | bytes 65568 | tf_op jit(solution)/shard_map/ppermute | solution.py:69
  88.0 0.7 adamw.1
  88.8 2.4 %collective-permute-start.21 = (bf16[2,4,32,128]{3,2,1,0:T(8,128)(2,1)S(1)}, bf16[2,4,32,128]{3,2,1,0:T(8,128)(2,1)S(1)}, u32[]{:S(2)}, u32[]{:S(2)}) collective-permute-start(bf16[2,4,32,128]{3,2,1,0:T(8,128)(2,1)S(1)} %get-tuple-element.106), channel_id=1, source_target_pairs={{0,24},{1,25},{2,26},{3,27},{4,28},{5,29},{6,30},{7,31},{8,16},{9,... | collective-permute-start | bytes 196616 | tf_op jit(solution)/shard_map/ppermute | solution.py:69
  91.1 1.2 %collective-permute-start.19 = (bf16[2,4,32,128]{3,2,1,0:T(8,128)(2,1)S(1)}, bf16[2,4,32,128]{3,2,1,0:T(8,128)(2,1)S(1)}, u32[]{:S(2)}, u32[]{:S(2)}) collective-permute-start(bf16[2,4,32,128]{3,2,1,0:T(8,128)(2,1)S(1)} %get-tuple-element.106), channel_id=1, source_target_pairs={{0,8},{1,9},{2,10},{3,11},{4,12},{5,13},{6,14},{7,15},{8,0},{9,1},... | collective-permute-start | bytes 196616 | tf_op jit(solution)/shard_map/ppermute | solution.py:69
  92.3 2.1 %collective-permute-done.19 = bf16[2,4,32,128]{3,2,1,0:T(8,128)(2,1)S(1)} collective-permute-done((bf16[2,4,32,128]{3,2,1,0:T(8,128)(2,1)S(1)}, bf16[2,4,32,128]{3,2,1,0:T(8,128)(2,1)S(1)}, u32[]{:S(2)}, u32[]{:S(2)}) %collective-permute-start.19) | collective-permute-done | bytes 65568 | tf_op jit(solution)/shard_map/ppermute | solution.py:69
  94.4 0.8 collective-permute-done.20
  95.2 0.0 collective-permute-done.21
  95.2 0.3 collective-permute-start.24
  95.5 2.5 %collective-permute-start.23 = (bf16[8,4,32,128]{3,2,1,0:T(8,128)(2,1)S(1)}, bf16[8,4,32,128]{3,2,1,0:T(8,128)(2,1)S(1)}, u32[]{:S(2)}, u32[]{:S(2)}) collective-permute-start(bf16[8,4,32,128]{3,2,1,0:T(8,128)(2,1)S(1)} %constant_dynamic-update-slice_fusion.refs_0_), channel_id=1, source_target_pairs={{0,6},{1,7},{2,0},{3,1},{4,2},{5,3},{6,4},{7,5},{8,14},{9,15},{10,... | collective-permute-start | bytes 786440 | tf_op jit(solution)/shard_map/ppermute | solution.py:69
  98.0 0.6 collective-permute-start.22
  98.6 6.0 %collective-permute-start.25 = (bf16[8,4,32,128]{3,2,1,0:T(8,128)(2,1)S(1)}, bf16[8,4,32,128]{3,2,1,0:T(8,128)(2,1)S(1)}, u32[]{:S(2)}, u32[]{:S(2)}) collective-permute-start(bf16[8,4,32,128]{3,2,1,0:T(8,128)(2,1)S(1)} %constant_dynamic-update-slice_fusion.refs_0_), channel_id=1, source_target_pairs={{0,1},{1,0},{2,3},{3,2},{4,5},{5,4},{6,7},{7,6},{8,9},{9,8},{10,11... | collective-permute-start | bytes 786440 | tf_op jit(solution)/shard_map/ppermute | solution.py:69
  104.6 0.0 collective-permute-done.24.refs_3_
  104.6 3.7 %collective-permute-start.28 = (bf16[8,4,32,128]{3,2,1,0:T(8,128)(2,1)S(1)}, bf16[8,4,32,128]{3,2,1,0:T(8,128)(2,1)S(1)}, u32[]{:S(2)}, u32[]{:S(2)}) collective-permute-start(bf16[8,4,32,128]{3,2,1,0:T(8,128)(2,1)S(1)} %collective-permute-done.24.refs_3_), channel_id=1, source_target_pairs={{0,1},{1,0},{2,3},{3,2},{4,5},{5,4},{6,7},{7,6},{8,9},{9,8},{10,11... | collective-permute-start | bytes 786440 | tf_op jit(solution)/shard_map/ppermute | solution.py:69
  108.3 1.8 %collective-permute-start.27 = (bf16[8,4,32,128]{3,2,1,0:T(8,128)(2,1)S(1)}, bf16[8,4,32,128]{3,2,1,0:T(8,128)(2,1)S(1)}, u32[]{:S(2)}, u32[]{:S(2)}) collective-permute-start(bf16[8,4,32,128]{3,2,1,0:T(8,128)(2,1)S(1)} %collective-permute-done.23.refs_2_), channel_id=1, source_target_pairs={{0,1},{1,0},{2,3},{3,2},{4,5},{5,4},{6,7},{7,6},{8,9},{9,8},{10,11... | collective-permute-start | bytes 786440 | tf_op jit(solution)/shard_map/ppermute | solution.py:69
  110.1 1.0 collective-permute-start.26
  111.1 0.0 collective-permute-done.25.refs_4_
  111.2 0.1 collective-permute-done.27.refs_6_
  111.3 1.0 collective-permute-done.26.refs_5_
  112.3 2.5 %assemble.1 = bf16[32,27648]{1,0:T(8,128)(2,1)} custom-call(bf16[8,4,32,128]{3,2,1,0:T(8,128)(2,1)S(1)} %constant_dynamic-update-slice_fusion.refs_0_, bf16[8,4,32,128]{3,2,1,0:T(8,128)(2,1)S(1)} %collective-permute-done.22.refs_1_, bf16[8,4,32,128]{3,2,1,0:T(8,128)(2,1)S(1)} %collective-permute-done.23.refs_2_, ...), custom_call_target="tpu_custom_call" | custom-call | tf_op jit(solution)/shard_map/assemble/pallas_call | solution.py:422
  (28 shorter events, 0.2 us)
Async XLA Ops:
  1.9 11.4 %collective-permute-start = (bf16[64,1280]{1,0:T(8,128)(2,1)S(1)}, bf16[64,1280]{1,0:T(8,128)(2,1)S(1)}, u32[]{:S(2)}, u32[]{:S(2)}) collective-permute-start(bf16[64,1280]{1,0:T(8,128)(2,1)S(1)} %get-tuple-element.58), channel_id=1, source_target_pairs={{0,64},{64,128},{128,192},{192,0},{1,65},{65,129},{129,193},{193,1... | collective-permute-start | bytes 491528 | tf_op jit(solution)/shard_map/ppermute | solution.py:73
  4.0 9.3 %collective-permute-start.1 = (bf16[64,1280]{1,0:T(8,128)(2,1)S(1)}, bf16[64,1280]{1,0:T(8,128)(2,1)S(1)}, u32[]{:S(2)}, u32[]{:S(2)}) collective-permute-start(bf16[64,1280]{1,0:T(8,128)(2,1)S(1)} %get-tuple-element.59), channel_id=1, source_target_pairs={{0,192},{64,0},{128,64},{192,128},{1,193},{65,1},{129,65},{193,129... | collective-permute-start | bytes 491528 | tf_op jit(solution)/shard_map/ppermute | solution.py:73
  5.4 8.0 %collective-permute-start.2 = (bf16[64,1280]{1,0:T(8,128)(2,1)S(1)}, bf16[64,1280]{1,0:T(8,128)(2,1)S(1)}, u32[]{:S(2)}, u32[]{:S(2)}) collective-permute-start(bf16[64,1280]{1,0:T(8,128)(2,1)S(1)} %get-tuple-element.60), channel_id=1, source_target_pairs={{0,128},{64,192},{128,0},{192,64},{1,129},{65,193},{129,1},{193,65... | collective-permute-start | bytes 491528 | tf_op jit(solution)/shard_map/ppermute | solution.py:73
  7.0 6.3 %copy-start.2 = (bf16[128,1280]{1,0:T(8,128)(2,1)S(1)}, bf16[128,1280]{1,0:T(8,128)(2,1)}, u32[]{:S(2)}) copy-start(bf16[128,1280]{1,0:T(8,128)(2,1)} %g_ref.1) | copy-start | bytes 983044
  14.3 4.9 %collective-permute-start.3 = (f32[32,256]{1,0:T(8,128)S(1)}, f32[32,256]{1,0:T(8,128)S(1)}, u32[]{:S(2)}, u32[]{:S(2)}) collective-permute-start(f32[32,256]{1,0:T(8,128)S(1)} %get-tuple-element.66), channel_id=1, source_target_pairs={{0,192},{64,0},{128,64},{192,128},{1,193},{65,1},{129,65},{193,129... | collective-permute-start | bytes 98312 | tf_op jit(solution)/shard_map/ppermute | solution.py:73
  15.4 4.0 %collective-permute-start.4 = (f32[32,256]{1,0:T(8,128)S(1)}, f32[32,256]{1,0:T(8,128)S(1)}, u32[]{:S(2)}, u32[]{:S(2)}) collective-permute-start(f32[32,256]{1,0:T(8,128)S(1)} %get-tuple-element.67), channel_id=1, source_target_pairs={{0,64},{64,128},{128,192},{192,0},{1,65},{65,129},{129,193},{193,1... | collective-permute-start | bytes 98312 | tf_op jit(solution)/shard_map/ppermute | solution.py:73
  15.8 4.3 %collective-permute-start.5 = (f32[32,256]{1,0:T(8,128)S(1)}, f32[32,256]{1,0:T(8,128)S(1)}, u32[]{:S(2)}, u32[]{:S(2)}) collective-permute-start(f32[32,256]{1,0:T(8,128)S(1)} %get-tuple-element.68), channel_id=1, source_target_pairs={{0,128},{64,192},{128,0},{192,64},{1,129},{65,193},{129,1},{193,65... | collective-permute-start | bytes 98312 | tf_op jit(solution)/shard_map/ppermute | solution.py:73
  17.1 2.9 %copy-start = (bf16[1,27648,32]{1,2,0:T(8,128)(2,1)S(1)}, bf16[1,27648,32]{1,2,0:T(8,128)(2,1)}, u32[]{:S(2)}) copy-start(bf16[1,27648,32]{1,2,0:T(8,128)(2,1)} %param.11) | copy-start | bytes 5308420
  17.1 2.9 %copy-start.1 = (bf16[1,27648,32]{1,2,0:T(8,128)(2,1)S(1)}, bf16[1,27648,32]{1,2,0:T(8,128)(2,1)}, u32[]{:S(2)}) copy-start(bf16[1,27648,32]{1,2,0:T(8,128)(2,1)} %param.14) | copy-start | bytes 5308420
  20.1 5.6 %copy-start.3 = (f32[1,4,108,32]{2,3,1,0:T(8,128)S(1)}, f32[1,4,108,32]{2,3,1,0:T(8,128)}, u32[]{:S(2)}) copy-start(f32[1,4,108,32]{2,3,1,0:T(8,128)} %param.17) | copy-start | bytes 165892
  20.1 5.6 %copy-start.4 = (f32[1,4,108,32]{2,3,1,0:T(8,128)S(1)}, f32[1,4,108,32]{2,3,1,0:T(8,128)}, u32[]{:S(2)}) copy-start(f32[1,4,108,32]{2,3,1,0:T(8,128)} %param.16) | copy-start | bytes 165892
  20.1 5.6 %copy-start.5 = (f32[1,4,108,32]{2,3,1,0:T(8,128)S(1)}, f32[1,4,108,32]{2,3,1,0:T(8,128)}, u32[]{:S(2)}) copy-start(f32[1,4,108,32]{2,3,1,0:T(8,128)} %param.15) | copy-start | bytes 165892
  24.1 5.4 %collective-permute-start.6 = (bf16[96,128]{1,0:T(8,128)(2,1)S(1)}, bf16[96,128]{1,0:T(8,128)(2,1)S(1)}, u32[]{:S(2)}, u32[]{:S(2)}) collective-permute-start(bf16[96,128]{1,0:T(8,128)(2,1)S(1)} %relay_first.1), channel_id=1, source_target_pairs={{64,0},{128,64},{192,128},{65,1},{129,65},{193,129},{66,2},{130,66... | collective-permute-start | bytes 73736 | tf_op jit(solution)/shard_map/ppermute | solution.py:452
  33.8 5.2 %collective-permute-start.7 = (bf16[96,128]{1,0:T(8,128)(2,1)S(1)}, bf16[96,128]{1,0:T(8,128)(2,1)S(1)}, u32[]{:S(2)}, u32[]{:S(2)}) collective-permute-start(bf16[96,128]{1,0:T(8,128)(2,1)S(1)} %relay.2), channel_id=1, source_target_pairs={{64,0},{128,64},{192,128},{65,1},{129,65},{193,129},{66,2},{130,66... | collective-permute-start | bytes 73736 | tf_op jit(solution)/shard_map/ppermute | solution.py:452
  43.2 4.6 %collective-permute-start.8 = (bf16[96,128]{1,0:T(8,128)(2,1)S(1)}, bf16[96,128]{1,0:T(8,128)(2,1)S(1)}, u32[]{:S(2)}, u32[]{:S(2)}) collective-permute-start(bf16[96,128]{1,0:T(8,128)(2,1)S(1)} %relay.3), channel_id=1, source_target_pairs={{64,0},{128,64},{192,128},{65,1},{129,65},{193,129},{66,2},{130,66... | collective-permute-start | bytes 73736 | tf_op jit(solution)/shard_map/ppermute | solution.py:452
  49.2 8.8 %collective-permute-start.9 = (bf16[4,8,4,32,128]{4,3,2,1,0:T(8,128)(2,1)S(1)}, bf16[4,8,4,32,128]{4,3,2,1,0:T(8,128)(2,1)S(1)}, u32[]{:S(2)}, u32[]{:S(2)}) collective-permute-start(bf16[4,8,4,32,128]{4,3,2,1,0:T(8,128)(2,1)S(1)} %get-tuple-element.90), channel_id=1, source_target_pairs={{0,1},{1,0},{2,3},{3,2},{4,5},{5,4},{6,7},{7,6},{8,9},{9,8},{10,11... | collective-permute-start | bytes 3145736 | tf_op jit(solution)/shard_map/ppermute | solution.py:69
  58.2 8.8 %collective-permute-start.10 = (bf16[2,4,4,32,128]{4,3,2,1,0:T(8,128)(2,1)S(1)}, bf16[2,4,4,32,128]{4,3,2,1,0:T(8,128)(2,1)S(1)}, u32[]{:S(2)}, u32[]{:S(2)}) collective-permute-start(bf16[2,4,4,32,128]{4,3,2,1,0:T(8,128)(2,1)S(1)} %get-tuple-element.93), channel_id=1, source_target_pairs={{0,2},{1,3},{2,4},{3,5},{4,6},{5,7},{6,0},{7,1},{8,10},{9,11},{10,... | collective-permute-start | bytes 786440 | tf_op jit(solution)/shard_map/ppermute | solution.py:69
  59.0 8.0 %collective-permute-start.11 = (bf16[2,4,4,32,128]{4,3,2,1,0:T(8,128)(2,1)S(1)}, bf16[2,4,4,32,128]{4,3,2,1,0:T(8,128)(2,1)S(1)}, u32[]{:S(2)}, u32[]{:S(2)}) collective-permute-start(bf16[2,4,4,32,128]{4,3,2,1,0:T(8,128)(2,1)S(1)} %get-tuple-element.94), channel_id=1, source_target_pairs={{0,6},{1,7},{2,0},{3,1},{4,2},{5,3},{6,4},{7,5},{8,14},{9,15},{10,... | collective-permute-start | bytes 786440 | tf_op jit(solution)/shard_map/ppermute | solution.py:69
  61.0 14.3 %collective-permute-start.13 = (f32[3,4,32,108]{3,2,1,0:T(8,128)S(1)}, f32[3,4,32,108]{3,2,1,0:T(8,128)S(1)}, u32[]{:S(2)}, u32[]{:S(2)}) collective-permute-start(f32[3,4,32,108]{3,2,1,0:T(8,128)S(1)} %pad_maximum_fusion.state_ref), channel_id=1, source_target_pairs={{0,56},{1,57},{2,58},{3,59},{4,60},{5,61},{6,62},{7,63},{8,48},{9,... | collective-permute-start | bytes 497672 | tf_op jit(solution)/shard_map/ppermute | solution.py:69
  67.1 8.2 %collective-permute-start.12 = (bf16[4,4,32,128]{3,2,1,0:T(8,128)(2,1)S(1)}, bf16[4,4,32,128]{3,2,1,0:T(8,128)(2,1)S(1)}, u32[]{:S(2)}, u32[]{:S(2)}) collective-permute-start(bf16[4,4,32,128]{3,2,1,0:T(8,128)(2,1)S(1)} %get-tuple-element.97), channel_id=1, source_target_pairs={{0,2},{1,3},{2,4},{3,5},{4,6},{5,7},{6,0},{7,1},{8,10},{9,11},{10,... | collective-permute-start | bytes 393224 | tf_op jit(solution)/shard_map/ppermute | solution.py:69
  67.6 7.6 %collective-permute-start.14 = (bf16[4,4,32,128]{3,2,1,0:T(8,128)(2,1)S(1)}, bf16[4,4,32,128]{3,2,1,0:T(8,128)(2,1)S(1)}, u32[]{:S(2)}, u32[]{:S(2)}) collective-permute-start(bf16[4,4,32,128]{3,2,1,0:T(8,128)(2,1)S(1)} %get-tuple-element.100), channel_id=1, source_target_pairs={{0,6},{1,7},{2,0},{3,1},{4,2},{5,3},{6,4},{7,5},{8,14},{9,15},{10,... | collective-permute-start | bytes 393224 | tf_op jit(solution)/shard_map/ppermute | solution.py:69
  75.4 5.0 %collective-permute-start.15 = (bf16[2,4,32,128]{3,2,1,0:T(8,128)(2,1)S(1)}, bf16[2,4,32,128]{3,2,1,0:T(8,128)(2,1)S(1)}, u32[]{:S(2)}, u32[]{:S(2)}) collective-permute-start(bf16[2,4,32,128]{3,2,1,0:T(8,128)(2,1)S(1)} %get-tuple-element.102), channel_id=1, source_target_pairs={{0,24},{1,25},{2,26},{3,27},{4,28},{5,29},{6,30},{7,31},{8,16},{9,... | collective-permute-start | bytes 196616 | tf_op jit(solution)/shard_map/ppermute | solution.py:69
  77.1 5.8 %collective-permute-start.16 = (bf16[2,4,32,128]{3,2,1,0:T(8,128)(2,1)S(1)}, bf16[2,4,32,128]{3,2,1,0:T(8,128)(2,1)S(1)}, u32[]{:S(2)}, u32[]{:S(2)}) collective-permute-start(bf16[2,4,32,128]{3,2,1,0:T(8,128)(2,1)S(1)} %get-tuple-element.103), channel_id=1, source_target_pairs={{0,16},{1,17},{2,18},{3,19},{4,20},{5,21},{6,22},{7,23},{8,24},{9,... | collective-permute-start | bytes 196616 | tf_op jit(solution)/shard_map/ppermute | solution.py:69
  77.1 5.8 %collective-permute-start.17 = (bf16[2,4,32,128]{3,2,1,0:T(8,128)(2,1)S(1)}, bf16[2,4,32,128]{3,2,1,0:T(8,128)(2,1)S(1)}, u32[]{:S(2)}, u32[]{:S(2)}) collective-permute-start(bf16[2,4,32,128]{3,2,1,0:T(8,128)(2,1)S(1)} %get-tuple-element.104), channel_id=1, source_target_pairs={{0,8},{1,9},{2,10},{3,11},{4,12},{5,13},{6,14},{7,15},{8,0},{9,1},... | collective-permute-start | bytes 196616 | tf_op jit(solution)/shard_map/ppermute | solution.py:69
  82.9 5.1 %collective-permute-start.18 = (bf16[2,4,32,128]{3,2,1,0:T(8,128)(2,1)S(1)}, bf16[2,4,32,128]{3,2,1,0:T(8,128)(2,1)S(1)}, u32[]{:S(2)}, u32[]{:S(2)}) collective-permute-start(bf16[2,4,32,128]{3,2,1,0:T(8,128)(2,1)S(1)} %z_sum.1.mine_ref), channel_id=1, source_target_pairs={{0,56},{1,57},{2,58},{3,59},{4,60},{5,61},{6,62},{7,63},{8,48},{9,... | collective-permute-start | bytes 196616 | tf_op jit(solution)/shard_map/ppermute | solution.py:69
  88.8 6.4 %collective-permute-start.21 = (bf16[2,4,32,128]{3,2,1,0:T(8,128)(2,1)S(1)}, bf16[2,4,32,128]{3,2,1,0:T(8,128)(2,1)S(1)}, u32[]{:S(2)}, u32[]{:S(2)}) collective-permute-start(bf16[2,4,32,128]{3,2,1,0:T(8,128)(2,1)S(1)} %get-tuple-element.106), channel_id=1, source_target_pairs={{0,24},{1,25},{2,26},{3,27},{4,28},{5,29},{6,30},{7,31},{8,16},{9,... | collective-permute-start | bytes 196616 | tf_op jit(solution)/shard_map/ppermute | solution.py:69
  91.1 4.0 %collective-permute-start.20 = (bf16[2,4,32,128]{3,2,1,0:T(8,128)(2,1)S(1)}, bf16[2,4,32,128]{3,2,1,0:T(8,128)(2,1)S(1)}, u32[]{:S(2)}, u32[]{:S(2)}) collective-permute-start(bf16[2,4,32,128]{3,2,1,0:T(8,128)(2,1)S(1)} %get-tuple-element.106), channel_id=1, source_target_pairs={{0,16},{1,17},{2,18},{3,19},{4,20},{5,21},{6,22},{7,23},{8,24},{9,... | collective-permute-start | bytes 196616 | tf_op jit(solution)/shard_map/ppermute | solution.py:69
  91.1 3.2 %collective-permute-start.19 = (bf16[2,4,32,128]{3,2,1,0:T(8,128)(2,1)S(1)}, bf16[2,4,32,128]{3,2,1,0:T(8,128)(2,1)S(1)}, u32[]{:S(2)}, u32[]{:S(2)}) collective-permute-start(bf16[2,4,32,128]{3,2,1,0:T(8,128)(2,1)S(1)} %get-tuple-element.106), channel_id=1, source_target_pairs={{0,8},{1,9},{2,10},{3,11},{4,12},{5,13},{6,14},{7,15},{8,0},{9,1},... | collective-permute-start | bytes 196616 | tf_op jit(solution)/shard_map/ppermute | solution.py:69
  95.2 9.4 %collective-permute-start.24 = (bf16[8,4,32,128]{3,2,1,0:T(8,128)(2,1)S(1)}, bf16[8,4,32,128]{3,2,1,0:T(8,128)(2,1)S(1)}, u32[]{:S(2)}, u32[]{:S(2)}) collective-permute-start(bf16[8,4,32,128]{3,2,1,0:T(8,128)(2,1)S(1)} %constant_dynamic-update-slice_fusion.refs_0_), channel_id=1, source_target_pairs={{0,2},{1,3},{2,4},{3,5},{4,6},{5,7},{6,0},{7,1},{8,10},{9,11},{10,... | collective-permute-start | bytes 786440 | tf_op jit(solution)/shard_map/ppermute | solution.py:69
  95.5 12.8 %collective-permute-start.23 = (bf16[8,4,32,128]{3,2,1,0:T(8,128)(2,1)S(1)}, bf16[8,4,32,128]{3,2,1,0:T(8,128)(2,1)S(1)}, u32[]{:S(2)}, u32[]{:S(2)}) collective-permute-start(bf16[8,4,32,128]{3,2,1,0:T(8,128)(2,1)S(1)} %constant_dynamic-update-slice_fusion.refs_0_), channel_id=1, source_target_pairs={{0,6},{1,7},{2,0},{3,1},{4,2},{5,3},{6,4},{7,5},{8,14},{9,15},{10,... | collective-permute-start | bytes 786440 | tf_op jit(solution)/shard_map/ppermute | solution.py:69
  98.0 12.2 %collective-permute-start.22 = (bf16[8,4,32,128]{3,2,1,0:T(8,128)(2,1)S(1)}, bf16[8,4,32,128]{3,2,1,0:T(8,128)(2,1)S(1)}, u32[]{:S(2)}, u32[]{:S(2)}) collective-permute-start(bf16[8,4,32,128]{3,2,1,0:T(8,128)(2,1)S(1)} %constant_dynamic-update-slice_fusion.refs_0_), channel_id=1, source_target_pairs={{0,4},{1,5},{2,6},{3,7},{4,0},{5,1},{6,2},{7,3},{8,12},{9,13},{10,... | collective-permute-start | bytes 786440 | tf_op jit(solution)/shard_map/ppermute | solution.py:69
  98.6 12.6 %collective-permute-start.25 = (bf16[8,4,32,128]{3,2,1,0:T(8,128)(2,1)S(1)}, bf16[8,4,32,128]{3,2,1,0:T(8,128)(2,1)S(1)}, u32[]{:S(2)}, u32[]{:S(2)}) collective-permute-start(bf16[8,4,32,128]{3,2,1,0:T(8,128)(2,1)S(1)} %constant_dynamic-update-slice_fusion.refs_0_), channel_id=1, source_target_pairs={{0,1},{1,0},{2,3},{3,2},{4,5},{5,4},{6,7},{7,6},{8,9},{9,8},{10,11... | collective-permute-start | bytes 786440 | tf_op jit(solution)/shard_map/ppermute | solution.py:69
  104.6 6.6 %collective-permute-start.28 = (bf16[8,4,32,128]{3,2,1,0:T(8,128)(2,1)S(1)}, bf16[8,4,32,128]{3,2,1,0:T(8,128)(2,1)S(1)}, u32[]{:S(2)}, u32[]{:S(2)}) collective-permute-start(bf16[8,4,32,128]{3,2,1,0:T(8,128)(2,1)S(1)} %collective-permute-done.24.refs_3_), channel_id=1, source_target_pairs={{0,1},{1,0},{2,3},{3,2},{4,5},{5,4},{6,7},{7,6},{8,9},{9,8},{10,11... | collective-permute-start | bytes 786440 | tf_op jit(solution)/shard_map/ppermute | solution.py:69
  108.3 3.0 %collective-permute-start.27 = (bf16[8,4,32,128]{3,2,1,0:T(8,128)(2,1)S(1)}, bf16[8,4,32,128]{3,2,1,0:T(8,128)(2,1)S(1)}, u32[]{:S(2)}, u32[]{:S(2)}) collective-permute-start(bf16[8,4,32,128]{3,2,1,0:T(8,128)(2,1)S(1)} %collective-permute-done.23.refs_2_), channel_id=1, source_target_pairs={{0,1},{1,0},{2,3},{3,2},{4,5},{5,4},{6,7},{7,6},{8,9},{9,8},{10,11... | collective-permute-start | bytes 786440 | tf_op jit(solution)/shard_map/ppermute | solution.py:69
  110.1 2.2 %collective-permute-start.26 = (bf16[8,4,32,128]{3,2,1,0:T(8,128)(2,1)S(1)}, bf16[8,4,32,128]{3,2,1,0:T(8,128)(2,1)S(1)}, u32[]{:S(2)}, u32[]{:S(2)}) collective-permute-start(bf16[8,4,32,128]{3,2,1,0:T(8,128)(2,1)S(1)} %collective-permute-done.22.refs_1_), channel_id=1, source_target_pairs={{0,1},{1,0},{2,3},{3,2},{4,5},{5,4},{6,7},{7,6},{8,9},{9,8},{10,11... | collective-permute-start | bytes 786440 | tf_op jit(solution)/shard_map/ppermute | solution.py:69

commit v7 on v6

--- a/solution.py
+++ b/solution.py
@@ -27,7 +27,7 @@
 HALF = ZS // 2
 Z_STEPS = (3, 2, 1)
 Z_PARTNER = 7
-Y_ORDER = (0, 2, 3, 1)
+Y_ORDER = (0, 1, 3, 2)
 BF16, F32 = jnp.bfloat16, jnp.float32
 VMEM = pl.BlockSpec(memory_space=pltpu.VMEM)
 ANY = pl.BlockSpec(memory_space=pl.ANY)
@@ -48,15 +48,15 @@
 
 
 def z_pos():
-    return lax.axis_index("dp") // 8
+    return lax.axis_index("dp") >> 3
 
 
 def y_pos():
-    return (lax.axis_index("dp") // 2) % YS
+    return (lax.axis_index("dp") >> 1) & (YS - 1)
 
 
 def core_pos():
-    return lax.axis_index("dp") % 2
+    return lax.axis_index("dp") & 1
 
 
 def over_dp(value, zx=0, dy=0, dc=0):
@@ -382,27 +382,15 @@
     )(mine, got, state, partner_state)
 
 
-def assemble_kernel(*refs):
-    arrays, (out_ref, blocks, sems) = refs[:8], refs[8:]
-    core, y_here, z_here = core_pos(), y_pos(), z_pos()
-    copies = []
-    for side in range(2):
-        for i, k in enumerate(Y_ORDER):
-            copies.append(
-                pltpu.make_async_copy(
-                    arrays[side * YS + i],
-                    blocks.at[lax.rem(core + side, 2), lax.rem(y_here + YS - k, YS)],
-                    sems.at[side * YS + i],
-                )
-            )
-            copies[-1].start()
-    for copy in copies:
-        copy.wait()
+def assemble_kernel(blocks, out_ref):
+    z_here = z_pos()
     lane = lax.broadcasted_iota(jnp.int32, (RANK, LANES), 1)
     places = []
     for z in range(ZS):
         apart = z_here ^ z
-        places.append(jnp.where(apart < 4, 2 * apart, 2 * (apart ^ Z_PARTNER) + 1))
+        far = jnp.where(apart < HALF, 0, 1)
+        step = apart ^ (far * Z_PARTNER)
+        places.append(2 * ((HALF - step) & (HALF - 1)) + far)
     for tile in range(FF // LANES):
         value = None
         first = tile * LANES // OWNED
@@ -418,19 +406,15 @@
         out_ref[:, tile * LANES : (tile + 1) * LANES] = value.astype(BF16)
 
 
-def assemble(arrays):
+def assemble(blocks):
     return pl.pallas_call(
         assemble_kernel,
         out_shape=shaped((RANK, FF), BF16),
-        in_specs=[ANY] * 8,
+        in_specs=[VMEM],
         out_specs=VMEM,
-        scratch_shapes=[
-            pltpu.VMEM((2, YS, ZS, BUCKETS, RANK, LANES), BF16),
-            pltpu.SemaphoreType.DMA((8,)),
-        ],
-        compiler_params=params(),
+        compiler_params=params(8),
         name="assemble",
-    )(*arrays)
+    )(blocks)
 
 
 def per_device(out_grad, pre_act, down_a, down_b, up_a, up_b, master, moment, second):
@@ -447,7 +431,7 @@
     state = jnp.stack([a[0].transpose(0, 2, 1) for a in (master, moment, second)])
     *share, first_hidden = lax.optimization_barrier((*share, hidden[0]))
     above, hidden = None, [first_hidden]
-    for buckets in ((1, 2), (3,), ()):
+    for buckets in ((1,), (2, 3), ()):
         sent = relay(share, above, slope, da, ub)
         above = lax.ppermute(sent, "section", [(1, 0), (2, 1), (3, 2)])
         if buckets:
@@ -461,13 +445,19 @@
     from_below, from_above = over_dp(up, dy=1), over_dp(down, dy=-1)
     up, down = y_pass(up_held, from_below, down_held, from_above)
     last_below, last_above = over_dp(up, dy=1), over_dp(down, dy=-1)
-    last_below, partner_state = lax.optimization_barrier((last_below, partner_state))
     own, *sends = y_sum(own, from_below, from_above, last_below, last_above)
-    mine = z_sum(own, [over_dp(a, zx=k) for a, k in zip(sends, Z_STEPS)])
+    got = [over_dp(a, zx=k) for a, k in zip(sends, Z_STEPS)]
+    *got, partner_state = lax.optimization_barrier((*got, partner_state))
+    mine = z_sum(own, got)
     pair, *state = adamw(mine, over_dp(mine, zx=Z_PARTNER), state, partner_state)
-    column = jnp.concatenate([pair] + [over_dp(pair, zx=k) for k in Z_STEPS[::-1]])
+    column = jnp.concatenate([pair] + [over_dp(pair, zx=k) for k in Z_STEPS])
     plane = [column] + [over_dp(column, dy=k) for k in Y_ORDER[1:]]
-    rows = assemble(plane + [over_dp(a, dc=1) for a in plane])
+    plane += [over_dp(a, dc=1) for a in plane]
+    blocks = jnp.zeros((2, YS, *column.shape), BF16)
+    for i, array in enumerate(plane):
+        core, y = core_pos() ^ (i // YS), (y_pos() + YS - Y_ORDER[i % YS]) & (YS - 1)
+        blocks = lax.dynamic_update_slice(blocks, array[None, None], (core, y, 0, 0, 0, 0))
+    rows = assemble(blocks)
     return (rows.T[None], *[a.transpose(0, 2, 1)[None] for a in state])
 
 

time: 115 us -> 118 us (1.026)
  starting transfers between devices: 54.2 us -> 56.8 us
    ppermute x20, starting transfers between devices: 42.2 us -> 44.8 us  [over_dp(): return lax.ppermute(value, 'dp', pairs)]
  transfers between devices with their start and end apart: 29 -> 29, of which waited for: 14 -> 13; matrix products, arithmetic and copies ran while one was open for 0% -> 1% of each run, Pallas kernels for 12% -> 12%
where the time goes in v7:
time: 118 us
  starting transfers between devices  56.8 us (48%)
  Pallas kernels  33.7 us (29%)
  waiting for transfers between devices  25.5 us (22%)
    ppermute x20, starting transfers between devices, over_dp(): return lax.ppermute(value, 'dp', pairs)  44.8 us
    ppermute x20, waiting for transfers between devices, over_dp(): return lax.ppermute(value, 'dp', pairs)  19.7 us
    pallas_call x5, Pallas kernels, activation(): pl.pallas_call(functools.partial(activation_kernel, slope, bucket * BUCKE...  14.1 us
    pallas_call x3, Pallas kernels, relay(): pl.pallas_call(functools.partial(relay_kernel, first), out_shape=shaped((...  12.5 us
    ppermute x6, starting transfers between devices, over_section(): lax.ppermute(value, 'section', [(i, (i + steps) % 4) for i in range(4)])  7.94 us
    ppermute x3, waiting for transfers between devices, per_device(): above = lax.ppermute(sent, 'section', [(1, 0), (2, 1), (3, 2)])  4.99 us
    ppermute x3, starting transfers between devices, per_device(): above = lax.ppermute(sent, 'section', [(1, 0), (2, 1), (3, 2)])  4.09 us
  transfers between devices with their start and end apart: 29, of which 13 were waited for; matrix products, arithmetic and copies ran while one was open for 1% of the time, Pallas kernels for 12%

profile of v7, /device:TPU:1, one launch (start us, length us, event | category | flops | bytes accessed | tf_op | source)
XLA Modules:
  0.0 117.9 jit_solution(3760666987854277211)
XLA Ops:
  0.6 1.3 %slices.1 = (bf16[64,1280]{1,0:T(8,128)(2,1)S(1)}, bf16[64,1280]{1,0:T(8,128)(2,1)S(1)}, bf16[64,1280]{1,0:T(8,128)(2,1)S(1)}, bf16[64,1280]{1,0:T(8,128)(2,1)S(1)}) custom-call(bf16[32,5120]{1,0:T(8,128)(2,1)} %bitcast.66, bf16[32,5120]{1,0:T(8,128)(2,1)} %bitcast.67), custom_call_target="tpu_custom_call" | custom-call | tf_op jit(solution)/shard_map/slices/pallas_call | solution.py:94
  1.9 2.1 %collective-permute-start = (bf16[64,1280]{1,0:T(8,128)(2,1)S(1)}, bf16[64,1280]{1,0:T(8,128)(2,1)S(1)}, u32[]{:S(2)}, u32[]{:S(2)}) collective-permute-start(bf16[64,1280]{1,0:T(8,128)(2,1)S(1)} %get-tuple-element.59), channel_id=1, source_target_pairs={{0,64},{64,128},{128,192},{192,0},{1,65},{65,129},{129,193},{193,1... | collective-permute-start | bytes 491528 | tf_op jit(solution)/shard_map/ppermute | solution.py:73
  4.0 1.4 %collective-permute-start.1 = (bf16[64,1280]{1,0:T(8,128)(2,1)S(1)}, bf16[64,1280]{1,0:T(8,128)(2,1)S(1)}, u32[]{:S(2)}, u32[]{:S(2)}) collective-permute-start(bf16[64,1280]{1,0:T(8,128)(2,1)S(1)} %get-tuple-element.60), channel_id=1, source_target_pairs={{0,192},{64,0},{128,64},{192,128},{1,193},{65,1},{129,65},{193,129... | collective-permute-start | bytes 491528 | tf_op jit(solution)/shard_map/ppermute | solution.py:73
  5.4 1.6 %collective-permute-start.2 = (bf16[64,1280]{1,0:T(8,128)(2,1)S(1)}, bf16[64,1280]{1,0:T(8,128)(2,1)S(1)}, u32[]{:S(2)}, u32[]{:S(2)}) collective-permute-start(bf16[64,1280]{1,0:T(8,128)(2,1)S(1)} %get-tuple-element.61), channel_id=1, source_target_pairs={{0,128},{64,192},{128,0},{192,64},{1,129},{65,193},{129,1},{193,65... | collective-permute-start | bytes 491528 | tf_op jit(solution)/shard_map/ppermute | solution.py:73
  7.0 6.3 %slope.1.refs_4_.refs_5_ = bf16[128,27648]{1,0:T(8,128)(2,1)S(1)} custom-call(bf16[128,27648]{1,0:T(8,128)(2,1)} %bitcast.60), custom_call_target="tpu_custom_call" | custom-call | flops 35389440 | bytes 14155776 | tf_op jit(solution)/shard_map/slope/pallas_call | solution.py:135
  13.3 0.0 collective-permute-done.w1
  13.3 0.0 collective-permute-done.2.w2
  13.3 0.9 shares.1
  14.3 1.2 collective-permute-start.3
  15.4 0.3 collective-permute-start.4
  15.8 1.3 %collective-permute-start.5 = (f32[32,256]{1,0:T(8,128)S(1)}, f32[32,256]{1,0:T(8,128)S(1)}, u32[]{:S(2)}, u32[]{:S(2)}) collective-permute-start(f32[32,256]{1,0:T(8,128)S(1)} %get-tuple-element.69), channel_id=1, source_target_pairs={{0,128},{64,192},{128,0},{192,64},{1,129},{65,193},{129,1},{193,65... | collective-permute-start | bytes 98312 | tf_op jit(solution)/shard_map/ppermute | solution.py:73
  17.1 2.1 %hidden.4.h0 = bf16[128,6912]{1,0:T(8,128)(2,1)S(1)} custom-call(bf16[128,27648]{1,0:T(8,128)(2,1)} %bitcast.61), custom_call_target="tpu_custom_call" | custom-call | flops 8847360 | bytes 3538944 | tf_op jit(solution)/shard_map/hidden/pallas_call | solution.py:135
  19.2 0.2 collective-permute-done.4.refs_2_.s2
  19.4 0.6 collective-permute-done.5.refs_3_.s3
  20.1 0.0 copy-start.5
  20.1 4.1 %relay_first.1 = bf16[96,128]{1,0:T(8,128)(2,1)S(1)} custom-call(f32[32,256]{1,0:T(8,128)S(1)} %get-tuple-element.71.refs_0_.s0, f32[32,256]{1,0:T(8,128)S(1)} %collective-permute-done.3.refs_1_.s1, f32[32,256]{1,0:T(8,128)S(1)} %collective-permute-done.4.refs_2_.s2, f32[32,256]{1,0:T(8,128)S(1)} %collective-permute-done.5.refs_3_.s3, ...), custom_call_target="tpu_custom_call" | custom-call | tf_op jit(solution)/shard_map/relay_first/pallas_call | solution.py:214
  24.1 1.5 %collective-permute-start.6 = (bf16[96,128]{1,0:T(8,128)(2,1)S(1)}, bf16[96,128]{1,0:T(8,128)(2,1)S(1)}, u32[]{:S(2)}, u32[]{:S(2)}) collective-permute-start(bf16[96,128]{1,0:T(8,128)(2,1)S(1)} %relay_first.1), channel_id=1, source_target_pairs={{64,0},{128,64},{192,128},{65,1},{129,65},{193,129},{66,2},{130,66... | collective-permute-start | bytes 73736 | tf_op jit(solution)/shard_map/ppermute | solution.py:436
  25.7 1.9 %hidden.5.h1 = bf16[128,6912]{1,0:T(8,128)(2,1)S(1)} custom-call(bf16[128,27648]{1,0:T(8,128)(2,1)} %bitcast.62), custom_call_target="tpu_custom_call" | custom-call | flops 8847360 | bytes 3538944 | tf_op jit(solution)/shard_map/hidden/pallas_call | solution.py:135
  27.6 1.1 collective-permute-done.6.refs_4_
  28.7 4.2 %relay.2 = bf16[96,128]{1,0:T(8,128)(2,1)S(1)} custom-call(f32[32,256]{1,0:T(8,128)S(1)} %get-tuple-element.71.refs_0_.s0, f32[32,256]{1,0:T(8,128)S(1)} %collective-permute-done.3.refs_1_.s1, f32[32,256]{1,0:T(8,128)S(1)} %collective-permute-done.4.refs_2_.s2, f32[32,256]{1,0:T(8,128)S(1)} %collective-permute-done.5.refs_3_.s3, ...), custom_call_target="tpu_custom_call" | custom-call | tf_op jit(solution)/shard_map/relay/pallas_call | solution.py:214
  33.0 1.3 %collective-permute-start.7 = (bf16[96,128]{1,0:T(8,128)(2,1)S(1)}, bf16[96,128]{1,0:T(8,128)(2,1)S(1)}, u32[]{:S(2)}, u32[]{:S(2)}) collective-permute-start(bf16[96,128]{1,0:T(8,128)(2,1)S(1)} %relay.2), channel_id=1, source_target_pairs={{64,0},{128,64},{192,128},{65,1},{129,65},{193,129},{66,2},{130,66... | collective-permute-start | bytes 73736 | tf_op jit(solution)/shard_map/ppermute | solution.py:436
  34.3 1.9 %hidden.6.h2 = bf16[128,6912]{1,0:T(8,128)(2,1)S(1)} custom-call(bf16[128,27648]{1,0:T(8,128)(2,1)} %bitcast.63), custom_call_target="tpu_custom_call" | custom-call | flops 8847360 | bytes 3538944 | tf_op jit(solution)/shard_map/hidden/pallas_call | solution.py:135
  36.2 1.9 %hidden.7.h3 = bf16[128,6912]{1,0:T(8,128)(2,1)S(1)} custom-call(bf16[128,27648]{1,0:T(8,128)(2,1)} %bitcast.64), custom_call_target="tpu_custom_call" | custom-call | flops 8847360 | bytes 3538944 | tf_op jit(solution)/shard_map/hidden/pallas_call | solution.py:135
  38.1 0.0 collective-permute-done.7.refs_4_
  38.1 4.2 %relay.3 = bf16[96,128]{1,0:T(8,128)(2,1)S(1)} custom-call(f32[32,256]{1,0:T(8,128)S(1)} %get-tuple-element.71.refs_0_.s0, f32[32,256]{1,0:T(8,128)S(1)} %collective-permute-done.3.refs_1_.s1, f32[32,256]{1,0:T(8,128)S(1)} %collective-permute-done.4.refs_2_.s2, f32[32,256]{1,0:T(8,128)S(1)} %collective-permute-done.5.refs_3_.s3, ...), custom_call_target="tpu_custom_call" | custom-call | tf_op jit(solution)/shard_map/relay/pallas_call | solution.py:214
  42.4 1.3 %collective-permute-start.8 = (bf16[96,128]{1,0:T(8,128)(2,1)S(1)}, bf16[96,128]{1,0:T(8,128)(2,1)S(1)}, u32[]{:S(2)}, u32[]{:S(2)}) collective-permute-start(bf16[96,128]{1,0:T(8,128)(2,1)S(1)} %relay.3), channel_id=1, source_target_pairs={{64,0},{128,64},{192,128},{65,1},{129,65},{193,129},{66,2},{130,66... | collective-permute-start | bytes 73736 | tf_op jit(solution)/shard_map/ppermute | solution.py:436
  43.7 3.9 %collective-permute-done.8.above_ref = bf16[96,128]{1,0:T(8,128)(2,1)S(1)} collective-permute-done((bf16[96,128]{1,0:T(8,128)(2,1)S(1)}, bf16[96,128]{1,0:T(8,128)(2,1)S(1)}, u32[]{:S(2)}, u32[]{:S(2)}) %collective-permute-start.8) | collective-permute-done | bytes 24608 | tf_op jit(solution)/shard_map/ppermute | solution.py:436
  47.6 1.4 %grads.1 = (bf16[4,8,4,32,128]{4,3,2,1,0:T(8,128)(2,1)S(1)}, bf16[4,8,4,32,128]{4,3,2,1,0:T(8,128)(2,1)S(1)}) custom-call(f32[32,256]{1,0:T(8,128)S(1)} %get-tuple-element.71.refs_0_.s0, f32[32,256]{1,0:T(8,128)S(1)} %collective-permute-done.3.refs_1_.s1, f32[32,256]{1,0:T(8,128)S(1)} %collective-permute-done.4.refs_2_.s2, ...), custom_call_target="tpu_custom_call" | custom-call | tf_op jit(solution)/shard_map/grads/pallas_call | solution.py:250
  49.0 6.5 %collective-permute-start.9 = (bf16[4,8,4,32,128]{4,3,2,1,0:T(8,128)(2,1)S(1)}, bf16[4,8,4,32,128]{4,3,2,1,0:T(8,128)(2,1)S(1)}, u32[]{:S(2)}, u32[]{:S(2)}) collective-permute-start(bf16[4,8,4,32,128]{4,3,2,1,0:T(8,128)(2,1)S(1)} %get-tuple-element.90), channel_id=1, source_target_pairs={{0,1},{1,0},{2,3},{3,2},{4,5},{5,4},{6,7},{7,6},{8,9},{9,8},{10,11... | collective-permute-start | bytes 3145736 | tf_op jit(solution)/shard_map/ppermute | solution.py:69
  55.5 2.3 %collective-permute-done.9.got_ref = bf16[4,8,4,32,128]{4,3,2,1,0:T(8,128)(2,1)S(1)} collective-permute-done((bf16[4,8,4,32,128]{4,3,2,1,0:T(8,128)(2,1)S(1)}, bf16[4,8,4,32,128]{4,3,2,1,0:T(8,128)(2,1)S(1)}, u32[]{:S(2)}, u32[]{:S(2)}) %collective-permute-start.9) | collective-permute-done | bytes 1048608 | tf_op jit(solution)/shard_map/ppermute | solution.py:69
  57.8 0.2 core_sum.1
  58.0 0.8 collective-permute-start.10
  58.8 2.0 %collective-permute-start.11 = (bf16[2,4,4,32,128]{4,3,2,1,0:T(8,128)(2,1)S(1)}, bf16[2,4,4,32,128]{4,3,2,1,0:T(8,128)(2,1)S(1)}, u32[]{:S(2)}, u32[]{:S(2)}) collective-permute-start(bf16[2,4,4,32,128]{4,3,2,1,0:T(8,128)(2,1)S(1)} %get-tuple-element.94), channel_id=1, source_target_pairs={{0,6},{1,7},{2,0},{3,1},{4,2},{5,3},{6,4},{7,5},{8,14},{9,15},{10,... | collective-permute-start | bytes 786440 | tf_op jit(solution)/shard_map/ppermute | solution.py:69
  60.7 6.1 %collective-permute-done.10.from_below = bf16[2,4,4,32,128]{4,3,2,1,0:T(8,128)(2,1)S(1)} collective-permute-done((bf16[2,4,4,32,128]{4,3,2,1,0:T(8,128)(2,1)S(1)}, bf16[2,4,4,32,128]{4,3,2,1,0:T(8,128)(2,1)S(1)}, u32[]{:S(2)}, u32[]{:S(2)}) %collective-permute-start.10) | collective-permute-done | bytes 262176 | tf_op jit(solution)/shard_map/ppermute | solution.py:69
  66.8 0.8 collective-permute-start.12
  67.6 2.2 %collective-permute-start.13 = (bf16[4,4,32,128]{3,2,1,0:T(8,128)(2,1)S(1)}, bf16[4,4,32,128]{3,2,1,0:T(8,128)(2,1)S(1)}, u32[]{:S(2)}, u32[]{:S(2)}) collective-permute-start(bf16[4,4,32,128]{3,2,1,0:T(8,128)(2,1)S(1)} %get-tuple-element.98), channel_id=1, source_target_pairs={{0,6},{1,7},{2,0},{3,1},{4,2},{5,3},{6,4},{7,5},{8,14},{9,15},{10,... | collective-permute-start | bytes 393224 | tf_op jit(solution)/shard_map/ppermute | solution.py:69
  69.8 5.1 %collective-permute-start.17 = (f32[3,4,32,108]{3,2,1,0:T(8,128)S(1)}, f32[3,4,32,108]{3,2,1,0:T(8,128)S(1)}, u32[]{:S(2)}, u32[]{:S(2)}) collective-permute-start(f32[3,4,32,108]{3,2,1,0:T(8,128)S(1)} %pad_maximum_fusion.state_ref), channel_id=1, source_target_pairs={{0,56},{1,57},{2,58},{3,59},{4,60},{5,61},{6,62},{7,63},{8,48},{9,... | collective-permute-start | bytes 497672 | tf_op jit(solution)/shard_map/ppermute | solution.py:69
  74.9 0.0 collective-permute-done.12.last_below
  74.9 0.0 collective-permute-done.13.last_above
  75.0 0.1 y_sum.1
  75.1 1.7 %collective-permute-start.14 = (bf16[2,4,32,128]{3,2,1,0:T(8,128)(2,1)S(1)}, bf16[2,4,32,128]{3,2,1,0:T(8,128)(2,1)S(1)}, u32[]{:S(2)}, u32[]{:S(2)}) collective-permute-start(bf16[2,4,32,128]{3,2,1,0:T(8,128)(2,1)S(1)} %get-tuple-element.100), channel_id=1, source_target_pairs={{0,24},{1,25},{2,26},{3,27},{4,28},{5,29},{6,30},{7,31},{8,16},{9,... | collective-permute-start | bytes 196616 | tf_op jit(solution)/shard_map/ppermute | solution.py:69
  76.8 1.2 collective-permute-start.15
  78.0 0.8 collective-permute-start.16
  78.7 5.3 %collective-permute-done.17.partner_ref = f32[3,4,32,108]{3,2,1,0:T(8,128)S(1)} collective-permute-done((f32[3,4,32,108]{3,2,1,0:T(8,128)S(1)}, f32[3,4,32,108]{3,2,1,0:T(8,128)S(1)}, u32[]{:S(2)}, u32[]{:S(2)}) %collective-permute-start.17) | collective-permute-done | bytes 165920 | tf_op jit(solution)/shard_map/ppermute | solution.py:69
  84.0 0.0 collective-permute-done.14.g1
  84.1 0.0 collective-permute-done.16.g3
  84.1 2.6 %collective-permute-start.18 = (bf16[2,4,32,128]{3,2,1,0:T(8,128)(2,1)S(1)}, bf16[2,4,32,128]{3,2,1,0:T(8,128)(2,1)S(1)}, u32[]{:S(2)}, u32[]{:S(2)}) collective-permute-start(bf16[2,4,32,128]{3,2,1,0:T(8,128)(2,1)S(1)} %z_sum.1.mine_ref), channel_id=1, source_target_pairs={{0,56},{1,57},{2,58},{3,59},{4,60},{5,61},{6,62},{7,63},{8,48},{9,... | collective-permute-start | bytes 196616 | tf_op jit(solution)/shard_map/ppermute | solution.py:69
  86.7 1.8 %collective-permute-done.18.got_ref = bf16[2,4,32,128]{3,2,1,0:T(8,128)(2,1)S(1)} collective-permute-done((bf16[2,4,32,128]{3,2,1,0:T(8,128)(2,1)S(1)}, bf16[2,4,32,128]{3,2,1,0:T(8,128)(2,1)S(1)}, u32[]{:S(2)}, u32[]{:S(2)}) %collective-permute-start.18) | collective-permute-done | bytes 65568 | tf_op jit(solution)/shard_map/ppermute | solution.py:69
  88.5 0.7 adamw.1
  89.2 1.7 %collective-permute-start.19 = (bf16[2,4,32,128]{3,2,1,0:T(8,128)(2,1)S(1)}, bf16[2,4,32,128]{3,2,1,0:T(8,128)(2,1)S(1)}, u32[]{:S(2)}, u32[]{:S(2)}) collective-permute-start(bf16[2,4,32,128]{3,2,1,0:T(8,128)(2,1)S(1)} %get-tuple-element.108), channel_id=1, source_target_pairs={{0,24},{1,25},{2,26},{3,27},{4,28},{5,29},{6,30},{7,31},{8,16},{9,... | collective-permute-start | bytes 196616 | tf_op jit(solution)/shard_map/ppermute | solution.py:69
  90.9 3.6 %collective-permute-start.20 = (bf16[2,4,32,128]{3,2,1,0:T(8,128)(2,1)S(1)}, bf16[2,4,32,128]{3,2,1,0:T(8,128)(2,1)S(1)}, u32[]{:S(2)}, u32[]{:S(2)}) collective-permute-start(bf16[2,4,32,128]{3,2,1,0:T(8,128)(2,1)S(1)} %get-tuple-element.108), channel_id=1, source_target_pairs={{0,16},{1,17},{2,18},{3,19},{4,20},{5,21},{6,22},{7,23},{8,24},{9,... | collective-permute-start | bytes 196616 | tf_op jit(solution)/shard_map/ppermute | solution.py:69
  94.5 2.3 %collective-permute-done.20 = bf16[2,4,32,128]{3,2,1,0:T(8,128)(2,1)S(1)} collective-permute-done((bf16[2,4,32,128]{3,2,1,0:T(8,128)(2,1)S(1)}, bf16[2,4,32,128]{3,2,1,0:T(8,128)(2,1)S(1)}, u32[]{:S(2)}, u32[]{:S(2)}) %collective-permute-start.20) | collective-permute-done | bytes 65568 | tf_op jit(solution)/shard_map/ppermute | solution.py:69
  96.8 0.8 collective-permute-done.21
  97.6 0.1 collective-permute-start.22
  97.7 2.7 %collective-permute-start.23 = (bf16[8,4,32,128]{3,2,1,0:T(8,128)(2,1)S(1)}, bf16[8,4,32,128]{3,2,1,0:T(8,128)(2,1)S(1)}, u32[]{:S(2)}, u32[]{:S(2)}) collective-permute-start(bf16[8,4,32,128]{3,2,1,0:T(8,128)(2,1)S(1)} %constant_dynamic-update-slice_fusion), channel_id=1, source_target_pairs={{0,6},{1,7},{2,0},{3,1},{4,2},{5,3},{6,4},{7,5},{8,14},{9,15},{10,... | collective-permute-start | bytes 786440 | tf_op jit(solution)/shard_map/ppermute | solution.py:69
  100.4 4.7 %collective-permute-start.25 = (bf16[8,4,32,128]{3,2,1,0:T(8,128)(2,1)S(1)}, bf16[8,4,32,128]{3,2,1,0:T(8,128)(2,1)S(1)}, u32[]{:S(2)}, u32[]{:S(2)}) collective-permute-start(bf16[8,4,32,128]{3,2,1,0:T(8,128)(2,1)S(1)} %constant_dynamic-update-slice_fusion), channel_id=1, source_target_pairs={{0,1},{1,0},{2,3},{3,2},{4,5},{5,4},{6,7},{7,6},{8,9},{9,8},{10,11... | collective-permute-start | bytes 786440 | tf_op jit(solution)/shard_map/ppermute | solution.py:69
  105.0 0.5 broadcast_in_dim.39
  105.6 8.0 %collective-permute-start.26 = (bf16[8,4,32,128]{3,2,1,0:T(8,128)(2,1)S(1)}, bf16[8,4,32,128]{3,2,1,0:T(8,128)(2,1)S(1)}, u32[]{:S(2)}, u32[]{:S(2)}) collective-permute-start(bf16[8,4,32,128]{3,2,1,0:T(8,128)(2,1)S(1)} %collective-permute-done.22), channel_id=1, source_target_pairs={{0,1},{1,0},{2,3},{3,2},{4,5},{5,4},{6,7},{7,6},{8,9},{9,8},{10,11... | collective-permute-start | bytes 786440 | tf_op jit(solution)/shard_map/ppermute | solution.py:69
  113.7 0.0 collective-permute-start.27
  113.7 0.5 collective-permute-start.28
  114.4 0.4 collective-permute-done.26
  114.9 0.3 collective-permute-done.27
  115.2 0.3 collective-permute-done.28
  115.6 2.3 %assemble.1 = bf16[32,27648]{1,0:T(8,128)(2,1)} custom-call(bf16[2,4,8,4,32,128]{5,4,3,2,1,0:T(8,128)(2,1)S(1)} %bitcast_dynamic-update-slice_fusion.blocks), custom_call_target="tpu_custom_call" | custom-call | tf_op jit(solution)/shard_map/assemble/pallas_call | solution.py:410
  (37 shorter events, 0.5 us)
Async XLA Ops:
  1.9 11.4 %collective-permute-start = (bf16[64,1280]{1,0:T(8,128)(2,1)S(1)}, bf16[64,1280]{1,0:T(8,128)(2,1)S(1)}, u32[]{:S(2)}, u32[]{:S(2)}) collective-permute-start(bf16[64,1280]{1,0:T(8,128)(2,1)S(1)} %get-tuple-element.59), channel_id=1, source_target_pairs={{0,64},{64,128},{128,192},{192,0},{1,65},{65,129},{129,193},{193,1... | collective-permute-start | bytes 491528 | tf_op jit(solution)/shard_map/ppermute | solution.py:73
  4.0 9.3 %collective-permute-start.1 = (bf16[64,1280]{1,0:T(8,128)(2,1)S(1)}, bf16[64,1280]{1,0:T(8,128)(2,1)S(1)}, u32[]{:S(2)}, u32[]{:S(2)}) collective-permute-start(bf16[64,1280]{1,0:T(8,128)(2,1)S(1)} %get-tuple-element.60), channel_id=1, source_target_pairs={{0,192},{64,0},{128,64},{192,128},{1,193},{65,1},{129,65},{193,129... | collective-permute-start | bytes 491528 | tf_op jit(solution)/shard_map/ppermute | solution.py:73
  5.4 8.0 %collective-permute-start.2 = (bf16[64,1280]{1,0:T(8,128)(2,1)S(1)}, bf16[64,1280]{1,0:T(8,128)(2,1)S(1)}, u32[]{:S(2)}, u32[]{:S(2)}) collective-permute-start(bf16[64,1280]{1,0:T(8,128)(2,1)S(1)} %get-tuple-element.61), channel_id=1, source_target_pairs={{0,128},{64,192},{128,0},{192,64},{1,129},{65,193},{129,1},{193,65... | collective-permute-start | bytes 491528 | tf_op jit(solution)/shard_map/ppermute | solution.py:73
  7.0 6.3 %copy-start.2 = (bf16[128,1280]{1,0:T(8,128)(2,1)S(1)}, bf16[128,1280]{1,0:T(8,128)(2,1)}, u32[]{:S(2)}) copy-start(bf16[128,1280]{1,0:T(8,128)(2,1)} %g_ref.1) | copy-start | bytes 983044
  14.3 4.9 %collective-permute-start.3 = (f32[32,256]{1,0:T(8,128)S(1)}, f32[32,256]{1,0:T(8,128)S(1)}, u32[]{:S(2)}, u32[]{:S(2)}) collective-permute-start(f32[32,256]{1,0:T(8,128)S(1)} %get-tuple-element.67), channel_id=1, source_target_pairs={{0,192},{64,0},{128,64},{192,128},{1,193},{65,1},{129,65},{193,129... | collective-permute-start | bytes 98312 | tf_op jit(solution)/shard_map/ppermute | solution.py:73
  15.4 4.0 %collective-permute-start.4 = (f32[32,256]{1,0:T(8,128)S(1)}, f32[32,256]{1,0:T(8,128)S(1)}, u32[]{:S(2)}, u32[]{:S(2)}) collective-permute-start(f32[32,256]{1,0:T(8,128)S(1)} %get-tuple-element.68), channel_id=1, source_target_pairs={{0,64},{64,128},{128,192},{192,0},{1,65},{65,129},{129,193},{193,1... | collective-permute-start | bytes 98312 | tf_op jit(solution)/shard_map/ppermute | solution.py:73
  15.8 4.3 %collective-permute-start.5 = (f32[32,256]{1,0:T(8,128)S(1)}, f32[32,256]{1,0:T(8,128)S(1)}, u32[]{:S(2)}, u32[]{:S(2)}) collective-permute-start(f32[32,256]{1,0:T(8,128)S(1)} %get-tuple-element.69), channel_id=1, source_target_pairs={{0,128},{64,192},{128,0},{192,64},{1,129},{65,193},{129,1},{193,65... | collective-permute-start | bytes 98312 | tf_op jit(solution)/shard_map/ppermute | solution.py:73
  17.1 2.9 %copy-start = (bf16[1,27648,32]{1,2,0:T(8,128)(2,1)S(1)}, bf16[1,27648,32]{1,2,0:T(8,128)(2,1)}, u32[]{:S(2)}) copy-start(bf16[1,27648,32]{1,2,0:T(8,128)(2,1)} %param.11) | copy-start | bytes 5308420
  17.1 2.9 %copy-start.1 = (bf16[1,27648,32]{1,2,0:T(8,128)(2,1)S(1)}, bf16[1,27648,32]{1,2,0:T(8,128)(2,1)}, u32[]{:S(2)}) copy-start(bf16[1,27648,32]{1,2,0:T(8,128)(2,1)} %param.14) | copy-start | bytes 5308420
  20.1 5.6 %copy-start.3 = (f32[1,4,108,32]{2,3,1,0:T(8,128)S(1)}, f32[1,4,108,32]{2,3,1,0:T(8,128)}, u32[]{:S(2)}) copy-start(f32[1,4,108,32]{2,3,1,0:T(8,128)} %param.17) | copy-start | bytes 165892
  20.1 5.6 %copy-start.4 = (f32[1,4,108,32]{2,3,1,0:T(8,128)S(1)}, f32[1,4,108,32]{2,3,1,0:T(8,128)}, u32[]{:S(2)}) copy-start(f32[1,4,108,32]{2,3,1,0:T(8,128)} %param.16) | copy-start | bytes 165892
  20.1 5.6 %copy-start.5 = (f32[1,4,108,32]{2,3,1,0:T(8,128)S(1)}, f32[1,4,108,32]{2,3,1,0:T(8,128)}, u32[]{:S(2)}) copy-start(f32[1,4,108,32]{2,3,1,0:T(8,128)} %param.15) | copy-start | bytes 165892
  24.1 4.6 %collective-permute-start.6 = (bf16[96,128]{1,0:T(8,128)(2,1)S(1)}, bf16[96,128]{1,0:T(8,128)(2,1)S(1)}, u32[]{:S(2)}, u32[]{:S(2)}) collective-permute-start(bf16[96,128]{1,0:T(8,128)(2,1)S(1)} %relay_first.1), channel_id=1, source_target_pairs={{64,0},{128,64},{192,128},{65,1},{129,65},{193,129},{66,2},{130,66... | collective-permute-start | bytes 73736 | tf_op jit(solution)/shard_map/ppermute | solution.py:436
  33.0 5.2 %collective-permute-start.7 = (bf16[96,128]{1,0:T(8,128)(2,1)S(1)}, bf16[96,128]{1,0:T(8,128)(2,1)S(1)}, u32[]{:S(2)}, u32[]{:S(2)}) collective-permute-start(bf16[96,128]{1,0:T(8,128)(2,1)S(1)} %relay.2), channel_id=1, source_target_pairs={{64,0},{128,64},{192,128},{65,1},{129,65},{193,129},{66,2},{130,66... | collective-permute-start | bytes 73736 | tf_op jit(solution)/shard_map/ppermute | solution.py:436
  42.4 5.2 %collective-permute-start.8 = (bf16[96,128]{1,0:T(8,128)(2,1)S(1)}, bf16[96,128]{1,0:T(8,128)(2,1)S(1)}, u32[]{:S(2)}, u32[]{:S(2)}) collective-permute-start(bf16[96,128]{1,0:T(8,128)(2,1)S(1)} %relay.3), channel_id=1, source_target_pairs={{64,0},{128,64},{192,128},{65,1},{129,65},{193,129},{66,2},{130,66... | collective-permute-start | bytes 73736 | tf_op jit(solution)/shard_map/ppermute | solution.py:436
  49.0 8.8 %collective-permute-start.9 = (bf16[4,8,4,32,128]{4,3,2,1,0:T(8,128)(2,1)S(1)}, bf16[4,8,4,32,128]{4,3,2,1,0:T(8,128)(2,1)S(1)}, u32[]{:S(2)}, u32[]{:S(2)}) collective-permute-start(bf16[4,8,4,32,128]{4,3,2,1,0:T(8,128)(2,1)S(1)} %get-tuple-element.90), channel_id=1, source_target_pairs={{0,1},{1,0},{2,3},{3,2},{4,5},{5,4},{6,7},{7,6},{8,9},{9,8},{10,11... | collective-permute-start | bytes 3145736 | tf_op jit(solution)/shard_map/ppermute | solution.py:69
  58.0 8.8 %collective-permute-start.10 = (bf16[2,4,4,32,128]{4,3,2,1,0:T(8,128)(2,1)S(1)}, bf16[2,4,4,32,128]{4,3,2,1,0:T(8,128)(2,1)S(1)}, u32[]{:S(2)}, u32[]{:S(2)}) collective-permute-start(bf16[2,4,4,32,128]{4,3,2,1,0:T(8,128)(2,1)S(1)} %get-tuple-element.93), channel_id=1, source_target_pairs={{0,2},{1,3},{2,4},{3,5},{4,6},{5,7},{6,0},{7,1},{8,10},{9,11},{10,... | collective-permute-start | bytes 786440 | tf_op jit(solution)/shard_map/ppermute | solution.py:69
  58.8 8.0 %collective-permute-start.11 = (bf16[2,4,4,32,128]{4,3,2,1,0:T(8,128)(2,1)S(1)}, bf16[2,4,4,32,128]{4,3,2,1,0:T(8,128)(2,1)S(1)}, u32[]{:S(2)}, u32[]{:S(2)}) collective-permute-start(bf16[2,4,4,32,128]{4,3,2,1,0:T(8,128)(2,1)S(1)} %get-tuple-element.94), channel_id=1, source_target_pairs={{0,6},{1,7},{2,0},{3,1},{4,2},{5,3},{6,4},{7,5},{8,14},{9,15},{10,... | collective-permute-start | bytes 786440 | tf_op jit(solution)/shard_map/ppermute | solution.py:69
  66.8 8.1 %collective-permute-start.12 = (bf16[4,4,32,128]{3,2,1,0:T(8,128)(2,1)S(1)}, bf16[4,4,32,128]{3,2,1,0:T(8,128)(2,1)S(1)}, u32[]{:S(2)}, u32[]{:S(2)}) collective-permute-start(bf16[4,4,32,128]{3,2,1,0:T(8,128)(2,1)S(1)} %get-tuple-element.97), channel_id=1, source_target_pairs={{0,2},{1,3},{2,4},{3,5},{4,6},{5,7},{6,0},{7,1},{8,10},{9,11},{10,... | collective-permute-start | bytes 393224 | tf_op jit(solution)/shard_map/ppermute | solution.py:69
  67.6 7.3 %collective-permute-start.13 = (bf16[4,4,32,128]{3,2,1,0:T(8,128)(2,1)S(1)}, bf16[4,4,32,128]{3,2,1,0:T(8,128)(2,1)S(1)}, u32[]{:S(2)}, u32[]{:S(2)}) collective-permute-start(bf16[4,4,32,128]{3,2,1,0:T(8,128)(2,1)S(1)} %get-tuple-element.98), channel_id=1, source_target_pairs={{0,6},{1,7},{2,0},{3,1},{4,2},{5,3},{6,4},{7,5},{8,14},{9,15},{10,... | collective-permute-start | bytes 393224 | tf_op jit(solution)/shard_map/ppermute | solution.py:69
  69.8 14.2 %collective-permute-start.17 = (f32[3,4,32,108]{3,2,1,0:T(8,128)S(1)}, f32[3,4,32,108]{3,2,1,0:T(8,128)S(1)}, u32[]{:S(2)}, u32[]{:S(2)}) collective-permute-start(f32[3,4,32,108]{3,2,1,0:T(8,128)S(1)} %pad_maximum_fusion.state_ref), channel_id=1, source_target_pairs={{0,56},{1,57},{2,58},{3,59},{4,60},{5,61},{6,62},{7,63},{8,48},{9,... | collective-permute-start | bytes 497672 | tf_op jit(solution)/shard_map/ppermute | solution.py:69
  75.1 8.9 %collective-permute-start.14 = (bf16[2,4,32,128]{3,2,1,0:T(8,128)(2,1)S(1)}, bf16[2,4,32,128]{3,2,1,0:T(8,128)(2,1)S(1)}, u32[]{:S(2)}, u32[]{:S(2)}) collective-permute-start(bf16[2,4,32,128]{3,2,1,0:T(8,128)(2,1)S(1)} %get-tuple-element.100), channel_id=1, source_target_pairs={{0,24},{1,25},{2,26},{3,27},{4,28},{5,29},{6,30},{7,31},{8,16},{9,... | collective-permute-start | bytes 196616 | tf_op jit(solution)/shard_map/ppermute | solution.py:69
  76.8 7.3 %collective-permute-start.15 = (bf16[2,4,32,128]{3,2,1,0:T(8,128)(2,1)S(1)}, bf16[2,4,32,128]{3,2,1,0:T(8,128)(2,1)S(1)}, u32[]{:S(2)}, u32[]{:S(2)}) collective-permute-start(bf16[2,4,32,128]{3,2,1,0:T(8,128)(2,1)S(1)} %get-tuple-element.101), channel_id=1, source_target_pairs={{0,16},{1,17},{2,18},{3,19},{4,20},{5,21},{6,22},{7,23},{8,24},{9,... | collective-permute-start | bytes 196616 | tf_op jit(solution)/shard_map/ppermute | solution.py:69
  78.0 6.1 %collective-permute-start.16 = (bf16[2,4,32,128]{3,2,1,0:T(8,128)(2,1)S(1)}, bf16[2,4,32,128]{3,2,1,0:T(8,128)(2,1)S(1)}, u32[]{:S(2)}, u32[]{:S(2)}) collective-permute-start(bf16[2,4,32,128]{3,2,1,0:T(8,128)(2,1)S(1)} %get-tuple-element.102), channel_id=1, source_target_pairs={{0,8},{1,9},{2,10},{3,11},{4,12},{5,13},{6,14},{7,15},{8,0},{9,1},... | collective-permute-start | bytes 196616 | tf_op jit(solution)/shard_map/ppermute | solution.py:69
  84.1 4.4 %collective-permute-start.18 = (bf16[2,4,32,128]{3,2,1,0:T(8,128)(2,1)S(1)}, bf16[2,4,32,128]{3,2,1,0:T(8,128)(2,1)S(1)}, u32[]{:S(2)}, u32[]{:S(2)}) collective-permute-start(bf16[2,4,32,128]{3,2,1,0:T(8,128)(2,1)S(1)} %z_sum.1.mine_ref), channel_id=1, source_target_pairs={{0,56},{1,57},{2,58},{3,59},{4,60},{5,61},{6,62},{7,63},{8,48},{9,... | collective-permute-start | bytes 196616 | tf_op jit(solution)/shard_map/ppermute | solution.py:69
  89.2 5.2 %collective-permute-start.19 = (bf16[2,4,32,128]{3,2,1,0:T(8,128)(2,1)S(1)}, bf16[2,4,32,128]{3,2,1,0:T(8,128)(2,1)S(1)}, u32[]{:S(2)}, u32[]{:S(2)}) collective-permute-start(bf16[2,4,32,128]{3,2,1,0:T(8,128)(2,1)S(1)} %get-tuple-element.108), channel_id=1, source_target_pairs={{0,24},{1,25},{2,26},{3,27},{4,28},{5,29},{6,30},{7,31},{8,16},{9,... | collective-permute-start | bytes 196616 | tf_op jit(solution)/shard_map/ppermute | solution.py:69
  90.9 5.9 %collective-permute-start.20 = (bf16[2,4,32,128]{3,2,1,0:T(8,128)(2,1)S(1)}, bf16[2,4,32,128]{3,2,1,0:T(8,128)(2,1)S(1)}, u32[]{:S(2)}, u32[]{:S(2)}) collective-permute-start(bf16[2,4,32,128]{3,2,1,0:T(8,128)(2,1)S(1)} %get-tuple-element.108), channel_id=1, source_target_pairs={{0,16},{1,17},{2,18},{3,19},{4,20},{5,21},{6,22},{7,23},{8,24},{9,... | collective-permute-start | bytes 196616 | tf_op jit(solution)/shard_map/ppermute | solution.py:69
  94.5 3.1 %collective-permute-start.21 = (bf16[2,4,32,128]{3,2,1,0:T(8,128)(2,1)S(1)}, bf16[2,4,32,128]{3,2,1,0:T(8,128)(2,1)S(1)}, u32[]{:S(2)}, u32[]{:S(2)}) collective-permute-start(bf16[2,4,32,128]{3,2,1,0:T(8,128)(2,1)S(1)} %get-tuple-element.108), channel_id=1, source_target_pairs={{0,8},{1,9},{2,10},{3,11},{4,12},{5,13},{6,14},{7,15},{8,0},{9,1},... | collective-permute-start | bytes 196616 | tf_op jit(solution)/shard_map/ppermute | solution.py:69
  97.6 8.0 %collective-permute-start.22 = (bf16[8,4,32,128]{3,2,1,0:T(8,128)(2,1)S(1)}, bf16[8,4,32,128]{3,2,1,0:T(8,128)(2,1)S(1)}, u32[]{:S(2)}, u32[]{:S(2)}) collective-permute-start(bf16[8,4,32,128]{3,2,1,0:T(8,128)(2,1)S(1)} %constant_dynamic-update-slice_fusion), channel_id=1, source_target_pairs={{0,2},{1,3},{2,4},{3,5},{4,6},{5,7},{6,0},{7,1},{8,10},{9,11},{10,... | collective-permute-start | bytes 786440 | tf_op jit(solution)/shard_map/ppermute | solution.py:69
  97.7 16.0 %collective-permute-start.23 = (bf16[8,4,32,128]{3,2,1,0:T(8,128)(2,1)S(1)}, bf16[8,4,32,128]{3,2,1,0:T(8,128)(2,1)S(1)}, u32[]{:S(2)}, u32[]{:S(2)}) collective-permute-start(bf16[8,4,32,128]{3,2,1,0:T(8,128)(2,1)S(1)} %constant_dynamic-update-slice_fusion), channel_id=1, source_target_pairs={{0,6},{1,7},{2,0},{3,1},{4,2},{5,3},{6,4},{7,5},{8,14},{9,15},{10,... | collective-permute-start | bytes 786440 | tf_op jit(solution)/shard_map/ppermute | solution.py:69
  100.4 13.3 %collective-permute-start.24 = (bf16[8,4,32,128]{3,2,1,0:T(8,128)(2,1)S(1)}, bf16[8,4,32,128]{3,2,1,0:T(8,128)(2,1)S(1)}, u32[]{:S(2)}, u32[]{:S(2)}) collective-permute-start(bf16[8,4,32,128]{3,2,1,0:T(8,128)(2,1)S(1)} %constant_dynamic-update-slice_fusion), channel_id=1, source_target_pairs={{0,4},{1,5},{2,6},{3,7},{4,0},{5,1},{6,2},{7,3},{8,12},{9,13},{10,... | collective-permute-start | bytes 786440 | tf_op jit(solution)/shard_map/ppermute | solution.py:69
  100.4 14.0 %collective-permute-start.25 = (bf16[8,4,32,128]{3,2,1,0:T(8,128)(2,1)S(1)}, bf16[8,4,32,128]{3,2,1,0:T(8,128)(2,1)S(1)}, u32[]{:S(2)}, u32[]{:S(2)}) collective-permute-start(bf16[8,4,32,128]{3,2,1,0:T(8,128)(2,1)S(1)} %constant_dynamic-update-slice_fusion), channel_id=1, source_target_pairs={{0,1},{1,0},{2,3},{3,2},{4,5},{5,4},{6,7},{7,6},{8,9},{9,8},{10,11... | collective-permute-start | bytes 786440 | tf_op jit(solution)/shard_map/ppermute | solution.py:69
  105.6 9.2 %collective-permute-start.26 = (bf16[8,4,32,128]{3,2,1,0:T(8,128)(2,1)S(1)}, bf16[8,4,32,128]{3,2,1,0:T(8,128)(2,1)S(1)}, u32[]{:S(2)}, u32[]{:S(2)}) collective-permute-start(bf16[8,4,32,128]{3,2,1,0:T(8,128)(2,1)S(1)} %collective-permute-done.22), channel_id=1, source_target_pairs={{0,1},{1,0},{2,3},{3,2},{4,5},{5,4},{6,7},{7,6},{8,9},{9,8},{10,11... | collective-permute-start | bytes 786440 | tf_op jit(solution)/shard_map/ppermute | solution.py:69
  113.7 1.5 %collective-permute-start.27 = (bf16[8,4,32,128]{3,2,1,0:T(8,128)(2,1)S(1)}, bf16[8,4,32,128]{3,2,1,0:T(8,128)(2,1)S(1)}, u32[]{:S(2)}, u32[]{:S(2)}) collective-permute-start(bf16[8,4,32,128]{3,2,1,0:T(8,128)(2,1)S(1)} %collective-permute-done.23), channel_id=1, source_target_pairs={{0,1},{1,0},{2,3},{3,2},{4,5},{5,4},{6,7},{7,6},{8,9},{9,8},{10,11... | collective-permute-start | bytes 786440 | tf_op jit(solution)/shard_map/ppermute | solution.py:69
  113.7 1.9 %collective-permute-start.28 = (bf16[8,4,32,128]{3,2,1,0:T(8,128)(2,1)S(1)}, bf16[8,4,32,128]{3,2,1,0:T(8,128)(2,1)S(1)}, u32[]{:S(2)}, u32[]{:S(2)}) collective-permute-start(bf16[8,4,32,128]{3,2,1,0:T(8,128)(2,1)S(1)} %collective-permute-done.24), channel_id=1, source_target_pairs={{0,1},{1,0},{2,3},{3,2},{4,5},{5,4},{6,7},{7,6},{8,9},{9,8},{10,11... | collective-permute-start | bytes 786440 | tf_op jit(solution)/shard_map/ppermute | solution.py:69

commit v8 on v6

--- a/solution.py
+++ b/solution.py
@@ -75,16 +75,19 @@
 
 def slice_kernel(db_ref, ua_ref, *refs):
     outs, sems = refs[:4], refs[4]
-    here = lax.axis_index("section")
+    here, core = lax.axis_index("section"), core_pos()
     copies = []
     for k, out in enumerate(outs):
-        columns = pl.ds(pl.multiple_of(lax.rem(here + k, 4) * WIDTH, LANES), WIDTH)
-        for i, ref in enumerate((db_ref, ua_ref)):
-            copies.append(
-                pltpu.make_async_copy(
-                    ref.at[:, columns], out.at[pl.ds(i * RANK, RANK), :], sems.at[2 * k + i]
-                )
+        start = lax.rem(here + k, 4) * WIDTH
+        whole = pl.ds(pl.multiple_of(start, LANES), WIDTH)
+        half = pl.ds(pl.multiple_of(start + core * (WIDTH // 2), LANES), WIDTH // 2)
+        for i, (source, target) in enumerate(
+            (
+                (db_ref.at[:, whole], out.at[:, pl.ds(0, WIDTH)]),
+                (ua_ref.at[:, half], out.at[:, pl.ds(WIDTH, WIDTH // 2)]),
             )
+        ):
+            copies.append(pltpu.make_async_copy(source, target, sems.at[2 * k + i]))
             copies[-1].start()
     for copy in copies:
         copy.wait()
@@ -93,7 +96,7 @@
 def slices(db, ua):
     return pl.pallas_call(
         slice_kernel,
-        out_shape=[shaped((2 * RANK, WIDTH), BF16)] * 4,
+        out_shape=[shaped((RANK, WIDTH + WIDTH // 2), BF16)] * 4,
         in_specs=[HBM] * 2,
         out_specs=[VMEM] * 4,
         scratch_shapes=[pltpu.SemaphoreType.DMA((8,))],
@@ -153,13 +156,15 @@
 
 def share_kernel(g_ref, w0, w1, w2, w3, *outs):
     ws = (w0, w1, w2, w3)
+    half = pl.ds(pl.multiple_of(core_pos() * (WIDTH // 2), LANES), WIDTH // 2)
     for k, out in enumerate(outs):
-        db = ws[k][0:RANK, :]
         out[:, 0:LANES] = lax.dot_general(
-            db, g_ref[...], CONTRACT_LAST, preferred_element_type=F32
+            ws[k][:, 0:WIDTH], g_ref[...], CONTRACT_LAST, preferred_element_type=F32
         )
-        rows = jnp.concatenate([ws[(k - m) % 4][RANK:, :] for m in (1, 2, 3, 0)], axis=0)
-        out[:, LANES:] = lax.dot_general(db, rows, CONTRACT_LAST, preferred_element_type=F32)
+        rows = jnp.concatenate([ws[(k - m) % 4][:, WIDTH:] for m in (1, 2, 3, 0)], axis=0)
+        out[:, LANES:] = lax.dot_general(
+            ws[k][:, half], rows, CONTRACT_LAST, preferred_element_type=F32
+        )
 
 
 def shares(g, ws):
@@ -173,35 +178,38 @@
     )(g, *ws)
 
 
-def low_of(share_refs, above_ref):
-    total = share_refs[0][...] + share_refs[1][...] + share_refs[2][...] + share_refs[3][...]
-    low = total[:, 0:LANES]
-    if above_ref is not None:
-        low = low + jnp.dot(
-            total[:, LANES : LANES + 3 * RANK],
-            above_ref[...].astype(F32),
-            preferred_element_type=F32,
-            precision=lax.Precision.HIGHEST,
-        )
-    return low
-
-
-def relay_kernel(top, *refs):
-    share_refs, refs = refs[:4], refs[4:]
-    above_ref = None
-    if not top:
-        above_ref, refs = refs[0], refs[1:]
-    slope_ref, da_ref, ub_ref, out_ref = refs
-    low = low_of(share_refs, above_ref).T.astype(BF16)
+def low_of(total, other_ref, above_ref):
+    factors = total[:, LANES:] + other_ref[...]
+    return total[:, 0:LANES] + jnp.dot(
+        factors[:, 0 : 3 * RANK],
+        above_ref[...].astype(F32),
+        preferred_element_type=F32,
+        precision=lax.Precision.HIGHEST,
+    )
+
+
+def relay_kernel(top, s0, s1, s2, s3, *refs):
+    total = s0[...] + s1[...] + s2[...] + s3[...]
+    if top:
+        *slope_refs, da_ref, ub_ref, out_ref, part_ref = refs
+        part_ref[...] = total[:, LANES:]
+        low = total[:, 0:LANES]
+    else:
+        other_ref, above_ref, *slope_refs, da_ref, ub_ref, out_ref = refs
+        low = low_of(total, other_ref, above_ref)
+    low = low.T.astype(BF16)
     total = jnp.zeros((RANK, TOKENS), F32)
-
-    for start in range(0, FF, 768):
-        columns = slice(start, start + 768)
-        upstream = jnp.dot(low, da_ref[:, columns], preferred_element_type=F32)
-        delta = (upstream * slope_ref[:, columns].astype(F32)).astype(BF16)
-        total = total + lax.dot_general(
-            ub_ref[:, columns], delta, CONTRACT_LAST, preferred_element_type=F32
-        )
+    start = 0
+    for slope_ref in slope_refs:
+        for first in range(0, slope_ref.shape[1], 768):
+            columns = slice(start, start + 768)
+            upstream = jnp.dot(low, da_ref[:, columns], preferred_element_type=F32)
+            slope = slope_ref[:, first : first + 768].astype(F32)
+            delta = (upstream * slope).astype(BF16)
+            total = total + lax.dot_general(
+                ub_ref[:, columns], delta, CONTRACT_LAST, preferred_element_type=F32
+            )
+            start += 768
     out_ref[0:RANK, :] = (0.5 * total).astype(BF16)
     if top:
         out_ref[RANK:, :] = jnp.zeros((2 * RANK, LANES), BF16)
@@ -210,19 +218,21 @@
 
 
 def relay(share, above, slope, da, ub):
-    first = above is None
-    return pl.pallas_call(
-        functools.partial(relay_kernel, first),
-        out_shape=shaped((3 * RANK, LANES), BF16),
-        in_specs=[VMEM] * (7 if first else 8),
-        out_specs=VMEM,
+    message = shaped((3 * RANK, LANES), BF16)
+    top = not above
+    return pl.pallas_call(
+        functools.partial(relay_kernel, top),
+        out_shape=[message, shaped((RANK, LANES), F32)] if top else message,
+        in_specs=[VMEM] * (8 + len(above)),
+        out_specs=[VMEM] * 2 if top else VMEM,
         compiler_params=params(14),
-        name="relay_first" if first else "relay",
-    )(*share, *([] if first else [above]), slope, da, ub)
-
-
-def grad_kernel(s0, s1, s2, s3, above_ref, h0, h1, h2, h3, keep_ref, send_ref, grad):
-    low = low_of((s0, s1, s2, s3), above_ref).astype(BF16)
+        name="relay_first" if top else "relay",
+    )(*share, *above, *slope, da, ub)
+
+
+def grad_kernel(s0, s1, s2, s3, other_ref, above_ref, h0, h1, h2, h3, keep_ref, send_ref, grad):
+    total = s0[...] + s1[...] + s2[...] + s3[...]
+    low = low_of(total, other_ref, above_ref).astype(BF16)
     core = core_pos()
     lane = lax.broadcasted_iota(jnp.int32, (RANK, LANES), 1)
     for bucket, hidden_ref in enumerate((h0, h1, h2, h3)):
@@ -250,12 +260,12 @@
     return pl.pallas_call(
         grad_kernel,
         out_shape=[shaped((YS, ZS, BUCKETS, RANK, LANES), BF16)] * 2,
-        in_specs=[VMEM] * 9,
+        in_specs=[VMEM] * 10,
         out_specs=[VMEM] * 2,
         scratch_shapes=[pltpu.VMEM((RANK, BUCKET_ROWS), F32)],
         compiler_params=params(14),
         name="grads",
-    )(*share, above, *hidden)
+    )(*share, *above, *hidden)
 
 
 def core_sum_kernel(keep_ref, got_ref, own_ref, up_ref, down_ref, up_held, down_held):
@@ -438,18 +448,21 @@
     mine = slices(down_b[0], up_a[0].T)
     ws = [mine[0]] + [over_section(mine[k], k) for k in (1, 3, 2)]
     pre = pre_act[0]
-    slope = activation(pre, True, 0, BUCKETS)
+    slope = activation(pre, True, 0, 3)
     ws, slope = lax.optimization_barrier((ws, slope))
     share = shares(out_grad, [ws[0], ws[1], ws[3], ws[2]])
     pre, _ = lax.optimization_barrier((pre, share[0]))
-    hidden = [activation(pre, False, 0)]
+    slope = [slope, activation(pre, True, 3)]
     share = [share[0]] + [over_section(share[k], -k) for k in (1, 3, 2)]
     state = jnp.stack([a[0].transpose(0, 2, 1) for a in (master, moment, second)])
-    *share, first_hidden = lax.optimization_barrier((*share, hidden[0]))
-    above, hidden = None, [first_hidden]
-    for buckets in ((1, 2), (3,), ()):
-        sent = relay(share, above, slope, da, ub)
-        above = lax.ppermute(sent, "section", [(1, 0), (2, 1), (3, 2)])
+    above, hidden = [], []
+    for buckets in ((0, 1), (2, 3), ()):
+        if above:
+            sent = relay(share, above, slope, da, ub)
+        else:
+            sent, part = relay(share, above, slope, da, ub)
+            above = [over_dp(part, dc=1)]
+        above = [above[0], lax.ppermute(sent, "section", [(1, 0), (2, 1), (3, 2)])]
         if buckets:
             pre, _ = lax.optimization_barrier((pre, sent))
             hidden += [activation(pre, False, b) for b in buckets]

time: 115 us -> 115 us (level)
  waiting for transfers between devices: 25.7 us -> 24.3 us
    pallas_call x5 -> x6, Pallas kernels: 14.1 us -> 15.2 us  [activation(): pl.pallas_call(functools.partial(activation_kernel, slope, bucket * BUCKE...]
    ppermute x20 -> x21, waiting for transfers between devices: 19.6 us -> 19.3 us  [over_dp(): return lax.ppermute(value, 'dp', pairs)]
    ppermute x20 -> x21, starting transfers between devices: 42.2 us -> 42.1 us  [over_dp(): return lax.ppermute(value, 'dp', pairs)]
  transfers between devices with their start and end apart: 29 -> 30, of which waited for: 14 -> 13; matrix products, arithmetic and copies ran while one was open for 0% -> 0% of each run, Pallas kernels for 12% -> 13%
where the time goes in v8:
time: 115 us; the launch traced here: 114 us
  starting transfers between devices  54.2 us (47%)
  Pallas kernels  34.7 us (30%)
  waiting for transfers between devices  24.3 us (21%)
    ppermute x21, starting transfers between devices, over_dp(): return lax.ppermute(value, 'dp', pairs)  42.1 us
    ppermute x21, waiting for transfers between devices, over_dp(): return lax.ppermute(value, 'dp', pairs)  19.3 us
    pallas_call x6, Pallas kernels, activation(): pl.pallas_call(functools.partial(activation_kernel, slope, bucket * BUCKE...  15.2 us
    pallas_call x3, Pallas kernels, relay(): pl.pallas_call(functools.partial(relay_kernel, top), out_shape=[message,...  12.5 us
    ppermute x6, starting transfers between devices, over_section(): lax.ppermute(value, 'section', [(i, (i + steps) % 4) for i in range(4)])  8 us
    ppermute x3, waiting for transfers between devices, per_device(): above = [above[0], lax.ppermute(sent, 'section', [(1, 0), (2, 1), (3, 2)])]  4.55 us
    ppermute x3, starting transfers between devices, per_device(): above = [above[0], lax.ppermute(sent, 'section', [(1, 0), (2, 1), (3, 2)])]  4.07 us
    pallas_call x1, Pallas kernels, assemble(): pl.pallas_call(assemble_kernel, out_shape=shaped((RANK, FF), BF16), in_sp...  2.48 us
  transfers between devices with their start and end apart: 30, of which 13 were waited for; matrix products, arithmetic and copies ran while one was open for 0% of the time, Pallas kernels for 13%

profile of v8, /device:TPU:1, one launch (start us, length us, event | category | flops | bytes accessed | tf_op | source)
XLA Modules:
  0.0 114.4 jit_solution(661779060841261926)
XLA Ops:
  0.6 1.2 %slices.1 = (bf16[32,1920]{1,0:T(8,128)(2,1)S(1)}, bf16[32,1920]{1,0:T(8,128)(2,1)S(1)}, bf16[32,1920]{1,0:T(8,128)(2,1)S(1)}, bf16[32,1920]{1,0:T(8,128)(2,1)S(1)}) custom-call(bf16[32,5120]{1,0:T(8,128)(2,1)} %bitcast.51, bf16[32,5120]{1,0:T(8,128)(2,1)} %bitcast.52), custom_call_target="tpu_custom_call" | custom-call | tf_op jit(solution)/shard_map/slices/pallas_call | solution.py:97
  1.8 2.1 %collective-permute-start = (bf16[32,1920]{1,0:T(8,128)(2,1)S(1)}, bf16[32,1920]{1,0:T(8,128)(2,1)S(1)}, u32[]{:S(2)}, u32[]{:S(2)}) collective-permute-start(bf16[32,1920]{1,0:T(8,128)(2,1)S(1)} %get-tuple-element.56), channel_id=1, source_target_pairs={{0,64},{64,128},{128,192},{192,0},{1,65},{65,129},{129,193},{193,1... | collective-permute-start | bytes 368648 | tf_op jit(solution)/shard_map/ppermute | solution.py:73
  3.9 1.4 %collective-permute-start.1 = (bf16[32,1920]{1,0:T(8,128)(2,1)S(1)}, bf16[32,1920]{1,0:T(8,128)(2,1)S(1)}, u32[]{:S(2)}, u32[]{:S(2)}) collective-permute-start(bf16[32,1920]{1,0:T(8,128)(2,1)S(1)} %get-tuple-element.57), channel_id=1, source_target_pairs={{0,192},{64,0},{128,64},{192,128},{1,193},{65,1},{129,65},{193,129... | collective-permute-start | bytes 368648 | tf_op jit(solution)/shard_map/ppermute | solution.py:73
  5.3 1.6 %collective-permute-start.2 = (bf16[32,1920]{1,0:T(8,128)(2,1)S(1)}, bf16[32,1920]{1,0:T(8,128)(2,1)S(1)}, u32[]{:S(2)}, u32[]{:S(2)}) collective-permute-start(bf16[32,1920]{1,0:T(8,128)(2,1)S(1)} %get-tuple-element.58), channel_id=1, source_target_pairs={{0,128},{64,192},{128,0},{192,64},{1,129},{65,193},{129,1},{193,65... | collective-permute-start | bytes 368648 | tf_op jit(solution)/shard_map/ppermute | solution.py:73
  6.9 5.0 %slope.2.refs_0_.refs_2_ = bf16[128,20736]{1,0:T(8,128)(2,1)S(1)} custom-call(bf16[128,27648]{1,0:T(8,128)(2,1)} %bitcast.44), custom_call_target="tpu_custom_call" | custom-call | flops 26542080 | bytes 10616832 | tf_op jit(solution)/shard_map/slope/pallas_call | solution.py:138
  11.9 0.0 collective-permute-done.1.w3
  11.9 0.0 collective-permute-done.2.w2
  12.0 0.7 shares.1
  12.7 1.6 %collective-permute-start.3 = (f32[32,256]{1,0:T(8,128)S(1)}, f32[32,256]{1,0:T(8,128)S(1)}, u32[]{:S(2)}, u32[]{:S(2)}) collective-permute-start(f32[32,256]{1,0:T(8,128)S(1)} %get-tuple-element.64), channel_id=1, source_target_pairs={{0,192},{64,0},{128,64},{192,128},{1,193},{65,1},{129,65},{193,129... | collective-permute-start | bytes 98312 | tf_op jit(solution)/shard_map/ppermute | solution.py:73
  14.3 0.0 collective-permute-start.4
  14.3 1.3 %collective-permute-start.5 = (f32[32,256]{1,0:T(8,128)S(1)}, f32[32,256]{1,0:T(8,128)S(1)}, u32[]{:S(2)}, u32[]{:S(2)}) collective-permute-start(f32[32,256]{1,0:T(8,128)S(1)} %get-tuple-element.66), channel_id=1, source_target_pairs={{0,128},{64,192},{128,0},{192,64},{1,129},{65,193},{129,1},{193,65... | collective-permute-start | bytes 98312 | tf_op jit(solution)/shard_map/ppermute | solution.py:73
  15.6 2.5 %slope.3.refs_1_.refs_3_ = bf16[128,6912]{1,0:T(8,128)(2,1)S(1)} custom-call(bf16[128,27648]{1,0:T(8,128)(2,1)} %bitcast.45), custom_call_target="tpu_custom_call" | custom-call | flops 8847360 | bytes 3538944 | tf_op jit(solution)/shard_map/slope/pallas_call | solution.py:138
  18.1 0.2 collective-permute-done.4.s2
  18.3 0.3 collective-permute-done.5.s3
  18.7 0.0 copy-start.5
  18.7 4.1 %relay_first.1 = (bf16[96,128]{1,0:T(8,128)(2,1)S(1)}, f32[32,128]{1,0:T(8,128)S(1)}) custom-call(f32[32,256]{1,0:T(8,128)S(1)} %get-tuple-element.63.s0, f32[32,256]{1,0:T(8,128)S(1)} %collective-permute-done.3.s1, f32[32,256]{1,0:T(8,128)S(1)} %collective-permute-done.4.s2, f32[32,256]{1,0:T(8,128)S(1)} %collective-permute-done.5.s3, ...), custom_call_target="tpu_custom_call" | custom-call | tf_op jit(solution)/shard_map/relay_first/pallas_call | solution.py:223
  22.8 4.4 %collective-permute-start.6 = (f32[32,128]{1,0:T(8,128)S(1)}, f32[32,128]{1,0:T(8,128)S(1)}, u32[]{:S(2)}, u32[]{:S(2)}) collective-permute-start(f32[32,128]{1,0:T(8,128)S(1)} %get-tuple-element.69), channel_id=1, source_target_pairs={{0,1},{1,0},{2,3},{3,2},{4,5},{5,4},{6,7},{7,6},{8,9},{9,8},{10,11... | collective-permute-start | bytes 49160 | tf_op jit(solution)/shard_map/ppermute | solution.py:69
  27.1 1.5 %collective-permute-start.7 = (bf16[96,128]{1,0:T(8,128)(2,1)S(1)}, bf16[96,128]{1,0:T(8,128)(2,1)S(1)}, u32[]{:S(2)}, u32[]{:S(2)}) collective-permute-start(bf16[96,128]{1,0:T(8,128)(2,1)S(1)} %get-tuple-element.70), channel_id=1, source_target_pairs={{64,0},{128,64},{192,128},{65,1},{129,65},{193,129},{66,2},{130,66... | collective-permute-start | bytes 73736 | tf_op jit(solution)/shard_map/ppermute | solution.py:465
  28.7 1.9 %hidden.5.h1 = bf16[128,6912]{1,0:T(8,128)(2,1)S(1)} custom-call(bf16[128,27648]{1,0:T(8,128)(2,1)} %bitcast.46), custom_call_target="tpu_custom_call" | custom-call | flops 8847360 | bytes 3538944 | tf_op jit(solution)/shard_map/hidden/pallas_call | solution.py:138
  30.6 1.9 %hidden.4.h0 = bf16[128,6912]{1,0:T(8,128)(2,1)S(1)} custom-call(bf16[128,27648]{1,0:T(8,128)(2,1)} %bitcast.47), custom_call_target="tpu_custom_call" | custom-call | flops 8847360 | bytes 3538944 | tf_op jit(solution)/shard_map/hidden/pallas_call | solution.py:138
  32.5 0.0 collective-permute-done.6.refs_0_.other_ref
  32.5 0.0 collective-permute-done.7.refs_1_
  32.6 4.2 %relay.2 = bf16[96,128]{1,0:T(8,128)(2,1)S(1)} custom-call(f32[32,256]{1,0:T(8,128)S(1)} %get-tuple-element.63.s0, f32[32,256]{1,0:T(8,128)S(1)} %collective-permute-done.3.s1, f32[32,256]{1,0:T(8,128)S(1)} %collective-permute-done.4.s2, f32[32,256]{1,0:T(8,128)S(1)} %collective-permute-done.5.s3, f32[32,128]{1,0:T(8,128)S(1)} %collective-permute-done.6.refs_0_.other_ref, ...), custom_call_target="tpu_custom_call" | custom-call | tf_op jit(solution)/shard_map/relay/pallas_call | solution.py:223
  36.8 1.3 %collective-permute-start.8 = (bf16[96,128]{1,0:T(8,128)(2,1)S(1)}, bf16[96,128]{1,0:T(8,128)(2,1)S(1)}, u32[]{:S(2)}, u32[]{:S(2)}) collective-permute-start(bf16[96,128]{1,0:T(8,128)(2,1)S(1)} %relay.2), channel_id=1, source_target_pairs={{64,0},{128,64},{192,128},{65,1},{129,65},{193,129},{66,2},{130,66... | collective-permute-start | bytes 73736 | tf_op jit(solution)/shard_map/ppermute | solution.py:465
  38.1 1.9 %hidden.7.h3 = bf16[128,6912]{1,0:T(8,128)(2,1)S(1)} custom-call(bf16[128,27648]{1,0:T(8,128)(2,1)} %bitcast.48), custom_call_target="tpu_custom_call" | custom-call | flops 8847360 | bytes 3538944 | tf_op jit(solution)/shard_map/hidden/pallas_call | solution.py:138
  40.0 1.9 %hidden.6.h2 = bf16[128,6912]{1,0:T(8,128)(2,1)S(1)} custom-call(bf16[128,27648]{1,0:T(8,128)(2,1)} %bitcast.49), custom_call_target="tpu_custom_call" | custom-call | flops 8847360 | bytes 3538944 | tf_op jit(solution)/shard_map/hidden/pallas_call | solution.py:138
  42.0 0.0 collective-permute-done.8.refs_1_
  42.0 4.2 %relay.3 = bf16[96,128]{1,0:T(8,128)(2,1)S(1)} custom-call(f32[32,256]{1,0:T(8,128)S(1)} %get-tuple-element.63.s0, f32[32,256]{1,0:T(8,128)S(1)} %collective-permute-done.3.s1, f32[32,256]{1,0:T(8,128)S(1)} %collective-permute-done.4.s2, f32[32,256]{1,0:T(8,128)S(1)} %collective-permute-done.5.s3, f32[32,128]{1,0:T(8,128)S(1)} %collective-permute-done.6.refs_0_.other_ref, ...), custom_call_target="tpu_custom_call" | custom-call | tf_op jit(solution)/shard_map/relay/pallas_call | solution.py:223
  46.2 1.3 %collective-permute-start.9 = (bf16[96,128]{1,0:T(8,128)(2,1)S(1)}, bf16[96,128]{1,0:T(8,128)(2,1)S(1)}, u32[]{:S(2)}, u32[]{:S(2)}) collective-permute-start(bf16[96,128]{1,0:T(8,128)(2,1)S(1)} %relay.3), channel_id=1, source_target_pairs={{64,0},{128,64},{192,128},{65,1},{129,65},{193,129},{66,2},{130,66... | collective-permute-start | bytes 73736 | tf_op jit(solution)/shard_map/ppermute | solution.py:465
  47.5 4.5 %collective-permute-done.9.above_ref = bf16[96,128]{1,0:T(8,128)(2,1)S(1)} collective-permute-done((bf16[96,128]{1,0:T(8,128)(2,1)S(1)}, bf16[96,128]{1,0:T(8,128)(2,1)S(1)}, u32[]{:S(2)}, u32[]{:S(2)}) %collective-permute-start.9) | collective-permute-done | bytes 24608 | tf_op jit(solution)/shard_map/ppermute | solution.py:465
  52.0 1.4 %grads.1 = (bf16[4,8,4,32,128]{4,3,2,1,0:T(8,128)(2,1)S(1)}, bf16[4,8,4,32,128]{4,3,2,1,0:T(8,128)(2,1)S(1)}) custom-call(f32[32,256]{1,0:T(8,128)S(1)} %get-tuple-element.63.s0, f32[32,256]{1,0:T(8,128)S(1)} %collective-permute-done.3.s1, f32[32,256]{1,0:T(8,128)S(1)} %collective-permute-done.4.s2, f32[32,256]{1,0:T(8,128)S(1)} %collective-permute-done.5.s3, ...), custom_call_target="tpu_custom_call" | custom-call | tf_op jit(solution)/shard_map/grads/pallas_call | solution.py:260
  53.4 1.3 %collective-permute-start.10 = (bf16[4,8,4,32,128]{4,3,2,1,0:T(8,128)(2,1)S(1)}, bf16[4,8,4,32,128]{4,3,2,1,0:T(8,128)(2,1)S(1)}, u32[]{:S(2)}, u32[]{:S(2)}) collective-permute-start(bf16[4,8,4,32,128]{4,3,2,1,0:T(8,128)(2,1)S(1)} %get-tuple-element.86), channel_id=1, source_target_pairs={{0,1},{1,0},{2,3},{3,2},{4,5},{5,4},{6,7},{7,6},{8,9},{9,8},{10,11... | collective-permute-start | bytes 3145736 | tf_op jit(solution)/shard_map/ppermute | solution.py:69
  54.7 2.3 %collective-permute-done.10.got_ref = bf16[4,8,4,32,128]{4,3,2,1,0:T(8,128)(2,1)S(1)} collective-permute-done((bf16[4,8,4,32,128]{4,3,2,1,0:T(8,128)(2,1)S(1)}, bf16[4,8,4,32,128]{4,3,2,1,0:T(8,128)(2,1)S(1)}, u32[]{:S(2)}, u32[]{:S(2)}) %collective-permute-start.10) | collective-permute-done | bytes 1048608 | tf_op jit(solution)/shard_map/ppermute | solution.py:69
  57.0 0.2 core_sum.1
  57.2 0.1 collective-permute-start.11
  57.3 2.7 %collective-permute-start.12 = (bf16[2,4,4,32,128]{4,3,2,1,0:T(8,128)(2,1)S(1)}, bf16[2,4,4,32,128]{4,3,2,1,0:T(8,128)(2,1)S(1)}, u32[]{:S(2)}, u32[]{:S(2)}) collective-permute-start(bf16[2,4,4,32,128]{4,3,2,1,0:T(8,128)(2,1)S(1)} %get-tuple-element.90), channel_id=1, source_target_pairs={{0,6},{1,7},{2,0},{3,1},{4,2},{5,3},{6,4},{7,5},{8,14},{9,15},{10,... | collective-permute-start | bytes 786440 | tf_op jit(solution)/shard_map/ppermute | solution.py:69
  60.0 4.7 %collective-permute-start.14 = (f32[3,4,32,108]{3,2,1,0:T(8,128)S(1)}, f32[3,4,32,108]{3,2,1,0:T(8,128)S(1)}, u32[]{:S(2)}, u32[]{:S(2)}) collective-permute-start(f32[3,4,32,108]{3,2,1,0:T(8,128)S(1)} %pad_maximum_fusion.state_ref), channel_id=1, source_target_pairs={{0,56},{1,57},{2,58},{3,59},{4,60},{5,61},{6,62},{7,63},{8,48},{9,... | collective-permute-start | bytes 497672 | tf_op jit(solution)/shard_map/ppermute | solution.py:69
  64.6 1.4 %collective-permute-done.11.from_below = bf16[2,4,4,32,128]{4,3,2,1,0:T(8,128)(2,1)S(1)} collective-permute-done((bf16[2,4,4,32,128]{4,3,2,1,0:T(8,128)(2,1)S(1)}, bf16[2,4,4,32,128]{4,3,2,1,0:T(8,128)(2,1)S(1)}, u32[]{:S(2)}, u32[]{:S(2)}) %collective-permute-start.11) | collective-permute-done | bytes 262176 | tf_op jit(solution)/shard_map/ppermute | solution.py:69
  66.1 0.1 collective-permute-start.13
  66.2 2.7 %collective-permute-start.15 = (bf16[4,4,32,128]{3,2,1,0:T(8,128)(2,1)S(1)}, bf16[4,4,32,128]{3,2,1,0:T(8,128)(2,1)S(1)}, u32[]{:S(2)}, u32[]{:S(2)}) collective-permute-start(bf16[4,4,32,128]{3,2,1,0:T(8,128)(2,1)S(1)} %get-tuple-element.96), channel_id=1, source_target_pairs={{0,6},{1,7},{2,0},{3,1},{4,2},{5,3},{6,4},{7,5},{8,14},{9,15},{10,... | collective-permute-start | bytes 393224 | tf_op jit(solution)/shard_map/ppermute | solution.py:69
  68.8 5.0 %collective-permute-done.14.partner_ref = f32[3,4,32,108]{3,2,1,0:T(8,128)S(1)} collective-permute-done((f32[3,4,32,108]{3,2,1,0:T(8,128)S(1)}, f32[3,4,32,108]{3,2,1,0:T(8,128)S(1)}, u32[]{:S(2)}, u32[]{:S(2)}) %collective-permute-start.14) | collective-permute-done | bytes 165920 | tf_op jit(solution)/shard_map/ppermute | solution.py:69
  73.8 0.1 y_sum.1
  73.9 1.7 %collective-permute-start.16 = (bf16[2,4,32,128]{3,2,1,0:T(8,128)(2,1)S(1)}, bf16[2,4,32,128]{3,2,1,0:T(8,128)(2,1)S(1)}, u32[]{:S(2)}, u32[]{:S(2)}) collective-permute-start(bf16[2,4,32,128]{3,2,1,0:T(8,128)(2,1)S(1)} %get-tuple-element.98), channel_id=1, source_target_pairs={{0,24},{1,25},{2,26},{3,27},{4,28},{5,29},{6,30},{7,31},{8,16},{9,... | collective-permute-start | bytes 196616 | tf_op jit(solution)/shard_map/ppermute | solution.py:69
  75.6 1.9 %collective-permute-start.18 = (bf16[2,4,32,128]{3,2,1,0:T(8,128)(2,1)S(1)}, bf16[2,4,32,128]{3,2,1,0:T(8,128)(2,1)S(1)}, u32[]{:S(2)}, u32[]{:S(2)}) collective-permute-start(bf16[2,4,32,128]{3,2,1,0:T(8,128)(2,1)S(1)} %get-tuple-element.100), channel_id=1, source_target_pairs={{0,8},{1,9},{2,10},{3,11},{4,12},{5,13},{6,14},{7,15},{8,0},{9,1},... | collective-permute-start | bytes 196616 | tf_op jit(solution)/shard_map/ppermute | solution.py:69
  77.6 1.4 %collective-permute-done.16.g1 = bf16[2,4,32,128]{3,2,1,0:T(8,128)(2,1)S(1)} collective-permute-done((bf16[2,4,32,128]{3,2,1,0:T(8,128)(2,1)S(1)}, bf16[2,4,32,128]{3,2,1,0:T(8,128)(2,1)S(1)}, u32[]{:S(2)}, u32[]{:S(2)}) %collective-permute-start.16) | collective-permute-done | bytes 65568 | tf_op jit(solution)/shard_map/ppermute | solution.py:69
  79.0 2.5 %collective-permute-done.17.g2 = bf16[2,4,32,128]{3,2,1,0:T(8,128)(2,1)S(1)} collective-permute-done((bf16[2,4,32,128]{3,2,1,0:T(8,128)(2,1)S(1)}, bf16[2,4,32,128]{3,2,1,0:T(8,128)(2,1)S(1)}, u32[]{:S(2)}, u32[]{:S(2)}) %collective-permute-start.17) | collective-permute-done | bytes 65568 | tf_op jit(solution)/shard_map/ppermute | solution.py:69
  81.5 3.4 %collective-permute-start.19 = (bf16[2,4,32,128]{3,2,1,0:T(8,128)(2,1)S(1)}, bf16[2,4,32,128]{3,2,1,0:T(8,128)(2,1)S(1)}, u32[]{:S(2)}, u32[]{:S(2)}) collective-permute-start(bf16[2,4,32,128]{3,2,1,0:T(8,128)(2,1)S(1)} %z_sum.1.mine_ref), channel_id=1, source_target_pairs={{0,56},{1,57},{2,58},{3,59},{4,60},{5,61},{6,62},{7,63},{8,48},{9,... | collective-permute-start | bytes 196616 | tf_op jit(solution)/shard_map/ppermute | solution.py:69
  84.9 2.4 %collective-permute-done.19.got_ref = bf16[2,4,32,128]{3,2,1,0:T(8,128)(2,1)S(1)} collective-permute-done((bf16[2,4,32,128]{3,2,1,0:T(8,128)(2,1)S(1)}, bf16[2,4,32,128]{3,2,1,0:T(8,128)(2,1)S(1)}, u32[]{:S(2)}, u32[]{:S(2)}) %collective-permute-start.19) | collective-permute-done | bytes 65568 | tf_op jit(solution)/shard_map/ppermute | solution.py:69
  87.2 0.7 adamw.1
  88.0 1.7 %collective-permute-start.22 = (bf16[2,4,32,128]{3,2,1,0:T(8,128)(2,1)S(1)}, bf16[2,4,32,128]{3,2,1,0:T(8,128)(2,1)S(1)}, u32[]{:S(2)}, u32[]{:S(2)}) collective-permute-start(bf16[2,4,32,128]{3,2,1,0:T(8,128)(2,1)S(1)} %get-tuple-element.102), channel_id=1, source_target_pairs={{0,24},{1,25},{2,26},{3,27},{4,28},{5,29},{6,30},{7,31},{8,16},{9,... | collective-permute-start | bytes 196616 | tf_op jit(solution)/shard_map/ppermute | solution.py:69
  89.7 0.1 collective-permute-start.21
  89.8 1.7 %collective-permute-start.20 = (bf16[2,4,32,128]{3,2,1,0:T(8,128)(2,1)S(1)}, bf16[2,4,32,128]{3,2,1,0:T(8,128)(2,1)S(1)}, u32[]{:S(2)}, u32[]{:S(2)}) collective-permute-start(bf16[2,4,32,128]{3,2,1,0:T(8,128)(2,1)S(1)} %get-tuple-element.102), channel_id=1, source_target_pairs={{0,8},{1,9},{2,10},{3,11},{4,12},{5,13},{6,14},{7,15},{8,0},{9,1},... | collective-permute-start | bytes 196616 | tf_op jit(solution)/shard_map/ppermute | solution.py:69
  91.5 2.1 %collective-permute-done.20 = bf16[2,4,32,128]{3,2,1,0:T(8,128)(2,1)S(1)} collective-permute-done((bf16[2,4,32,128]{3,2,1,0:T(8,128)(2,1)S(1)}, bf16[2,4,32,128]{3,2,1,0:T(8,128)(2,1)S(1)}, u32[]{:S(2)}, u32[]{:S(2)}) %collective-permute-start.20) | collective-permute-done | bytes 65568 | tf_op jit(solution)/shard_map/ppermute | solution.py:69
  93.7 1.1 collective-permute-done.21
  94.8 0.0 collective-permute-done.22
  94.8 0.1 collective-permute-start.25
  94.9 2.7 %collective-permute-start.24 = (bf16[8,4,32,128]{3,2,1,0:T(8,128)(2,1)S(1)}, bf16[8,4,32,128]{3,2,1,0:T(8,128)(2,1)S(1)}, u32[]{:S(2)}, u32[]{:S(2)}) collective-permute-start(bf16[8,4,32,128]{3,2,1,0:T(8,128)(2,1)S(1)} %constant_dynamic-update-slice_fusion.refs_0_), channel_id=1, source_target_pairs={{0,6},{1,7},{2,0},{3,1},{4,2},{5,3},{6,4},{7,5},{8,14},{9,15},{10,... | collective-permute-start | bytes 786440 | tf_op jit(solution)/shard_map/ppermute | solution.py:69
  97.5 5.5 %collective-permute-start.26 = (bf16[8,4,32,128]{3,2,1,0:T(8,128)(2,1)S(1)}, bf16[8,4,32,128]{3,2,1,0:T(8,128)(2,1)S(1)}, u32[]{:S(2)}, u32[]{:S(2)}) collective-permute-start(bf16[8,4,32,128]{3,2,1,0:T(8,128)(2,1)S(1)} %constant_dynamic-update-slice_fusion.refs_0_), channel_id=1, source_target_pairs={{0,1},{1,0},{2,3},{3,2},{4,5},{5,4},{6,7},{7,6},{8,9},{9,8},{10,11... | collective-permute-start | bytes 786440 | tf_op jit(solution)/shard_map/ppermute | solution.py:69
  103.1 4.7 %collective-permute-start.29 = (bf16[8,4,32,128]{3,2,1,0:T(8,128)(2,1)S(1)}, bf16[8,4,32,128]{3,2,1,0:T(8,128)(2,1)S(1)}, u32[]{:S(2)}, u32[]{:S(2)}) collective-permute-start(bf16[8,4,32,128]{3,2,1,0:T(8,128)(2,1)S(1)} %collective-permute-done.25.refs_3_), channel_id=1, source_target_pairs={{0,1},{1,0},{2,3},{3,2},{4,5},{5,4},{6,7},{7,6},{8,9},{9,8},{10,11... | collective-permute-start | bytes 786440 | tf_op jit(solution)/shard_map/ppermute | solution.py:69
  107.8 1.9 %collective-permute-start.28 = (bf16[8,4,32,128]{3,2,1,0:T(8,128)(2,1)S(1)}, bf16[8,4,32,128]{3,2,1,0:T(8,128)(2,1)S(1)}, u32[]{:S(2)}, u32[]{:S(2)}) collective-permute-start(bf16[8,4,32,128]{3,2,1,0:T(8,128)(2,1)S(1)} %collective-permute-done.24.refs_2_), channel_id=1, source_target_pairs={{0,1},{1,0},{2,3},{3,2},{4,5},{5,4},{6,7},{7,6},{8,9},{9,8},{10,11... | collective-permute-start | bytes 786440 | tf_op jit(solution)/shard_map/ppermute | solution.py:69
  109.7 0.9 collective-permute-start.27
  110.6 0.3 collective-permute-done.28.refs_6_
  110.8 0.9 collective-permute-done.27.refs_5_
  111.7 2.5 %assemble.1 = bf16[32,27648]{1,0:T(8,128)(2,1)} custom-call(bf16[8,4,32,128]{3,2,1,0:T(8,128)(2,1)S(1)} %constant_dynamic-update-slice_fusion.refs_0_, bf16[8,4,32,128]{3,2,1,0:T(8,128)(2,1)S(1)} %collective-permute-done.23.refs_1_, bf16[8,4,32,128]{3,2,1,0:T(8,128)(2,1)S(1)} %collective-permute-done.24.refs_2_, ...), custom_call_target="tpu_custom_call" | custom-call | tf_op jit(solution)/shard_map/assemble/pallas_call | solution.py:432
  (31 shorter events, 0.2 us)
Async XLA Ops:
  1.8 10.1 %collective-permute-start = (bf16[32,1920]{1,0:T(8,128)(2,1)S(1)}, bf16[32,1920]{1,0:T(8,128)(2,1)S(1)}, u32[]{:S(2)}, u32[]{:S(2)}) collective-permute-start(bf16[32,1920]{1,0:T(8,128)(2,1)S(1)} %get-tuple-element.56), channel_id=1, source_target_pairs={{0,64},{64,128},{128,192},{192,0},{1,65},{65,129},{129,193},{193,1... | collective-permute-start | bytes 368648 | tf_op jit(solution)/shard_map/ppermute | solution.py:73
  3.9 8.0 %collective-permute-start.1 = (bf16[32,1920]{1,0:T(8,128)(2,1)S(1)}, bf16[32,1920]{1,0:T(8,128)(2,1)S(1)}, u32[]{:S(2)}, u32[]{:S(2)}) collective-permute-start(bf16[32,1920]{1,0:T(8,128)(2,1)S(1)} %get-tuple-element.57), channel_id=1, source_target_pairs={{0,192},{64,0},{128,64},{192,128},{1,193},{65,1},{129,65},{193,129... | collective-permute-start | bytes 368648 | tf_op jit(solution)/shard_map/ppermute | solution.py:73
  5.3 6.7 %collective-permute-start.2 = (bf16[32,1920]{1,0:T(8,128)(2,1)S(1)}, bf16[32,1920]{1,0:T(8,128)(2,1)S(1)}, u32[]{:S(2)}, u32[]{:S(2)}) collective-permute-start(bf16[32,1920]{1,0:T(8,128)(2,1)S(1)} %get-tuple-element.58), channel_id=1, source_target_pairs={{0,128},{64,192},{128,0},{192,64},{1,129},{65,193},{129,1},{193,65... | collective-permute-start | bytes 368648 | tf_op jit(solution)/shard_map/ppermute | solution.py:73
  6.9 5.0 %copy-start.2 = (bf16[128,1280]{1,0:T(8,128)(2,1)S(1)}, bf16[128,1280]{1,0:T(8,128)(2,1)}, u32[]{:S(2)}) copy-start(bf16[128,1280]{1,0:T(8,128)(2,1)} %g_ref.1) | copy-start | bytes 983044
  12.7 5.4 %collective-permute-start.3 = (f32[32,256]{1,0:T(8,128)S(1)}, f32[32,256]{1,0:T(8,128)S(1)}, u32[]{:S(2)}, u32[]{:S(2)}) collective-permute-start(f32[32,256]{1,0:T(8,128)S(1)} %get-tuple-element.64), channel_id=1, source_target_pairs={{0,192},{64,0},{128,64},{192,128},{1,193},{65,1},{129,65},{193,129... | collective-permute-start | bytes 98312 | tf_op jit(solution)/shard_map/ppermute | solution.py:73
  14.3 4.0 %collective-permute-start.4 = (f32[32,256]{1,0:T(8,128)S(1)}, f32[32,256]{1,0:T(8,128)S(1)}, u32[]{:S(2)}, u32[]{:S(2)}) collective-permute-start(f32[32,256]{1,0:T(8,128)S(1)} %get-tuple-element.65), channel_id=1, source_target_pairs={{0,64},{64,128},{128,192},{192,0},{1,65},{65,129},{129,193},{193,1... | collective-permute-start | bytes 98312 | tf_op jit(solution)/shard_map/ppermute | solution.py:73
  14.3 4.3 %collective-permute-start.5 = (f32[32,256]{1,0:T(8,128)S(1)}, f32[32,256]{1,0:T(8,128)S(1)}, u32[]{:S(2)}, u32[]{:S(2)}) collective-permute-start(f32[32,256]{1,0:T(8,128)S(1)} %get-tuple-element.66), channel_id=1, source_target_pairs={{0,128},{64,192},{128,0},{192,64},{1,129},{65,193},{129,1},{193,65... | collective-permute-start | bytes 98312 | tf_op jit(solution)/shard_map/ppermute | solution.py:73
  15.6 3.1 %copy-start = (bf16[1,27648,32]{1,2,0:T(8,128)(2,1)S(1)}, bf16[1,27648,32]{1,2,0:T(8,128)(2,1)}, u32[]{:S(2)}) copy-start(bf16[1,27648,32]{1,2,0:T(8,128)(2,1)} %param.11) | copy-start | bytes 5308420
  15.6 3.1 %copy-start.1 = (bf16[1,27648,32]{1,2,0:T(8,128)(2,1)S(1)}, bf16[1,27648,32]{1,2,0:T(8,128)(2,1)}, u32[]{:S(2)}) copy-start(bf16[1,27648,32]{1,2,0:T(8,128)(2,1)} %param.14) | copy-start | bytes 5308420
  18.7 10.0 %copy-start.3 = (f32[1,4,108,32]{2,3,1,0:T(8,128)S(1)}, f32[1,4,108,32]{2,3,1,0:T(8,128)}, u32[]{:S(2)}) copy-start(f32[1,4,108,32]{2,3,1,0:T(8,128)} %param.17) | copy-start | bytes 165892
  18.7 10.0 %copy-start.4 = (f32[1,4,108,32]{2,3,1,0:T(8,128)S(1)}, f32[1,4,108,32]{2,3,1,0:T(8,128)}, u32[]{:S(2)}) copy-start(f32[1,4,108,32]{2,3,1,0:T(8,128)} %param.16) | copy-start | bytes 165892
  18.7 10.0 %copy-start.5 = (f32[1,4,108,32]{2,3,1,0:T(8,128)S(1)}, f32[1,4,108,32]{2,3,1,0:T(8,128)}, u32[]{:S(2)}) copy-start(f32[1,4,108,32]{2,3,1,0:T(8,128)} %param.15) | copy-start | bytes 165892
  22.8 9.8 %collective-permute-start.6 = (f32[32,128]{1,0:T(8,128)S(1)}, f32[32,128]{1,0:T(8,128)S(1)}, u32[]{:S(2)}, u32[]{:S(2)}) collective-permute-start(f32[32,128]{1,0:T(8,128)S(1)} %get-tuple-element.69), channel_id=1, source_target_pairs={{0,1},{1,0},{2,3},{3,2},{4,5},{5,4},{6,7},{7,6},{8,9},{9,8},{10,11... | collective-permute-start | bytes 49160 | tf_op jit(solution)/shard_map/ppermute | solution.py:69
  27.1 5.4 %collective-permute-start.7 = (bf16[96,128]{1,0:T(8,128)(2,1)S(1)}, bf16[96,128]{1,0:T(8,128)(2,1)S(1)}, u32[]{:S(2)}, u32[]{:S(2)}) collective-permute-start(bf16[96,128]{1,0:T(8,128)(2,1)S(1)} %get-tuple-element.70), channel_id=1, source_target_pairs={{64,0},{128,64},{192,128},{65,1},{129,65},{193,129},{66,2},{130,66... | collective-permute-start | bytes 73736 | tf_op jit(solution)/shard_map/ppermute | solution.py:465
  36.8 5.2 %collective-permute-start.8 = (bf16[96,128]{1,0:T(8,128)(2,1)S(1)}, bf16[96,128]{1,0:T(8,128)(2,1)S(1)}, u32[]{:S(2)}, u32[]{:S(2)}) collective-permute-start(bf16[96,128]{1,0:T(8,128)(2,1)S(1)} %relay.2), channel_id=1, source_target_pairs={{64,0},{128,64},{192,128},{65,1},{129,65},{193,129},{66,2},{130,66... | collective-permute-start | bytes 73736 | tf_op jit(solution)/shard_map/ppermute | solution.py:465
  46.2 5.8 %collective-permute-start.9 = (bf16[96,128]{1,0:T(8,128)(2,1)S(1)}, bf16[96,128]{1,0:T(8,128)(2,1)S(1)}, u32[]{:S(2)}, u32[]{:S(2)}) collective-permute-start(bf16[96,128]{1,0:T(8,128)(2,1)S(1)} %relay.3), channel_id=1, source_target_pairs={{64,0},{128,64},{192,128},{65,1},{129,65},{193,129},{66,2},{130,66... | collective-permute-start | bytes 73736 | tf_op jit(solution)/shard_map/ppermute | solution.py:465
  53.4 3.5 %collective-permute-start.10 = (bf16[4,8,4,32,128]{4,3,2,1,0:T(8,128)(2,1)S(1)}, bf16[4,8,4,32,128]{4,3,2,1,0:T(8,128)(2,1)S(1)}, u32[]{:S(2)}, u32[]{:S(2)}) collective-permute-start(bf16[4,8,4,32,128]{4,3,2,1,0:T(8,128)(2,1)S(1)} %get-tuple-element.86), channel_id=1, source_target_pairs={{0,1},{1,0},{2,3},{3,2},{4,5},{5,4},{6,7},{7,6},{8,9},{9,8},{10,11... | collective-permute-start | bytes 3145736 | tf_op jit(solution)/shard_map/ppermute | solution.py:69
  57.2 8.8 %collective-permute-start.11 = (bf16[2,4,4,32,128]{4,3,2,1,0:T(8,128)(2,1)S(1)}, bf16[2,4,4,32,128]{4,3,2,1,0:T(8,128)(2,1)S(1)}, u32[]{:S(2)}, u32[]{:S(2)}) collective-permute-start(bf16[2,4,4,32,128]{4,3,2,1,0:T(8,128)(2,1)S(1)} %get-tuple-element.89), channel_id=1, source_target_pairs={{0,2},{1,3},{2,4},{3,5},{4,6},{5,7},{6,0},{7,1},{8,10},{9,11},{10,... | collective-permute-start | bytes 786440 | tf_op jit(solution)/shard_map/ppermute | solution.py:69
  57.3 8.7 %collective-permute-start.12 = (bf16[2,4,4,32,128]{4,3,2,1,0:T(8,128)(2,1)S(1)}, bf16[2,4,4,32,128]{4,3,2,1,0:T(8,128)(2,1)S(1)}, u32[]{:S(2)}, u32[]{:S(2)}) collective-permute-start(bf16[2,4,4,32,128]{4,3,2,1,0:T(8,128)(2,1)S(1)} %get-tuple-element.90), channel_id=1, source_target_pairs={{0,6},{1,7},{2,0},{3,1},{4,2},{5,3},{6,4},{7,5},{8,14},{9,15},{10,... | collective-permute-start | bytes 786440 | tf_op jit(solution)/shard_map/ppermute | solution.py:69
  60.0 13.8 %collective-permute-start.14 = (f32[3,4,32,108]{3,2,1,0:T(8,128)S(1)}, f32[3,4,32,108]{3,2,1,0:T(8,128)S(1)}, u32[]{:S(2)}, u32[]{:S(2)}) collective-permute-start(f32[3,4,32,108]{3,2,1,0:T(8,128)S(1)} %pad_maximum_fusion.state_ref), channel_id=1, source_target_pairs={{0,56},{1,57},{2,58},{3,59},{4,60},{5,61},{6,62},{7,63},{8,48},{9,... | collective-permute-start | bytes 497672 | tf_op jit(solution)/shard_map/ppermute | solution.py:69
  66.1 7.7 %collective-permute-start.13 = (bf16[4,4,32,128]{3,2,1,0:T(8,128)(2,1)S(1)}, bf16[4,4,32,128]{3,2,1,0:T(8,128)(2,1)S(1)}, u32[]{:S(2)}, u32[]{:S(2)}) collective-permute-start(bf16[4,4,32,128]{3,2,1,0:T(8,128)(2,1)S(1)} %get-tuple-element.93), channel_id=1, source_target_pairs={{0,2},{1,3},{2,4},{3,5},{4,6},{5,7},{6,0},{7,1},{8,10},{9,11},{10,... | collective-permute-start | bytes 393224 | tf_op jit(solution)/shard_map/ppermute | solution.py:69
  66.2 7.6 %collective-permute-start.15 = (bf16[4,4,32,128]{3,2,1,0:T(8,128)(2,1)S(1)}, bf16[4,4,32,128]{3,2,1,0:T(8,128)(2,1)S(1)}, u32[]{:S(2)}, u32[]{:S(2)}) collective-permute-start(bf16[4,4,32,128]{3,2,1,0:T(8,128)(2,1)S(1)} %get-tuple-element.96), channel_id=1, source_target_pairs={{0,6},{1,7},{2,0},{3,1},{4,2},{5,3},{6,4},{7,5},{8,14},{9,15},{10,... | collective-permute-start | bytes 393224 | tf_op jit(solution)/shard_map/ppermute | solution.py:69
  73.9 5.0 %collective-permute-start.16 = (bf16[2,4,32,128]{3,2,1,0:T(8,128)(2,1)S(1)}, bf16[2,4,32,128]{3,2,1,0:T(8,128)(2,1)S(1)}, u32[]{:S(2)}, u32[]{:S(2)}) collective-permute-start(bf16[2,4,32,128]{3,2,1,0:T(8,128)(2,1)S(1)} %get-tuple-element.98), channel_id=1, source_target_pairs={{0,24},{1,25},{2,26},{3,27},{4,28},{5,29},{6,30},{7,31},{8,16},{9,... | collective-permute-start | bytes 196616 | tf_op jit(solution)/shard_map/ppermute | solution.py:69
  75.6 5.8 %collective-permute-start.17 = (bf16[2,4,32,128]{3,2,1,0:T(8,128)(2,1)S(1)}, bf16[2,4,32,128]{3,2,1,0:T(8,128)(2,1)S(1)}, u32[]{:S(2)}, u32[]{:S(2)}) collective-permute-start(bf16[2,4,32,128]{3,2,1,0:T(8,128)(2,1)S(1)} %get-tuple-element.99), channel_id=1, source_target_pairs={{0,16},{1,17},{2,18},{3,19},{4,20},{5,21},{6,22},{7,23},{8,24},{9,... | collective-permute-start | bytes 196616 | tf_op jit(solution)/shard_map/ppermute | solution.py:69
  75.6 5.8 %collective-permute-start.18 = (bf16[2,4,32,128]{3,2,1,0:T(8,128)(2,1)S(1)}, bf16[2,4,32,128]{3,2,1,0:T(8,128)(2,1)S(1)}, u32[]{:S(2)}, u32[]{:S(2)}) collective-permute-start(bf16[2,4,32,128]{3,2,1,0:T(8,128)(2,1)S(1)} %get-tuple-element.100), channel_id=1, source_target_pairs={{0,8},{1,9},{2,10},{3,11},{4,12},{5,13},{6,14},{7,15},{8,0},{9,1},... | collective-permute-start | bytes 196616 | tf_op jit(solution)/shard_map/ppermute | solution.py:69
  81.5 5.7 %collective-permute-start.19 = (bf16[2,4,32,128]{3,2,1,0:T(8,128)(2,1)S(1)}, bf16[2,4,32,128]{3,2,1,0:T(8,128)(2,1)S(1)}, u32[]{:S(2)}, u32[]{:S(2)}) collective-permute-start(bf16[2,4,32,128]{3,2,1,0:T(8,128)(2,1)S(1)} %z_sum.1.mine_ref), channel_id=1, source_target_pairs={{0,56},{1,57},{2,58},{3,59},{4,60},{5,61},{6,62},{7,63},{8,48},{9,... | collective-permute-start | bytes 196616 | tf_op jit(solution)/shard_map/ppermute | solution.py:69
  88.0 6.8 %collective-permute-start.22 = (bf16[2,4,32,128]{3,2,1,0:T(8,128)(2,1)S(1)}, bf16[2,4,32,128]{3,2,1,0:T(8,128)(2,1)S(1)}, u32[]{:S(2)}, u32[]{:S(2)}) collective-permute-start(bf16[2,4,32,128]{3,2,1,0:T(8,128)(2,1)S(1)} %get-tuple-element.102), channel_id=1, source_target_pairs={{0,24},{1,25},{2,26},{3,27},{4,28},{5,29},{6,30},{7,31},{8,16},{9,... | collective-permute-start | bytes 196616 | tf_op jit(solution)/shard_map/ppermute | solution.py:69
  89.7 5.1 %collective-permute-start.21 = (bf16[2,4,32,128]{3,2,1,0:T(8,128)(2,1)S(1)}, bf16[2,4,32,128]{3,2,1,0:T(8,128)(2,1)S(1)}, u32[]{:S(2)}, u32[]{:S(2)}) collective-permute-start(bf16[2,4,32,128]{3,2,1,0:T(8,128)(2,1)S(1)} %get-tuple-element.102), channel_id=1, source_target_pairs={{0,16},{1,17},{2,18},{3,19},{4,20},{5,21},{6,22},{7,23},{8,24},{9,... | collective-permute-start | bytes 196616 | tf_op jit(solution)/shard_map/ppermute | solution.py:69
  89.8 3.9 %collective-permute-start.20 = (bf16[2,4,32,128]{3,2,1,0:T(8,128)(2,1)S(1)}, bf16[2,4,32,128]{3,2,1,0:T(8,128)(2,1)S(1)}, u32[]{:S(2)}, u32[]{:S(2)}) collective-permute-start(bf16[2,4,32,128]{3,2,1,0:T(8,128)(2,1)S(1)} %get-tuple-element.102), channel_id=1, source_target_pairs={{0,8},{1,9},{2,10},{3,11},{4,12},{5,13},{6,14},{7,15},{8,0},{9,1},... | collective-permute-start | bytes 196616 | tf_op jit(solution)/shard_map/ppermute | solution.py:69
  94.8 8.3 %collective-permute-start.25 = (bf16[8,4,32,128]{3,2,1,0:T(8,128)(2,1)S(1)}, bf16[8,4,32,128]{3,2,1,0:T(8,128)(2,1)S(1)}, u32[]{:S(2)}, u32[]{:S(2)}) collective-permute-start(bf16[8,4,32,128]{3,2,1,0:T(8,128)(2,1)S(1)} %constant_dynamic-update-slice_fusion.refs_0_), channel_id=1, source_target_pairs={{0,2},{1,3},{2,4},{3,5},{4,6},{5,7},{6,0},{7,1},{8,10},{9,11},{10,... | collective-permute-start | bytes 786440 | tf_op jit(solution)/shard_map/ppermute | solution.py:69
  94.9 12.9 %collective-permute-start.24 = (bf16[8,4,32,128]{3,2,1,0:T(8,128)(2,1)S(1)}, bf16[8,4,32,128]{3,2,1,0:T(8,128)(2,1)S(1)}, u32[]{:S(2)}, u32[]{:S(2)}) collective-permute-start(bf16[8,4,32,128]{3,2,1,0:T(8,128)(2,1)S(1)} %constant_dynamic-update-slice_fusion.refs_0_), channel_id=1, source_target_pairs={{0,6},{1,7},{2,0},{3,1},{4,2},{5,3},{6,4},{7,5},{8,14},{9,15},{10,... | collective-permute-start | bytes 786440 | tf_op jit(solution)/shard_map/ppermute | solution.py:69
  97.5 12.1 %collective-permute-start.23 = (bf16[8,4,32,128]{3,2,1,0:T(8,128)(2,1)S(1)}, bf16[8,4,32,128]{3,2,1,0:T(8,128)(2,1)S(1)}, u32[]{:S(2)}, u32[]{:S(2)}) collective-permute-start(bf16[8,4,32,128]{3,2,1,0:T(8,128)(2,1)S(1)} %constant_dynamic-update-slice_fusion.refs_0_), channel_id=1, source_target_pairs={{0,4},{1,5},{2,6},{3,7},{4,0},{5,1},{6,2},{7,3},{8,12},{9,13},{10,... | collective-permute-start | bytes 786440 | tf_op jit(solution)/shard_map/ppermute | solution.py:69
  97.5 13.0 %collective-permute-start.26 = (bf16[8,4,32,128]{3,2,1,0:T(8,128)(2,1)S(1)}, bf16[8,4,32,128]{3,2,1,0:T(8,128)(2,1)S(1)}, u32[]{:S(2)}, u32[]{:S(2)}) collective-permute-start(bf16[8,4,32,128]{3,2,1,0:T(8,128)(2,1)S(1)} %constant_dynamic-update-slice_fusion.refs_0_), channel_id=1, source_target_pairs={{0,1},{1,0},{2,3},{3,2},{4,5},{5,4},{6,7},{7,6},{8,9},{9,8},{10,11... | collective-permute-start | bytes 786440 | tf_op jit(solution)/shard_map/ppermute | solution.py:69
  103.1 7.5 %collective-permute-start.29 = (bf16[8,4,32,128]{3,2,1,0:T(8,128)(2,1)S(1)}, bf16[8,4,32,128]{3,2,1,0:T(8,128)(2,1)S(1)}, u32[]{:S(2)}, u32[]{:S(2)}) collective-permute-start(bf16[8,4,32,128]{3,2,1,0:T(8,128)(2,1)S(1)} %collective-permute-done.25.refs_3_), channel_id=1, source_target_pairs={{0,1},{1,0},{2,3},{3,2},{4,5},{5,4},{6,7},{7,6},{8,9},{9,8},{10,11... | collective-permute-start | bytes 786440 | tf_op jit(solution)/shard_map/ppermute | solution.py:69
  107.8 3.1 %collective-permute-start.28 = (bf16[8,4,32,128]{3,2,1,0:T(8,128)(2,1)S(1)}, bf16[8,4,32,128]{3,2,1,0:T(8,128)(2,1)S(1)}, u32[]{:S(2)}, u32[]{:S(2)}) collective-permute-start(bf16[8,4,32,128]{3,2,1,0:T(8,128)(2,1)S(1)} %collective-permute-done.24.refs_2_), channel_id=1, source_target_pairs={{0,1},{1,0},{2,3},{3,2},{4,5},{5,4},{6,7},{7,6},{8,9},{9,8},{10,11... | collective-permute-start | bytes 786440 | tf_op jit(solution)/shard_map/ppermute | solution.py:69
  109.7 2.1 %collective-permute-start.27 = (bf16[8,4,32,128]{3,2,1,0:T(8,128)(2,1)S(1)}, bf16[8,4,32,128]{3,2,1,0:T(8,128)(2,1)S(1)}, u32[]{:S(2)}, u32[]{:S(2)}) collective-permute-start(bf16[8,4,32,128]{3,2,1,0:T(8,128)(2,1)S(1)} %collective-permute-done.23.refs_1_), channel_id=1, source_target_pairs={{0,1},{1,0},{2,3},{3,2},{4,5},{5,4},{6,7},{7,6},{8,9},{9,8},{10,11... | collective-permute-start | bytes 786440 | tf_op jit(solution)/shard_map/ppermute | solution.py:69

commit v9 on v8

--- a/solution.py
+++ b/solution.py
@@ -393,8 +393,9 @@
 
 
 def assemble_kernel(*refs):
-    arrays, (out_ref, blocks, sems) = refs[:8], refs[8:]
+    arrays, (out_ref, blocks, rows, sems, out_sems) = refs[:8], refs[8:]
     core, y_here, z_here = core_pos(), y_pos(), z_pos()
+
     copies = []
     for side in range(2):
         for i, k in enumerate(Y_ORDER):
@@ -413,19 +414,30 @@
     for z in range(ZS):
         apart = z_here ^ z
         places.append(jnp.where(apart < 4, 2 * apart, 2 * (apart ^ Z_PARTNER) + 1))
-    for tile in range(FF // LANES):
-        value = None
-        first = tile * LANES // OWNED
-        last = (tile * LANES + LANES - 1) // OWNED
-        for piece in range(first, last + 1):
-            bucket, owner = divmod(piece, 64)
-            z, y, c = owner // 8, owner // 2 % YS, owner % 2
-            block = blocks[c, y, places[z], bucket].astype(F32)
-            start = piece * OWNED - tile * LANES
-            if start % LANES:
-                block = pltpu.roll(block, start % LANES, 1)
-            value = block if value is None else jnp.where(lane < start, value, block)
-        out_ref[:, tile * LANES : (tile + 1) * LANES] = value.astype(BF16)
+    copies = []
+    for bucket in range(BUCKETS):
+        for tile in range(BUCKET_ROWS // LANES):
+            value = None
+            first = tile * LANES // OWNED
+            last = (tile * LANES + LANES - 1) // OWNED
+            for owner in range(first, last + 1):
+                z, y, c = owner // 8, owner // 2 % YS, owner % 2
+                block = blocks[c, y, places[z], bucket]
+                start = owner * OWNED - tile * LANES
+                if start % LANES:
+                    block = pltpu.roll(block, start % LANES, 1)
+                value = block if value is None else jnp.where(lane < start, value, block)
+            at = bucket * BUCKET_ROWS + tile * LANES
+            rows[:, at : at + LANES] = value
+        columns = pl.ds(bucket * BUCKET_ROWS, BUCKET_ROWS)
+        copies.append(
+            pltpu.make_async_copy(
+                rows.at[:, columns], out_ref.at[:, columns], out_sems.at[bucket]
+            )
+        )
+        copies[-1].start()
+    for copy in copies:
+        copy.wait()
 
 
 def assemble(arrays):
@@ -433,10 +445,12 @@
         assemble_kernel,
         out_shape=shaped((RANK, FF), BF16),
         in_specs=[ANY] * 8,
-        out_specs=VMEM,
+        out_specs=ANY,
         scratch_shapes=[
             pltpu.VMEM((2, YS, ZS, BUCKETS, RANK, LANES), BF16),
+            pltpu.VMEM((RANK, FF), BF16),
             pltpu.SemaphoreType.DMA((8,)),
+            pltpu.SemaphoreType.DMA((BUCKETS,)),
         ],
         compiler_params=params(),
         name="assemble",

time: 115 us -> 115 us (level)
  no operation moved by 1% of the time
where the time goes in v9:
time: 115 us; the launch traced here: 114 us
  starting transfers between devices  54.2 us (47%)
  Pallas kernels  34.3 us (30%)
  waiting for transfers between devices  24.3 us (21%)
    ppermute x21, starting transfers between devices, over_dp(): return lax.ppermute(value, 'dp', pairs)  42.1 us
    ppermute x21, waiting for transfers between devices, over_dp(): return lax.ppermute(value, 'dp', pairs)  19.3 us
    pallas_call x6, Pallas kernels, activation(): pl.pallas_call(functools.partial(activation_kernel, slope, bucket * BUCKE...  15.2 us
    pallas_call x3, Pallas kernels, relay(): pl.pallas_call(functools.partial(relay_kernel, top), out_shape=[message,...  12.5 us
    ppermute x6, starting transfers between devices, over_section(): lax.ppermute(value, 'section', [(i, (i + steps) % 4) for i in range(4)])  8 us
    ppermute x3, waiting for transfers between devices, per_device(): above = [above[0], lax.ppermute(sent, 'section', [(1, 0), (2, 1), (3, 2)])]  4.55 us
    ppermute x3, starting transfers between devices, per_device(): above = [above[0], lax.ppermute(sent, 'section', [(1, 0), (2, 1), (3, 2)])]  4.07 us
  transfers between devices with their start and end apart: 30, of which 13 were waited for; matrix products, arithmetic and copies ran while one was open for 0% of the time, Pallas kernels for 13%

profile of v9, /device:TPU:1, one launch (start us, length us, event | category | flops | bytes accessed | tf_op | source)
XLA Modules:
  0.0 114.0 jit_solution(17357141660336831157)
XLA Ops:
  0.6 1.2 %slices.1 = (bf16[32,1920]{1,0:T(8,128)(2,1)S(1)}, bf16[32,1920]{1,0:T(8,128)(2,1)S(1)}, bf16[32,1920]{1,0:T(8,128)(2,1)S(1)}, bf16[32,1920]{1,0:T(8,128)(2,1)S(1)}) custom-call(bf16[32,5120]{1,0:T(8,128)(2,1)} %bitcast.51, bf16[32,5120]{1,0:T(8,128)(2,1)} %bitcast.52), custom_call_target="tpu_custom_call" | custom-call | tf_op jit(solution)/shard_map/slices/pallas_call | solution.py:97
  1.8 2.1 %collective-permute-start = (bf16[32,1920]{1,0:T(8,128)(2,1)S(1)}, bf16[32,1920]{1,0:T(8,128)(2,1)S(1)}, u32[]{:S(2)}, u32[]{:S(2)}) collective-permute-start(bf16[32,1920]{1,0:T(8,128)(2,1)S(1)} %get-tuple-element.56), channel_id=1, source_target_pairs={{0,64},{64,128},{128,192},{192,0},{1,65},{65,129},{129,193},{193,1... | collective-permute-start | bytes 368648 | tf_op jit(solution)/shard_map/ppermute | solution.py:73
  3.9 1.4 %collective-permute-start.1 = (bf16[32,1920]{1,0:T(8,128)(2,1)S(1)}, bf16[32,1920]{1,0:T(8,128)(2,1)S(1)}, u32[]{:S(2)}, u32[]{:S(2)}) collective-permute-start(bf16[32,1920]{1,0:T(8,128)(2,1)S(1)} %get-tuple-element.57), channel_id=1, source_target_pairs={{0,192},{64,0},{128,64},{192,128},{1,193},{65,1},{129,65},{193,129... | collective-permute-start | bytes 368648 | tf_op jit(solution)/shard_map/ppermute | solution.py:73
  5.3 1.6 %collective-permute-start.2 = (bf16[32,1920]{1,0:T(8,128)(2,1)S(1)}, bf16[32,1920]{1,0:T(8,128)(2,1)S(1)}, u32[]{:S(2)}, u32[]{:S(2)}) collective-permute-start(bf16[32,1920]{1,0:T(8,128)(2,1)S(1)} %get-tuple-element.58), channel_id=1, source_target_pairs={{0,128},{64,192},{128,0},{192,64},{1,129},{65,193},{129,1},{193,65... | collective-permute-start | bytes 368648 | tf_op jit(solution)/shard_map/ppermute | solution.py:73
  6.9 5.0 %slope.2.refs_0_.refs_2_ = bf16[128,20736]{1,0:T(8,128)(2,1)S(1)} custom-call(bf16[128,27648]{1,0:T(8,128)(2,1)} %bitcast.44), custom_call_target="tpu_custom_call" | custom-call | flops 26542080 | bytes 10616832 | tf_op jit(solution)/shard_map/slope/pallas_call | solution.py:138
  11.9 0.0 collective-permute-done.1.w3
  11.9 0.0 collective-permute-done.2.w2
  12.0 0.7 shares.1
  12.7 1.6 %collective-permute-start.3 = (f32[32,256]{1,0:T(8,128)S(1)}, f32[32,256]{1,0:T(8,128)S(1)}, u32[]{:S(2)}, u32[]{:S(2)}) collective-permute-start(f32[32,256]{1,0:T(8,128)S(1)} %get-tuple-element.64), channel_id=1, source_target_pairs={{0,192},{64,0},{128,64},{192,128},{1,193},{65,1},{129,65},{193,129... | collective-permute-start | bytes 98312 | tf_op jit(solution)/shard_map/ppermute | solution.py:73
  14.3 0.0 collective-permute-start.4
  14.3 1.3 %collective-permute-start.5 = (f32[32,256]{1,0:T(8,128)S(1)}, f32[32,256]{1,0:T(8,128)S(1)}, u32[]{:S(2)}, u32[]{:S(2)}) collective-permute-start(f32[32,256]{1,0:T(8,128)S(1)} %get-tuple-element.66), channel_id=1, source_target_pairs={{0,128},{64,192},{128,0},{192,64},{1,129},{65,193},{129,1},{193,65... | collective-permute-start | bytes 98312 | tf_op jit(solution)/shard_map/ppermute | solution.py:73
  15.6 2.5 %slope.3.refs_1_.refs_3_ = bf16[128,6912]{1,0:T(8,128)(2,1)S(1)} custom-call(bf16[128,27648]{1,0:T(8,128)(2,1)} %bitcast.45), custom_call_target="tpu_custom_call" | custom-call | flops 8847360 | bytes 3538944 | tf_op jit(solution)/shard_map/slope/pallas_call | solution.py:138
  18.1 0.2 collective-permute-done.4.s2
  18.3 0.3 collective-permute-done.5.s3
  18.7 0.0 copy-start.5
  18.7 4.1 %relay_first.1 = (bf16[96,128]{1,0:T(8,128)(2,1)S(1)}, f32[32,128]{1,0:T(8,128)S(1)}) custom-call(f32[32,256]{1,0:T(8,128)S(1)} %get-tuple-element.63.s0, f32[32,256]{1,0:T(8,128)S(1)} %collective-permute-done.3.s1, f32[32,256]{1,0:T(8,128)S(1)} %collective-permute-done.4.s2, f32[32,256]{1,0:T(8,128)S(1)} %collective-permute-done.5.s3, ...), custom_call_target="tpu_custom_call" | custom-call | tf_op jit(solution)/shard_map/relay_first/pallas_call | solution.py:223
  22.8 4.4 %collective-permute-start.6 = (f32[32,128]{1,0:T(8,128)S(1)}, f32[32,128]{1,0:T(8,128)S(1)}, u32[]{:S(2)}, u32[]{:S(2)}) collective-permute-start(f32[32,128]{1,0:T(8,128)S(1)} %get-tuple-element.69), channel_id=1, source_target_pairs={{0,1},{1,0},{2,3},{3,2},{4,5},{5,4},{6,7},{7,6},{8,9},{9,8},{10,11... | collective-permute-start | bytes 49160 | tf_op jit(solution)/shard_map/ppermute | solution.py:69
  27.1 1.5 %collective-permute-start.7 = (bf16[96,128]{1,0:T(8,128)(2,1)S(1)}, bf16[96,128]{1,0:T(8,128)(2,1)S(1)}, u32[]{:S(2)}, u32[]{:S(2)}) collective-permute-start(bf16[96,128]{1,0:T(8,128)(2,1)S(1)} %get-tuple-element.70), channel_id=1, source_target_pairs={{64,0},{128,64},{192,128},{65,1},{129,65},{193,129},{66,2},{130,66... | collective-permute-start | bytes 73736 | tf_op jit(solution)/shard_map/ppermute | solution.py:479
  28.7 1.9 %hidden.5.h1 = bf16[128,6912]{1,0:T(8,128)(2,1)S(1)} custom-call(bf16[128,27648]{1,0:T(8,128)(2,1)} %bitcast.46), custom_call_target="tpu_custom_call" | custom-call | flops 8847360 | bytes 3538944 | tf_op jit(solution)/shard_map/hidden/pallas_call | solution.py:138
  30.6 1.9 %hidden.4.h0 = bf16[128,6912]{1,0:T(8,128)(2,1)S(1)} custom-call(bf16[128,27648]{1,0:T(8,128)(2,1)} %bitcast.47), custom_call_target="tpu_custom_call" | custom-call | flops 8847360 | bytes 3538944 | tf_op jit(solution)/shard_map/hidden/pallas_call | solution.py:138
  32.5 0.0 collective-permute-done.6.refs_0_.other_ref
  32.5 0.0 collective-permute-done.7.refs_1_
  32.6 4.2 %relay.2 = bf16[96,128]{1,0:T(8,128)(2,1)S(1)} custom-call(f32[32,256]{1,0:T(8,128)S(1)} %get-tuple-element.63.s0, f32[32,256]{1,0:T(8,128)S(1)} %collective-permute-done.3.s1, f32[32,256]{1,0:T(8,128)S(1)} %collective-permute-done.4.s2, f32[32,256]{1,0:T(8,128)S(1)} %collective-permute-done.5.s3, f32[32,128]{1,0:T(8,128)S(1)} %collective-permute-done.6.refs_0_.other_ref, ...), custom_call_target="tpu_custom_call" | custom-call | tf_op jit(solution)/shard_map/relay/pallas_call | solution.py:223
  36.8 1.3 %collective-permute-start.8 = (bf16[96,128]{1,0:T(8,128)(2,1)S(1)}, bf16[96,128]{1,0:T(8,128)(2,1)S(1)}, u32[]{:S(2)}, u32[]{:S(2)}) collective-permute-start(bf16[96,128]{1,0:T(8,128)(2,1)S(1)} %relay.2), channel_id=1, source_target_pairs={{64,0},{128,64},{192,128},{65,1},{129,65},{193,129},{66,2},{130,66... | collective-permute-start | bytes 73736 | tf_op jit(solution)/shard_map/ppermute | solution.py:479
  38.1 1.9 %hidden.7.h3 = bf16[128,6912]{1,0:T(8,128)(2,1)S(1)} custom-call(bf16[128,27648]{1,0:T(8,128)(2,1)} %bitcast.48), custom_call_target="tpu_custom_call" | custom-call | flops 8847360 | bytes 3538944 | tf_op jit(solution)/shard_map/hidden/pallas_call | solution.py:138
  40.0 1.9 %hidden.6.h2 = bf16[128,6912]{1,0:T(8,128)(2,1)S(1)} custom-call(bf16[128,27648]{1,0:T(8,128)(2,1)} %bitcast.49), custom_call_target="tpu_custom_call" | custom-call | flops 8847360 | bytes 3538944 | tf_op jit(solution)/shard_map/hidden/pallas_call | solution.py:138
  42.0 0.0 collective-permute-done.8.refs_1_
  42.0 4.2 %relay.3 = bf16[96,128]{1,0:T(8,128)(2,1)S(1)} custom-call(f32[32,256]{1,0:T(8,128)S(1)} %get-tuple-element.63.s0, f32[32,256]{1,0:T(8,128)S(1)} %collective-permute-done.3.s1, f32[32,256]{1,0:T(8,128)S(1)} %collective-permute-done.4.s2, f32[32,256]{1,0:T(8,128)S(1)} %collective-permute-done.5.s3, f32[32,128]{1,0:T(8,128)S(1)} %collective-permute-done.6.refs_0_.other_ref, ...), custom_call_target="tpu_custom_call" | custom-call | tf_op jit(solution)/shard_map/relay/pallas_call | solution.py:223
  46.2 1.3 %collective-permute-start.9 = (bf16[96,128]{1,0:T(8,128)(2,1)S(1)}, bf16[96,128]{1,0:T(8,128)(2,1)S(1)}, u32[]{:S(2)}, u32[]{:S(2)}) collective-permute-start(bf16[96,128]{1,0:T(8,128)(2,1)S(1)} %relay.3), channel_id=1, source_target_pairs={{64,0},{128,64},{192,128},{65,1},{129,65},{193,129},{66,2},{130,66... | collective-permute-start | bytes 73736 | tf_op jit(solution)/shard_map/ppermute | solution.py:479
  47.5 4.5 %collective-permute-done.9.above_ref = bf16[96,128]{1,0:T(8,128)(2,1)S(1)} collective-permute-done((bf16[96,128]{1,0:T(8,128)(2,1)S(1)}, bf16[96,128]{1,0:T(8,128)(2,1)S(1)}, u32[]{:S(2)}, u32[]{:S(2)}) %collective-permute-start.9) | collective-permute-done | bytes 24608 | tf_op jit(solution)/shard_map/ppermute | solution.py:479
  52.0 1.4 %grads.1 = (bf16[4,8,4,32,128]{4,3,2,1,0:T(8,128)(2,1)S(1)}, bf16[4,8,4,32,128]{4,3,2,1,0:T(8,128)(2,1)S(1)}) custom-call(f32[32,256]{1,0:T(8,128)S(1)} %get-tuple-element.63.s0, f32[32,256]{1,0:T(8,128)S(1)} %collective-permute-done.3.s1, f32[32,256]{1,0:T(8,128)S(1)} %collective-permute-done.4.s2, f32[32,256]{1,0:T(8,128)S(1)} %collective-permute-done.5.s3, ...), custom_call_target="tpu_custom_call" | custom-call | tf_op jit(solution)/shard_map/grads/pallas_call | solution.py:260
  53.4 1.3 %collective-permute-start.10 = (bf16[4,8,4,32,128]{4,3,2,1,0:T(8,128)(2,1)S(1)}, bf16[4,8,4,32,128]{4,3,2,1,0:T(8,128)(2,1)S(1)}, u32[]{:S(2)}, u32[]{:S(2)}) collective-permute-start(bf16[4,8,4,32,128]{4,3,2,1,0:T(8,128)(2,1)S(1)} %get-tuple-element.86), channel_id=1, source_target_pairs={{0,1},{1,0},{2,3},{3,2},{4,5},{5,4},{6,7},{7,6},{8,9},{9,8},{10,11... | collective-permute-start | bytes 3145736 | tf_op jit(solution)/shard_map/ppermute | solution.py:69
  54.7 2.3 %collective-permute-done.10.got_ref = bf16[4,8,4,32,128]{4,3,2,1,0:T(8,128)(2,1)S(1)} collective-permute-done((bf16[4,8,4,32,128]{4,3,2,1,0:T(8,128)(2,1)S(1)}, bf16[4,8,4,32,128]{4,3,2,1,0:T(8,128)(2,1)S(1)}, u32[]{:S(2)}, u32[]{:S(2)}) %collective-permute-start.10) | collective-permute-done | bytes 1048608 | tf_op jit(solution)/shard_map/ppermute | solution.py:69
  57.0 0.2 core_sum.1
  57.2 0.1 collective-permute-start.11
  57.3 2.7 %collective-permute-start.12 = (bf16[2,4,4,32,128]{4,3,2,1,0:T(8,128)(2,1)S(1)}, bf16[2,4,4,32,128]{4,3,2,1,0:T(8,128)(2,1)S(1)}, u32[]{:S(2)}, u32[]{:S(2)}) collective-permute-start(bf16[2,4,4,32,128]{4,3,2,1,0:T(8,128)(2,1)S(1)} %get-tuple-element.90), channel_id=1, source_target_pairs={{0,6},{1,7},{2,0},{3,1},{4,2},{5,3},{6,4},{7,5},{8,14},{9,15},{10,... | collective-permute-start | bytes 786440 | tf_op jit(solution)/shard_map/ppermute | solution.py:69
  60.0 4.7 %collective-permute-start.14 = (f32[3,4,32,108]{3,2,1,0:T(8,128)S(1)}, f32[3,4,32,108]{3,2,1,0:T(8,128)S(1)}, u32[]{:S(2)}, u32[]{:S(2)}) collective-permute-start(f32[3,4,32,108]{3,2,1,0:T(8,128)S(1)} %pad_maximum_fusion.state_ref), channel_id=1, source_target_pairs={{0,56},{1,57},{2,58},{3,59},{4,60},{5,61},{6,62},{7,63},{8,48},{9,... | collective-permute-start | bytes 497672 | tf_op jit(solution)/shard_map/ppermute | solution.py:69
  64.6 1.4 %collective-permute-done.11.from_below = bf16[2,4,4,32,128]{4,3,2,1,0:T(8,128)(2,1)S(1)} collective-permute-done((bf16[2,4,4,32,128]{4,3,2,1,0:T(8,128)(2,1)S(1)}, bf16[2,4,4,32,128]{4,3,2,1,0:T(8,128)(2,1)S(1)}, u32[]{:S(2)}, u32[]{:S(2)}) %collective-permute-start.11) | collective-permute-done | bytes 262176 | tf_op jit(solution)/shard_map/ppermute | solution.py:69
  66.1 0.1 collective-permute-start.13
  66.2 2.7 %collective-permute-start.15 = (bf16[4,4,32,128]{3,2,1,0:T(8,128)(2,1)S(1)}, bf16[4,4,32,128]{3,2,1,0:T(8,128)(2,1)S(1)}, u32[]{:S(2)}, u32[]{:S(2)}) collective-permute-start(bf16[4,4,32,128]{3,2,1,0:T(8,128)(2,1)S(1)} %get-tuple-element.96), channel_id=1, source_target_pairs={{0,6},{1,7},{2,0},{3,1},{4,2},{5,3},{6,4},{7,5},{8,14},{9,15},{10,... | collective-permute-start | bytes 393224 | tf_op jit(solution)/shard_map/ppermute | solution.py:69
  68.8 5.0 %collective-permute-done.14.partner_ref = f32[3,4,32,108]{3,2,1,0:T(8,128)S(1)} collective-permute-done((f32[3,4,32,108]{3,2,1,0:T(8,128)S(1)}, f32[3,4,32,108]{3,2,1,0:T(8,128)S(1)}, u32[]{:S(2)}, u32[]{:S(2)}) %collective-permute-start.14) | collective-permute-done | bytes 165920 | tf_op jit(solution)/shard_map/ppermute | solution.py:69
  73.8 0.1 y_sum.1
  73.9 1.7 %collective-permute-start.16 = (bf16[2,4,32,128]{3,2,1,0:T(8,128)(2,1)S(1)}, bf16[2,4,32,128]{3,2,1,0:T(8,128)(2,1)S(1)}, u32[]{:S(2)}, u32[]{:S(2)}) collective-permute-start(bf16[2,4,32,128]{3,2,1,0:T(8,128)(2,1)S(1)} %get-tuple-element.98), channel_id=1, source_target_pairs={{0,24},{1,25},{2,26},{3,27},{4,28},{5,29},{6,30},{7,31},{8,16},{9,... | collective-permute-start | bytes 196616 | tf_op jit(solution)/shard_map/ppermute | solution.py:69
  75.6 1.9 %collective-permute-start.18 = (bf16[2,4,32,128]{3,2,1,0:T(8,128)(2,1)S(1)}, bf16[2,4,32,128]{3,2,1,0:T(8,128)(2,1)S(1)}, u32[]{:S(2)}, u32[]{:S(2)}) collective-permute-start(bf16[2,4,32,128]{3,2,1,0:T(8,128)(2,1)S(1)} %get-tuple-element.100), channel_id=1, source_target_pairs={{0,8},{1,9},{2,10},{3,11},{4,12},{5,13},{6,14},{7,15},{8,0},{9,1},... | collective-permute-start | bytes 196616 | tf_op jit(solution)/shard_map/ppermute | solution.py:69
  77.6 1.4 %collective-permute-done.16.g1 = bf16[2,4,32,128]{3,2,1,0:T(8,128)(2,1)S(1)} collective-permute-done((bf16[2,4,32,128]{3,2,1,0:T(8,128)(2,1)S(1)}, bf16[2,4,32,128]{3,2,1,0:T(8,128)(2,1)S(1)}, u32[]{:S(2)}, u32[]{:S(2)}) %collective-permute-start.16) | collective-permute-done | bytes 65568 | tf_op jit(solution)/shard_map/ppermute | solution.py:69
  79.0 2.5 %collective-permute-done.17.g2 = bf16[2,4,32,128]{3,2,1,0:T(8,128)(2,1)S(1)} collective-permute-done((bf16[2,4,32,128]{3,2,1,0:T(8,128)(2,1)S(1)}, bf16[2,4,32,128]{3,2,1,0:T(8,128)(2,1)S(1)}, u32[]{:S(2)}, u32[]{:S(2)}) %collective-permute-start.17) | collective-permute-done | bytes 65568 | tf_op jit(solution)/shard_map/ppermute | solution.py:69
  81.5 3.4 %collective-permute-start.19 = (bf16[2,4,32,128]{3,2,1,0:T(8,128)(2,1)S(1)}, bf16[2,4,32,128]{3,2,1,0:T(8,128)(2,1)S(1)}, u32[]{:S(2)}, u32[]{:S(2)}) collective-permute-start(bf16[2,4,32,128]{3,2,1,0:T(8,128)(2,1)S(1)} %z_sum.1.mine_ref), channel_id=1, source_target_pairs={{0,56},{1,57},{2,58},{3,59},{4,60},{5,61},{6,62},{7,63},{8,48},{9,... | collective-permute-start | bytes 196616 | tf_op jit(solution)/shard_map/ppermute | solution.py:69
  84.9 2.4 %collective-permute-done.19.got_ref = bf16[2,4,32,128]{3,2,1,0:T(8,128)(2,1)S(1)} collective-permute-done((bf16[2,4,32,128]{3,2,1,0:T(8,128)(2,1)S(1)}, bf16[2,4,32,128]{3,2,1,0:T(8,128)(2,1)S(1)}, u32[]{:S(2)}, u32[]{:S(2)}) %collective-permute-start.19) | collective-permute-done | bytes 65568 | tf_op jit(solution)/shard_map/ppermute | solution.py:69
  87.2 0.7 adamw.1
  88.0 1.7 %collective-permute-start.22 = (bf16[2,4,32,128]{3,2,1,0:T(8,128)(2,1)S(1)}, bf16[2,4,32,128]{3,2,1,0:T(8,128)(2,1)S(1)}, u32[]{:S(2)}, u32[]{:S(2)}) collective-permute-start(bf16[2,4,32,128]{3,2,1,0:T(8,128)(2,1)S(1)} %get-tuple-element.102), channel_id=1, source_target_pairs={{0,24},{1,25},{2,26},{3,27},{4,28},{5,29},{6,30},{7,31},{8,16},{9,... | collective-permute-start | bytes 196616 | tf_op jit(solution)/shard_map/ppermute | solution.py:69
  89.7 0.1 collective-permute-start.21
  89.8 1.7 %collective-permute-start.20 = (bf16[2,4,32,128]{3,2,1,0:T(8,128)(2,1)S(1)}, bf16[2,4,32,128]{3,2,1,0:T(8,128)(2,1)S(1)}, u32[]{:S(2)}, u32[]{:S(2)}) collective-permute-start(bf16[2,4,32,128]{3,2,1,0:T(8,128)(2,1)S(1)} %get-tuple-element.102), channel_id=1, source_target_pairs={{0,8},{1,9},{2,10},{3,11},{4,12},{5,13},{6,14},{7,15},{8,0},{9,1},... | collective-permute-start | bytes 196616 | tf_op jit(solution)/shard_map/ppermute | solution.py:69
  91.5 2.1 %collective-permute-done.20 = bf16[2,4,32,128]{3,2,1,0:T(8,128)(2,1)S(1)} collective-permute-done((bf16[2,4,32,128]{3,2,1,0:T(8,128)(2,1)S(1)}, bf16[2,4,32,128]{3,2,1,0:T(8,128)(2,1)S(1)}, u32[]{:S(2)}, u32[]{:S(2)}) %collective-permute-start.20) | collective-permute-done | bytes 65568 | tf_op jit(solution)/shard_map/ppermute | solution.py:69
  93.7 1.1 collective-permute-done.21
  94.8 0.0 collective-permute-done.22
  94.8 0.1 collective-permute-start.25
  94.9 2.7 %collective-permute-start.24 = (bf16[8,4,32,128]{3,2,1,0:T(8,128)(2,1)S(1)}, bf16[8,4,32,128]{3,2,1,0:T(8,128)(2,1)S(1)}, u32[]{:S(2)}, u32[]{:S(2)}) collective-permute-start(bf16[8,4,32,128]{3,2,1,0:T(8,128)(2,1)S(1)} %constant_dynamic-update-slice_fusion.refs_0_), channel_id=1, source_target_pairs={{0,6},{1,7},{2,0},{3,1},{4,2},{5,3},{6,4},{7,5},{8,14},{9,15},{10,... | collective-permute-start | bytes 786440 | tf_op jit(solution)/shard_map/ppermute | solution.py:69
  97.5 5.5 %collective-permute-start.26 = (bf16[8,4,32,128]{3,2,1,0:T(8,128)(2,1)S(1)}, bf16[8,4,32,128]{3,2,1,0:T(8,128)(2,1)S(1)}, u32[]{:S(2)}, u32[]{:S(2)}) collective-permute-start(bf16[8,4,32,128]{3,2,1,0:T(8,128)(2,1)S(1)} %constant_dynamic-update-slice_fusion.refs_0_), channel_id=1, source_target_pairs={{0,1},{1,0},{2,3},{3,2},{4,5},{5,4},{6,7},{7,6},{8,9},{9,8},{10,11... | collective-permute-start | bytes 786440 | tf_op jit(solution)/shard_map/ppermute | solution.py:69
  103.1 4.7 %collective-permute-start.29 = (bf16[8,4,32,128]{3,2,1,0:T(8,128)(2,1)S(1)}, bf16[8,4,32,128]{3,2,1,0:T(8,128)(2,1)S(1)}, u32[]{:S(2)}, u32[]{:S(2)}) collective-permute-start(bf16[8,4,32,128]{3,2,1,0:T(8,128)(2,1)S(1)} %collective-permute-done.25.refs_3_), channel_id=1, source_target_pairs={{0,1},{1,0},{2,3},{3,2},{4,5},{5,4},{6,7},{7,6},{8,9},{9,8},{10,11... | collective-permute-start | bytes 786440 | tf_op jit(solution)/shard_map/ppermute | solution.py:69
  107.8 1.9 %collective-permute-start.28 = (bf16[8,4,32,128]{3,2,1,0:T(8,128)(2,1)S(1)}, bf16[8,4,32,128]{3,2,1,0:T(8,128)(2,1)S(1)}, u32[]{:S(2)}, u32[]{:S(2)}) collective-permute-start(bf16[8,4,32,128]{3,2,1,0:T(8,128)(2,1)S(1)} %collective-permute-done.24.refs_2_), channel_id=1, source_target_pairs={{0,1},{1,0},{2,3},{3,2},{4,5},{5,4},{6,7},{7,6},{8,9},{9,8},{10,11... | collective-permute-start | bytes 786440 | tf_op jit(solution)/shard_map/ppermute | solution.py:69
  109.7 0.9 collective-permute-start.27
  110.6 0.3 collective-permute-done.28.refs_6_
  110.8 0.9 collective-permute-done.27.refs_5_
  111.7 2.1 %assemble.1 = bf16[32,27648]{1,0:T(8,128)(2,1)} custom-call(bf16[8,4,32,128]{3,2,1,0:T(8,128)(2,1)S(1)} %constant_dynamic-update-slice_fusion.refs_0_, bf16[8,4,32,128]{3,2,1,0:T(8,128)(2,1)S(1)} %collective-permute-done.23.refs_1_, bf16[8,4,32,128]{3,2,1,0:T(8,128)(2,1)S(1)} %collective-permute-done.24.refs_2_, ...), custom_call_target="tpu_custom_call" | custom-call | tf_op jit(solution)/shard_map/assemble/pallas_call | solution.py:444
  (31 shorter events, 0.2 us)
Async XLA Ops:
  1.8 10.1 %collective-permute-start = (bf16[32,1920]{1,0:T(8,128)(2,1)S(1)}, bf16[32,1920]{1,0:T(8,128)(2,1)S(1)}, u32[]{:S(2)}, u32[]{:S(2)}) collective-permute-start(bf16[32,1920]{1,0:T(8,128)(2,1)S(1)} %get-tuple-element.56), channel_id=1, source_target_pairs={{0,64},{64,128},{128,192},{192,0},{1,65},{65,129},{129,193},{193,1... | collective-permute-start | bytes 368648 | tf_op jit(solution)/shard_map/ppermute | solution.py:73
  3.9 8.0 %collective-permute-start.1 = (bf16[32,1920]{1,0:T(8,128)(2,1)S(1)}, bf16[32,1920]{1,0:T(8,128)(2,1)S(1)}, u32[]{:S(2)}, u32[]{:S(2)}) collective-permute-start(bf16[32,1920]{1,0:T(8,128)(2,1)S(1)} %get-tuple-element.57), channel_id=1, source_target_pairs={{0,192},{64,0},{128,64},{192,128},{1,193},{65,1},{129,65},{193,129... | collective-permute-start | bytes 368648 | tf_op jit(solution)/shard_map/ppermute | solution.py:73
  5.3 6.7 %collective-permute-start.2 = (bf16[32,1920]{1,0:T(8,128)(2,1)S(1)}, bf16[32,1920]{1,0:T(8,128)(2,1)S(1)}, u32[]{:S(2)}, u32[]{:S(2)}) collective-permute-start(bf16[32,1920]{1,0:T(8,128)(2,1)S(1)} %get-tuple-element.58), channel_id=1, source_target_pairs={{0,128},{64,192},{128,0},{192,64},{1,129},{65,193},{129,1},{193,65... | collective-permute-start | bytes 368648 | tf_op jit(solution)/shard_map/ppermute | solution.py:73
  6.9 5.0 %copy-start.2 = (bf16[128,1280]{1,0:T(8,128)(2,1)S(1)}, bf16[128,1280]{1,0:T(8,128)(2,1)}, u32[]{:S(2)}) copy-start(bf16[128,1280]{1,0:T(8,128)(2,1)} %g_ref.1) | copy-start | bytes 983044
  12.7 5.4 %collective-permute-start.3 = (f32[32,256]{1,0:T(8,128)S(1)}, f32[32,256]{1,0:T(8,128)S(1)}, u32[]{:S(2)}, u32[]{:S(2)}) collective-permute-start(f32[32,256]{1,0:T(8,128)S(1)} %get-tuple-element.64), channel_id=1, source_target_pairs={{0,192},{64,0},{128,64},{192,128},{1,193},{65,1},{129,65},{193,129... | collective-permute-start | bytes 98312 | tf_op jit(solution)/shard_map/ppermute | solution.py:73
  14.3 4.0 %collective-permute-start.4 = (f32[32,256]{1,0:T(8,128)S(1)}, f32[32,256]{1,0:T(8,128)S(1)}, u32[]{:S(2)}, u32[]{:S(2)}) collective-permute-start(f32[32,256]{1,0:T(8,128)S(1)} %get-tuple-element.65), channel_id=1, source_target_pairs={{0,64},{64,128},{128,192},{192,0},{1,65},{65,129},{129,193},{193,1... | collective-permute-start | bytes 98312 | tf_op jit(solution)/shard_map/ppermute | solution.py:73
  14.3 4.3 %collective-permute-start.5 = (f32[32,256]{1,0:T(8,128)S(1)}, f32[32,256]{1,0:T(8,128)S(1)}, u32[]{:S(2)}, u32[]{:S(2)}) collective-permute-start(f32[32,256]{1,0:T(8,128)S(1)} %get-tuple-element.66), channel_id=1, source_target_pairs={{0,128},{64,192},{128,0},{192,64},{1,129},{65,193},{129,1},{193,65... | collective-permute-start | bytes 98312 | tf_op jit(solution)/shard_map/ppermute | solution.py:73
  15.6 3.1 %copy-start = (bf16[1,27648,32]{1,2,0:T(8,128)(2,1)S(1)}, bf16[1,27648,32]{1,2,0:T(8,128)(2,1)}, u32[]{:S(2)}) copy-start(bf16[1,27648,32]{1,2,0:T(8,128)(2,1)} %param.11) | copy-start | bytes 5308420
  15.6 3.1 %copy-start.1 = (bf16[1,27648,32]{1,2,0:T(8,128)(2,1)S(1)}, bf16[1,27648,32]{1,2,0:T(8,128)(2,1)}, u32[]{:S(2)}) copy-start(bf16[1,27648,32]{1,2,0:T(8,128)(2,1)} %param.14) | copy-start | bytes 5308420
  18.7 10.0 %copy-start.3 = (f32[1,4,108,32]{2,3,1,0:T(8,128)S(1)}, f32[1,4,108,32]{2,3,1,0:T(8,128)}, u32[]{:S(2)}) copy-start(f32[1,4,108,32]{2,3,1,0:T(8,128)} %param.17) | copy-start | bytes 165892
  18.7 10.0 %copy-start.4 = (f32[1,4,108,32]{2,3,1,0:T(8,128)S(1)}, f32[1,4,108,32]{2,3,1,0:T(8,128)}, u32[]{:S(2)}) copy-start(f32[1,4,108,32]{2,3,1,0:T(8,128)} %param.16) | copy-start | bytes 165892
  18.7 10.0 %copy-start.5 = (f32[1,4,108,32]{2,3,1,0:T(8,128)S(1)}, f32[1,4,108,32]{2,3,1,0:T(8,128)}, u32[]{:S(2)}) copy-start(f32[1,4,108,32]{2,3,1,0:T(8,128)} %param.15) | copy-start | bytes 165892
  22.8 9.8 %collective-permute-start.6 = (f32[32,128]{1,0:T(8,128)S(1)}, f32[32,128]{1,0:T(8,128)S(1)}, u32[]{:S(2)}, u32[]{:S(2)}) collective-permute-start(f32[32,128]{1,0:T(8,128)S(1)} %get-tuple-element.69), channel_id=1, source_target_pairs={{0,1},{1,0},{2,3},{3,2},{4,5},{5,4},{6,7},{7,6},{8,9},{9,8},{10,11... | collective-permute-start | bytes 49160 | tf_op jit(solution)/shard_map/ppermute | solution.py:69
  27.1 5.4 %collective-permute-start.7 = (bf16[96,128]{1,0:T(8,128)(2,1)S(1)}, bf16[96,128]{1,0:T(8,128)(2,1)S(1)}, u32[]{:S(2)}, u32[]{:S(2)}) collective-permute-start(bf16[96,128]{1,0:T(8,128)(2,1)S(1)} %get-tuple-element.70), channel_id=1, source_target_pairs={{64,0},{128,64},{192,128},{65,1},{129,65},{193,129},{66,2},{130,66... | collective-permute-start | bytes 73736 | tf_op jit(solution)/shard_map/ppermute | solution.py:479
  36.8 5.2 %collective-permute-start.8 = (bf16[96,128]{1,0:T(8,128)(2,1)S(1)}, bf16[96,128]{1,0:T(8,128)(2,1)S(1)}, u32[]{:S(2)}, u32[]{:S(2)}) collective-permute-start(bf16[96,128]{1,0:T(8,128)(2,1)S(1)} %relay.2), channel_id=1, source_target_pairs={{64,0},{128,64},{192,128},{65,1},{129,65},{193,129},{66,2},{130,66... | collective-permute-start | bytes 73736 | tf_op jit(solution)/shard_map/ppermute | solution.py:479
  46.2 5.8 %collective-permute-start.9 = (bf16[96,128]{1,0:T(8,128)(2,1)S(1)}, bf16[96,128]{1,0:T(8,128)(2,1)S(1)}, u32[]{:S(2)}, u32[]{:S(2)}) collective-permute-start(bf16[96,128]{1,0:T(8,128)(2,1)S(1)} %relay.3), channel_id=1, source_target_pairs={{64,0},{128,64},{192,128},{65,1},{129,65},{193,129},{66,2},{130,66... | collective-permute-start | bytes 73736 | tf_op jit(solution)/shard_map/ppermute | solution.py:479
  53.4 3.5 %collective-permute-start.10 = (bf16[4,8,4,32,128]{4,3,2,1,0:T(8,128)(2,1)S(1)}, bf16[4,8,4,32,128]{4,3,2,1,0:T(8,128)(2,1)S(1)}, u32[]{:S(2)}, u32[]{:S(2)}) collective-permute-start(bf16[4,8,4,32,128]{4,3,2,1,0:T(8,128)(2,1)S(1)} %get-tuple-element.86), channel_id=1, source_target_pairs={{0,1},{1,0},{2,3},{3,2},{4,5},{5,4},{6,7},{7,6},{8,9},{9,8},{10,11... | collective-permute-start | bytes 3145736 | tf_op jit(solution)/shard_map/ppermute | solution.py:69
  57.2 8.8 %collective-permute-start.11 = (bf16[2,4,4,32,128]{4,3,2,1,0:T(8,128)(2,1)S(1)}, bf16[2,4,4,32,128]{4,3,2,1,0:T(8,128)(2,1)S(1)}, u32[]{:S(2)}, u32[]{:S(2)}) collective-permute-start(bf16[2,4,4,32,128]{4,3,2,1,0:T(8,128)(2,1)S(1)} %get-tuple-element.89), channel_id=1, source_target_pairs={{0,2},{1,3},{2,4},{3,5},{4,6},{5,7},{6,0},{7,1},{8,10},{9,11},{10,... | collective-permute-start | bytes 786440 | tf_op jit(solution)/shard_map/ppermute | solution.py:69
  57.3 8.7 %collective-permute-start.12 = (bf16[2,4,4,32,128]{4,3,2,1,0:T(8,128)(2,1)S(1)}, bf16[2,4,4,32,128]{4,3,2,1,0:T(8,128)(2,1)S(1)}, u32[]{:S(2)}, u32[]{:S(2)}) collective-permute-start(bf16[2,4,4,32,128]{4,3,2,1,0:T(8,128)(2,1)S(1)} %get-tuple-element.90), channel_id=1, source_target_pairs={{0,6},{1,7},{2,0},{3,1},{4,2},{5,3},{6,4},{7,5},{8,14},{9,15},{10,... | collective-permute-start | bytes 786440 | tf_op jit(solution)/shard_map/ppermute | solution.py:69
  60.0 13.8 %collective-permute-start.14 = (f32[3,4,32,108]{3,2,1,0:T(8,128)S(1)}, f32[3,4,32,108]{3,2,1,0:T(8,128)S(1)}, u32[]{:S(2)}, u32[]{:S(2)}) collective-permute-start(f32[3,4,32,108]{3,2,1,0:T(8,128)S(1)} %pad_maximum_fusion.state_ref), channel_id=1, source_target_pairs={{0,56},{1,57},{2,58},{3,59},{4,60},{5,61},{6,62},{7,63},{8,48},{9,... | collective-permute-start | bytes 497672 | tf_op jit(solution)/shard_map/ppermute | solution.py:69
  66.1 7.7 %collective-permute-start.13 = (bf16[4,4,32,128]{3,2,1,0:T(8,128)(2,1)S(1)}, bf16[4,4,32,128]{3,2,1,0:T(8,128)(2,1)S(1)}, u32[]{:S(2)}, u32[]{:S(2)}) collective-permute-start(bf16[4,4,32,128]{3,2,1,0:T(8,128)(2,1)S(1)} %get-tuple-element.93), channel_id=1, source_target_pairs={{0,2},{1,3},{2,4},{3,5},{4,6},{5,7},{6,0},{7,1},{8,10},{9,11},{10,... | collective-permute-start | bytes 393224 | tf_op jit(solution)/shard_map/ppermute | solution.py:69
  66.2 7.6 %collective-permute-start.15 = (bf16[4,4,32,128]{3,2,1,0:T(8,128)(2,1)S(1)}, bf16[4,4,32,128]{3,2,1,0:T(8,128)(2,1)S(1)}, u32[]{:S(2)}, u32[]{:S(2)}) collective-permute-start(bf16[4,4,32,128]{3,2,1,0:T(8,128)(2,1)S(1)} %get-tuple-element.96), channel_id=1, source_target_pairs={{0,6},{1,7},{2,0},{3,1},{4,2},{5,3},{6,4},{7,5},{8,14},{9,15},{10,... | collective-permute-start | bytes 393224 | tf_op jit(solution)/shard_map/ppermute | solution.py:69
  73.9 5.0 %collective-permute-start.16 = (bf16[2,4,32,128]{3,2,1,0:T(8,128)(2,1)S(1)}, bf16[2,4,32,128]{3,2,1,0:T(8,128)(2,1)S(1)}, u32[]{:S(2)}, u32[]{:S(2)}) collective-permute-start(bf16[2,4,32,128]{3,2,1,0:T(8,128)(2,1)S(1)} %get-tuple-element.98), channel_id=1, source_target_pairs={{0,24},{1,25},{2,26},{3,27},{4,28},{5,29},{6,30},{7,31},{8,16},{9,... | collective-permute-start | bytes 196616 | tf_op jit(solution)/shard_map/ppermute | solution.py:69
  75.6 5.8 %collective-permute-start.17 = (bf16[2,4,32,128]{3,2,1,0:T(8,128)(2,1)S(1)}, bf16[2,4,32,128]{3,2,1,0:T(8,128)(2,1)S(1)}, u32[]{:S(2)}, u32[]{:S(2)}) collective-permute-start(bf16[2,4,32,128]{3,2,1,0:T(8,128)(2,1)S(1)} %get-tuple-element.99), channel_id=1, source_target_pairs={{0,16},{1,17},{2,18},{3,19},{4,20},{5,21},{6,22},{7,23},{8,24},{9,... | collective-permute-start | bytes 196616 | tf_op jit(solution)/shard_map/ppermute | solution.py:69
  75.6 5.8 %collective-permute-start.18 = (bf16[2,4,32,128]{3,2,1,0:T(8,128)(2,1)S(1)}, bf16[2,4,32,128]{3,2,1,0:T(8,128)(2,1)S(1)}, u32[]{:S(2)}, u32[]{:S(2)}) collective-permute-start(bf16[2,4,32,128]{3,2,1,0:T(8,128)(2,1)S(1)} %get-tuple-element.100), channel_id=1, source_target_pairs={{0,8},{1,9},{2,10},{3,11},{4,12},{5,13},{6,14},{7,15},{8,0},{9,1},... | collective-permute-start | bytes 196616 | tf_op jit(solution)/shard_map/ppermute | solution.py:69
  81.5 5.7 %collective-permute-start.19 = (bf16[2,4,32,128]{3,2,1,0:T(8,128)(2,1)S(1)}, bf16[2,4,32,128]{3,2,1,0:T(8,128)(2,1)S(1)}, u32[]{:S(2)}, u32[]{:S(2)}) collective-permute-start(bf16[2,4,32,128]{3,2,1,0:T(8,128)(2,1)S(1)} %z_sum.1.mine_ref), channel_id=1, source_target_pairs={{0,56},{1,57},{2,58},{3,59},{4,60},{5,61},{6,62},{7,63},{8,48},{9,... | collective-permute-start | bytes 196616 | tf_op jit(solution)/shard_map/ppermute | solution.py:69
  88.0 6.8 %collective-permute-start.22 = (bf16[2,4,32,128]{3,2,1,0:T(8,128)(2,1)S(1)}, bf16[2,4,32,128]{3,2,1,0:T(8,128)(2,1)S(1)}, u32[]{:S(2)}, u32[]{:S(2)}) collective-permute-start(bf16[2,4,32,128]{3,2,1,0:T(8,128)(2,1)S(1)} %get-tuple-element.102), channel_id=1, source_target_pairs={{0,24},{1,25},{2,26},{3,27},{4,28},{5,29},{6,30},{7,31},{8,16},{9,... | collective-permute-start | bytes 196616 | tf_op jit(solution)/shard_map/ppermute | solution.py:69
  89.7 5.1 %collective-permute-start.21 = (bf16[2,4,32,128]{3,2,1,0:T(8,128)(2,1)S(1)}, bf16[2,4,32,128]{3,2,1,0:T(8,128)(2,1)S(1)}, u32[]{:S(2)}, u32[]{:S(2)}) collective-permute-start(bf16[2,4,32,128]{3,2,1,0:T(8,128)(2,1)S(1)} %get-tuple-element.102), channel_id=1, source_target_pairs={{0,16},{1,17},{2,18},{3,19},{4,20},{5,21},{6,22},{7,23},{8,24},{9,... | collective-permute-start | bytes 196616 | tf_op jit(solution)/shard_map/ppermute | solution.py:69
  89.8 3.9 %collective-permute-start.20 = (bf16[2,4,32,128]{3,2,1,0:T(8,128)(2,1)S(1)}, bf16[2,4,32,128]{3,2,1,0:T(8,128)(2,1)S(1)}, u32[]{:S(2)}, u32[]{:S(2)}) collective-permute-start(bf16[2,4,32,128]{3,2,1,0:T(8,128)(2,1)S(1)} %get-tuple-element.102), channel_id=1, source_target_pairs={{0,8},{1,9},{2,10},{3,11},{4,12},{5,13},{6,14},{7,15},{8,0},{9,1},... | collective-permute-start | bytes 196616 | tf_op jit(solution)/shard_map/ppermute | solution.py:69
  94.8 8.3 %collective-permute-start.25 = (bf16[8,4,32,128]{3,2,1,0:T(8,128)(2,1)S(1)}, bf16[8,4,32,128]{3,2,1,0:T(8,128)(2,1)S(1)}, u32[]{:S(2)}, u32[]{:S(2)}) collective-permute-start(bf16[8,4,32,128]{3,2,1,0:T(8,128)(2,1)S(1)} %constant_dynamic-update-slice_fusion.refs_0_), channel_id=1, source_target_pairs={{0,2},{1,3},{2,4},{3,5},{4,6},{5,7},{6,0},{7,1},{8,10},{9,11},{10,... | collective-permute-start | bytes 786440 | tf_op jit(solution)/shard_map/ppermute | solution.py:69
  94.9 12.9 %collective-permute-start.24 = (bf16[8,4,32,128]{3,2,1,0:T(8,128)(2,1)S(1)}, bf16[8,4,32,128]{3,2,1,0:T(8,128)(2,1)S(1)}, u32[]{:S(2)}, u32[]{:S(2)}) collective-permute-start(bf16[8,4,32,128]{3,2,1,0:T(8,128)(2,1)S(1)} %constant_dynamic-update-slice_fusion.refs_0_), channel_id=1, source_target_pairs={{0,6},{1,7},{2,0},{3,1},{4,2},{5,3},{6,4},{7,5},{8,14},{9,15},{10,... | collective-permute-start | bytes 786440 | tf_op jit(solution)/shard_map/ppermute | solution.py:69
  97.5 12.1 %collective-permute-start.23 = (bf16[8,4,32,128]{3,2,1,0:T(8,128)(2,1)S(1)}, bf16[8,4,32,128]{3,2,1,0:T(8,128)(2,1)S(1)}, u32[]{:S(2)}, u32[]{:S(2)}) collective-permute-start(bf16[8,4,32,128]{3,2,1,0:T(8,128)(2,1)S(1)} %constant_dynamic-update-slice_fusion.refs_0_), channel_id=1, source_target_pairs={{0,4},{1,5},{2,6},{3,7},{4,0},{5,1},{6,2},{7,3},{8,12},{9,13},{10,... | collective-permute-start | bytes 786440 | tf_op jit(solution)/shard_map/ppermute | solution.py:69
  97.5 13.0 %collective-permute-start.26 = (bf16[8,4,32,128]{3,2,1,0:T(8,128)(2,1)S(1)}, bf16[8,4,32,128]{3,2,1,0:T(8,128)(2,1)S(1)}, u32[]{:S(2)}, u32[]{:S(2)}) collective-permute-start(bf16[8,4,32,128]{3,2,1,0:T(8,128)(2,1)S(1)} %constant_dynamic-update-slice_fusion.refs_0_), channel_id=1, source_target_pairs={{0,1},{1,0},{2,3},{3,2},{4,5},{5,4},{6,7},{7,6},{8,9},{9,8},{10,11... | collective-permute-start | bytes 786440 | tf_op jit(solution)/shard_map/ppermute | solution.py:69
  103.1 7.5 %collective-permute-start.29 = (bf16[8,4,32,128]{3,2,1,0:T(8,128)(2,1)S(1)}, bf16[8,4,32,128]{3,2,1,0:T(8,128)(2,1)S(1)}, u32[]{:S(2)}, u32[]{:S(2)}) collective-permute-start(bf16[8,4,32,128]{3,2,1,0:T(8,128)(2,1)S(1)} %collective-permute-done.25.refs_3_), channel_id=1, source_target_pairs={{0,1},{1,0},{2,3},{3,2},{4,5},{5,4},{6,7},{7,6},{8,9},{9,8},{10,11... | collective-permute-start | bytes 786440 | tf_op jit(solution)/shard_map/ppermute | solution.py:69
  107.8 3.1 %collective-permute-start.28 = (bf16[8,4,32,128]{3,2,1,0:T(8,128)(2,1)S(1)}, bf16[8,4,32,128]{3,2,1,0:T(8,128)(2,1)S(1)}, u32[]{:S(2)}, u32[]{:S(2)}) collective-permute-start(bf16[8,4,32,128]{3,2,1,0:T(8,128)(2,1)S(1)} %collective-permute-done.24.refs_2_), channel_id=1, source_target_pairs={{0,1},{1,0},{2,3},{3,2},{4,5},{5,4},{6,7},{7,6},{8,9},{9,8},{10,11... | collective-permute-start | bytes 786440 | tf_op jit(solution)/shard_map/ppermute | solution.py:69
  109.7 2.1 %collective-permute-start.27 = (bf16[8,4,32,128]{3,2,1,0:T(8,128)(2,1)S(1)}, bf16[8,4,32,128]{3,2,1,0:T(8,128)(2,1)S(1)}, u32[]{:S(2)}, u32[]{:S(2)}) collective-permute-start(bf16[8,4,32,128]{3,2,1,0:T(8,128)(2,1)S(1)} %collective-permute-done.23.refs_1_), channel_id=1, source_target_pairs={{0,1},{1,0},{2,3},{3,2},{4,5},{5,4},{6,7},{7,6},{8,9},{9,8},{10,11... | collective-permute-start | bytes 786440 | tf_op jit(solution)/shard_map/ppermute | solution.py:69

commit v10 on v9

--- a/solution.py
+++ b/solution.py
@@ -25,6 +25,7 @@
 LANES = 128
 ZS, YS = 8, 4
 HALF = ZS // 2
+EARLY = 3
 Z_STEPS = (3, 2, 1)
 Z_PARTNER = 7
 Y_ORDER = (0, 2, 3, 1)
@@ -268,9 +269,12 @@
     )(*share, *above, *hidden)
 
 
-def core_sum_kernel(keep_ref, got_ref, own_ref, up_ref, down_ref, up_held, down_held):
+def core_sum_kernel(
+    keep_ref, got_ref, own_ref, up_ref, down_ref, up_held, down_held, up_late, down_late
+):
     here = y_pos()
     first, second = slice(0, HALF), slice(HALF, ZS)
+    direct = slice(HALF, HALF + EARLY)
 
     def block(ahead, half):
         y = lax.rem(here + ahead, YS)
@@ -278,10 +282,12 @@
 
     own_ref[first] = block(0, first)
     own_ref[second] = block(0, second)
-    up_ref[0] = block(2, first).astype(BF16)
-    up_ref[1] = block(1, second).astype(BF16)
-    down_ref[0] = block(2, second).astype(BF16)
-    down_ref[1] = block(3, first).astype(BF16)
+    up_ref[first] = block(2, first).astype(BF16)
+    up_ref[direct] = block(1, slice(HALF, HALF + EARLY)).astype(BF16)
+    up_late[...] = block(1, slice(HALF + EARLY, ZS)).astype(BF16)
+    down_ref[first] = block(2, second).astype(BF16)
+    down_ref[direct] = block(3, slice(0, EARLY)).astype(BF16)
+    down_late[...] = block(3, slice(EARLY, HALF)).astype(BF16)
     up_held[...] = block(1, first)
     down_held[...] = block(3, second)
 
@@ -291,29 +297,36 @@
     return pl.pallas_call(
         core_sum_kernel,
         out_shape=[shaped((ZS, BUCKETS, RANK, LANES), F32)]
-        + [shaped((2, *half), BF16)] * 2
-        + [shaped(half, F32)] * 2,
+        + [shaped((HALF + EARLY, *half[1:]), BF16)] * 2
+        + [shaped(half, F32)] * 2
+        + [shaped((HALF - EARLY, *half[1:]), BF16)] * 2,
         in_specs=[VMEM] * 2,
-        out_specs=[VMEM] * 5,
+        out_specs=[VMEM] * 7,
         compiler_params=params(8),
         name="core_sum",
     )(keep, got)
 
 
-def y_pass_kernel(up_held, from_below, down_held, from_above, up_ref, down_ref):
-    up_ref[...] = (up_held[...] + from_below[0].astype(F32)).astype(BF16)
-    down_ref[...] = (down_held[...] + from_above[0].astype(F32)).astype(BF16)
-
-
-def y_pass(up_held, from_below, down_held, from_above):
+def y_pass_kernel(
+    up_held, up_late, from_below, down_held, down_late, from_above, up_ref, down_ref
+):
+    for out, held, late, got in (
+        (up_ref, up_held, up_late, from_below),
+        (down_ref, down_held, down_late, from_above),
+    ):
+        out[0:HALF] = (held[...] + got[0:HALF].astype(F32)).astype(BF16)
+        out[HALF:] = late[...]
+
+
+def y_pass(*terms):
     return pl.pallas_call(
         y_pass_kernel,
-        out_shape=[shaped((HALF, BUCKETS, RANK, LANES), BF16)] * 2,
-        in_specs=[VMEM] * 4,
+        out_shape=[shaped((ZS - EARLY, BUCKETS, RANK, LANES), BF16)] * 2,
+        in_specs=[VMEM] * 6,
         out_specs=[VMEM] * 2,
         compiler_params=params(4),
         name="y_pass",
-    )(up_held, from_below, down_held, from_above)
+    )(*terms)
 
 
 def y_sum_kernel(own_ref, from_below, from_above, last_below, last_above, out_own, *outs):
@@ -322,8 +335,12 @@
         for far in range(2):
             z = here ^ (step ^ (far * Z_PARTNER))
             place = z & (HALF - 1)
-            first = from_above[1, place].astype(F32) + last_below[place].astype(F32)
-            second = from_below[1, place].astype(F32) + last_above[place].astype(F32)
+            early = HALF + jnp.minimum(place, EARLY - 1)
+            late = HALF + jnp.maximum(place - EARLY, 0)
+            above = jnp.where(place < EARLY, from_above[early], last_above[late])
+            below = jnp.where(place < EARLY, from_below[early], last_below[late])
+            first = above.astype(F32) + last_below[place].astype(F32)
+            second = below.astype(F32) + last_above[place].astype(F32)
             total = own_ref[z] + jnp.where(z < HALF, first, second)
             out[far] = total.astype(out.dtype)
 
@@ -482,11 +499,13 @@
             hidden += [activation(pre, False, b) for b in buckets]
             above, state, *hidden = lax.optimization_barrier((above, state, *hidden))
     keep, send = grads(share, above, hidden)
-    own, up, down, up_held, down_held = core_sum(keep, over_dp(send, dc=1))
+    own, up, down, up_held, down_held, up_late, down_late = core_sum(
+        keep, over_dp(send, dc=1)
+    )
     state, own = lax.optimization_barrier((state, own))
     partner_state = over_dp(state, zx=Z_PARTNER)
     from_below, from_above = over_dp(up, dy=1), over_dp(down, dy=-1)
-    up, down = y_pass(up_held, from_below, down_held, from_above)
+    up, down = y_pass(up_held, up_late, from_below, down_held, down_late, from_above)
     last_below, last_above = over_dp(up, dy=1), over_dp(down, dy=-1)
     last_below, partner_state = lax.optimization_barrier((last_below, partner_state))
     own, *sends = y_sum(own, from_below, from_above, last_below, last_above)

time: 115 us -> 116 us (level)
  waiting for transfers between devices: 24.3 us -> 26 us
    ppermute x21, waiting for transfers between devices: 19.3 us -> 20.9 us  [over_dp(): return lax.ppermute(value, 'dp', pairs)]
where the time goes in v10:
time: 116 us; the launch traced here: 115 us
  starting transfers between devices  53.5 us (46%)
  Pallas kernels  34.3 us (30%)
  waiting for transfers between devices  26 us (22%)
    ppermute x21, starting transfers between devices, over_dp(): return lax.ppermute(value, 'dp', pairs)  41.4 us
    ppermute x21, waiting for transfers between devices, over_dp(): return lax.ppermute(value, 'dp', pairs)  20.9 us
    pallas_call x6, Pallas kernels, activation(): pl.pallas_call(functools.partial(activation_kernel, slope, bucket * BUCKE...  15.2 us
    pallas_call x3, Pallas kernels, relay(): pl.pallas_call(functools.partial(relay_kernel, top), out_shape=[message,...  12.5 us
    ppermute x6, starting transfers between devices, over_section(): lax.ppermute(value, 'section', [(i, (i + steps) % 4) for i in range(4)])  8 us
    ppermute x3, waiting for transfers between devices, per_device(): above = [above[0], lax.ppermute(sent, 'section', [(1, 0), (2, 1), (3, 2)])]  4.55 us
    ppermute x3, starting transfers between devices, per_device(): above = [above[0], lax.ppermute(sent, 'section', [(1, 0), (2, 1), (3, 2)])]  4.07 us
  transfers between devices with their start and end apart: 30, of which 13 were waited for; matrix products, arithmetic and copies ran while one was open for 0% of the time, Pallas kernels for 13%

profile of v10, /device:TPU:1, one launch (start us, length us, event | category | flops | bytes accessed | tf_op | source)
XLA Modules:
  0.0 114.9 jit_solution(14399063077994571517)
XLA Ops:
  0.6 1.2 %slices.1 = (bf16[32,1920]{1,0:T(8,128)(2,1)S(1)}, bf16[32,1920]{1,0:T(8,128)(2,1)S(1)}, bf16[32,1920]{1,0:T(8,128)(2,1)S(1)}, bf16[32,1920]{1,0:T(8,128)(2,1)S(1)}) custom-call(bf16[32,5120]{1,0:T(8,128)(2,1)} %bitcast.51, bf16[32,5120]{1,0:T(8,128)(2,1)} %bitcast.52), custom_call_target="tpu_custom_call" | custom-call | tf_op jit(solution)/shard_map/slices/pallas_call | solution.py:98
  1.8 2.1 %collective-permute-start = (bf16[32,1920]{1,0:T(8,128)(2,1)S(1)}, bf16[32,1920]{1,0:T(8,128)(2,1)S(1)}, u32[]{:S(2)}, u32[]{:S(2)}) collective-permute-start(bf16[32,1920]{1,0:T(8,128)(2,1)S(1)} %get-tuple-element.58), channel_id=1, source_target_pairs={{0,64},{64,128},{128,192},{192,0},{1,65},{65,129},{129,193},{193,1... | collective-permute-start | bytes 368648 | tf_op jit(solution)/shard_map/ppermute | solution.py:74
  3.9 1.4 %collective-permute-start.1 = (bf16[32,1920]{1,0:T(8,128)(2,1)S(1)}, bf16[32,1920]{1,0:T(8,128)(2,1)S(1)}, u32[]{:S(2)}, u32[]{:S(2)}) collective-permute-start(bf16[32,1920]{1,0:T(8,128)(2,1)S(1)} %get-tuple-element.59), channel_id=1, source_target_pairs={{0,192},{64,0},{128,64},{192,128},{1,193},{65,1},{129,65},{193,129... | collective-permute-start | bytes 368648 | tf_op jit(solution)/shard_map/ppermute | solution.py:74
  5.3 1.6 %collective-permute-start.2 = (bf16[32,1920]{1,0:T(8,128)(2,1)S(1)}, bf16[32,1920]{1,0:T(8,128)(2,1)S(1)}, u32[]{:S(2)}, u32[]{:S(2)}) collective-permute-start(bf16[32,1920]{1,0:T(8,128)(2,1)S(1)} %get-tuple-element.60), channel_id=1, source_target_pairs={{0,128},{64,192},{128,0},{192,64},{1,129},{65,193},{129,1},{193,65... | collective-permute-start | bytes 368648 | tf_op jit(solution)/shard_map/ppermute | solution.py:74
  6.9 5.0 %slope.2.refs_0_.refs_2_ = bf16[128,20736]{1,0:T(8,128)(2,1)S(1)} custom-call(bf16[128,27648]{1,0:T(8,128)(2,1)} %bitcast.44), custom_call_target="tpu_custom_call" | custom-call | flops 26542080 | bytes 10616832 | tf_op jit(solution)/shard_map/slope/pallas_call | solution.py:139
  11.9 0.0 collective-permute-done.w1
  11.9 0.0 collective-permute-done.2.w2
  12.0 0.7 shares.1
  12.7 1.6 %collective-permute-start.3 = (f32[32,256]{1,0:T(8,128)S(1)}, f32[32,256]{1,0:T(8,128)S(1)}, u32[]{:S(2)}, u32[]{:S(2)}) collective-permute-start(f32[32,256]{1,0:T(8,128)S(1)} %get-tuple-element.66), channel_id=1, source_target_pairs={{0,192},{64,0},{128,64},{192,128},{1,193},{65,1},{129,65},{193,129... | collective-permute-start | bytes 98312 | tf_op jit(solution)/shard_map/ppermute | solution.py:74
  14.3 0.0 collective-permute-start.4
  14.3 1.3 %collective-permute-start.5 = (f32[32,256]{1,0:T(8,128)S(1)}, f32[32,256]{1,0:T(8,128)S(1)}, u32[]{:S(2)}, u32[]{:S(2)}) collective-permute-start(f32[32,256]{1,0:T(8,128)S(1)} %get-tuple-element.68), channel_id=1, source_target_pairs={{0,128},{64,192},{128,0},{192,64},{1,129},{65,193},{129,1},{193,65... | collective-permute-start | bytes 98312 | tf_op jit(solution)/shard_map/ppermute | solution.py:74
  15.6 2.5 %slope.3.refs_1_.refs_3_ = bf16[128,6912]{1,0:T(8,128)(2,1)S(1)} custom-call(bf16[128,27648]{1,0:T(8,128)(2,1)} %bitcast.45), custom_call_target="tpu_custom_call" | custom-call | flops 8847360 | bytes 3538944 | tf_op jit(solution)/shard_map/slope/pallas_call | solution.py:139
  18.1 0.0 collective-permute-done.3.s1
  18.1 0.2 collective-permute-done.4.s2
  18.3 0.3 collective-permute-done.5.s3
  18.7 0.0 copy-start.5
  18.7 4.1 %relay_first.1 = (bf16[96,128]{1,0:T(8,128)(2,1)S(1)}, f32[32,128]{1,0:T(8,128)S(1)}) custom-call(f32[32,256]{1,0:T(8,128)S(1)} %get-tuple-element.65.s0, f32[32,256]{1,0:T(8,128)S(1)} %collective-permute-done.3.s1, f32[32,256]{1,0:T(8,128)S(1)} %collective-permute-done.4.s2, f32[32,256]{1,0:T(8,128)S(1)} %collective-permute-done.5.s3, ...), custom_call_target="tpu_custom_call" | custom-call | tf_op jit(solution)/shard_map/relay_first/pallas_call | solution.py:224
  22.8 4.4 %collective-permute-start.6 = (f32[32,128]{1,0:T(8,128)S(1)}, f32[32,128]{1,0:T(8,128)S(1)}, u32[]{:S(2)}, u32[]{:S(2)}) collective-permute-start(f32[32,128]{1,0:T(8,128)S(1)} %get-tuple-element.71), channel_id=1, source_target_pairs={{0,1},{1,0},{2,3},{3,2},{4,5},{5,4},{6,7},{7,6},{8,9},{9,8},{10,11... | collective-permute-start | bytes 49160 | tf_op jit(solution)/shard_map/ppermute | solution.py:70
  27.1 1.5 %collective-permute-start.7 = (bf16[96,128]{1,0:T(8,128)(2,1)S(1)}, bf16[96,128]{1,0:T(8,128)(2,1)S(1)}, u32[]{:S(2)}, u32[]{:S(2)}) collective-permute-start(bf16[96,128]{1,0:T(8,128)(2,1)S(1)} %get-tuple-element.72), channel_id=1, source_target_pairs={{64,0},{128,64},{192,128},{65,1},{129,65},{193,129},{66,2},{130,66... | collective-permute-start | bytes 73736 | tf_op jit(solution)/shard_map/ppermute | solution.py:496
  28.7 1.9 %hidden.5.h1 = bf16[128,6912]{1,0:T(8,128)(2,1)S(1)} custom-call(bf16[128,27648]{1,0:T(8,128)(2,1)} %bitcast.46), custom_call_target="tpu_custom_call" | custom-call | flops 8847360 | bytes 3538944 | tf_op jit(solution)/shard_map/hidden/pallas_call | solution.py:139
  30.6 1.9 %hidden.4.h0 = bf16[128,6912]{1,0:T(8,128)(2,1)S(1)} custom-call(bf16[128,27648]{1,0:T(8,128)(2,1)} %bitcast.47), custom_call_target="tpu_custom_call" | custom-call | flops 8847360 | bytes 3538944 | tf_op jit(solution)/shard_map/hidden/pallas_call | solution.py:139
  32.5 0.0 collective-permute-done.7.refs_1_
  32.6 4.2 %relay.2 = bf16[96,128]{1,0:T(8,128)(2,1)S(1)} custom-call(f32[32,256]{1,0:T(8,128)S(1)} %get-tuple-element.65.s0, f32[32,256]{1,0:T(8,128)S(1)} %collective-permute-done.3.s1, f32[32,256]{1,0:T(8,128)S(1)} %collective-permute-done.4.s2, f32[32,256]{1,0:T(8,128)S(1)} %collective-permute-done.5.s3, f32[32,128]{1,0:T(8,128)S(1)} %collective-permute-done.6.refs_0_.other_ref, ...), custom_call_target="tpu_custom_call" | custom-call | tf_op jit(solution)/shard_map/relay/pallas_call | solution.py:224
  36.8 1.3 %collective-permute-start.8 = (bf16[96,128]{1,0:T(8,128)(2,1)S(1)}, bf16[96,128]{1,0:T(8,128)(2,1)S(1)}, u32[]{:S(2)}, u32[]{:S(2)}) collective-permute-start(bf16[96,128]{1,0:T(8,128)(2,1)S(1)} %relay.2), channel_id=1, source_target_pairs={{64,0},{128,64},{192,128},{65,1},{129,65},{193,129},{66,2},{130,66... | collective-permute-start | bytes 73736 | tf_op jit(solution)/shard_map/ppermute | solution.py:496
  38.1 1.9 %hidden.7.h3 = bf16[128,6912]{1,0:T(8,128)(2,1)S(1)} custom-call(bf16[128,27648]{1,0:T(8,128)(2,1)} %bitcast.48), custom_call_target="tpu_custom_call" | custom-call | flops 8847360 | bytes 3538944 | tf_op jit(solution)/shard_map/hidden/pallas_call | solution.py:139
  40.0 1.9 %hidden.6.h2 = bf16[128,6912]{1,0:T(8,128)(2,1)S(1)} custom-call(bf16[128,27648]{1,0:T(8,128)(2,1)} %bitcast.49), custom_call_target="tpu_custom_call" | custom-call | flops 8847360 | bytes 3538944 | tf_op jit(solution)/shard_map/hidden/pallas_call | solution.py:139
  42.0 0.0 collective-permute-done.8.refs_1_
  42.0 4.2 %relay.3 = bf16[96,128]{1,0:T(8,128)(2,1)S(1)} custom-call(f32[32,256]{1,0:T(8,128)S(1)} %get-tuple-element.65.s0, f32[32,256]{1,0:T(8,128)S(1)} %collective-permute-done.3.s1, f32[32,256]{1,0:T(8,128)S(1)} %collective-permute-done.4.s2, f32[32,256]{1,0:T(8,128)S(1)} %collective-permute-done.5.s3, f32[32,128]{1,0:T(8,128)S(1)} %collective-permute-done.6.refs_0_.other_ref, ...), custom_call_target="tpu_custom_call" | custom-call | tf_op jit(solution)/shard_map/relay/pallas_call | solution.py:224
  46.2 1.3 %collective-permute-start.9 = (bf16[96,128]{1,0:T(8,128)(2,1)S(1)}, bf16[96,128]{1,0:T(8,128)(2,1)S(1)}, u32[]{:S(2)}, u32[]{:S(2)}) collective-permute-start(bf16[96,128]{1,0:T(8,128)(2,1)S(1)} %relay.3), channel_id=1, source_target_pairs={{64,0},{128,64},{192,128},{65,1},{129,65},{193,129},{66,2},{130,66... | collective-permute-start | bytes 73736 | tf_op jit(solution)/shard_map/ppermute | solution.py:496
  47.5 4.5 %collective-permute-done.9.above_ref = bf16[96,128]{1,0:T(8,128)(2,1)S(1)} collective-permute-done((bf16[96,128]{1,0:T(8,128)(2,1)S(1)}, bf16[96,128]{1,0:T(8,128)(2,1)S(1)}, u32[]{:S(2)}, u32[]{:S(2)}) %collective-permute-start.9) | collective-permute-done | bytes 24608 | tf_op jit(solution)/shard_map/ppermute | solution.py:496
  52.0 1.4 %grads.1 = (bf16[4,8,4,32,128]{4,3,2,1,0:T(8,128)(2,1)S(1)}, bf16[4,8,4,32,128]{4,3,2,1,0:T(8,128)(2,1)S(1)}) custom-call(f32[32,256]{1,0:T(8,128)S(1)} %get-tuple-element.65.s0, f32[32,256]{1,0:T(8,128)S(1)} %collective-permute-done.3.s1, f32[32,256]{1,0:T(8,128)S(1)} %collective-permute-done.4.s2, f32[32,256]{1,0:T(8,128)S(1)} %collective-permute-done.5.s3, ...), custom_call_target="tpu_custom_call" | custom-call | tf_op jit(solution)/shard_map/grads/pallas_call | solution.py:261
  53.4 1.3 %collective-permute-start.10 = (bf16[4,8,4,32,128]{4,3,2,1,0:T(8,128)(2,1)S(1)}, bf16[4,8,4,32,128]{4,3,2,1,0:T(8,128)(2,1)S(1)}, u32[]{:S(2)}, u32[]{:S(2)}) collective-permute-start(bf16[4,8,4,32,128]{4,3,2,1,0:T(8,128)(2,1)S(1)} %get-tuple-element.88), channel_id=1, source_target_pairs={{0,1},{1,0},{2,3},{3,2},{4,5},{5,4},{6,7},{7,6},{8,9},{9,8},{10,11... | collective-permute-start | bytes 3145736 | tf_op jit(solution)/shard_map/ppermute | solution.py:70
  54.7 2.3 %collective-permute-done.10.got_ref = bf16[4,8,4,32,128]{4,3,2,1,0:T(8,128)(2,1)S(1)} collective-permute-done((bf16[4,8,4,32,128]{4,3,2,1,0:T(8,128)(2,1)S(1)}, bf16[4,8,4,32,128]{4,3,2,1,0:T(8,128)(2,1)S(1)}, u32[]{:S(2)}, u32[]{:S(2)}) %collective-permute-start.10) | collective-permute-done | bytes 1048608 | tf_op jit(solution)/shard_map/ppermute | solution.py:70
  57.0 0.2 core_sum.1
  57.2 0.1 collective-permute-start.11
  57.3 2.7 %collective-permute-start.12 = (bf16[7,4,32,128]{3,2,1,0:T(8,128)(2,1)S(1)}, bf16[7,4,32,128]{3,2,1,0:T(8,128)(2,1)S(1)}, u32[]{:S(2)}, u32[]{:S(2)}) collective-permute-start(bf16[7,4,32,128]{3,2,1,0:T(8,128)(2,1)S(1)} %get-tuple-element.92), channel_id=1, source_target_pairs={{0,6},{1,7},{2,0},{3,1},{4,2},{5,3},{6,4},{7,5},{8,14},{9,15},{10,... | collective-permute-start | bytes 688136 | tf_op jit(solution)/shard_map/ppermute | solution.py:70
  60.0 4.7 %collective-permute-start.14 = (f32[3,4,32,108]{3,2,1,0:T(8,128)S(1)}, f32[3,4,32,108]{3,2,1,0:T(8,128)S(1)}, u32[]{:S(2)}, u32[]{:S(2)}) collective-permute-start(f32[3,4,32,108]{3,2,1,0:T(8,128)S(1)} %pad_maximum_fusion.state_ref), channel_id=1, source_target_pairs={{0,56},{1,57},{2,58},{3,59},{4,60},{5,61},{6,62},{7,63},{8,48},{9,... | collective-permute-start | bytes 497672 | tf_op jit(solution)/shard_map/ppermute | solution.py:70
  64.6 0.7 collective-permute-done.11.from_below
  65.3 0.0 collective-permute-done.12.from_above
  65.4 0.1 collective-permute-start.13
  65.5 2.7 %collective-permute-start.15 = (bf16[5,4,32,128]{3,2,1,0:T(8,128)(2,1)S(1)}, bf16[5,4,32,128]{3,2,1,0:T(8,128)(2,1)S(1)}, u32[]{:S(2)}, u32[]{:S(2)}) collective-permute-start(bf16[5,4,32,128]{3,2,1,0:T(8,128)(2,1)S(1)} %get-tuple-element.100), channel_id=1, source_target_pairs={{0,6},{1,7},{2,0},{3,1},{4,2},{5,3},{6,4},{7,5},{8,14},{9,15},{10,... | collective-permute-start | bytes 491528 | tf_op jit(solution)/shard_map/ppermute | solution.py:70
  68.1 5.7 %collective-permute-done.14.partner_ref = f32[3,4,32,108]{3,2,1,0:T(8,128)S(1)} collective-permute-done((f32[3,4,32,108]{3,2,1,0:T(8,128)S(1)}, f32[3,4,32,108]{3,2,1,0:T(8,128)S(1)}, u32[]{:S(2)}, u32[]{:S(2)}) %collective-permute-start.14) | collective-permute-done | bytes 165920 | tf_op jit(solution)/shard_map/ppermute | solution.py:70
  73.8 0.2 y_sum.1
  74.0 1.7 %collective-permute-start.16 = (bf16[2,4,32,128]{3,2,1,0:T(8,128)(2,1)S(1)}, bf16[2,4,32,128]{3,2,1,0:T(8,128)(2,1)S(1)}, u32[]{:S(2)}, u32[]{:S(2)}) collective-permute-start(bf16[2,4,32,128]{3,2,1,0:T(8,128)(2,1)S(1)} %get-tuple-element.102), channel_id=1, source_target_pairs={{0,24},{1,25},{2,26},{3,27},{4,28},{5,29},{6,30},{7,31},{8,16},{9,... | collective-permute-start | bytes 196616 | tf_op jit(solution)/shard_map/ppermute | solution.py:70
  75.7 1.9 %collective-permute-start.18 = (bf16[2,4,32,128]{3,2,1,0:T(8,128)(2,1)S(1)}, bf16[2,4,32,128]{3,2,1,0:T(8,128)(2,1)S(1)}, u32[]{:S(2)}, u32[]{:S(2)}) collective-permute-start(bf16[2,4,32,128]{3,2,1,0:T(8,128)(2,1)S(1)} %get-tuple-element.104), channel_id=1, source_target_pairs={{0,8},{1,9},{2,10},{3,11},{4,12},{5,13},{6,14},{7,15},{8,0},{9,1},... | collective-permute-start | bytes 196616 | tf_op jit(solution)/shard_map/ppermute | solution.py:70
  77.6 1.4 %collective-permute-done.16.g1 = bf16[2,4,32,128]{3,2,1,0:T(8,128)(2,1)S(1)} collective-permute-done((bf16[2,4,32,128]{3,2,1,0:T(8,128)(2,1)S(1)}, bf16[2,4,32,128]{3,2,1,0:T(8,128)(2,1)S(1)}, u32[]{:S(2)}, u32[]{:S(2)}) %collective-permute-start.16) | collective-permute-done | bytes 65568 | tf_op jit(solution)/shard_map/ppermute | solution.py:70
  79.0 3.2 %collective-permute-done.17.g2 = bf16[2,4,32,128]{3,2,1,0:T(8,128)(2,1)S(1)} collective-permute-done((bf16[2,4,32,128]{3,2,1,0:T(8,128)(2,1)S(1)}, bf16[2,4,32,128]{3,2,1,0:T(8,128)(2,1)S(1)}, u32[]{:S(2)}, u32[]{:S(2)}) %collective-permute-start.17) | collective-permute-done | bytes 65568 | tf_op jit(solution)/shard_map/ppermute | solution.py:70
  82.3 2.6 %collective-permute-start.19 = (bf16[2,4,32,128]{3,2,1,0:T(8,128)(2,1)S(1)}, bf16[2,4,32,128]{3,2,1,0:T(8,128)(2,1)S(1)}, u32[]{:S(2)}, u32[]{:S(2)}) collective-permute-start(bf16[2,4,32,128]{3,2,1,0:T(8,128)(2,1)S(1)} %z_sum.1.mine_ref), channel_id=1, source_target_pairs={{0,56},{1,57},{2,58},{3,59},{4,60},{5,61},{6,62},{7,63},{8,48},{9,... | collective-permute-start | bytes 196616 | tf_op jit(solution)/shard_map/ppermute | solution.py:70
  84.9 2.5 %collective-permute-done.19.got_ref = bf16[2,4,32,128]{3,2,1,0:T(8,128)(2,1)S(1)} collective-permute-done((bf16[2,4,32,128]{3,2,1,0:T(8,128)(2,1)S(1)}, bf16[2,4,32,128]{3,2,1,0:T(8,128)(2,1)S(1)}, u32[]{:S(2)}, u32[]{:S(2)}) %collective-permute-start.19) | collective-permute-done | bytes 65568 | tf_op jit(solution)/shard_map/ppermute | solution.py:70
  87.4 0.7 adamw.1
  88.1 1.3 %collective-permute-start.22 = (bf16[2,4,32,128]{3,2,1,0:T(8,128)(2,1)S(1)}, bf16[2,4,32,128]{3,2,1,0:T(8,128)(2,1)S(1)}, u32[]{:S(2)}, u32[]{:S(2)}) collective-permute-start(bf16[2,4,32,128]{3,2,1,0:T(8,128)(2,1)S(1)} %get-tuple-element.106), channel_id=1, source_target_pairs={{0,24},{1,25},{2,26},{3,27},{4,28},{5,29},{6,30},{7,31},{8,16},{9,... | collective-permute-start | bytes 196616 | tf_op jit(solution)/shard_map/ppermute | solution.py:70
  89.5 0.5 collective-permute-start.21
  90.0 1.7 %collective-permute-start.20 = (bf16[2,4,32,128]{3,2,1,0:T(8,128)(2,1)S(1)}, bf16[2,4,32,128]{3,2,1,0:T(8,128)(2,1)S(1)}, u32[]{:S(2)}, u32[]{:S(2)}) collective-permute-start(bf16[2,4,32,128]{3,2,1,0:T(8,128)(2,1)S(1)} %get-tuple-element.106), channel_id=1, source_target_pairs={{0,8},{1,9},{2,10},{3,11},{4,12},{5,13},{6,14},{7,15},{8,0},{9,1},... | collective-permute-start | bytes 196616 | tf_op jit(solution)/shard_map/ppermute | solution.py:70
  91.7 2.2 %collective-permute-done.20 = bf16[2,4,32,128]{3,2,1,0:T(8,128)(2,1)S(1)} collective-permute-done((bf16[2,4,32,128]{3,2,1,0:T(8,128)(2,1)S(1)}, bf16[2,4,32,128]{3,2,1,0:T(8,128)(2,1)S(1)}, u32[]{:S(2)}, u32[]{:S(2)}) %collective-permute-start.20) | collective-permute-done | bytes 65568 | tf_op jit(solution)/shard_map/ppermute | solution.py:70
  93.9 1.8 %collective-permute-done.21 = bf16[2,4,32,128]{3,2,1,0:T(8,128)(2,1)S(1)} collective-permute-done((bf16[2,4,32,128]{3,2,1,0:T(8,128)(2,1)S(1)}, bf16[2,4,32,128]{3,2,1,0:T(8,128)(2,1)S(1)}, u32[]{:S(2)}, u32[]{:S(2)}) %collective-permute-start.21) | collective-permute-done | bytes 65568 | tf_op jit(solution)/shard_map/ppermute | solution.py:70
  95.7 0.1 collective-permute-start.25
  95.8 2.7 %collective-permute-start.24 = (bf16[8,4,32,128]{3,2,1,0:T(8,128)(2,1)S(1)}, bf16[8,4,32,128]{3,2,1,0:T(8,128)(2,1)S(1)}, u32[]{:S(2)}, u32[]{:S(2)}) collective-permute-start(bf16[8,4,32,128]{3,2,1,0:T(8,128)(2,1)S(1)} %constant_dynamic-update-slice_fusion.refs_0_), channel_id=1, source_target_pairs={{0,6},{1,7},{2,0},{3,1},{4,2},{5,3},{6,4},{7,5},{8,14},{9,15},{10,... | collective-permute-start | bytes 786440 | tf_op jit(solution)/shard_map/ppermute | solution.py:70
  98.5 4.3 %collective-permute-start.26 = (bf16[8,4,32,128]{3,2,1,0:T(8,128)(2,1)S(1)}, bf16[8,4,32,128]{3,2,1,0:T(8,128)(2,1)S(1)}, u32[]{:S(2)}, u32[]{:S(2)}) collective-permute-start(bf16[8,4,32,128]{3,2,1,0:T(8,128)(2,1)S(1)} %constant_dynamic-update-slice_fusion.refs_0_), channel_id=1, source_target_pairs={{0,1},{1,0},{2,3},{3,2},{4,5},{5,4},{6,7},{7,6},{8,9},{9,8},{10,11... | collective-permute-start | bytes 786440 | tf_op jit(solution)/shard_map/ppermute | solution.py:70
  102.8 5.8 %collective-permute-start.29 = (bf16[8,4,32,128]{3,2,1,0:T(8,128)(2,1)S(1)}, bf16[8,4,32,128]{3,2,1,0:T(8,128)(2,1)S(1)}, u32[]{:S(2)}, u32[]{:S(2)}) collective-permute-start(bf16[8,4,32,128]{3,2,1,0:T(8,128)(2,1)S(1)} %collective-permute-done.25.refs_3_), channel_id=1, source_target_pairs={{0,1},{1,0},{2,3},{3,2},{4,5},{5,4},{6,7},{7,6},{8,9},{9,8},{10,11... | collective-permute-start | bytes 786440 | tf_op jit(solution)/shard_map/ppermute | solution.py:70
  108.5 2.1 %collective-permute-start.28 = (bf16[8,4,32,128]{3,2,1,0:T(8,128)(2,1)S(1)}, bf16[8,4,32,128]{3,2,1,0:T(8,128)(2,1)S(1)}, u32[]{:S(2)}, u32[]{:S(2)}) collective-permute-start(bf16[8,4,32,128]{3,2,1,0:T(8,128)(2,1)S(1)} %collective-permute-done.24.refs_2_), channel_id=1, source_target_pairs={{0,1},{1,0},{2,3},{3,2},{4,5},{5,4},{6,7},{7,6},{8,9},{9,8},{10,11... | collective-permute-start | bytes 786440 | tf_op jit(solution)/shard_map/ppermute | solution.py:70
  110.6 0.9 collective-permute-start.27
  111.5 0.3 collective-permute-done.28.refs_6_
  111.8 0.9 collective-permute-done.27.refs_5_
  112.7 2.1 %assemble.1 = bf16[32,27648]{1,0:T(8,128)(2,1)} custom-call(bf16[8,4,32,128]{3,2,1,0:T(8,128)(2,1)S(1)} %constant_dynamic-update-slice_fusion.refs_0_, bf16[8,4,32,128]{3,2,1,0:T(8,128)(2,1)S(1)} %collective-permute-done.23.refs_1_, bf16[8,4,32,128]{3,2,1,0:T(8,128)(2,1)S(1)} %collective-permute-done.24.refs_2_, ...), custom_call_target="tpu_custom_call" | custom-call | tf_op jit(solution)/shard_map/assemble/pallas_call | solution.py:461
  (31 shorter events, 0.2 us)
Async XLA Ops:
  1.8 10.1 %collective-permute-start = (bf16[32,1920]{1,0:T(8,128)(2,1)S(1)}, bf16[32,1920]{1,0:T(8,128)(2,1)S(1)}, u32[]{:S(2)}, u32[]{:S(2)}) collective-permute-start(bf16[32,1920]{1,0:T(8,128)(2,1)S(1)} %get-tuple-element.58), channel_id=1, source_target_pairs={{0,64},{64,128},{128,192},{192,0},{1,65},{65,129},{129,193},{193,1... | collective-permute-start | bytes 368648 | tf_op jit(solution)/shard_map/ppermute | solution.py:74
  3.9 8.0 %collective-permute-start.1 = (bf16[32,1920]{1,0:T(8,128)(2,1)S(1)}, bf16[32,1920]{1,0:T(8,128)(2,1)S(1)}, u32[]{:S(2)}, u32[]{:S(2)}) collective-permute-start(bf16[32,1920]{1,0:T(8,128)(2,1)S(1)} %get-tuple-element.59), channel_id=1, source_target_pairs={{0,192},{64,0},{128,64},{192,128},{1,193},{65,1},{129,65},{193,129... | collective-permute-start | bytes 368648 | tf_op jit(solution)/shard_map/ppermute | solution.py:74
  5.3 6.7 %collective-permute-start.2 = (bf16[32,1920]{1,0:T(8,128)(2,1)S(1)}, bf16[32,1920]{1,0:T(8,128)(2,1)S(1)}, u32[]{:S(2)}, u32[]{:S(2)}) collective-permute-start(bf16[32,1920]{1,0:T(8,128)(2,1)S(1)} %get-tuple-element.60), channel_id=1, source_target_pairs={{0,128},{64,192},{128,0},{192,64},{1,129},{65,193},{129,1},{193,65... | collective-permute-start | bytes 368648 | tf_op jit(solution)/shard_map/ppermute | solution.py:74
  6.9 5.0 %copy-start.2 = (bf16[128,1280]{1,0:T(8,128)(2,1)S(1)}, bf16[128,1280]{1,0:T(8,128)(2,1)}, u32[]{:S(2)}) copy-start(bf16[128,1280]{1,0:T(8,128)(2,1)} %g_ref.1) | copy-start | bytes 983044
  12.7 5.4 %collective-permute-start.3 = (f32[32,256]{1,0:T(8,128)S(1)}, f32[32,256]{1,0:T(8,128)S(1)}, u32[]{:S(2)}, u32[]{:S(2)}) collective-permute-start(f32[32,256]{1,0:T(8,128)S(1)} %get-tuple-element.66), channel_id=1, source_target_pairs={{0,192},{64,0},{128,64},{192,128},{1,193},{65,1},{129,65},{193,129... | collective-permute-start | bytes 98312 | tf_op jit(solution)/shard_map/ppermute | solution.py:74
  14.3 4.0 %collective-permute-start.4 = (f32[32,256]{1,0:T(8,128)S(1)}, f32[32,256]{1,0:T(8,128)S(1)}, u32[]{:S(2)}, u32[]{:S(2)}) collective-permute-start(f32[32,256]{1,0:T(8,128)S(1)} %get-tuple-element.67), channel_id=1, source_target_pairs={{0,64},{64,128},{128,192},{192,0},{1,65},{65,129},{129,193},{193,1... | collective-permute-start | bytes 98312 | tf_op jit(solution)/shard_map/ppermute | solution.py:74
  14.3 4.3 %collective-permute-start.5 = (f32[32,256]{1,0:T(8,128)S(1)}, f32[32,256]{1,0:T(8,128)S(1)}, u32[]{:S(2)}, u32[]{:S(2)}) collective-permute-start(f32[32,256]{1,0:T(8,128)S(1)} %get-tuple-element.68), channel_id=1, source_target_pairs={{0,128},{64,192},{128,0},{192,64},{1,129},{65,193},{129,1},{193,65... | collective-permute-start | bytes 98312 | tf_op jit(solution)/shard_map/ppermute | solution.py:74
  15.6 3.1 %copy-start = (bf16[1,27648,32]{1,2,0:T(8,128)(2,1)S(1)}, bf16[1,27648,32]{1,2,0:T(8,128)(2,1)}, u32[]{:S(2)}) copy-start(bf16[1,27648,32]{1,2,0:T(8,128)(2,1)} %param.11) | copy-start | bytes 5308420
  15.6 3.1 %copy-start.1 = (bf16[1,27648,32]{1,2,0:T(8,128)(2,1)S(1)}, bf16[1,27648,32]{1,2,0:T(8,128)(2,1)}, u32[]{:S(2)}) copy-start(bf16[1,27648,32]{1,2,0:T(8,128)(2,1)} %param.14) | copy-start | bytes 5308420
  18.7 10.0 %copy-start.3 = (f32[1,4,108,32]{2,3,1,0:T(8,128)S(1)}, f32[1,4,108,32]{2,3,1,0:T(8,128)}, u32[]{:S(2)}) copy-start(f32[1,4,108,32]{2,3,1,0:T(8,128)} %param.17) | copy-start | bytes 165892
  18.7 10.0 %copy-start.4 = (f32[1,4,108,32]{2,3,1,0:T(8,128)S(1)}, f32[1,4,108,32]{2,3,1,0:T(8,128)}, u32[]{:S(2)}) copy-start(f32[1,4,108,32]{2,3,1,0:T(8,128)} %param.16) | copy-start | bytes 165892
  18.7 10.0 %copy-start.5 = (f32[1,4,108,32]{2,3,1,0:T(8,128)S(1)}, f32[1,4,108,32]{2,3,1,0:T(8,128)}, u32[]{:S(2)}) copy-start(f32[1,4,108,32]{2,3,1,0:T(8,128)} %param.15) | copy-start | bytes 165892
  22.8 9.8 %collective-permute-start.6 = (f32[32,128]{1,0:T(8,128)S(1)}, f32[32,128]{1,0:T(8,128)S(1)}, u32[]{:S(2)}, u32[]{:S(2)}) collective-permute-start(f32[32,128]{1,0:T(8,128)S(1)} %get-tuple-element.71), channel_id=1, source_target_pairs={{0,1},{1,0},{2,3},{3,2},{4,5},{5,4},{6,7},{7,6},{8,9},{9,8},{10,11... | collective-permute-start | bytes 49160 | tf_op jit(solution)/shard_map/ppermute | solution.py:70
  27.1 5.4 %collective-permute-start.7 = (bf16[96,128]{1,0:T(8,128)(2,1)S(1)}, bf16[96,128]{1,0:T(8,128)(2,1)S(1)}, u32[]{:S(2)}, u32[]{:S(2)}) collective-permute-start(bf16[96,128]{1,0:T(8,128)(2,1)S(1)} %get-tuple-element.72), channel_id=1, source_target_pairs={{64,0},{128,64},{192,128},{65,1},{129,65},{193,129},{66,2},{130,66... | collective-permute-start | bytes 73736 | tf_op jit(solution)/shard_map/ppermute | solution.py:496
  36.8 5.2 %collective-permute-start.8 = (bf16[96,128]{1,0:T(8,128)(2,1)S(1)}, bf16[96,128]{1,0:T(8,128)(2,1)S(1)}, u32[]{:S(2)}, u32[]{:S(2)}) collective-permute-start(bf16[96,128]{1,0:T(8,128)(2,1)S(1)} %relay.2), channel_id=1, source_target_pairs={{64,0},{128,64},{192,128},{65,1},{129,65},{193,129},{66,2},{130,66... | collective-permute-start | bytes 73736 | tf_op jit(solution)/shard_map/ppermute | solution.py:496
  46.2 5.8 %collective-permute-start.9 = (bf16[96,128]{1,0:T(8,128)(2,1)S(1)}, bf16[96,128]{1,0:T(8,128)(2,1)S(1)}, u32[]{:S(2)}, u32[]{:S(2)}) collective-permute-start(bf16[96,128]{1,0:T(8,128)(2,1)S(1)} %relay.3), channel_id=1, source_target_pairs={{64,0},{128,64},{192,128},{65,1},{129,65},{193,129},{66,2},{130,66... | collective-permute-start | bytes 73736 | tf_op jit(solution)/shard_map/ppermute | solution.py:496
  53.4 3.5 %collective-permute-start.10 = (bf16[4,8,4,32,128]{4,3,2,1,0:T(8,128)(2,1)S(1)}, bf16[4,8,4,32,128]{4,3,2,1,0:T(8,128)(2,1)S(1)}, u32[]{:S(2)}, u32[]{:S(2)}) collective-permute-start(bf16[4,8,4,32,128]{4,3,2,1,0:T(8,128)(2,1)S(1)} %get-tuple-element.88), channel_id=1, source_target_pairs={{0,1},{1,0},{2,3},{3,2},{4,5},{5,4},{6,7},{7,6},{8,9},{9,8},{10,11... | collective-permute-start | bytes 3145736 | tf_op jit(solution)/shard_map/ppermute | solution.py:70
  57.2 8.1 %collective-permute-start.11 = (bf16[7,4,32,128]{3,2,1,0:T(8,128)(2,1)S(1)}, bf16[7,4,32,128]{3,2,1,0:T(8,128)(2,1)S(1)}, u32[]{:S(2)}, u32[]{:S(2)}) collective-permute-start(bf16[7,4,32,128]{3,2,1,0:T(8,128)(2,1)S(1)} %get-tuple-element.91), channel_id=1, source_target_pairs={{0,2},{1,3},{2,4},{3,5},{4,6},{5,7},{6,0},{7,1},{8,10},{9,11},{10,... | collective-permute-start | bytes 688136 | tf_op jit(solution)/shard_map/ppermute | solution.py:70
  57.3 8.0 %collective-permute-start.12 = (bf16[7,4,32,128]{3,2,1,0:T(8,128)(2,1)S(1)}, bf16[7,4,32,128]{3,2,1,0:T(8,128)(2,1)S(1)}, u32[]{:S(2)}, u32[]{:S(2)}) collective-permute-start(bf16[7,4,32,128]{3,2,1,0:T(8,128)(2,1)S(1)} %get-tuple-element.92), channel_id=1, source_target_pairs={{0,6},{1,7},{2,0},{3,1},{4,2},{5,3},{6,4},{7,5},{8,14},{9,15},{10,... | collective-permute-start | bytes 688136 | tf_op jit(solution)/shard_map/ppermute | solution.py:70
  60.0 13.8 %collective-permute-start.14 = (f32[3,4,32,108]{3,2,1,0:T(8,128)S(1)}, f32[3,4,32,108]{3,2,1,0:T(8,128)S(1)}, u32[]{:S(2)}, u32[]{:S(2)}) collective-permute-start(f32[3,4,32,108]{3,2,1,0:T(8,128)S(1)} %pad_maximum_fusion.state_ref), channel_id=1, source_target_pairs={{0,56},{1,57},{2,58},{3,59},{4,60},{5,61},{6,62},{7,63},{8,48},{9,... | collective-permute-start | bytes 497672 | tf_op jit(solution)/shard_map/ppermute | solution.py:70
  65.4 8.4 %collective-permute-start.13 = (bf16[5,4,32,128]{3,2,1,0:T(8,128)(2,1)S(1)}, bf16[5,4,32,128]{3,2,1,0:T(8,128)(2,1)S(1)}, u32[]{:S(2)}, u32[]{:S(2)}) collective-permute-start(bf16[5,4,32,128]{3,2,1,0:T(8,128)(2,1)S(1)} %get-tuple-element.97), channel_id=1, source_target_pairs={{0,2},{1,3},{2,4},{3,5},{4,6},{5,7},{6,0},{7,1},{8,10},{9,11},{10,... | collective-permute-start | bytes 491528 | tf_op jit(solution)/shard_map/ppermute | solution.py:70
  65.5 8.3 %collective-permute-start.15 = (bf16[5,4,32,128]{3,2,1,0:T(8,128)(2,1)S(1)}, bf16[5,4,32,128]{3,2,1,0:T(8,128)(2,1)S(1)}, u32[]{:S(2)}, u32[]{:S(2)}) collective-permute-start(bf16[5,4,32,128]{3,2,1,0:T(8,128)(2,1)S(1)} %get-tuple-element.100), channel_id=1, source_target_pairs={{0,6},{1,7},{2,0},{3,1},{4,2},{5,3},{6,4},{7,5},{8,14},{9,15},{10,... | collective-permute-start | bytes 491528 | tf_op jit(solution)/shard_map/ppermute | solution.py:70
  74.0 5.0 %collective-permute-start.16 = (bf16[2,4,32,128]{3,2,1,0:T(8,128)(2,1)S(1)}, bf16[2,4,32,128]{3,2,1,0:T(8,128)(2,1)S(1)}, u32[]{:S(2)}, u32[]{:S(2)}) collective-permute-start(bf16[2,4,32,128]{3,2,1,0:T(8,128)(2,1)S(1)} %get-tuple-element.102), channel_id=1, source_target_pairs={{0,24},{1,25},{2,26},{3,27},{4,28},{5,29},{6,30},{7,31},{8,16},{9,... | collective-permute-start | bytes 196616 | tf_op jit(solution)/shard_map/ppermute | solution.py:70
  75.7 6.6 %collective-permute-start.17 = (bf16[2,4,32,128]{3,2,1,0:T(8,128)(2,1)S(1)}, bf16[2,4,32,128]{3,2,1,0:T(8,128)(2,1)S(1)}, u32[]{:S(2)}, u32[]{:S(2)}) collective-permute-start(bf16[2,4,32,128]{3,2,1,0:T(8,128)(2,1)S(1)} %get-tuple-element.103), channel_id=1, source_target_pairs={{0,16},{1,17},{2,18},{3,19},{4,20},{5,21},{6,22},{7,23},{8,24},{9,... | collective-permute-start | bytes 196616 | tf_op jit(solution)/shard_map/ppermute | solution.py:70
  75.7 6.6 %collective-permute-start.18 = (bf16[2,4,32,128]{3,2,1,0:T(8,128)(2,1)S(1)}, bf16[2,4,32,128]{3,2,1,0:T(8,128)(2,1)S(1)}, u32[]{:S(2)}, u32[]{:S(2)}) collective-permute-start(bf16[2,4,32,128]{3,2,1,0:T(8,128)(2,1)S(1)} %get-tuple-element.104), channel_id=1, source_target_pairs={{0,8},{1,9},{2,10},{3,11},{4,12},{5,13},{6,14},{7,15},{8,0},{9,1},... | collective-permute-start | bytes 196616 | tf_op jit(solution)/shard_map/ppermute | solution.py:70
  82.3 5.1 %collective-permute-start.19 = (bf16[2,4,32,128]{3,2,1,0:T(8,128)(2,1)S(1)}, bf16[2,4,32,128]{3,2,1,0:T(8,128)(2,1)S(1)}, u32[]{:S(2)}, u32[]{:S(2)}) collective-permute-start(bf16[2,4,32,128]{3,2,1,0:T(8,128)(2,1)S(1)} %z_sum.1.mine_ref), channel_id=1, source_target_pairs={{0,56},{1,57},{2,58},{3,59},{4,60},{5,61},{6,62},{7,63},{8,48},{9,... | collective-permute-start | bytes 196616 | tf_op jit(solution)/shard_map/ppermute | solution.py:70
  88.1 7.5 %collective-permute-start.22 = (bf16[2,4,32,128]{3,2,1,0:T(8,128)(2,1)S(1)}, bf16[2,4,32,128]{3,2,1,0:T(8,128)(2,1)S(1)}, u32[]{:S(2)}, u32[]{:S(2)}) collective-permute-start(bf16[2,4,32,128]{3,2,1,0:T(8,128)(2,1)S(1)} %get-tuple-element.106), channel_id=1, source_target_pairs={{0,24},{1,25},{2,26},{3,27},{4,28},{5,29},{6,30},{7,31},{8,16},{9,... | collective-permute-start | bytes 196616 | tf_op jit(solution)/shard_map/ppermute | solution.py:70
  89.5 6.2 %collective-permute-start.21 = (bf16[2,4,32,128]{3,2,1,0:T(8,128)(2,1)S(1)}, bf16[2,4,32,128]{3,2,1,0:T(8,128)(2,1)S(1)}, u32[]{:S(2)}, u32[]{:S(2)}) collective-permute-start(bf16[2,4,32,128]{3,2,1,0:T(8,128)(2,1)S(1)} %get-tuple-element.106), channel_id=1, source_target_pairs={{0,16},{1,17},{2,18},{3,19},{4,20},{5,21},{6,22},{7,23},{8,24},{9,... | collective-permute-start | bytes 196616 | tf_op jit(solution)/shard_map/ppermute | solution.py:70
  90.0 3.9 %collective-permute-start.20 = (bf16[2,4,32,128]{3,2,1,0:T(8,128)(2,1)S(1)}, bf16[2,4,32,128]{3,2,1,0:T(8,128)(2,1)S(1)}, u32[]{:S(2)}, u32[]{:S(2)}) collective-permute-start(bf16[2,4,32,128]{3,2,1,0:T(8,128)(2,1)S(1)} %get-tuple-element.106), channel_id=1, source_target_pairs={{0,8},{1,9},{2,10},{3,11},{4,12},{5,13},{6,14},{7,15},{8,0},{9,1},... | collective-permute-start | bytes 196616 | tf_op jit(solution)/shard_map/ppermute | solution.py:70
  95.7 7.1 %collective-permute-start.25 = (bf16[8,4,32,128]{3,2,1,0:T(8,128)(2,1)S(1)}, bf16[8,4,32,128]{3,2,1,0:T(8,128)(2,1)S(1)}, u32[]{:S(2)}, u32[]{:S(2)}) collective-permute-start(bf16[8,4,32,128]{3,2,1,0:T(8,128)(2,1)S(1)} %constant_dynamic-update-slice_fusion.refs_0_), channel_id=1, source_target_pairs={{0,2},{1,3},{2,4},{3,5},{4,6},{5,7},{6,0},{7,1},{8,10},{9,11},{10,... | collective-permute-start | bytes 786440 | tf_op jit(solution)/shard_map/ppermute | solution.py:70
  95.8 12.7 %collective-permute-start.24 = (bf16[8,4,32,128]{3,2,1,0:T(8,128)(2,1)S(1)}, bf16[8,4,32,128]{3,2,1,0:T(8,128)(2,1)S(1)}, u32[]{:S(2)}, u32[]{:S(2)}) collective-permute-start(bf16[8,4,32,128]{3,2,1,0:T(8,128)(2,1)S(1)} %constant_dynamic-update-slice_fusion.refs_0_), channel_id=1, source_target_pairs={{0,6},{1,7},{2,0},{3,1},{4,2},{5,3},{6,4},{7,5},{8,14},{9,15},{10,... | collective-permute-start | bytes 786440 | tf_op jit(solution)/shard_map/ppermute | solution.py:70
  98.5 12.1 %collective-permute-start.23 = (bf16[8,4,32,128]{3,2,1,0:T(8,128)(2,1)S(1)}, bf16[8,4,32,128]{3,2,1,0:T(8,128)(2,1)S(1)}, u32[]{:S(2)}, u32[]{:S(2)}) collective-permute-start(bf16[8,4,32,128]{3,2,1,0:T(8,128)(2,1)S(1)} %constant_dynamic-update-slice_fusion.refs_0_), channel_id=1, source_target_pairs={{0,4},{1,5},{2,6},{3,7},{4,0},{5,1},{6,2},{7,3},{8,12},{9,13},{10,... | collective-permute-start | bytes 786440 | tf_op jit(solution)/shard_map/ppermute | solution.py:70
  98.5 13.0 %collective-permute-start.26 = (bf16[8,4,32,128]{3,2,1,0:T(8,128)(2,1)S(1)}, bf16[8,4,32,128]{3,2,1,0:T(8,128)(2,1)S(1)}, u32[]{:S(2)}, u32[]{:S(2)}) collective-permute-start(bf16[8,4,32,128]{3,2,1,0:T(8,128)(2,1)S(1)} %constant_dynamic-update-slice_fusion.refs_0_), channel_id=1, source_target_pairs={{0,1},{1,0},{2,3},{3,2},{4,5},{5,4},{6,7},{7,6},{8,9},{9,8},{10,11... | collective-permute-start | bytes 786440 | tf_op jit(solution)/shard_map/ppermute | solution.py:70
  102.8 8.7 %collective-permute-start.29 = (bf16[8,4,32,128]{3,2,1,0:T(8,128)(2,1)S(1)}, bf16[8,4,32,128]{3,2,1,0:T(8,128)(2,1)S(1)}, u32[]{:S(2)}, u32[]{:S(2)}) collective-permute-start(bf16[8,4,32,128]{3,2,1,0:T(8,128)(2,1)S(1)} %collective-permute-done.25.refs_3_), channel_id=1, source_target_pairs={{0,1},{1,0},{2,3},{3,2},{4,5},{5,4},{6,7},{7,6},{8,9},{9,8},{10,11... | collective-permute-start | bytes 786440 | tf_op jit(solution)/shard_map/ppermute | solution.py:70
  108.5 3.2 %collective-permute-start.28 = (bf16[8,4,32,128]{3,2,1,0:T(8,128)(2,1)S(1)}, bf16[8,4,32,128]{3,2,1,0:T(8,128)(2,1)S(1)}, u32[]{:S(2)}, u32[]{:S(2)}) collective-permute-start(bf16[8,4,32,128]{3,2,1,0:T(8,128)(2,1)S(1)} %collective-permute-done.24.refs_2_), channel_id=1, source_target_pairs={{0,1},{1,0},{2,3},{3,2},{4,5},{5,4},{6,7},{7,6},{8,9},{9,8},{10,11... | collective-permute-start | bytes 786440 | tf_op jit(solution)/shard_map/ppermute | solution.py:70
  110.6 2.1 %collective-permute-start.27 = (bf16[8,4,32,128]{3,2,1,0:T(8,128)(2,1)S(1)}, bf16[8,4,32,128]{3,2,1,0:T(8,128)(2,1)S(1)}, u32[]{:S(2)}, u32[]{:S(2)}) collective-permute-start(bf16[8,4,32,128]{3,2,1,0:T(8,128)(2,1)S(1)} %collective-permute-done.23.refs_1_), channel_id=1, source_target_pairs={{0,1},{1,0},{2,3},{3,2},{4,5},{5,4},{6,7},{7,6},{8,9},{9,8},{10,11... | collective-permute-start | bytes 786440 | tf_op jit(solution)/shard_map/ppermute | solution.py:70
